TPU v7x, 128 devices: a whole 4x4x4 slice. The times are simulated.
128 devices in a mesh: sens: 8 (over z, core), layer: 16 (over y, x).
Axes of the slice: x: 4, y: 4, z: 4, core: 2. Of those that a mesh axis runs over, the one named last changes fastest.
Arguments:
- slopes: bfloat16 [1024, 63600], P('layer', 'sens'), may hold values from -7 to 7
- valid: int32 [63600], P('sens'), may hold values from 0 to 1
- sensor_map: int32 [63600], P('sens'), may hold values from 0 to 5, as said below
- reconstructor: bfloat16 [16000, 63600], P('layer', 'sens'), may hold values from -0.0234375 to 0.0234375
- fitting: bfloat16 [7800, 16000], P('sens', 'layer'), may hold values from -0.046875 to 0.046875
Outputs:
- commands: float32 [1024, 7800], P(('sens', 'layer'))
Inputs may be any that keep to these rules, and one draw needn't show every extreme that they name: `sensor_map`: both slopes of a subaperture (indices 2 i and 2 i + 1) belong to one sensor.
All inputs are finite; a program needn't handle non-finite values.
Results may differ from a plain program's by a relative error of at most 0.02.
Values may be sent and summed in bfloat16 or wider, within the bound.
No kernel may reach another device: no remote copies, remote signals or barrier semaphores. Data moves between devices by JAX's collectives and lax.ppermute only.
A program may use at most 192 MiB of HBM per device.

v0:
```python
import jax
import jax.numpy as jnp
from jax import lax
from jax.sharding import PartitionSpec as P

SENSORS = 6


def copy_for_each(x, axis):
    length = lax.axis_size(axis)
    return lax.all_to_all(jnp.broadcast_to(x[None], (length, *x.shape)), axis, 0, 0, tiled=True)


def taken_together(x, axis):
    everything = copy_for_each(x, axis)
    return jnp.sum(everything.astype(jnp.float32), axis=0)


def cut_along(x, dim, length):
    dims = x.shape
    blocks = x.reshape(*dims[:dim], length, dims[dim] // length, *dims[dim + 1 :])
    return jnp.moveaxis(blocks, dim, 0)


def summed_on_arrival(x, axis, dim):
    blocks = cut_along(x, dim, lax.axis_size(axis))
    arrived = lax.all_to_all(blocks, axis, split_axis=0, concat_axis=0, tiled=True)
    return arrived.astype(jnp.float32).sum(axis=0)


def contract(left, right):
    return lax.dot_general(
        left, right, (((1,), (1,)), ((), ())), preferred_element_type=jnp.float32
    )


def cleaned(block, live, onehot_full, sums, counts):
    means = sums / jnp.maximum(counts, 1.0)
    spread = lax.dot_general(
        means, onehot_full, (((1,), (1,)), ((), ())), precision=lax.Precision.HIGHEST
    )
    return (live.astype(jnp.float32)[None, :] * (block.astype(jnp.float32) - spread)).astype(
        jnp.bfloat16
    )


def per_device(slopes, valid, sensor_map, reconstructor, fitting):
    width_local = slopes.shape[1]
    start = lax.axis_index("sens") * width_local
    parity = (lax.iota(jnp.int32, width_local) + start) % 2
    group = sensor_map * 2 + parity
    labels = lax.iota(jnp.int32, 2 * SENSORS)
    onehot_full = (group[:, None] == labels[None, :]).astype(jnp.float32)
    onehot_low = onehot_full.astype(jnp.bfloat16)
    live = valid.astype(jnp.bfloat16)
    count_terms = jnp.dot(live[None, :], onehot_low, preferred_element_type=jnp.float32)[0]
    whole = lax.all_gather(slopes, "layer", axis=0, tiled=True)
    masked = whole * live[None, :]
    sums = jnp.dot(masked, onehot_low, preferred_element_type=jnp.float32)
    sums, counts = (
        taken_together(sums.astype(jnp.bfloat16), "sens").astype(jnp.float32),
        taken_together(count_terms.astype(jnp.bfloat16), "sens").astype(jnp.float32),
    )
    clean = cleaned(whole, live, onehot_full, sums, counts)
    partial_points = contract(clean, reconstructor)
    points = summed_on_arrival(partial_points.astype(jnp.bfloat16), "sens", 0).astype(jnp.bfloat16)
    partial_commands = contract(points, lax.all_gather(fitting, "sens", axis=0, tiled=True))
    return summed_on_arrival(partial_commands.astype(jnp.bfloat16), "layer", 0)


def solution(mesh):
    placed = (P("layer", "sens"), P("sens"), P("sens"), P("layer", "sens"), P("sens", "layer"))
    return jax.shard_map(
        per_device,
        mesh=mesh,
        in_specs=placed,
        out_specs=P(("sens", "layer"), None),
        check_vma=False,
    )
```

profile of v0, /device:TPU:24, one launch (start us, length us, event | category | flops | bytes accessed | tf_op | source)
XLA Modules:
  0.0 281.7 jit_solution(14590893099064575598)
XLA Ops:
  6.5 0.7 all-gather.4.cloned.1.call-update
  7.3 0.0 all-gather.6.cloned.1.call-start
  7.3 0.7 all-gather.6.cloned.1.call-update
  8.0 0.8 fusion.17
  8.8 0.2 fusion.6
  9.0 10.4 %all_to_all.21 = bf16[8,1,12]{2,1,0:T(2,128)(2,1)S(1)} all-to-all(bf16[8,1,12]{2,1,0:T(2,128)(2,1)S(1)} %broadcast_in_dim.5), channel_id=1, replica_groups=mesh['sens'=8,'layer'=16] {'sens'}, dimensions={0} | all-to-all | bytes 384 | tf_op jit(solution)/shard_map/all_to_all | solution.py:11
  19.5 102.0 %all-gather.4.cloned.1.call-done = bf16[1024,7950]{1,0:T(8,128)(2,1)} async-done(((bf16[64,7950]{1,0:T(8,128)(2,1)}), bf16[1024,7950]{1,0:T(8,128)(2,1)}) %all-gather.4.cloned.1.call-update) | async-done | bytes 16281616 | tf_op jit(solution)/shard_map/all_gather | solution.py:57
  121.4 10.0 %fusion.3 = bf16[1024,12]{0,1:T(8,128)(2,1)S(1)} fusion(bf16[1024,7950]{1,0:T(8,128)(2,1)} %all-gather.4.cloned.1.call-done, bf16[7950]{0:T(1024)(128)(2,1)S(1)} %get-tuple-element.6, s32[7950]{0:T(1024)S(1)} %get-tuple-element.7), kind=kOutput, calls=%fused_computation.8 | convolution fusion | flops 203818496 | bytes 16353876 | tf_op jit(solution)/shard_map/dot_general | solution.py:59
  131.5 0.8 broadcast_in_dim.4
  132.3 4.4 %all-to-all-start = ((bf16[8,1024,12]{1,2,0:T(8,128)(2,1)}), bf16[8,1024,12]{1,2,0:T(8,128)(2,1)S(1)}, u32[]{:S(2)}, u32[]{:S(2)}) async-start(bf16[8,1024,12]{1,2,0:T(8,128)(2,1)} %broadcast_in_dim.4), calls=%async_computation | async-start | bytes 524288 | tf_op jit(solution)/shard_map/all_to_all | solution.py:11
  136.7 22.4 %copy.24 = bf16[1024,7950]{0,1:T(8,128)(2,1)} copy(bf16[1024,7950]{1,0:T(8,128)(2,1)} %all-gather.4.cloned.1.call-done) | data formatting | bytes 32563200 | tf_op jit(solution)/shard_map/all_gather | solution.py:57
  159.1 0.0 all-to-all-done
  159.1 19.0 %multiply_convert_fusion = bf16[1024,7950]{0,1:T(8,128)(2,1)S(1)} fusion(bf16[1024,7950]{0,1:T(8,128)(2,1)} %copy.24, f32[7950]{0:T(1024)S(1)} %get-tuple-element.5, s32[7950]{0:T(1024)S(1)} %get-tuple-element.7, f32[1024,12]{0,1:T(8,128)S(1)} %convert_reduce_fusion.1, f32[12]{0:T(128)S(1)} %broadcast_maximum_fusion), kind=kOutput, calls=%fused_computation | convolution fusion | flops 1204946048 | bytes 32676000 | tf_op jit(solution)/shard_map/dot_general | solution.py:39
  178.1 20.7 %convert_bitcast_fusion = bf16[125,8,8,128]{3,2,1,0:T(8,128)(2,1)S(1)} fusion(bf16[1024,7950]{0,1:T(8,128)(2,1)S(1)} %multiply_convert_fusion, bf16[1000,7950]{1,0:T(8,128)(2,1)} %param.8), kind=kOutput, calls=%fused_computation.7 | convolution fusion | flops 16282624000 | bytes 34229600 | tf_op jit(solution)/shard_map/dot_general | solution.py:32
  198.8 1.6 copy.33
  200.5 4.7 %all-to-all-start.2 = ((bf16[8,128,1000]{1,2,0:T(8,128)(2,1)}), bf16[8,128,1000]{1,2,0:T(8,128)(2,1)S(1)}, u32[]{:S(2)}, u32[]{:S(2)}) async-start(bf16[8,128,1000]{1,2,0:T(8,128)(2,1)} %bitcast.16), calls=%async_computation.2 | async-start | bytes 4096000 | tf_op jit(solution)/shard_map/all_to_all | solution.py:27
  205.2 2.4 all-gather.6.cloned.1.call-done
  207.6 20.5 %reshape.30 = bf16[7800,1000]{1,0:T(8,128)(2,1)} reshape(bf16[8,975,1000]{2,1,0:T(8,128)(2,1)} %all-gather.6.cloned.1.call-done) | data formatting | bytes 31200000
  228.2 3.7 %all-to-all-done.2 = bf16[8,128,1000]{1,2,0:T(8,128)(2,1)S(1)} async-done(((bf16[8,128,1000]{1,2,0:T(8,128)(2,1)}), bf16[8,128,1000]{1,2,0:T(8,128)(2,1)S(1)}, u32[]{:S(2)}, u32[]{:S(2)}) %all-to-all-start.2) | async-done | bytes 2048032 | tf_op jit(solution)/shard_map/all_to_all | solution.py:27
  231.9 0.4 reduce_sum.41
  232.3 9.3 %convolution_convert_fusion = bf16[128,7800]{0,1:T(8,128)(2,1)} fusion(bf16[128,1000]{0,1:T(8,128)(2,1)S(1)} %reduce_sum.41, bf16[7800,1000]{1,0:T(8,128)(2,1)} %reshape.30), kind=kOutput, calls=%fused_computation.3 | convolution fusion | flops 1997798400 | bytes 17852800 | tf_op jit(solution)/shard_map/dot_general | solution.py:32
  241.6 2.9 %copy.28 = bf16[128,7800]{1,0:T(8,128)(2,1)S(1)} copy(bf16[128,7800]{0,1:T(8,128)(2,1)} %convolution_convert_fusion) | data formatting | bytes 3993600 | tf_op jit(solution)/shard_map/convert_element_type | solution.py:68
  244.4 29.5 %all_to_all.22 = bf16[16,8,7800]{2,1,0:T(8,128)(2,1)S(1)} all-to-all(bf16[16,8,7800]{2,1,0:T(8,128)(2,1)S(1)} %bitcast.17), channel_id=1, replica_groups=mesh['sens'=8,'layer'=16] {'layer'}, dimensions={0} | all-to-all | bytes 3993600 | tf_op jit(solution)/shard_map/all_to_all | solution.py:27
  273.9 1.0 convert_reduce_fusion
  (6 shorter events, 0.1 us)
Async XLA Ops:
  6.5 114.9 %all-gather.4.cloned.1.call-start = ((), (), s32[]{:S(2)}) async-start(), calls=%async_computation.4 | async-start | bytes 17547264 | tf_op jit(solution)/shard_map/all_gather | solution.py:57
  7.3 200.4 %all-gather.6.cloned.1.call-start = ((), (), s32[]{:S(2)}) async-start(), calls=%async_computation.5 | async-start | bytes 17989632 | tf_op jit(solution)/shard_map/all_gather | solution.py:67
  132.3 26.8 %all-to-all-start = ((bf16[8,1024,12]{1,2,0:T(8,128)(2,1)}), bf16[8,1024,12]{1,2,0:T(8,128)(2,1)S(1)}, u32[]{:S(2)}, u32[]{:S(2)}) async-start(bf16[8,1024,12]{1,2,0:T(8,128)(2,1)} %broadcast_in_dim.4), calls=%async_computation | async-start | bytes 524288 | tf_op jit(solution)/shard_map/all_to_all | solution.py:11
  200.5 31.4 %all-to-all-start.2 = ((bf16[8,128,1000]{1,2,0:T(8,128)(2,1)}), bf16[8,128,1000]{1,2,0:T(8,128)(2,1)S(1)}, u32[]{:S(2)}, u32[]{:S(2)}) async-start(bf16[8,128,1000]{1,2,0:T(8,128)(2,1)} %bitcast.16), calls=%async_computation.2 | async-start | bytes 4096000 | tf_op jit(solution)/shard_map/all_to_all | solution.py:27
Sparse Core Ops, SparseCore 0:
  9.5 111.8 all-gather.3
  123.1 84.4 all-gather.5
where the time goes:
time: 285 us; the launch traced here: 282 us
  waiting for transfers between devices  110 us (39%)
  matrix products  59.2 us (21%)
  local copies, waits for them, and re-layouts  48.2 us (17%)
  blocking collectives  39.9 us (14%)
  between operations  13.5 us (5%)
  starting transfers between devices  9.18 us (3%)
    all_gather x1, waiting for transfers between devices, per_device(): whole = lax.all_gather(slopes, 'layer', axis=0, tiled=True)  102 us
    dot_general x2, matrix products, contract(): lax.dot_general(left, right, (((1,), (1,)), ((), ())), preferred_element_...  30 us
    all_to_all x1, blocking collectives, summed_on_arrival(): lax.all_to_all(blocks, axis, split_axis=0, concat_axis=0, tiled=True)  29.5 us
    all_gather x1, local copies, waits for them, and re-layouts, per_device(): whole = lax.all_gather(slopes, 'layer', axis=0, tiled=True)  22.4 us
    unnamed x1, local copies, waits for them, and re-layouts  20.5 us
    dot_general x1, matrix products, cleaned(): lax.dot_general(means, onehot_full, (((1,), (1,)), ((), ())), precision=l...  19 us
    all_to_all x1, blocking collectives, copy_for_each(): lax.all_to_all(jnp.broadcast_to(x[None], (length, *x.shape)), axis, 0, 0,...  10.4 us
    dot_general x1, matrix products, per_device(): sums = jnp.dot(masked, onehot_low, preferred_element_type=jnp.float32)  10 us
  transfers between devices with their start and end apart: 4, of which 3 were waited for; matrix products, arithmetic and copies ran while one was open for 34% of the time, Pallas kernels for 0%

commit v1 on v0

v1 whole, which is shorter than its diff:
```python
import functools

import jax
import jax.numpy as jnp
import numpy as np
from jax import lax
from jax.experimental import pallas as pl
from jax.experimental.pallas import tpu as pltpu
from jax.sharding import PartitionSpec as P

SENSORS = 6
GROUPS = 2 * SENSORS
AXES = ("sens", "layer")
SIDE = 4
ROWS = 64
QUARTER = 2048
LAST = 1920
PBLOCK = 256


def moved(fn):
    pairs = []
    for z in range(4):
        for c in range(2):
            for y in range(4):
                for x in range(4):
                    z2, c2, y2, x2 = fn(z, c, y, x)
                    pairs.append(
                        ((z * 2 + c) * 16 + y * 4 + x,
                         ((z2 % 4) * 2 + c2 % 2) * 16 + (y2 % 4) * 4 + x2 % 4)
                    )
    return pairs


def send(x, fn):
    return lax.ppermute(x, AXES, moved(fn))


def ring_x(v):
    return send(v, lambda z, c, y, x: (z, c, y, x + 1 - 2 * c))


def ring_y(v):
    return send(v, lambda z, c, y, x: (z, c, y + 1 - 2 * c, x))


def ring(v, step):
    held = [v]
    for _ in range(3):
        held.append(step(held[-1]))
    return held


def nt(a, b):
    return lax.dot_general(a, b, (((1,), (1,)), ((), ())), preferred_element_type=jnp.float32)


def mm_kernel(first, idx, x0, x1, r, *rest):
    if first:
        acc, out = rest
        val = nt(x0[...], r[:, :QUARTER]) + nt(x1[...], r[:, QUARTER:])
    else:
        rw, acc, out = rest
        cut = LAST - 128
        lane = lax.broadcasted_iota(jnp.int32, (r.shape[0], 128), 1)
        edge = r[:, QUARTER + cut : QUARTER + LAST]
        edge = jnp.where(lane < 14, edge.astype(jnp.float32), 0.0).astype(jnp.bfloat16)
        tail = x1[:, cut:]
        val = nt(x0[...], r[:, :QUARTER]) + nt(x1[:, :cut], r[:, QUARTER : QUARTER + cut])
        val = val + nt(tail, edge)
        val = val + lax.dot_general(
            tail.astype(jnp.float32), rw[...], (((1,), (1,)), ((), ())),
            preferred_element_type=jnp.float32, precision=lax.Precision.HIGHEST,
        )
    for u in range(SIDE):
        part = val[u * ROWS : (u + 1) * ROWS]
        w = idx[1 + u]
        if first:
            out[0, w] = acc[0, w] + part
        else:
            out[w, 0] = acc[w, 0] + part


def accumulate(first, idx, x0, x1, r, rw, acc):
    n = SIDE * ROWS
    blocks = pl.cdiv(r.shape[0], PBLOCK)
    half = 0 if first else 1
    if first:
        acc_spec = pl.BlockSpec((1, SIDE, ROWS, PBLOCK), lambda j, i: (i[0], 0, 0, j))
    else:
        acc_spec = pl.BlockSpec((SIDE, 1, ROWS, PBLOCK), lambda j, i: (0, i[0], 0, j))
    specs = [
        pl.BlockSpec((n, x0.shape[1]), lambda j, i: (0, 0)),
        pl.BlockSpec((n, x1.shape[1]), lambda j, i: (0, 0)),
        pl.BlockSpec((PBLOCK, 2 * QUARTER), lambda j, i: (j, half)),
    ]
    args = [x0, x1, r]
    if not first:
        specs.append(pl.BlockSpec((PBLOCK, 128), lambda j, i: (j, 0)))
        args.append(rw)
    specs.append(acc_spec)
    args.append(acc)
    return pl.pallas_call(
        functools.partial(mm_kernel, first),
        grid_spec=pltpu.PrefetchScalarGridSpec(
            num_scalar_prefetch=1, grid=(blocks,), in_specs=specs, out_specs=acc_spec
        ),
        out_shape=jax.ShapeDtypeStruct(acc.shape, acc.dtype),
        input_output_aliases={len(args): 0},
        compiler_params=pltpu.CompilerParams(vmem_limit_bytes=40 * 2**20),
        cost_estimate=pl.CostEstimate(
            flops=2 * n * 4096 * 1000, bytes_accessed=12 * 2**20, transcendentals=0
        ),
    )(idx, *args)


def fit_kernel(p, f, out):
    out[0] = nt(p[...], f[0]).astype(jnp.bfloat16)


def fit(points, fitting, start, count):
    n, k = points.shape
    m = fitting.shape[1]
    return pl.pallas_call(
        fit_kernel,
        grid=(count,),
        in_specs=[
            pl.BlockSpec((n, k), lambda s: (0, 0)),
            pl.BlockSpec((1, m, k), lambda s: (s + start, 0, 0)),
        ],
        out_specs=pl.BlockSpec((1, n, m), lambda s: (s, 0, 0)),
        out_shape=jax.ShapeDtypeStruct((count, n, m), jnp.bfloat16),
        compiler_params=pltpu.CompilerParams(vmem_limit_bytes=40 * 2**20),
        cost_estimate=pl.CostEstimate(
            flops=2 * n * m * k * count, bytes_accessed=2 * count * m * k, transcendentals=0
        ),
    )(points, fitting)


def summed(blocks, mine, hop, size):
    def pick(d):
        return lax.dynamic_index_in_dim(blocks, (mine + d) % size, 0, keepdims=False)

    got = [send(pick(d).astype(jnp.bfloat16), hop(d)) for d in (1, 3, 2)]
    total = pick(0).astype(jnp.float32)
    for g in got:
        total = total + g.astype(jnp.float32)
    return total


def per_device(slopes, valid, sensor_map, reconstructor, fitting):
    s_idx = lax.axis_index("sens")
    l_idx = lax.axis_index("layer")
    z, c = s_idx // 2, s_idx % 2
    y, x = l_idx // 4, l_idx % 4
    width = slopes.shape[1]
    sign = 1 - 2 * c
    spread = jnp.arange(SIDE, dtype=jnp.int32)
    ys = (y - sign * spread + 4) % 4
    xs = (x - sign * spread + 4) % 4

    everything = lax.all_gather(fitting, "sens", axis=0)

    masked = slopes * valid.astype(jnp.bfloat16)[None, :]
    group = sensor_map * 2 + (lax.iota(jnp.int32, width) + s_idx * width) % 2
    lane = lax.iota(jnp.int32, 128)
    label = jnp.where(lane < 26, lane - 14, lane - 26)
    label = jnp.where((lane >= 14) & (lane < 38), label, -1)
    member = ((group[None, :] == label[:, None]) & (valid[None, :] == 1)).astype(jnp.bfloat16)

    x_first = [masked[:, :QUARTER], masked[:, QUARTER : 2 * QUARTER]]
    y_first = [masked[:, 2 * QUARTER : 3 * QUARTER]]

    sums = nt(masked, member)
    counts = jnp.sum(member.astype(jnp.float32), axis=1)
    stats = jnp.concatenate([sums, jnp.broadcast_to(counts[None], (8, 128))], axis=0)
    stats = stats + send(stats, lambda z, c, y, x: (z, c + 1, y, x))
    others = [send(stats, lambda z, c, y, x, d=d: (z + d, c, y, x)) for d in (1, 3, 2)]
    stats = (stats + others[2]) + (others[0] + others[1])
    means = stats[:ROWS] / jnp.maximum(stats[ROWS:ROWS + 1], 1.0)
    high = lax.reduce_precision(means, 8, 7)
    low = means - high
    rows = jnp.where(lane[None, :] < 26, high, low)
    rows = jnp.where((lane[None, :] >= 14) & (lane[None, :] < 38), rows, 0.0).astype(jnp.bfloat16)
    last = masked[:, 3 * QUARTER :]
    last = jnp.pad(last, ((0, 0), (0, LAST - last.shape[1])))
    last = last + jnp.pad(rows, ((0, 0), (LAST - 128, 0)))
    y_first.append(last)

    rw = -nt(reconstructor, member)

    def gathered(v, one, two):
        block = jnp.concatenate(ring(v, one), axis=0)
        return ring(block, two)

    a = [gathered(v, ring_x, ring_y) for v in x_first]
    b = [gathered(v, ring_y, ring_x) for v in y_first]

    acc = jnp.zeros((SIDE, SIDE, ROWS, reconstructor.shape[0]), jnp.float32)
    for t in range(SIDE):
        ia = jnp.concatenate([ys[t : t + 1], xs])
        acc = accumulate(True, ia, a[0][t], a[1][t], reconstructor, None, acc)
        ib = jnp.concatenate([xs[t : t + 1], ys])
        acc = accumulate(False, ib, b[0][t], b[1][t], reconstructor, rw, acc)

    width_p = reconstructor.shape[0]
    cores = acc.reshape(SIDE, 2, 2 * ROWS, width_p)
    other = lax.dynamic_index_in_dim(cores, 1 - c, 1, keepdims=False).astype(jnp.bfloat16)
    mine = lax.dynamic_index_in_dim(cores, c, 1, keepdims=False)
    arrived = send(other, lambda z, c, y, x: (z, c + 1, y, x))
    layers = mine + arrived.astype(jnp.float32)
    points = summed(layers, z, lambda d: lambda z, c, y, x: (z + d, c, y, x), 4)
    points = points.astype(jnp.bfloat16)

    def hop_y(d):
        return lambda z, c, y, x: (z, c, y + d, x)

    def hop_x(d):
        return lambda z, c, y, x: (z, c, y, x + d)

    act = fitting.shape[0]
    out_a = fit(points, everything, 0, 4).reshape(4, 4, 4, 8, act)
    out_b = fit(points, everything, 4, 4).reshape(4, 4, 4, 8, act)
    part_a = summed(jnp.moveaxis(out_a, 1, 0), y, hop_y, 4)
    part_b = summed(jnp.moveaxis(out_b, 2, 0), x, hop_x, 4)
    done_a = summed(jnp.moveaxis(part_a, 1, 0), x, hop_x, 4)
    done_b = summed(jnp.moveaxis(part_b, 1, 0), y, hop_y, 4)
    done = jnp.concatenate([done_a, done_b], axis=0)
    return jnp.moveaxis(done, 0, 1).reshape(8, 8 * act)


def solution(mesh):
    placed = (P("layer", "sens"), P("sens"), P("sens"), P("layer", "sens"), P("sens", "layer"))
    return jax.shard_map(
        per_device,
        mesh=mesh,
        in_specs=placed,
        out_specs=P(("sens", "layer"), None),
        check_vma=False,
    )
```

time: 285 us -> 230 us (0.81)
  Pallas kernels: 0 us -> 64.6 us
  waiting for transfers between devices: 110 us -> 55.8 us
  starting transfers between devices: 9.18 us -> 58.3 us
  matrix products: 59.2 us -> 11.1 us
  local copies, waits for them, and re-layouts: 48.2 us -> 6.62 us
  blocking collectives: 39.9 us -> 0 us
  other arithmetic: 2.25 us -> 16.6 us
    all_gather x2 -> x1, waiting for transfers between devices: 104 us -> 0.02 us  [per_device(): everything = lax.all_gather(fitting, 'sens', axis=0)]
    pallas_call x0 -> x10, Pallas kernels: none -> 64.6 us  [the longest x8 53.4 us: accumulate(): pl.pallas_call(functools.partial(mm_kernel, first), grid_spec=pltpu.Prefe...]
    ppermute x0 -> x44, starting transfers between devices: none -> 58.3 us  [send(): return lax.ppermute(x, AXES, moved(fn))]
    ppermute x0 -> x44, waiting for transfers between devices: none -> 55 us  [send(): return lax.ppermute(x, AXES, moved(fn))]
    dot_general x5 -> x2, matrix products: 59.2 us -> 11.1 us  [nt(): lax.dot_general(a, b, (((1,), (1,)), ((), ())), preferred_element_type=jn...]
    all_to_all x2 -> x0, blocking collectives: 39.9 us -> none  [the longest x1 29.5 us: summed_on_arrival(): lax.all_to_all(blocks, axis, split_axis=0, concat_axis=0, tiled=True)]
    all_gather x1 -> x0, local copies, waits for them, and re-layouts: 22.4 us -> none  [per_device(): whole = lax.all_gather(slopes, 'layer', axis=0, tiled=True)]
    unnamed x1 -> x6, local copies, waits for them, and re-layouts: 20.5 us -> 1.95 us
  transfers between devices with their start and end apart: 4 -> 45, of which waited for: 3 -> 19; matrix products, arithmetic and copies ran while one was open for 34% -> 14% of each run, Pallas kernels for 0% -> 26%
where the time goes in v1:
time: 230 us; the launch traced here: 227 us
  Pallas kernels  64.6 us (28%)
  starting transfers between devices  58.3 us (25%)
  waiting for transfers between devices  55.8 us (24%)
  other arithmetic  16.6 us (7%)
  between operations  14.1 us (6%)
  matrix products  11.1 us (5%)
  local copies, waits for them, and re-layouts  6.62 us (3%)
    ppermute x44, starting transfers between devices, send(): return lax.ppermute(x, AXES, moved(fn))  58.3 us
    ppermute x44, waiting for transfers between devices, send(): return lax.ppermute(x, AXES, moved(fn))  55 us
    pallas_call x8, Pallas kernels, accumulate(): pl.pallas_call(functools.partial(mm_kernel, first), grid_spec=pltpu.Prefe...  53.4 us
    pallas_call x2, Pallas kernels, fit(): pl.pallas_call(fit_kernel, grid=(count,), in_specs=[pl.BlockSpec((n, k),...  11.2 us
    dot_general x2, matrix products, nt(): lax.dot_general(a, b, (((1,), (1,)), ((), ())), preferred_element_type=jn...  11.1 us
    reduce_sum x1, other arithmetic, per_device(): counts = jnp.sum(member.astype(jnp.float32), axis=1)  5.02 us
  transfers between devices with their start and end apart: 45, of which 19 were waited for; matrix products, arithmetic and copies ran while one was open for 14% of the time, Pallas kernels for 26%

profile of v1, /device:TPU:24, one launch (start us, length us, event | category | flops | bytes accessed | tf_op | source)
XLA Modules:
  0.0 227.1 jit_solution(16630504271020068784)
XLA Ops:
  8.8 5.0 %convert_reduce_fusion = f32[128]{0:T(128)S(1)} fusion(s32[128]{0:T(128)S(1)} %fusion.40, s32[7950]{0:T(1024)S(1)} %fusion.33, pred[7950]{0:T(1024)(128)(4,1)S(1)} %broadcast_compare_fusion), kind=kLoop, calls=%fused_computation | loop fusion | flops 5087872 | bytes 40774 | tf_op jit(solution)/shard_map/reduce_sum | solution.py:175
  19.6 4.0 %collective-permute-start.7 = (f32[72,128]{1,0:T(8,128)S(1)}, f32[72,128]{1,0:T(8,128)S(1)}, u32[]{:S(2)}, u32[]{:S(2)}) collective-permute-start(f32[72,128]{1,0:T(8,128)S(1)} %fusion.44), channel_id=1, source_target_pairs={{0,64},{1,65},{2,66},{3,67},{4,68},{5,69},{6,70},{7,71},{8,72},{9,... | collective-permute-start | bytes 110600 | tf_op jit(solution)/shard_map/ppermute | solution.py:36
  54.9 6.1 %collective-permute-done.19.x0 = bf16[256,2048]{1,0:T(8,128)(2,1)} collective-permute-done((bf16[256,2048]{1,0:T(8,128)(2,1)S(1)}, bf16[256,2048]{1,0:T(8,128)(2,1)}, u32[]{:S(2)}, u32[]{:S(2)}) %collective-permute-start.19) | collective-permute-done | bytes 1048608 | tf_op jit(solution)/shard_map/ppermute | solution.py:36
  61.0 3.6 %collective-permute-start.20 = (bf16[256,2048]{1,0:T(8,128)(2,1)}, bf16[256,2048]{1,0:T(8,128)(2,1)S(1)}, u32[]{:S(2)}, u32[]{:S(2)}) collective-permute-start(bf16[256,2048]{1,0:T(8,128)(2,1)} %collective-permute-done.19.x0), channel_id=1, source_target_pairs={{0,4},{1,5},{2,6},{3,7},{4,8},{5,9},{6,10},{7,11},{8,12},{9,13},{1... | collective-permute-start | bytes 3145736 | tf_op jit(solution)/shard_map/ppermute | solution.py:36
  64.6 7.6 %collective-permute-done.25.x1 = bf16[256,2048]{1,0:T(8,128)(2,1)} collective-permute-done((bf16[256,2048]{1,0:T(8,128)(2,1)S(1)}, bf16[256,2048]{1,0:T(8,128)(2,1)}, u32[]{:S(2)}, u32[]{:S(2)}) %collective-permute-start.25) | collective-permute-done | bytes 1048608 | tf_op jit(solution)/shard_map/ppermute | solution.py:36
  72.2 3.6 %collective-permute-start.26 = (bf16[256,2048]{1,0:T(8,128)(2,1)}, bf16[256,2048]{1,0:T(8,128)(2,1)S(1)}, u32[]{:S(2)}, u32[]{:S(2)}) collective-permute-start(bf16[256,2048]{1,0:T(8,128)(2,1)} %collective-permute-done.25.x1), channel_id=1, source_target_pairs={{0,4},{1,5},{2,6},{3,7},{4,8},{5,9},{6,10},{7,11},{8,12},{9,13},{1... | collective-permute-start | bytes 3145736 | tf_op jit(solution)/shard_map/ppermute | solution.py:36
  80.4 8.7 %fusion.10.rest_0_ = f32[1000,128]{1,0:T(8,128)S(1)} fusion(bf16[1000,7950]{1,0:T(8,128)(2,1)} %r.15, s32[128]{0:T(128)S(1)} %fusion.40, s32[7950]{0:T(1024)S(1)} %fusion.33, pred[7950]{0:T(1024)(128)(4,1)S(1)} %broadcast_compare_fusion), kind=kOutput, calls=%fused_computation.14 | convolution fusion | flops 2037363200 | bytes 16452262 | tf_op jit(solution)/shard_map/dot_general | solution.py:55
  89.3 5.3 %collective-permute-done.26.x1 = bf16[256,2048]{1,0:T(8,128)(2,1)S(1)} collective-permute-done((bf16[256,2048]{1,0:T(8,128)(2,1)}, bf16[256,2048]{1,0:T(8,128)(2,1)S(1)}, u32[]{:S(2)}, u32[]{:S(2)}) %collective-permute-start.26) | collective-permute-done | bytes 1048608 | tf_op jit(solution)/shard_map/ppermute | solution.py:36
  94.6 3.6 %collective-permute-start.27 = (bf16[256,2048]{1,0:T(8,128)(2,1)S(1)}, bf16[256,2048]{1,0:T(8,128)(2,1)S(1)}, u32[]{:S(2)}, u32[]{:S(2)}) collective-permute-start(bf16[256,2048]{1,0:T(8,128)(2,1)S(1)} %collective-permute-done.26.x1), channel_id=1, source_target_pairs={{0,4},{1,5},{2,6},{3,7},{4,8},{5,9},{6,10},{7,11},{8,12},{9,13},{1... | collective-permute-start | bytes 3145736 | tf_op jit(solution)/shard_map/ppermute | solution.py:36
  98.7 6.2 %shard_map.55.rest_1_ = f32[4,4,64,1000]{3,2,1,0:T(8,128)S(1)} custom-call(s32[5]{0:T(128)S(1)} %get-tuple-element.24.idx, bf16[256,2048]{1,0:T(8,128)(2,1)S(1)} %pad_maximum_fusion.1.x0, bf16[256,2048]{1,0:T(8,128)(2,1)S(1)} %pad_maximum_fusion.2.x1, bf16[1000,7950]{1,0:T(8,128)(2,1)} %r.15, ...), custom_call_target="tpu_custom_call", output_to_operand_aliasing={{}: (4, {})} | custom-call | flops 2097152000 | bytes 12582912 | tf_op jit(solution)/shard_map/pallas_call | solution.py:103
  105.5 7.0 %shard_map.56.rest_0_ = f32[4,4,64,1000]{3,2,1,0:T(8,128)S(1)} custom-call(s32[5]{0:T(128)S(1)} %get-tuple-element.32.idx, bf16[256,2048]{1,0:T(8,128)(2,1)S(1)} %pad_maximum_fusion.x0, bf16[256,1920]{1,0:T(8,128)(2,1)} %pad_maximum_fusion.3.x1, bf16[1000,7950]{1,0:T(8,128)(2,1)} %r.15, ...), custom_call_target="tpu_custom_call", output_to_operand_aliasing={{}: (5, {})} | custom-call | flops 2097152000 | bytes 12582912 | tf_op jit(solution)/shard_map/pallas_call | solution.py:103
  114.0 6.8 %shard_map.57.rest_1_ = f32[4,4,64,1000]{3,2,1,0:T(8,128)S(1)} custom-call(s32[5]{0:T(128)S(1)} %get-tuple-element.26.idx, bf16[256,2048]{1,0:T(8,128)(2,1)} %collective-permute-done.19.x0, bf16[256,2048]{1,0:T(8,128)(2,1)} %collective-permute-done.25.x1, bf16[1000,7950]{1,0:T(8,128)(2,1)} %r.15, ...), custom_call_target="tpu_custom_call", output_to_operand_aliasing={{}: (4, {})} | custom-call | flops 2097152000 | bytes 12582912 | tf_op jit(solution)/shard_map/pallas_call | solution.py:103
  120.8 7.3 %shard_map.58.rest_0_ = f32[4,4,64,1000]{3,2,1,0:T(8,128)S(1)} custom-call(s32[5]{0:T(128)S(1)} %get-tuple-element.34.idx, bf16[256,2048]{1,0:T(8,128)(2,1)} %collective-permute-done.3.x0, bf16[256,1920]{1,0:T(8,128)(2,1)} %collective-permute-done.13.x1, bf16[1000,7950]{1,0:T(8,128)(2,1)} %r.15, ...), custom_call_target="tpu_custom_call", output_to_operand_aliasing={{}: (5, {})} | custom-call | flops 2097152000 | bytes 12582912 | tf_op jit(solution)/shard_map/pallas_call | solution.py:103
  128.1 6.2 %shard_map.59.rest_1_ = f32[4,4,64,1000]{3,2,1,0:T(8,128)S(1)} custom-call(s32[5]{0:T(128)S(1)} %get-tuple-element.25.idx, bf16[256,2048]{1,0:T(8,128)(2,1)S(1)} %collective-permute-done.20.x0, bf16[256,2048]{1,0:T(8,128)(2,1)S(1)} %collective-permute-done.26.x1, bf16[1000,7950]{1,0:T(8,128)(2,1)} %r.15, ...), custom_call_target="tpu_custom_call", output_to_operand_aliasing={{}: (4, {})} | custom-call | flops 2097152000 | bytes 12582912 | tf_op jit(solution)/shard_map/pallas_call | solution.py:103
  134.4 6.8 %shard_map.60.rest_0_ = f32[4,4,64,1000]{3,2,1,0:T(8,128)S(1)} custom-call(s32[5]{0:T(128)S(1)} %get-tuple-element.33.idx, bf16[256,2048]{1,0:T(8,128)(2,1)S(1)} %collective-permute-done.4.x0, bf16[256,1920]{1,0:T(8,128)(2,1)S(1)} %collective-permute-done.14.x1, bf16[1000,7950]{1,0:T(8,128)(2,1)} %r.15, ...), custom_call_target="tpu_custom_call", output_to_operand_aliasing={{}: (5, {})} | custom-call | flops 2097152000 | bytes 12582912 | tf_op jit(solution)/shard_map/pallas_call | solution.py:103
  141.2 6.2 %shard_map.61.rest_1_ = f32[4,4,64,1000]{3,2,1,0:T(8,128)S(1)} custom-call(s32[5]{0:T(128)S(1)} %get-tuple-element.27.idx, bf16[256,2048]{1,0:T(8,128)(2,1)S(1)} %collective-permute-done.21.x0, bf16[256,2048]{1,0:T(8,128)(2,1)S(1)} %collective-permute-done.27.x1, bf16[1000,7950]{1,0:T(8,128)(2,1)} %r.15, ...), custom_call_target="tpu_custom_call", output_to_operand_aliasing={{}: (4, {})} | custom-call | flops 2097152000 | bytes 12582912 | tf_op jit(solution)/shard_map/pallas_call | solution.py:103
  147.5 6.8 %shard_map.62 = f32[4,4,64,1000]{3,2,1,0:T(8,128)S(1)} custom-call(s32[5]{0:T(128)S(1)} %get-tuple-element.35.idx, bf16[256,2048]{1,0:T(8,128)(2,1)S(1)} %collective-permute-done.5.x0, bf16[256,1920]{1,0:T(8,128)(2,1)S(1)} %collective-permute-done.15.x1, bf16[1000,7950]{1,0:T(8,128)(2,1)} %r.15, ...), custom_call_target="tpu_custom_call", output_to_operand_aliasing={{}: (5, {})} | custom-call | flops 2097152000 | bytes 12582912 | tf_op jit(solution)/shard_map/pallas_call | solution.py:103
  162.4 3.6 %collective-permute-start.30 = (bf16[128,1000]{1,0:T(8,128)(2,1)S(1)}, bf16[128,1000]{1,0:T(8,128)(2,1)S(1)}, u32[]{:S(2)}, u32[]{:S(2)}) collective-permute-start(bf16[128,1000]{1,0:T(8,128)(2,1)S(1)} %get-tuple-element.7), channel_id=1, source_target_pairs={{0,96},{1,97},{2,98},{3,99},{4,100},{5,101},{6,102},{7,103},{8,104... | collective-permute-start | bytes 768008 | tf_op jit(solution)/shard_map/ppermute | solution.py:36
  167.4 5.1 %collective-permute-done.29 = bf16[128,1000]{1,0:T(8,128)(2,1)S(1)} collective-permute-done((bf16[128,1000]{1,0:T(8,128)(2,1)S(1)}, bf16[128,1000]{1,0:T(8,128)(2,1)S(1)}, u32[]{:S(2)}, u32[]{:S(2)}) %collective-permute-start.29) | collective-permute-done | bytes 256032 | tf_op jit(solution)/shard_map/ppermute | solution.py:36
  172.5 5.0 %collective-permute-done.30 = bf16[128,1000]{1,0:T(8,128)(2,1)S(1)} collective-permute-done((bf16[128,1000]{1,0:T(8,128)(2,1)S(1)}, bf16[128,1000]{1,0:T(8,128)(2,1)S(1)}, u32[]{:S(2)}, u32[]{:S(2)}) %collective-permute-start.30) | collective-permute-done | bytes 256032 | tf_op jit(solution)/shard_map/ppermute | solution.py:36
  180.5 5.6 %shard_map.63 = bf16[4,128,975]{2,1,0:T(8,128)(2,1)S(1)} custom-call(bf16[128,1000]{1,0:T(8,128)(2,1)S(1)} %fusion.18.p, bf16[8,975,1000]{2,1,0:T(8,128)(2,1)} %all-gather.4.cloned.1.call-done.f), custom_call_target="tpu_custom_call" | custom-call | flops 998400000 | bytes 7800000 | tf_op jit(solution)/shard_map/pallas_call | solution.py:124
  188.9 5.6 %shard_map.64 = bf16[4,128,975]{2,1,0:T(8,128)(2,1)S(1)} custom-call(bf16[128,1000]{1,0:T(8,128)(2,1)S(1)} %fusion.18.p, bf16[8,975,1000]{2,1,0:T(8,128)(2,1)} %all-gather.4.cloned.1.call-done.f), custom_call_target="tpu_custom_call" | custom-call | flops 998400000 | bytes 7800000 | tf_op jit(solution)/shard_map/pallas_call | solution.py:124
  204.5 2.9 %collective-permute-done.38 = bf16[4,4,8,975]{3,2,1,0:T(8,128)(2,1)S(1)} collective-permute-done((bf16[4,4,8,975]{3,2,1,0:T(8,128)(2,1)S(1)}, bf16[4,4,8,975]{3,2,1,0:T(8,128)(2,1)S(1)}, u32[]{:S(2)}, u32[]{:S(2)}) %collective-permute-start.38) | collective-permute-done | bytes 249632 | tf_op jit(solution)/shard_map/ppermute | solution.py:36
  215.5 3.6 %collective-permute-done.42 = bf16[4,8,975]{2,1,0:T(8,128)(2,1)S(1)} collective-permute-done((bf16[4,8,975]{2,1,0:T(8,128)(2,1)S(1)}, bf16[4,8,975]{2,1,0:T(8,128)(2,1)S(1)}, u32[]{:S(2)}, u32[]{:S(2)}) %collective-permute-start.42) | collective-permute-done | bytes 62432 | tf_op jit(solution)/shard_map/ppermute | solution.py:36
  (131 shorter events, 80.7 us)
Async XLA Ops:
  6.5 174.0 %all-gather.4.cloned.1.call-start = ((), (), s32[]{:S(2)}) async-start(), calls=%async_computation | async-start | bytes 17989632 | tf_op jit(solution)/shard_map/all_gather | solution.py:162
  16.6 13.0 %collective-permute-start.16 = (bf16[64,2048]{1,0:T(8,128)(2,1)S(1)}, bf16[64,2048]{1,0:T(8,128)(2,1)S(1)}, u32[]{:S(2)}, u32[]{:S(2)}) collective-permute-start(bf16[64,2048]{1,0:T(8,128)(2,1)S(1)} %get-tuple-element.16), channel_id=1, source_target_pairs={{0,1},{1,2},{2,3},{3,0},{4,5},{5,6},{6,7},{7,4},{8,9},{9,10},{10,1... | collective-permute-start | bytes 786440 | tf_op jit(solution)/shard_map/ppermute | solution.py:36
  18.1 12.9 %collective-permute-start.22 = (bf16[64,2048]{1,0:T(8,128)(2,1)S(1)}, bf16[64,2048]{1,0:T(8,128)(2,1)S(1)}, u32[]{:S(2)}, u32[]{:S(2)}) collective-permute-start(bf16[64,2048]{1,0:T(8,128)(2,1)S(1)} %get-tuple-element.15), channel_id=1, source_target_pairs={{0,1},{1,2},{2,3},{3,0},{4,5},{5,6},{6,7},{7,4},{8,9},{9,10},{10,1... | collective-permute-start | bytes 786440 | tf_op jit(solution)/shard_map/ppermute | solution.py:36
  45.9 15.0 %collective-permute-start.19 = (bf16[256,2048]{1,0:T(8,128)(2,1)S(1)}, bf16[256,2048]{1,0:T(8,128)(2,1)}, u32[]{:S(2)}, u32[]{:S(2)}) collective-permute-start(bf16[256,2048]{1,0:T(8,128)(2,1)S(1)} %pad_maximum_fusion.1.x0), channel_id=1, source_target_pairs={{0,4},{1,5},{2,6},{3,7},{4,8},{5,9},{6,10},{7,11},{8,12},{9,13},{1... | collective-permute-start | bytes 3145736 | tf_op jit(solution)/shard_map/ppermute | solution.py:36
  47.7 24.5 %collective-permute-start.25 = (bf16[256,2048]{1,0:T(8,128)(2,1)S(1)}, bf16[256,2048]{1,0:T(8,128)(2,1)}, u32[]{:S(2)}, u32[]{:S(2)}) collective-permute-start(bf16[256,2048]{1,0:T(8,128)(2,1)S(1)} %pad_maximum_fusion.2.x1), channel_id=1, source_target_pairs={{0,4},{1,5},{2,6},{3,7},{4,8},{5,9},{6,10},{7,11},{8,12},{9,13},{1... | collective-permute-start | bytes 3145736 | tf_op jit(solution)/shard_map/ppermute | solution.py:36
  48.0 31.0 %collective-permute-start.3 = (bf16[256,2048]{1,0:T(8,128)(2,1)S(1)}, bf16[256,2048]{1,0:T(8,128)(2,1)}, u32[]{:S(2)}, u32[]{:S(2)}) collective-permute-start(bf16[256,2048]{1,0:T(8,128)(2,1)S(1)} %pad_maximum_fusion.x0), channel_id=1, source_target_pairs={{0,1},{1,2},{2,3},{3,0},{4,5},{5,6},{6,7},{7,4},{8,9},{9,10},{10,1... | collective-permute-start | bytes 3145736 | tf_op jit(solution)/shard_map/ppermute | solution.py:36
  50.6 27.7 %collective-permute-start.13 = (bf16[256,1920]{1,0:T(8,128)(2,1)}, bf16[256,1920]{1,0:T(8,128)(2,1)}, u32[]{:S(2)}, u32[]{:S(2)}) collective-permute-start(bf16[256,1920]{1,0:T(8,128)(2,1)} %pad_maximum_fusion.3.x1), channel_id=1, source_target_pairs={{0,1},{1,2},{2,3},{3,0},{4,5},{5,6},{6,7},{7,4},{8,9},{9,10},{10,1... | collective-permute-start | bytes 2949128 | tf_op jit(solution)/shard_map/ppermute | solution.py:36
  61.0 28.2 %collective-permute-start.20 = (bf16[256,2048]{1,0:T(8,128)(2,1)}, bf16[256,2048]{1,0:T(8,128)(2,1)S(1)}, u32[]{:S(2)}, u32[]{:S(2)}) collective-permute-start(bf16[256,2048]{1,0:T(8,128)(2,1)} %collective-permute-done.19.x0), channel_id=1, source_target_pairs={{0,4},{1,5},{2,6},{3,7},{4,8},{5,9},{6,10},{7,11},{8,12},{9,13},{1... | collective-permute-start | bytes 3145736 | tf_op jit(solution)/shard_map/ppermute | solution.py:36
  72.2 22.4 %collective-permute-start.26 = (bf16[256,2048]{1,0:T(8,128)(2,1)}, bf16[256,2048]{1,0:T(8,128)(2,1)S(1)}, u32[]{:S(2)}, u32[]{:S(2)}) collective-permute-start(bf16[256,2048]{1,0:T(8,128)(2,1)} %collective-permute-done.25.x1), channel_id=1, source_target_pairs={{0,4},{1,5},{2,6},{3,7},{4,8},{5,9},{6,10},{7,11},{8,12},{9,13},{1... | collective-permute-start | bytes 3145736 | tf_op jit(solution)/shard_map/ppermute | solution.py:36
  78.4 34.2 %collective-permute-start.14 = (bf16[256,1920]{1,0:T(8,128)(2,1)}, bf16[256,1920]{1,0:T(8,128)(2,1)S(1)}, u32[]{:S(2)}, u32[]{:S(2)}) collective-permute-start(bf16[256,1920]{1,0:T(8,128)(2,1)} %collective-permute-done.13.x1), channel_id=1, source_target_pairs={{0,1},{1,2},{2,3},{3,0},{4,5},{5,6},{6,7},{7,4},{8,9},{9,10},{10,1... | collective-permute-start | bytes 2949128 | tf_op jit(solution)/shard_map/ppermute | solution.py:36
  79.1 26.2 %collective-permute-start.4 = (bf16[256,2048]{1,0:T(8,128)(2,1)}, bf16[256,2048]{1,0:T(8,128)(2,1)S(1)}, u32[]{:S(2)}, u32[]{:S(2)}) collective-permute-start(bf16[256,2048]{1,0:T(8,128)(2,1)} %collective-permute-done.3.x0), channel_id=1, source_target_pairs={{0,1},{1,2},{2,3},{3,0},{4,5},{5,6},{6,7},{7,4},{8,9},{9,10},{10,1... | collective-permute-start | bytes 3145736 | tf_op jit(solution)/shard_map/ppermute | solution.py:36
  89.2 52.0 %collective-permute-start.21 = (bf16[256,2048]{1,0:T(8,128)(2,1)S(1)}, bf16[256,2048]{1,0:T(8,128)(2,1)S(1)}, u32[]{:S(2)}, u32[]{:S(2)}) collective-permute-start(bf16[256,2048]{1,0:T(8,128)(2,1)S(1)} %collective-permute-done.20.x0), channel_id=1, source_target_pairs={{0,4},{1,5},{2,6},{3,7},{4,8},{5,9},{6,10},{7,11},{8,12},{9,13},{1... | collective-permute-start | bytes 3145736 | tf_op jit(solution)/shard_map/ppermute | solution.py:36
  94.6 46.6 %collective-permute-start.27 = (bf16[256,2048]{1,0:T(8,128)(2,1)S(1)}, bf16[256,2048]{1,0:T(8,128)(2,1)S(1)}, u32[]{:S(2)}, u32[]{:S(2)}) collective-permute-start(bf16[256,2048]{1,0:T(8,128)(2,1)S(1)} %collective-permute-done.26.x1), channel_id=1, source_target_pairs={{0,4},{1,5},{2,6},{3,7},{4,8},{5,9},{6,10},{7,11},{8,12},{9,13},{1... | collective-permute-start | bytes 3145736 | tf_op jit(solution)/shard_map/ppermute | solution.py:36
  105.3 42.1 %collective-permute-start.5 = (bf16[256,2048]{1,0:T(8,128)(2,1)S(1)}, bf16[256,2048]{1,0:T(8,128)(2,1)S(1)}, u32[]{:S(2)}, u32[]{:S(2)}) collective-permute-start(bf16[256,2048]{1,0:T(8,128)(2,1)S(1)} %collective-permute-done.4.x0), channel_id=1, source_target_pairs={{0,1},{1,2},{2,3},{3,0},{4,5},{5,6},{6,7},{7,4},{8,9},{9,10},{10,1... | collective-permute-start | bytes 3145736 | tf_op jit(solution)/shard_map/ppermute | solution.py:36
  112.5 34.9 %collective-permute-start.15 = (bf16[256,1920]{1,0:T(8,128)(2,1)S(1)}, bf16[256,1920]{1,0:T(8,128)(2,1)S(1)}, u32[]{:S(2)}, u32[]{:S(2)}) collective-permute-start(bf16[256,1920]{1,0:T(8,128)(2,1)S(1)} %collective-permute-done.14.x1), channel_id=1, source_target_pairs={{0,1},{1,2},{2,3},{3,0},{4,5},{5,6},{6,7},{7,4},{8,9},{9,10},{10,1... | collective-permute-start | bytes 2949128 | tf_op jit(solution)/shard_map/ppermute | solution.py:36
  162.4 15.1 %collective-permute-start.30 = (bf16[128,1000]{1,0:T(8,128)(2,1)S(1)}, bf16[128,1000]{1,0:T(8,128)(2,1)S(1)}, u32[]{:S(2)}, u32[]{:S(2)}) collective-permute-start(bf16[128,1000]{1,0:T(8,128)(2,1)S(1)} %get-tuple-element.7), channel_id=1, source_target_pairs={{0,96},{1,97},{2,98},{3,99},{4,100},{5,101},{6,102},{7,103},{8,104... | collective-permute-start | bytes 768008 | tf_op jit(solution)/shard_map/ppermute | solution.py:36
  166.0 13.4 %collective-permute-start.31 = (bf16[128,1000]{1,0:T(8,128)(2,1)S(1)}, bf16[128,1000]{1,0:T(8,128)(2,1)}, u32[]{:S(2)}, u32[]{:S(2)}) collective-permute-start(bf16[128,1000]{1,0:T(8,128)(2,1)S(1)} %get-tuple-element.6), channel_id=1, source_target_pairs={{0,64},{1,65},{2,66},{3,67},{4,68},{5,69},{6,70},{7,71},{8,72},{9,... | collective-permute-start | bytes 768008 | tf_op jit(solution)/shard_map/ppermute | solution.py:36
  186.6 14.4 %collective-permute-start.33 = (bf16[4,4,8,975]{3,2,0,1:T(8,128)(2,1)S(1)}, bf16[4,4,8,975]{3,2,0,1:T(8,128)(2,1)S(1)}, u32[]{:S(2)}, u32[]{:S(2)}) collective-permute-start(bf16[4,4,8,975]{3,2,0,1:T(8,128)(2,1)S(1)} %bitcast.91), channel_id=1, source_target_pairs={{0,12},{1,13},{2,14},{3,15},{4,0},{5,1},{6,2},{7,3},{8,4},{9,5},{1... | collective-permute-start | bytes 748808 | tf_op jit(solution)/shard_map/ppermute | solution.py:36
  188.7 12.3 %collective-permute-start.34 = (bf16[4,4,8,975]{3,2,0,1:T(8,128)(2,1)S(1)}, bf16[4,4,8,975]{3,2,0,1:T(8,128)(2,1)S(1)}, u32[]{:S(2)}, u32[]{:S(2)}) collective-permute-start(bf16[4,4,8,975]{3,2,0,1:T(8,128)(2,1)S(1)} %bitcast.92), channel_id=1, source_target_pairs={{0,8},{1,9},{2,10},{3,11},{4,12},{5,13},{6,14},{7,15},{8,0},{9,1},... | collective-permute-start | bytes 748808 | tf_op jit(solution)/shard_map/ppermute | solution.py:36
  194.5 12.9 %collective-permute-start.38 = (bf16[4,4,8,975]{3,2,1,0:T(8,128)(2,1)S(1)}, bf16[4,4,8,975]{3,2,1,0:T(8,128)(2,1)S(1)}, u32[]{:S(2)}, u32[]{:S(2)}) collective-permute-start(bf16[4,4,8,975]{3,2,1,0:T(8,128)(2,1)S(1)} %get-tuple-element.12), channel_id=1, source_target_pairs={{0,1},{1,2},{2,3},{3,0},{4,5},{5,6},{6,7},{7,4},{8,9},{9,10},{10,1... | collective-permute-start | bytes 748808 | tf_op jit(solution)/shard_map/ppermute | solution.py:36
  196.3 13.0 %collective-permute-start.39 = (bf16[4,4,8,975]{3,2,1,0:T(8,128)(2,1)S(1)}, bf16[4,4,8,975]{3,2,1,0:T(8,128)(2,1)S(1)}, u32[]{:S(2)}, u32[]{:S(2)}) collective-permute-start(bf16[4,4,8,975]{3,2,1,0:T(8,128)(2,1)S(1)} %get-tuple-element.14), channel_id=1, source_target_pairs={{0,3},{1,0},{2,1},{3,2},{4,7},{5,4},{6,5},{7,6},{8,11},{9,8},{10,9... | collective-permute-start | bytes 748808 | tf_op jit(solution)/shard_map/ppermute | solution.py:36
  197.9 12.2 %collective-permute-start.40 = (bf16[4,4,8,975]{3,2,1,0:T(8,128)(2,1)S(1)}, bf16[4,4,8,975]{3,2,1,0:T(8,128)(2,1)S(1)}, u32[]{:S(2)}, u32[]{:S(2)}) collective-permute-start(bf16[4,4,8,975]{3,2,1,0:T(8,128)(2,1)S(1)} %get-tuple-element.13), channel_id=1, source_target_pairs={{0,2},{1,3},{2,0},{3,1},{4,6},{5,7},{6,4},{7,5},{8,10},{9,11},{10,... | collective-permute-start | bytes 748808 | tf_op jit(solution)/shard_map/ppermute | solution.py:36
  201.2 11.7 %collective-permute-start.35 = (bf16[4,8,975]{2,1,0:T(8,128)(2,1)S(1)}, bf16[4,8,975]{2,1,0:T(8,128)(2,1)S(1)}, u32[]{:S(2)}, u32[]{:S(2)}) collective-permute-start(bf16[4,8,975]{2,1,0:T(8,128)(2,1)S(1)} %get-tuple-element.18), channel_id=1, source_target_pairs={{0,1},{1,2},{2,3},{3,0},{4,5},{5,6},{6,7},{7,4},{8,9},{9,10},{10,1... | collective-permute-start | bytes 187208 | tf_op jit(solution)/shard_map/ppermute | solution.py:36
  202.9 12.5 %collective-permute-start.36 = (bf16[4,8,975]{2,1,0:T(8,128)(2,1)S(1)}, bf16[4,8,975]{2,1,0:T(8,128)(2,1)S(1)}, u32[]{:S(2)}, u32[]{:S(2)}) collective-permute-start(bf16[4,8,975]{2,1,0:T(8,128)(2,1)S(1)} %get-tuple-element.20), channel_id=1, source_target_pairs={{0,3},{1,0},{2,1},{3,2},{4,7},{5,4},{6,5},{7,6},{8,11},{9,8},{10,9... | collective-permute-start | bytes 187208 | tf_op jit(solution)/shard_map/ppermute | solution.py:36
  (24 other events, 155.6 us)
Sparse Core Ops, SparseCore 0:
  9.1 84.7 all-gather.3

commit v2 on v0

v2 whole, which is shorter than its diff:
```python
import functools

import jax
import jax.numpy as jnp
from jax import lax
from jax.experimental import pallas as pl
from jax.experimental.pallas import tpu as pltpu
from jax.sharding import PartitionSpec as P

SENSORS = 6
AXES = ("sens", "layer")
SIDE = 4
ROWS = 64
CUTS = (32, 32)
HALF = 4096
BWIDTH = 3968
EDGE = BWIDTH - 128
INSIDE = 14
SPAN = 24
PBLOCK = 256
VMEM = 48 * 2**20


def moved(fn):
    pairs = []
    for z in range(4):
        for c in range(2):
            for y in range(4):
                for x in range(4):
                    z2, c2, y2, x2 = fn(z, c, y, x)
                    pairs.append(
                        ((z * 2 + c) * 16 + y * 4 + x,
                         ((z2 % 4) * 2 + c2 % 2) * 16 + (y2 % 4) * 4 + x2 % 4)
                    )
    return pairs


def send(x, fn):
    return lax.ppermute(x, AXES, moved(fn))


def ring_x(v):
    return send(v, lambda z, c, y, x: (z, c, y, x + 1 - 2 * c))


def ring_y(v):
    return send(v, lambda z, c, y, x: (z, c, y + 1 - 2 * c, x))


def swap_core(v):
    return send(v, lambda z, c, y, x: (z, c + 1, y, x))


def hop_z(d):
    return lambda z, c, y, x: (z + d, c, y, x)


def hop_one(d):
    return lambda z, c, y, x: (z, c, y + d * (1 - c), x + d * c)


def hop_two(d):
    return lambda z, c, y, x: (z, c, y + d * c, x + d * (1 - c))


def after(value, *others):
    return lax.optimization_barrier((value, *others))


def nt(a, b, **kw):
    return lax.dot_general(
        a, b, (((1,), (1,)), ((), ())), preferred_element_type=jnp.float32, **kw
    )


def place(first, t, u):
    s_idx, l_idx = lax.axis_index("sens"), lax.axis_index("layer")
    core = lax.rem(s_idx, 2)
    sign = 1 - 2 * core
    ry, rx = (t, u) if first else (u, t)
    y = lax.rem(l_idx // SIDE - sign * ry + SIDE, SIDE)
    x = lax.rem(lax.rem(l_idx, SIDE) - sign * rx + SIDE, SIDE)
    other = lax.rem(x // 2 + core, 2)
    return other * 8 + y * 2 + lax.rem(x, 2)


def fetches(first, size, blocks, held, sems):
    copies = []
    for t in range(SIDE):
        for u in range(SIDE):
            row = pl.multiple_of(place(first, t, u) * size, size)
            copies.append(
                pltpu.make_async_copy(
                    blocks[t].at[pl.ds(u * size, size)],
                    held.at[pl.ds(row, size)],
                    sems.at[t * SIDE + u],
                )
            )
    return copies


def load(first, size, blocks, held, sems):
    @pl.when(pl.program_id(0) == 0)
    def _():
        copies = fetches(first, size, blocks, held, sems)
        for copy in copies:
            copy.start()
        for copy in copies:
            copy.wait()


def kernel_a(size, x0, x1, x2, x3, r, out, held, sems):
    load(True, size, (x0, x1, x2, x3), held, sems)
    out[...] = nt(held[...], r[...])


def kernel_b(size, index, x0, x1, x2, x3, r, rw, acc, *rest):
    if index == 0:
        own, other, tail_out, held, sems = rest
    else:
        tail_in, own, other, held, sems = rest
    load(False, size, (x0, x1, x2, x3), held, sems)
    lane = lax.broadcasted_iota(jnp.int32, (r.shape[0], 128), 1)
    edge = r[:, EDGE:BWIDTH].astype(jnp.float32)
    edge = jnp.where(lane < INSIDE, edge, 0.0).astype(jnp.bfloat16)
    tail = held[:, EDGE:]
    val = acc[...] + nt(held[:, :EDGE], r[:, :EDGE]) + nt(tail, edge)
    if index == 0:
        means = tail
        tail_out[...] = tail
    else:
        means = tail_in[...]
    val = val + nt(means.astype(jnp.float32), rw[...], precision=lax.Precision.HIGHEST)
    half = val.shape[0] // 2
    own[...] = val[:half]
    other[...] = val[half:].astype(jnp.bfloat16)


ANY = pl.BlockSpec(memory_space=pl.ANY)


def matmul_a(size, blocks, r):
    n = 16 * size
    p = r.shape[0]
    return pl.pallas_call(
        functools.partial(kernel_a, size),
        grid=(pl.cdiv(p, PBLOCK),),
        in_specs=[ANY] * 4 + [pl.BlockSpec((PBLOCK, HALF), lambda j: (j, 0))],
        out_specs=pl.BlockSpec((n, PBLOCK), lambda j: (0, j)),
        out_shape=jax.ShapeDtypeStruct((n, p), jnp.float32),
        scratch_shapes=[pltpu.VMEM((n, HALF), jnp.bfloat16), pltpu.SemaphoreType.DMA((16,))],
        compiler_params=pltpu.CompilerParams(vmem_limit_bytes=VMEM),
        cost_estimate=pl.CostEstimate(
            flops=3 * 2 * n * HALF * p, bytes_accessed=16 * 2**20, transcendentals=0
        ),
    )(*blocks, r)


def matmul_b(size, index, blocks, r, rw, acc, tail):
    n = 16 * size
    p = r.shape[0]
    specs = [ANY] * 4 + [
        pl.BlockSpec((PBLOCK, HALF), lambda j: (j, 1)),
        pl.BlockSpec((PBLOCK, 128), lambda j: (j, 0)),
        pl.BlockSpec((n, PBLOCK), lambda j: (0, j)),
    ]
    args = [*blocks, r, rw, acc]
    half_spec = pl.BlockSpec((n // 2, PBLOCK), lambda j: (0, j))
    whole = pl.BlockSpec((n, 128), lambda j: (0, 0))
    outs = [half_spec, half_spec]
    shapes = [
        jax.ShapeDtypeStruct((n // 2, p), jnp.float32),
        jax.ShapeDtypeStruct((n // 2, p), jnp.bfloat16),
    ]
    if index == 0:
        outs.append(whole)
        shapes.append(jax.ShapeDtypeStruct((n, 128), jnp.bfloat16))
    else:
        specs.append(whole)
        args.append(tail)
    return pl.pallas_call(
        functools.partial(kernel_b, size, index),
        grid=(pl.cdiv(p, PBLOCK),),
        in_specs=specs,
        out_specs=outs,
        out_shape=shapes,
        scratch_shapes=[pltpu.VMEM((n, BWIDTH), jnp.bfloat16), pltpu.SemaphoreType.DMA((16,))],
        compiler_params=pltpu.CompilerParams(vmem_limit_bytes=VMEM),
        cost_estimate=pl.CostEstimate(
            flops=3 * 2 * n * HALF * p, bytes_accessed=16 * 2**20, transcendentals=0
        ),
    )(*args)


def fit_kernel(p, f, out):
    out[0] = nt(p[...], f[0]).astype(jnp.bfloat16)


def fit(points, fitting, start, count):
    n, k = points.shape
    m = fitting.shape[1]
    return pl.pallas_call(
        fit_kernel,
        grid=(count,),
        in_specs=[
            pl.BlockSpec((n, k), lambda s: (0, 0)),
            pl.BlockSpec((1, m, k), lambda s: (s + start, 0, 0)),
        ],
        out_specs=pl.BlockSpec((1, n, m), lambda s: (s, 0, 0)),
        out_shape=jax.ShapeDtypeStruct((count, n, m), jnp.bfloat16),
        compiler_params=pltpu.CompilerParams(vmem_limit_bytes=VMEM),
        cost_estimate=pl.CostEstimate(
            flops=6 * n * m * k * count, bytes_accessed=2 * count * m * k, transcendentals=0
        ),
    )(points, fitting)


def parts(blocks, axis, mine, hop):
    def pick(d):
        return lax.dynamic_index_in_dim(blocks, (mine + d) % SIDE, axis, keepdims=False)

    got = [send(pick(d).astype(jnp.bfloat16), hop(d)) for d in (1, 3, 2)]
    return [pick(0)] + got


def total(pieces):
    out = pieces[0].astype(jnp.float32)
    for piece in pieces[1:]:
        out = out + piece.astype(jnp.float32)
    return out


def per_device(slopes, valid, sensor_map, reconstructor, fitting):
    s_idx = lax.axis_index("sens")
    l_idx = lax.axis_index("layer")
    z, c = s_idx // 2, s_idx % 2
    y, x = l_idx // 4, l_idx % 4
    width = slopes.shape[1]
    width_p = reconstructor.shape[0]
    act = fitting.shape[0]

    everything = lax.all_gather(fitting, "sens", axis=0)

    masked = slopes * valid.astype(jnp.bfloat16)[None, :]
    first_rows, second_rows = masked[: CUTS[0]], masked[CUTS[0] :]
    pad = ((0, 0), (0, HALF + BWIDTH - width))
    a0 = [first_rows[:, :HALF]]
    a1 = [second_rows[:, :HALF]]
    b1 = [jnp.pad(second_rows[:, HALF:], pad)]
    a0.append(ring_x(a0[-1]))
    b1.append(ring_y(b1[-1]))

    group = sensor_map * 2 + (lax.iota(jnp.int32, width) + s_idx * width) % 2
    lane = lax.iota(jnp.int32, 128)
    label = jnp.where(lane < INSIDE, -1, (lane - INSIDE) % 12)
    label = jnp.where(lane < INSIDE + 2 * SPAN, label, -1)
    member = ((group[None, :] == label[:, None]) & (valid[None, :] == 1)).astype(jnp.bfloat16)
    counted = jnp.concatenate([masked, jnp.ones((8, width), jnp.bfloat16)], axis=0)
    stats = nt(counted, member)
    stats, a0[1], b1[1] = after(stats, a0[1], b1[1])

    a0.append(ring_x(a0[-1]))
    b1.append(ring_y(b1[-1]))
    stats = stats + swap_core(stats)
    a0.append(ring_x(a0[-1]))
    b1.append(ring_y(b1[-1]))
    others = [send(stats, hop_z(d)) for d in (1, 3, 2)]
    stats = (stats + others[2]) + (others[0] + others[1])
    means = stats[:ROWS] / jnp.maximum(stats[ROWS : ROWS + 1], 1.0)
    high = lax.reduce_precision(means, 8, 7)
    low = means - high
    order = (lane - INSIDE) % SPAN < 12
    split = jnp.where(order[None, :], high, low)
    here = (lane >= INSIDE) & (lane < INSIDE + SPAN)
    there = (lane >= INSIDE + SPAN) & (lane < INSIDE + 2 * SPAN)
    rows = jnp.where(here[None, :], split[: CUTS[0]], 0.0)
    rows = rows + jnp.where(there[None, :], split[CUTS[0] :], 0.0)
    b0 = [jnp.pad(first_rows[:, HALF:], pad)]
    b0[0] = b0[0] + jnp.pad(rows.astype(jnp.bfloat16), ((0, 0), (EDGE, 0)))

    rw = -nt(reconstructor, member)
    rw0 = jnp.where(here[None, :], rw, 0.0)
    rw1 = jnp.where(there[None, :], rw, 0.0)

    block_a0 = [jnp.concatenate(a0, axis=0)]
    block_a0.append(ring_y(block_a0[-1]))
    for _ in range(3):
        b0.append(ring_y(b0[-1]))
        a1.append(ring_x(a1[-1]))
    block_b0 = [jnp.concatenate(b0, axis=0)]
    for _ in range(2):
        block_a0.append(ring_y(block_a0[-1]))
    for _ in range(3):
        block_b0.append(ring_x(block_b0[-1]))

    block_a1 = [jnp.concatenate(a1, axis=0)]
    block_b1 = [jnp.concatenate(b1, axis=0)]
    block_a1.append(ring_y(block_a1[-1]))
    block_b1.append(ring_x(block_b1[-1]))

    acc = matmul_a(CUTS[0], block_a0, reconstructor)
    acc, block_a1[1] = after(acc, block_a1[1])
    block_a1.append(ring_y(block_a1[-1]))
    own, other, tail = matmul_b(CUTS[0], 0, block_b0, reconstructor, rw0, acc, None)
    own, other, block_b1[1] = after(own, other, block_b1[1])
    block_b1.append(ring_x(block_b1[-1]))

    def layers_of(own, other, size):
        got = own + swap_core(other).astype(jnp.float32)
        got = got.reshape(SIDE, 2, size, width_p)
        return got

    layers0 = layers_of(own, other, CUTS[0])
    layers0, block_a1[2] = after(layers0, block_a1[2])
    block_a1.append(ring_y(block_a1[-1]))
    block_b1.append(ring_x(block_b1[-1]))
    points0 = total(parts(layers0, 0, z, hop_z)).astype(jnp.bfloat16)

    acc = matmul_a(CUTS[1], block_a1, reconstructor)
    own, other = matmul_b(CUTS[1], 1, block_b1, reconstructor, rw1, acc, tail)
    layers1 = layers_of(own, other, CUTS[1])
    points1 = total(parts(layers1, 0, z, hop_z)).astype(jnp.bfloat16)
    points = jnp.concatenate([points0, points1], axis=1)

    rows = points.reshape(SIDE, SIDE, 8, width_p)
    rows = jnp.where(c == 0, rows, jnp.swapaxes(rows, 0, 1)).reshape(2 * ROWS, width_p)
    one = jnp.where(c == 0, y, x)
    two = jnp.where(c == 0, x, y)
    half_a = fit(rows, everything, 0, 4).reshape(4, SIDE, 4 * 8, act)
    part_a = parts(half_a, 1, one, hop_one)
    half_b = fit(rows, everything, 4, 4).reshape(4, SIDE, 4 * 8, act)
    part_b = parts(half_b, 1, one, hop_one)
    both = jnp.concatenate([total(part_a), total(part_b)], axis=0)
    done = total(parts(both.reshape(8, SIDE, 8, act), 1, two, hop_two))
    return jnp.moveaxis(done, 0, 1).reshape(8, 8 * act)


def solution(mesh):
    placed = (P("layer", "sens"), P("sens"), P("sens"), P("layer", "sens"), P("sens", "layer"))
    return jax.shard_map(
        per_device,
        mesh=mesh,
        in_specs=placed,
        out_specs=P(("sens", "layer"), None),
        check_vma=False,
    )
```

time: 285 us -> 264 us (0.926); the launches traced: 282 us -> 264 us
  Pallas kernels: 0 us -> 58.9 us
  starting transfers between devices: 9.18 us -> 61.6 us
  matrix products: 59.2 us -> 9.38 us
  local copies, waits for them, and re-layouts: 48.2 us -> 1.54 us
  blocking collectives: 39.9 us -> 0 us
  waiting for transfers between devices: 110 us -> 113 us
    ppermute x0 -> x45, waiting for transfers between devices: none -> 113 us  [send(): return lax.ppermute(x, AXES, moved(fn))]
    all_gather x2 -> x1, waiting for transfers between devices: 104 us -> 0.02 us  [per_device(): everything = lax.all_gather(fitting, 'sens', axis=0)]
    ppermute x0 -> x45, starting transfers between devices: none -> 61.6 us  [send(): return lax.ppermute(x, AXES, moved(fn))]
    pallas_call x0 -> x6, Pallas kernels: none -> 58.9 us  [the longest x2 30.4 us: matmul_b(): pl.pallas_call(functools.partial(kernel_b, size, index), grid=(pl.cdiv(p,...]
    dot_general x5 -> x2, matrix products: 59.2 us -> 9.38 us  [nt(): lax.dot_general(a, b, (((1,), (1,)), ((), ())), preferred_element_type=jn...]
    all_to_all x2 -> x0, blocking collectives: 39.9 us -> none  [the longest x1 29.5 us: summed_on_arrival(): lax.all_to_all(blocks, axis, split_axis=0, concat_axis=0, tiled=True)]
    all_gather x1 -> x0, local copies, waits for them, and re-layouts: 22.4 us -> none  [per_device(): whole = lax.all_gather(slopes, 'layer', axis=0, tiled=True)]
    unnamed x1 -> x9, local copies, waits for them, and re-layouts: 20.5 us -> 0.25 us
  transfers between devices with their start and end apart: 4 -> 46, of which waited for: 3 -> 27; matrix products, arithmetic and copies ran while one was open for 34% -> 5% of each run, Pallas kernels for 0% -> 20%
where the time goes in v2:
time: 264 us
  waiting for transfers between devices  113 us (43%)
  starting transfers between devices  61.6 us (23%)
  Pallas kernels  58.9 us (22%)
  between operations  14.1 us (5%)
  matrix products  9.38 us (4%)
  other arithmetic  4.87 us (2%)
    ppermute x45, waiting for transfers between devices, send(): return lax.ppermute(x, AXES, moved(fn))  113 us
    ppermute x45, starting transfers between devices, send(): return lax.ppermute(x, AXES, moved(fn))  61.6 us
    pallas_call x2, Pallas kernels, matmul_b(): pl.pallas_call(functools.partial(kernel_b, size, index), grid=(pl.cdiv(p,...  30.4 us
    pallas_call x2, Pallas kernels, matmul_a(): pl.pallas_call(functools.partial(kernel_a, size), grid=(pl.cdiv(p, PBLOCK...  17.4 us
    pallas_call x2, Pallas kernels, fit(): pl.pallas_call(fit_kernel, grid=(count,), in_specs=[pl.BlockSpec((n, k),...  11.2 us
    dot_general x2, matrix products, nt(): lax.dot_general(a, b, (((1,), (1,)), ((), ())), preferred_element_type=jn...  9.38 us
  transfers between devices with their start and end apart: 46, of which 27 were waited for; matrix products, arithmetic and copies ran while one was open for 5% of the time, Pallas kernels for 20%

profile of v2, /device:TPU:24, one launch (start us, length us, event | category | flops | bytes accessed | tf_op | source)
XLA Modules:
  0.0 263.8 jit_solution(6288531259060628844)
XLA Ops:
  17.4 4.0 %collective-permute-start.3 = (f32[72,128]{1,0:T(8,128)S(1)}, f32[72,128]{1,0:T(8,128)S(1)}, u32[]{:S(2)}, u32[]{:S(2)}) collective-permute-start(f32[72,128]{1,0:T(8,128)S(1)} %add.259), channel_id=1, source_target_pairs={{0,64},{1,65},{2,66},{3,67},{4,68},{5,69},{6,70},{7,71},{8,72},{9,... | collective-permute-start | bytes 110600 | tf_op jit(solution)/shard_map/ppermute | solution.py:39
  26.6 5.6 %collective-permute-done.12 = bf16[32,4096]{1,0:T(8,128)(2,1)S(1)} collective-permute-done((bf16[32,4096]{1,0:T(8,128)(2,1)S(1)}, bf16[32,4096]{1,0:T(8,128)(2,1)S(1)}, u32[]{:S(2)}, u32[]{:S(2)}) %collective-permute-start.12) | collective-permute-done | bytes 262176 | tf_op jit(solution)/shard_map/ppermute | solution.py:39
  32.3 7.5 %collective-permute-done.13 = bf16[32,4096]{1,0:T(8,128)(2,1)S(1)} collective-permute-done((bf16[32,4096]{1,0:T(8,128)(2,1)S(1)}, bf16[32,4096]{1,0:T(8,128)(2,1)S(1)}, u32[]{:S(2)}, u32[]{:S(2)}) %collective-permute-start.13) | collective-permute-done | bytes 262176 | tf_op jit(solution)/shard_map/ppermute | solution.py:39
  43.2 14.3 %collective-permute-done.6 = bf16[32,3968]{1,0:T(8,128)(2,1)S(1)} collective-permute-done((bf16[32,3968]{1,0:T(8,128)(2,1)S(1)}, bf16[32,3968]{1,0:T(8,128)(2,1)S(1)}, u32[]{:S(2)}, u32[]{:S(2)}) %collective-permute-start.6) | collective-permute-done | bytes 253984 | tf_op jit(solution)/shard_map/ppermute | solution.py:39
  60.3 3.8 %collective-permute-done.7 = bf16[32,3968]{1,0:T(8,128)(2,1)S(1)} collective-permute-done((bf16[32,3968]{1,0:T(8,128)(2,1)S(1)}, bf16[32,3968]{1,0:T(8,128)(2,1)S(1)}, u32[]{:S(2)}, u32[]{:S(2)}) %collective-permute-start.7) | collective-permute-done | bytes 253984 | tf_op jit(solution)/shard_map/ppermute | solution.py:39
  64.1 3.7 %collective-permute-start.8 = (bf16[32,3968]{1,0:T(8,128)(2,1)S(1)}, bf16[32,3968]{1,0:T(8,128)(2,1)S(1)}, u32[]{:S(2)}, u32[]{:S(2)}) collective-permute-start(bf16[32,3968]{1,0:T(8,128)(2,1)S(1)} %collective-permute-done.7), channel_id=1, source_target_pairs={{0,4},{1,5},{2,6},{3,7},{4,8},{5,9},{6,10},{7,11},{8,12},{9,13},{1... | collective-permute-start | bytes 761864 | tf_op jit(solution)/shard_map/ppermute | solution.py:39
  67.8 3.8 %collective-permute-done.8 = bf16[32,3968]{1,0:T(8,128)(2,1)S(1)} collective-permute-done((bf16[32,3968]{1,0:T(8,128)(2,1)S(1)}, bf16[32,3968]{1,0:T(8,128)(2,1)S(1)}, u32[]{:S(2)}, u32[]{:S(2)}) %collective-permute-start.8) | collective-permute-done | bytes 253984 | tf_op jit(solution)/shard_map/ppermute | solution.py:39
  71.8 3.8 %collective-permute-start.21 = (bf16[32,3968]{1,0:T(8,128)(2,1)S(1)}, bf16[32,3968]{1,0:T(8,128)(2,1)S(1)}, u32[]{:S(2)}, u32[]{:S(2)}) collective-permute-start(bf16[32,3968]{1,0:T(8,128)(2,1)S(1)} %collective-permute-done.1), channel_id=1, source_target_pairs={{0,4},{1,5},{2,6},{3,7},{4,8},{5,9},{6,10},{7,11},{8,12},{9,13},{1... | collective-permute-start | bytes 761864 | tf_op jit(solution)/shard_map/ppermute | solution.py:39
  75.6 14.6 %collective-permute-done.17 = bf16[32,4096]{1,0:T(8,128)(2,1)S(1)} collective-permute-done((bf16[32,4096]{1,0:T(8,128)(2,1)S(1)}, bf16[32,4096]{1,0:T(8,128)(2,1)S(1)}, u32[]{:S(2)}, u32[]{:S(2)}) %collective-permute-start.17) | collective-permute-done | bytes 262176 | tf_op jit(solution)/shard_map/ppermute | solution.py:39
  90.2 3.7 %collective-permute-start.22 = (bf16[32,3968]{1,0:T(8,128)(2,1)S(1)}, bf16[32,3968]{1,0:T(8,128)(2,1)S(1)}, u32[]{:S(2)}, u32[]{:S(2)}) collective-permute-start(bf16[32,3968]{1,0:T(8,128)(2,1)S(1)} %collective-permute-done.21), channel_id=1, source_target_pairs={{0,4},{1,5},{2,6},{3,7},{4,8},{5,9},{6,10},{7,11},{8,12},{9,13},{1... | collective-permute-start | bytes 761864 | tf_op jit(solution)/shard_map/ppermute | solution.py:39
  94.1 8.3 %select_bitcast_fusion = (f32[1000,128]{1,0:T(8,128)S(1)}, f32[1000,128]{1,0:T(8,128)S(1)}) fusion(pred[128]{0:T(512)(128)(4,1)S(1)} %get-tuple-element.56, pred[128]{0:T(512)(128)(4,1)S(1)} %get-tuple-element.57, bf16[1000,7950]{1,0:T(8,128)(2,1)} %r.7, s32[7950]{0:T(1024)S(1)} %fusion.33, s32[128]{0:T(128)S(1)} %compare_select_fusion.1, ...), kind=kOutput, calls=%fused_computation.25 | convolution fusion | flops 2037619200 | bytes 16964518 | tf_op jit(solution)/shard_map/dot_general | solution.py:71
  103.4 3.9 %collective-permute-start.23 = (bf16[128,3968]{1,0:T(8,128)(2,1)S(1)}, bf16[128,3968]{1,0:T(8,128)(2,1)S(1)}, u32[]{:S(2)}, u32[]{:S(2)}) collective-permute-start(bf16[128,3968]{1,0:T(8,128)(2,1)S(1)} %pad_maximum_fusion.3.x0), channel_id=1, source_target_pairs={{0,1},{1,2},{2,3},{3,0},{4,5},{5,6},{6,7},{7,4},{8,9},{9,10},{10,1... | collective-permute-start | bytes 3047432 | tf_op jit(solution)/shard_map/ppermute | solution.py:39
  107.3 5.0 %collective-permute-done.19 = bf16[32,4096]{1,0:T(8,128)(2,1)S(1)} collective-permute-done((bf16[32,4096]{1,0:T(8,128)(2,1)S(1)}, bf16[32,4096]{1,0:T(8,128)(2,1)S(1)}, u32[]{:S(2)}, u32[]{:S(2)}) %collective-permute-start.19) | collective-permute-done | bytes 262176 | tf_op jit(solution)/shard_map/ppermute | solution.py:39
  115.3 8.7 %shard_map.55.acc = f32[512,1000]{1,0:T(8,128)} custom-call(bf16[128,4096]{1,0:T(8,128)(2,1)S(1)} %pad_maximum_fusion.x0, bf16[128,4096]{1,0:T(8,128)(2,1)S(1)} %collective-permute-done.14.x1, bf16[128,4096]{1,0:T(8,128)(2,1)S(1)} %collective-permute-done.15.x2, bf16[128,4096]{1,0:T(8,128)(2,1)S(1)} %collective-permute-done.16.x3, bf16[1000,7950]{1,0:T(8,128)(2,1)} %r.7), custom_call_target="tpu_custom_call" | custom-call | flops 12582912000 | bytes 16777216 | tf_op jit(solution)/shard_map/pallas_call | solution.py:145
  124.0 3.6 %collective-permute-done.20.x1 = bf16[128,4096]{1,0:T(8,128)(2,1)S(1)} collective-permute-done((bf16[128,4096]{1,0:T(8,128)(2,1)S(1)}, bf16[128,4096]{1,0:T(8,128)(2,1)S(1)}, u32[]{:S(2)}, u32[]{:S(2)}) %collective-permute-start.20) | collective-permute-done | bytes 1048608 | tf_op jit(solution)/shard_map/ppermute | solution.py:39
  127.6 3.7 %collective-permute-start.25 = (bf16[128,4096]{1,0:T(8,128)(2,1)S(1)}, bf16[128,4096]{1,0:T(8,128)(2,1)S(1)}, u32[]{:S(2)}, u32[]{:S(2)}) collective-permute-start(bf16[128,4096]{1,0:T(8,128)(2,1)S(1)} %collective-permute-done.20.x1), channel_id=1, source_target_pairs={{0,4},{1,5},{2,6},{3,7},{4,8},{5,9},{6,10},{7,11},{8,12},{9,13},{1... | collective-permute-start | bytes 3145736 | tf_op jit(solution)/shard_map/ppermute | solution.py:39
  134.1 15.2 %shard_map.56 = (f32[256,1000]{1,0:T(8,128)}, bf16[256,1000]{1,0:T(8,128)(2,1)S(1)}, bf16[512,128]{1,0:T(8,128)(2,1)S(1)}) custom-call(bf16[128,3968]{1,0:T(8,128)(2,1)S(1)} %pad_maximum_fusion.2.x0, bf16[128,3968]{1,0:T(8,128)(2,1)S(1)} %collective-permute-done.9.x1, bf16[128,3968]{1,0:T(8,128)(2,1)S(1)} %collective-permute-done.10.x2, ...), custom_call_target="tpu_custom_call" | custom-call | flops 12582912000 | bytes 16777216 | tf_op jit(solution)/shard_map/pallas_call | solution.py:181
  155.6 15.7 %collective-permute-done.29.x2 = bf16[128,3968]{1,0:T(8,128)(2,1)S(1)} collective-permute-done((bf16[128,3968]{1,0:T(8,128)(2,1)S(1)}, bf16[128,3968]{1,0:T(8,128)(2,1)S(1)}, u32[]{:S(2)}, u32[]{:S(2)}) %collective-permute-start.29) | collective-permute-done | bytes 1015840 | tf_op jit(solution)/shard_map/ppermute | solution.py:39
  171.3 8.7 %shard_map.57.acc = f32[512,1000]{1,0:T(8,128)} custom-call(bf16[128,4096]{1,0:T(8,128)(2,1)S(1)} %pad_maximum_fusion.1.x0, bf16[128,4096]{1,0:T(8,128)(2,1)S(1)} %collective-permute-done.20.x1, bf16[128,4096]{1,0:T(8,128)(2,1)S(1)} %collective-permute-done.25.x2, bf16[128,4096]{1,0:T(8,128)(2,1)S(1)} %collective-permute-done.31.x3, bf16[1000,7950]{1,0:T(8,128)(2,1)} %r.7), custom_call_target="tpu_custom_call" | custom-call | flops 12582912000 | bytes 16777216 | tf_op jit(solution)/shard_map/pallas_call | solution.py:145
  180.0 7.0 %collective-permute-done.30.x3 = bf16[128,3968]{1,0:T(8,128)(2,1)S(1)} collective-permute-done((bf16[128,3968]{1,0:T(8,128)(2,1)S(1)}, bf16[128,3968]{1,0:T(8,128)(2,1)S(1)}, u32[]{:S(2)}, u32[]{:S(2)}) %collective-permute-start.30) | collective-permute-done | bytes 1015840 | tf_op jit(solution)/shard_map/ppermute | solution.py:39
  186.9 15.2 %shard_map.58 = (f32[256,1000]{1,0:T(8,128)}, bf16[256,1000]{1,0:T(8,128)(2,1)S(1)}) custom-call(bf16[128,3968]{1,0:T(8,128)(2,1)S(1)} %pad_maximum_fusion.3.x0, bf16[128,3968]{1,0:T(8,128)(2,1)S(1)} %collective-permute-done.23.x1, bf16[128,3968]{1,0:T(8,128)(2,1)S(1)} %collective-permute-done.29.x2, bf16[128,3968]{1,0:T(8,128)(2,1)S(1)} %collective-permute-done.30.x3, ...), custom_call_target="tpu_custom_call" | custom-call | flops 12582912000 | bytes 16777216 | tf_op jit(solution)/shard_map/pallas_call | solution.py:181
  218.2 5.6 %shard_map.59 = bf16[4,128,975]{2,1,0:T(8,128)(2,1)S(1)} custom-call(bf16[128,1000]{1,0:T(8,128)(2,1)S(1)} %bitcast.89, bf16[8,975,1000]{2,1,0:T(8,128)(2,1)} %all-gather.4.cloned.1.call-done.f), custom_call_target="tpu_custom_call" | custom-call | flops 2995200000 | bytes 7800000 | tf_op jit(solution)/shard_map/pallas_call | solution.py:202
  226.0 5.6 %shard_map.60 = bf16[4,128,975]{2,1,0:T(8,128)(2,1)S(1)} custom-call(bf16[128,1000]{1,0:T(8,128)(2,1)S(1)} %bitcast.90, bf16[8,975,1000]{2,1,0:T(8,128)(2,1)} %all-gather.4.cloned.1.call-done.f), custom_call_target="tpu_custom_call" | custom-call | flops 2995200000 | bytes 7800000 | tf_op jit(solution)/shard_map/pallas_call | solution.py:202
  238.3 5.9 %collective-permute-done.40 = bf16[4,32,975]{2,1,0:T(8,128)(2,1)S(1)} collective-permute-done((bf16[4,32,975]{2,1,0:T(8,128)(2,1)S(1)}, bf16[4,32,975]{2,1,0:T(8,128)(2,1)S(1)}, u32[]{:S(2)}, u32[]{:S(2)}) %collective-permute-start.40) | collective-permute-done | bytes 249632 | tf_op jit(solution)/shard_map/ppermute | solution.py:39
  (123 shorter events, 73.0 us)
Async XLA Ops:
  6.5 211.6 %all-gather.4.cloned.1.call-start = ((), (), s32[]{:S(2)}) async-start(), calls=%async_computation | async-start | bytes 17989632 | tf_op jit(solution)/shard_map/all_gather | solution.py:242
  39.9 27.9 %collective-permute-start.14 = (bf16[128,4096]{1,0:T(8,128)(2,1)S(1)}, bf16[128,4096]{1,0:T(8,128)(2,1)S(1)}, u32[]{:S(2)}, u32[]{:S(2)}) collective-permute-start(bf16[128,4096]{1,0:T(8,128)(2,1)S(1)} %pad_maximum_fusion.x0), channel_id=1, source_target_pairs={{0,4},{1,5},{2,6},{3,7},{4,8},{5,9},{6,10},{7,11},{8,12},{9,13},{1... | collective-permute-start | bytes 3145736 | tf_op jit(solution)/shard_map/ppermute | solution.py:39
  41.6 15.9 %collective-permute-start.6 = (bf16[32,3968]{1,0:T(8,128)(2,1)S(1)}, bf16[32,3968]{1,0:T(8,128)(2,1)S(1)}, u32[]{:S(2)}, u32[]{:S(2)}) collective-permute-start(bf16[32,3968]{1,0:T(8,128)(2,1)S(1)} %pad_add_fusion), channel_id=1, source_target_pairs={{0,4},{1,5},{2,6},{3,7},{4,8},{5,9},{6,10},{7,11},{8,12},{9,13},{1... | collective-permute-start | bytes 761864 | tf_op jit(solution)/shard_map/ppermute | solution.py:39
  67.8 26.1 %collective-permute-start.15 = (bf16[128,4096]{1,0:T(8,128)(2,1)S(1)}, bf16[128,4096]{1,0:T(8,128)(2,1)S(1)}, u32[]{:S(2)}, u32[]{:S(2)}) collective-permute-start(bf16[128,4096]{1,0:T(8,128)(2,1)S(1)} %collective-permute-done.14.x1), channel_id=1, source_target_pairs={{0,4},{1,5},{2,6},{3,7},{4,8},{5,9},{6,10},{7,11},{8,12},{9,13},{1... | collective-permute-start | bytes 3145736 | tf_op jit(solution)/shard_map/ppermute | solution.py:39
  71.7 22.2 %collective-permute-start.9 = (bf16[128,3968]{1,0:T(8,128)(2,1)S(1)}, bf16[128,3968]{1,0:T(8,128)(2,1)S(1)}, u32[]{:S(2)}, u32[]{:S(2)}) collective-permute-start(bf16[128,3968]{1,0:T(8,128)(2,1)S(1)} %pad_maximum_fusion.2.x0), channel_id=1, source_target_pairs={{0,1},{1,2},{2,3},{3,0},{4,5},{5,6},{6,7},{7,4},{8,9},{9,10},{10,1... | collective-permute-start | bytes 3047432 | tf_op jit(solution)/shard_map/ppermute | solution.py:39
  71.7 18.5 %collective-permute-start.17 = (bf16[32,4096]{1,0:T(8,128)(2,1)S(1)}, bf16[32,4096]{1,0:T(8,128)(2,1)S(1)}, u32[]{:S(2)}, u32[]{:S(2)}) collective-permute-start(bf16[32,4096]{1,0:T(8,128)(2,1)S(1)} %get-tuple-element.50), channel_id=1, source_target_pairs={{0,1},{1,2},{2,3},{3,0},{4,5},{5,6},{6,7},{7,4},{8,9},{9,10},{10,1... | collective-permute-start | bytes 786440 | tf_op jit(solution)/shard_map/ppermute | solution.py:39
  71.8 18.4 %collective-permute-start.21 = (bf16[32,3968]{1,0:T(8,128)(2,1)S(1)}, bf16[32,3968]{1,0:T(8,128)(2,1)S(1)}, u32[]{:S(2)}, u32[]{:S(2)}) collective-permute-start(bf16[32,3968]{1,0:T(8,128)(2,1)S(1)} %collective-permute-done.1), channel_id=1, source_target_pairs={{0,4},{1,5},{2,6},{3,7},{4,8},{5,9},{6,10},{7,11},{8,12},{9,13},{1... | collective-permute-start | bytes 761864 | tf_op jit(solution)/shard_map/ppermute | solution.py:39
  90.2 12.2 %collective-permute-start.18 = (bf16[32,4096]{1,0:T(8,128)(2,1)S(1)}, bf16[32,4096]{1,0:T(8,128)(2,1)S(1)}, u32[]{:S(2)}, u32[]{:S(2)}) collective-permute-start(bf16[32,4096]{1,0:T(8,128)(2,1)S(1)} %collective-permute-done.17), channel_id=1, source_target_pairs={{0,1},{1,2},{2,3},{3,0},{4,5},{5,6},{6,7},{7,4},{8,9},{9,10},{10,1... | collective-permute-start | bytes 786440 | tf_op jit(solution)/shard_map/ppermute | solution.py:39
  90.2 13.1 %collective-permute-start.22 = (bf16[32,3968]{1,0:T(8,128)(2,1)S(1)}, bf16[32,3968]{1,0:T(8,128)(2,1)S(1)}, u32[]{:S(2)}, u32[]{:S(2)}) collective-permute-start(bf16[32,3968]{1,0:T(8,128)(2,1)S(1)} %collective-permute-done.21), channel_id=1, source_target_pairs={{0,4},{1,5},{2,6},{3,7},{4,8},{5,9},{6,10},{7,11},{8,12},{9,13},{1... | collective-permute-start | bytes 761864 | tf_op jit(solution)/shard_map/ppermute | solution.py:39
  93.9 21.4 %collective-permute-start.10 = (bf16[128,3968]{1,0:T(8,128)(2,1)S(1)}, bf16[128,3968]{1,0:T(8,128)(2,1)S(1)}, u32[]{:S(2)}, u32[]{:S(2)}) collective-permute-start(bf16[128,3968]{1,0:T(8,128)(2,1)S(1)} %collective-permute-done.9.x1), channel_id=1, source_target_pairs={{0,1},{1,2},{2,3},{3,0},{4,5},{5,6},{6,7},{7,4},{8,9},{9,10},{10,1... | collective-permute-start | bytes 3047432 | tf_op jit(solution)/shard_map/ppermute | solution.py:39
  93.9 21.4 %collective-permute-start.16 = (bf16[128,4096]{1,0:T(8,128)(2,1)S(1)}, bf16[128,4096]{1,0:T(8,128)(2,1)S(1)}, u32[]{:S(2)}, u32[]{:S(2)}) collective-permute-start(bf16[128,4096]{1,0:T(8,128)(2,1)S(1)} %collective-permute-done.15.x2), channel_id=1, source_target_pairs={{0,4},{1,5},{2,6},{3,7},{4,8},{5,9},{6,10},{7,11},{8,12},{9,13},{1... | collective-permute-start | bytes 3145736 | tf_op jit(solution)/shard_map/ppermute | solution.py:39
  102.4 10.0 %collective-permute-start.19 = (bf16[32,4096]{1,0:T(8,128)(2,1)S(1)}, bf16[32,4096]{1,0:T(8,128)(2,1)S(1)}, u32[]{:S(2)}, u32[]{:S(2)}) collective-permute-start(bf16[32,4096]{1,0:T(8,128)(2,1)S(1)} %collective-permute-done.18), channel_id=1, source_target_pairs={{0,1},{1,2},{2,3},{3,0},{4,5},{5,6},{6,7},{7,4},{8,9},{9,10},{10,1... | collective-permute-start | bytes 786440 | tf_op jit(solution)/shard_map/ppermute | solution.py:39
  103.4 45.9 %collective-permute-start.23 = (bf16[128,3968]{1,0:T(8,128)(2,1)S(1)}, bf16[128,3968]{1,0:T(8,128)(2,1)S(1)}, u32[]{:S(2)}, u32[]{:S(2)}) collective-permute-start(bf16[128,3968]{1,0:T(8,128)(2,1)S(1)} %pad_maximum_fusion.3.x0), channel_id=1, source_target_pairs={{0,1},{1,2},{2,3},{3,0},{4,5},{5,6},{6,7},{7,4},{8,9},{9,10},{10,1... | collective-permute-start | bytes 3047432 | tf_op jit(solution)/shard_map/ppermute | solution.py:39
  112.4 15.2 %collective-permute-start.20 = (bf16[128,4096]{1,0:T(8,128)(2,1)S(1)}, bf16[128,4096]{1,0:T(8,128)(2,1)S(1)}, u32[]{:S(2)}, u32[]{:S(2)}) collective-permute-start(bf16[128,4096]{1,0:T(8,128)(2,1)S(1)} %pad_maximum_fusion.1.x0), channel_id=1, source_target_pairs={{0,4},{1,5},{2,6},{3,7},{4,8},{5,9},{6,10},{7,11},{8,12},{9,13},{1... | collective-permute-start | bytes 3145736 | tf_op jit(solution)/shard_map/ppermute | solution.py:39
  115.3 18.8 %collective-permute-start.11 = (bf16[128,3968]{1,0:T(8,128)(2,1)S(1)}, bf16[128,3968]{1,0:T(8,128)(2,1)S(1)}, u32[]{:S(2)}, u32[]{:S(2)}) collective-permute-start(bf16[128,3968]{1,0:T(8,128)(2,1)S(1)} %collective-permute-done.10.x2), channel_id=1, source_target_pairs={{0,1},{1,2},{2,3},{3,0},{4,5},{5,6},{6,7},{7,4},{8,9},{9,10},{10,1... | collective-permute-start | bytes 3047432 | tf_op jit(solution)/shard_map/ppermute | solution.py:39
  127.6 25.1 %collective-permute-start.25 = (bf16[128,4096]{1,0:T(8,128)(2,1)S(1)}, bf16[128,4096]{1,0:T(8,128)(2,1)S(1)}, u32[]{:S(2)}, u32[]{:S(2)}) collective-permute-start(bf16[128,4096]{1,0:T(8,128)(2,1)S(1)} %collective-permute-done.20.x1), channel_id=1, source_target_pairs={{0,4},{1,5},{2,6},{3,7},{4,8},{5,9},{6,10},{7,11},{8,12},{9,13},{1... | collective-permute-start | bytes 3145736 | tf_op jit(solution)/shard_map/ppermute | solution.py:39
  152.7 18.5 %collective-permute-start.31 = (bf16[128,4096]{1,0:T(8,128)(2,1)S(1)}, bf16[128,4096]{1,0:T(8,128)(2,1)S(1)}, u32[]{:S(2)}, u32[]{:S(2)}) collective-permute-start(bf16[128,4096]{1,0:T(8,128)(2,1)S(1)} %collective-permute-done.25.x2), channel_id=1, source_target_pairs={{0,4},{1,5},{2,6},{3,7},{4,8},{5,9},{6,10},{7,11},{8,12},{9,13},{1... | collective-permute-start | bytes 3145736 | tf_op jit(solution)/shard_map/ppermute | solution.py:39
  155.6 15.7 %collective-permute-start.29 = (bf16[128,3968]{1,0:T(8,128)(2,1)S(1)}, bf16[128,3968]{1,0:T(8,128)(2,1)S(1)}, u32[]{:S(2)}, u32[]{:S(2)}) collective-permute-start(bf16[128,3968]{1,0:T(8,128)(2,1)S(1)} %collective-permute-done.23.x1), channel_id=1, source_target_pairs={{0,1},{1,2},{2,3},{3,0},{4,5},{5,6},{6,7},{7,4},{8,9},{9,10},{10,1... | collective-permute-start | bytes 3047432 | tf_op jit(solution)/shard_map/ppermute | solution.py:39
  171.3 15.7 %collective-permute-start.30 = (bf16[128,3968]{1,0:T(8,128)(2,1)S(1)}, bf16[128,3968]{1,0:T(8,128)(2,1)S(1)}, u32[]{:S(2)}, u32[]{:S(2)}) collective-permute-start(bf16[128,3968]{1,0:T(8,128)(2,1)S(1)} %collective-permute-done.29.x2), channel_id=1, source_target_pairs={{0,1},{1,2},{2,3},{3,0},{4,5},{5,6},{6,7},{7,4},{8,9},{9,10},{10,1... | collective-permute-start | bytes 3047432 | tf_op jit(solution)/shard_map/ppermute | solution.py:39
  202.6 10.3 %collective-permute-start.27 = (bf16[2,32,1000]{2,1,0:T(8,128)(2,1)S(1)}, bf16[2,32,1000]{2,1,0:T(8,128)(2,1)S(1)}, u32[]{:S(2)}, u32[]{:S(2)}) collective-permute-start(bf16[2,32,1000]{2,1,0:T(8,128)(2,1)S(1)} %get-tuple-element.46), channel_id=1, source_target_pairs={{0,96},{1,97},{2,98},{3,99},{4,100},{5,101},{6,102},{7,103},{8,104... | collective-permute-start | bytes 384008 | tf_op jit(solution)/shard_map/ppermute | solution.py:39
  223.9 10.5 %collective-permute-start.36 = (bf16[4,32,975]{2,1,0:T(8,128)(2,1)S(1)}, bf16[4,32,975]{2,1,0:T(8,128)(2,1)S(1)}, u32[]{:S(2)}, u32[]{:S(2)}) collective-permute-start(bf16[4,32,975]{2,1,0:T(8,128)(2,1)S(1)} %get-tuple-element.38), channel_id=1, source_target_pairs={{0,4},{1,5},{2,6},{3,7},{4,8},{5,9},{6,10},{7,11},{8,12},{9,13},{1... | collective-permute-start | bytes 748808 | tf_op jit(solution)/shard_map/ppermute | solution.py:39
  224.0 13.3 %collective-permute-start.37 = (bf16[4,32,975]{2,1,0:T(8,128)(2,1)S(1)}, bf16[4,32,975]{2,1,0:T(8,128)(2,1)S(1)}, u32[]{:S(2)}, u32[]{:S(2)}) collective-permute-start(bf16[4,32,975]{2,1,0:T(8,128)(2,1)S(1)} %get-tuple-element.40), channel_id=1, source_target_pairs={{0,12},{1,13},{2,14},{3,15},{4,0},{5,1},{6,2},{7,3},{8,4},{9,5},{1... | collective-permute-start | bytes 748808 | tf_op jit(solution)/shard_map/ppermute | solution.py:39
  226.0 11.3 %collective-permute-start.38 = (bf16[4,32,975]{2,1,0:T(8,128)(2,1)S(1)}, bf16[4,32,975]{2,1,0:T(8,128)(2,1)S(1)}, u32[]{:S(2)}, u32[]{:S(2)}) collective-permute-start(bf16[4,32,975]{2,1,0:T(8,128)(2,1)S(1)} %get-tuple-element.39), channel_id=1, source_target_pairs={{0,8},{1,9},{2,10},{3,11},{4,12},{5,13},{6,14},{7,15},{8,0},{9,1},... | collective-permute-start | bytes 748808 | tf_op jit(solution)/shard_map/ppermute | solution.py:39
  234.4 11.0 %collective-permute-start.41 = (bf16[4,32,975]{2,1,0:T(8,128)(2,1)S(1)}, bf16[4,32,975]{2,1,0:T(8,128)(2,1)S(1)}, u32[]{:S(2)}, u32[]{:S(2)}) collective-permute-start(bf16[4,32,975]{2,1,0:T(8,128)(2,1)S(1)} %get-tuple-element.42), channel_id=1, source_target_pairs={{0,8},{1,9},{2,10},{3,11},{4,12},{5,13},{6,14},{7,15},{8,0},{9,1},... | collective-permute-start | bytes 748808 | tf_op jit(solution)/shard_map/ppermute | solution.py:39
  (25 other events, 150.9 us)
Sparse Core Ops, SparseCore 0:
  9.0 83.9 all-gather.3

commit v3 on v0

v3 whole, which is shorter than its diff:
```python
import functools

import jax
import jax.numpy as jnp
from jax import lax
from jax.experimental import pallas as pl
from jax.experimental.pallas import tpu as pltpu
from jax.sharding import PartitionSpec as P

SENSORS = 6
AXES = ("sens", "layer")
SIDE = 4
ROWS = 64
HALF = 4096
QUARTER = 2048
BWIDTH = 3968
EDGE = BWIDTH - 128
INSIDE = 14
SPAN = 24
PBLOCK = 256
VMEM = 52 * 2**20


def moved(fn):
    pairs = []
    for z in range(4):
        for c in range(2):
            for y in range(4):
                for x in range(4):
                    z2, c2, y2, x2 = fn(z, c, y, x)
                    pairs.append(
                        ((z * 2 + c) * 16 + y * 4 + x,
                         ((z2 % 4) * 2 + c2 % 2) * 16 + (y2 % 4) * 4 + x2 % 4)
                    )
    return pairs


def send(x, fn):
    return lax.ppermute(x, AXES, moved(fn))


def swap_core(v):
    return send(v, lambda z, c, y, x: (z, c + 1, y, x))


def right(v):
    return send(v, lambda z, c, y, x: (z, c, y, x + 1))


def left(v):
    return send(v, lambda z, c, y, x: (z, c, y, x - 1))


def up(v):
    return send(v, lambda z, c, y, x: (z, c, y + 1, x))


def down(v):
    return send(v, lambda z, c, y, x: (z, c, y - 1, x))


def hop_z(d):
    return lambda z, c, y, x: (z + d, c, y, x)


def hop_one(d):
    return lambda z, c, y, x: (z, c, y + d * (1 - c), x + d * c)


def hop_two(d):
    return lambda z, c, y, x: (z, c, y + d * c, x + d * (1 - c))


def home(z, c, y, x):
    layer = y * 4 + x
    sens, layer = layer // 2, 8 * (layer % 2) + z * 2 + c
    return (sens // 2, sens % 2, layer // 4, layer % 4)


def after(value, *others):
    return lax.optimization_barrier((value, *others))


def nt(a, b, **kw):
    return lax.dot_general(
        a, b, (((1,), (1,)), ((), ())), preferred_element_type=jnp.float32, **kw
    )


def reconstruct_kernel(pieces, count, *refs):
    arrays = refs[:count]
    core, ra, rb, rw, own, other, held, sems = refs[count:]

    @pl.when(pl.program_id(0) == 0)
    def _():
        copies = []
        for i, (a, row, rows, to_row, to_col) in enumerate(pieces):
            width = arrays[a].shape[1]
            copies.append(
                pltpu.make_async_copy(
                    arrays[a].at[pl.ds(row, rows)],
                    held.at[pl.ds(to_row, rows), pl.ds(to_col, width)],
                    sems.at[i],
                )
            )
        for copy in copies:
            copy.start()
        for copy in copies:
            copy.wait()

    lane = lax.broadcasted_iota(jnp.int32, (ra.shape[0], 128), 1)
    edge = jnp.where(
        lane < INSIDE, rb[:, EDGE:BWIDTH].astype(jnp.float32), rw[:, :128].astype(jnp.float32)
    ).astype(jnp.bfloat16)
    tail = held[:, HALF + EDGE :]
    val = nt(held[:, :HALF], ra[...]) + nt(held[:, HALF : HALF + EDGE], rb[:, :EDGE])
    val = val + nt(tail, edge) + nt(tail, rw[:, 128:])
    n = val.shape[0]
    pairs = val.reshape(n // 16, 2, 8, val.shape[1])
    first = pairs[:, 0].reshape(n // 2, val.shape[1])
    second = pairs[:, 1].reshape(n // 2, val.shape[1])
    swapped = core[0] == 1
    own[...] = jnp.where(swapped, second, first)
    other[...] = jnp.where(swapped, first, second).astype(jnp.bfloat16)


def reconstruct(sources, core, r, rw):
    arrays, pieces = [], []
    for k, source in enumerate(sources):
        for array, row, col in source:
            found = [i for i, a in enumerate(arrays) if a is array]
            if not found:
                arrays.append(array)
                found = [len(arrays) - 1]
            pieces.append((found[0], row, ROWS, k * ROWS, col))
    n = ROWS * len(sources)
    p = r.shape[0]
    half = pl.BlockSpec((n // 2, PBLOCK), lambda j: (0, j))
    return pl.pallas_call(
        functools.partial(reconstruct_kernel, tuple(pieces), len(arrays)),
        grid=(pl.cdiv(p, PBLOCK),),
        in_specs=[pl.BlockSpec(memory_space=pl.ANY)] * len(arrays)
        + [
            pl.BlockSpec(memory_space=pltpu.SMEM),
            pl.BlockSpec((PBLOCK, HALF), lambda j: (j, 0)),
            pl.BlockSpec((PBLOCK, HALF), lambda j: (j, 1)),
            pl.BlockSpec((PBLOCK, 256), lambda j: (j, 0)),
        ],
        out_specs=[half, half],
        out_shape=[
            jax.ShapeDtypeStruct((n // 2, p), jnp.float32),
            jax.ShapeDtypeStruct((n // 2, p), jnp.bfloat16),
        ],
        scratch_shapes=[
            pltpu.VMEM((n, HALF + BWIDTH), jnp.bfloat16),
            pltpu.SemaphoreType.DMA((len(pieces),)),
        ],
        compiler_params=pltpu.CompilerParams(vmem_limit_bytes=VMEM),
        cost_estimate=pl.CostEstimate(
            flops=4 * n * 8000 * p, bytes_accessed=24 * 2**20, transcendentals=0
        ),
    )(*arrays, core, r, r, rw)


def fit_kernel(p, f, out):
    out[0] = nt(p[...], f[0]).astype(jnp.bfloat16)


def fit(points, fitting, start, count):
    n, k = points.shape
    m = fitting.shape[1]
    return pl.pallas_call(
        fit_kernel,
        grid=(count,),
        in_specs=[
            pl.BlockSpec((n, k), lambda s: (0, 0)),
            pl.BlockSpec((1, m, k), lambda s: (s + start, 0, 0)),
        ],
        out_specs=pl.BlockSpec((1, n, m), lambda s: (s, 0, 0)),
        out_shape=jax.ShapeDtypeStruct((count, n, m), jnp.bfloat16),
        compiler_params=pltpu.CompilerParams(vmem_limit_bytes=VMEM),
        cost_estimate=pl.CostEstimate(
            flops=6 * n * m * k * count, bytes_accessed=2 * count * m * k, transcendentals=0
        ),
    )(points, fitting)


def sums_by_z(own, other, z):
    got = own + swap_core(other).astype(jnp.float32)
    got = got.reshape(-1, SIDE, 8, own.shape[1])

    def pick(d):
        return lax.dynamic_index_in_dim(got, (z + d) % SIDE, 1, keepdims=False)

    pieces = [pick(0)] + [send(pick(d).astype(jnp.bfloat16), hop_z(d)) for d in (1, 3, 2)]
    return total(pieces).astype(jnp.bfloat16)


def owned(blocks, hop):
    pieces = [blocks[:, 0]]
    pieces += [send(blocks[:, d].astype(jnp.bfloat16), hop(d)) for d in (1, 3, 2)]
    return pieces


def total(pieces):
    out = pieces[0].astype(jnp.float32)
    for piece in pieces[1:]:
        out = out + piece.astype(jnp.float32)
    return out


def per_device(slopes, valid, sensor_map, reconstructor, fitting):
    s_idx = lax.axis_index("sens")
    z, c = s_idx // 2, s_idx % 2
    width = slopes.shape[1]
    width_p = reconstructor.shape[0]
    act = fitting.shape[0]
    core = jnp.full((1,), c, jnp.int32)

    everything = lax.all_gather(fitting, "sens", axis=0)

    live = valid.astype(jnp.bfloat16)[None, :]
    a = {(0, 0): slopes[:, :HALF] * live[:, :HALF]}
    own_a = a[0, 0]
    from_left, from_right = right(own_a), left(own_a)
    from_down, from_up = up(own_a), down(own_a)

    masked = slopes * live
    group = sensor_map * 2 + (lax.iota(jnp.int32, width) + s_idx * width) % 2
    lane = lax.iota(jnp.int32, 128)
    inside = (lane >= INSIDE) & (lane < INSIDE + SPAN)
    label = jnp.where(inside, (lane - INSIDE) % 12, -1)
    member = ((group[None, :] == label[:, None]) & (valid[None, :] == 1)).astype(jnp.bfloat16)
    counted = jnp.concatenate([masked, jnp.ones((8, width), jnp.bfloat16)], axis=0)
    stats = nt(counted, member)
    stats = stats + swap_core(stats)
    others = [send(stats, hop_z(d)) for d in (1, 3, 2)]
    stats = (stats + others[2]) + (others[0] + others[1])
    means = stats[:ROWS] / jnp.maximum(stats[ROWS : ROWS + 1], 1.0)
    high = lax.reduce_precision(means, 8, 7)
    rows = jnp.where((lane < INSIDE + 12)[None, :], high, means - high)
    rows = jnp.where(inside[None, :], rows, 0.0).astype(jnp.bfloat16)
    own_b = jnp.pad(masked[:, HALF:], ((0, 0), (0, HALF + BWIDTH - width)))
    own_b = own_b + jnp.pad(rows, ((0, 0), (EDGE, 0)))

    b_left, b_right = right(own_b), left(own_b)
    b_down, b_up = up(own_b), down(own_b)

    rw = -nt(reconstructor, member)
    rw_high = lax.reduce_precision(rw, 8, 7)
    rw = jnp.concatenate([rw_high, rw - rw_high], axis=1).astype(jnp.bfloat16)

    pair = jnp.concatenate([from_left, from_right], axis=0)
    a_down, a_up = up(pair), down(pair)
    far_x_a = right(from_left)
    far_y_a = up(from_down)
    pair_b = jnp.concatenate([b_down, b_up], axis=0)
    bx_left, bx_right = right(pair_b), left(pair_b)
    far_x_b = left(b_right)
    far_y_b = down(b_up)

    def whole(array_a, array_b, row_a=0, row_b=0):
        return [(array_a, row_a, 0), (array_b, row_b, HALF)]

    own0, other0 = reconstruct(
        [
            whole(own_a, own_b),
            whole(from_left, b_left),
            whole(from_right, b_right),
            whole(from_down, b_down),
            whole(from_up, b_up),
        ],
        core, reconstructor, rw,
    )

    own0, other0, far_x_a, far_y_b = after(own0, other0, far_x_a, far_y_b)
    c_down, c_up = up(far_x_a), down(far_x_a)
    c_low = up(a_down[:, :QUARTER])
    c_high = down(a_up[:, QUARTER:])
    d_left, d_right = right(far_y_b), left(far_y_b)
    d_low = right(bx_left[:, :QUARTER])
    d_high = left(bx_right[:, QUARTER:])

    own1, other1 = reconstruct(
        [
            whole(a_down, bx_left, 0, 0),
            whole(a_down, bx_right, ROWS, 0),
            whole(a_up, bx_left, 0, ROWS),
            whole(a_up, bx_right, ROWS, ROWS),
            whole(far_x_a, far_x_b),
            whole(far_y_a, far_y_b),
        ],
        core, reconstructor, rw,
    )

    own1, other1, c_down, c_up, d_left, d_right = after(own1, other1, c_down, c_up, d_left, d_right)
    e_a_low = up(c_down[:, :QUARTER])
    e_a_high = down(c_up[:, QUARTER:])
    e_b_low = right(d_left[:, :QUARTER])
    e_b_high = left(d_right[:, QUARTER:])

    near = sums_by_z(
        jnp.concatenate([own0, own1], axis=0), jnp.concatenate([other0, other1], axis=0), z
    )
    near, e_a_low = after(near, e_a_low)

    own2, other2 = reconstruct(
        [
            [(c_down, 0, 0), (d_low, 0, HALF), (d_high, 0, HALF + QUARTER)],
            [(c_up, 0, 0), (d_low, ROWS, HALF), (d_high, ROWS, HALF + QUARTER)],
            [(c_low, 0, 0), (c_high, 0, QUARTER), (d_left, 0, HALF)],
            [(c_low, ROWS, 0), (c_high, ROWS, QUARTER), (d_right, 0, HALF)],
            [(e_a_low, 0, 0), (e_a_high, 0, QUARTER), (e_b_low, 0, HALF),
             (e_b_high, 0, HALF + QUARTER)],
        ],
        core, reconstructor, rw,
    )
    far = sums_by_z(own2, other2, z)

    names = [
        (0, 0), (0, 3), (0, 1), (3, 0), (1, 0),
        (3, 3), (3, 1), (1, 3), (1, 1), (0, 2), (2, 0),
        (3, 2), (1, 2), (2, 3), (2, 1), (2, 2),
    ]
    points = jnp.concatenate([near, far], axis=0)
    y_first = jnp.stack([points[names.index((i, j))] for i in range(4) for j in range(4)])
    x_first = jnp.stack([points[names.index((i, j))] for j in range(4) for i in range(4)])
    rows = jnp.where(c == 0, y_first, x_first).reshape(16 * 8, width_p)
    half_a = owned(fit(rows, everything, 0, 4).reshape(4, SIDE, SIDE * 8, act), hop_one)
    half_b = owned(fit(rows, everything, 4, 4).reshape(4, SIDE, SIDE * 8, act), hop_one)
    both = jnp.concatenate([total(half_a), total(half_b)], axis=0)
    done = total(owned(both.reshape(8, SIDE, 8, act), hop_two)).astype(jnp.bfloat16)
    done = jnp.moveaxis(done, 0, 1).reshape(8, 8 * act)
    return send(done, home).astype(jnp.float32)


def solution(mesh):
    placed = (P("layer", "sens"), P("sens"), P("sens"), P("layer", "sens"), P("sens", "layer"))
    return jax.shard_map(
        per_device,
        mesh=mesh,
        in_specs=placed,
        out_specs=P(("sens", "layer"), None),
        check_vma=False,
    )
```

time: 285 us -> 244 us (0.86)
  starting transfers between devices: 9.18 us -> 68.3 us
  Pallas kernels: 0 us -> 51 us
  matrix products: 59.2 us -> 9.4 us
  blocking collectives: 39.9 us -> 0 us
  local copies, waits for them, and re-layouts: 48.2 us -> 15.1 us
  waiting for transfers between devices: 110 us -> 78 us
  other arithmetic: 2.25 us -> 7.68 us
    all_gather x2 -> x1, waiting for transfers between devices: 104 us -> 0.02 us  [per_device(): everything = lax.all_gather(fitting, 'sens', axis=0)]
    ppermute x0 -> x50, waiting for transfers between devices: none -> 77.3 us  [send(): return lax.ppermute(x, AXES, moved(fn))]
    ppermute x0 -> x50, starting transfers between devices: none -> 68.3 us  [send(): return lax.ppermute(x, AXES, moved(fn))]
    pallas_call x0 -> x5, Pallas kernels: none -> 51 us  [the longest x3 39.8 us: reconstruct(): pl.pallas_call(functools.partial(reconstruct_kernel, tuple(pieces), len(a...]
    dot_general x5 -> x2, matrix products: 59.2 us -> 9.4 us  [nt(): lax.dot_general(a, b, (((1,), (1,)), ((), ())), preferred_element_type=jn...]
    all_to_all x2 -> x0, blocking collectives: 39.9 us -> none  [the longest x1 29.5 us: summed_on_arrival(): lax.all_to_all(blocks, axis, split_axis=0, concat_axis=0, tiled=True)]
    all_gather x1 -> x0, local copies, waits for them, and re-layouts: 22.4 us -> none  [per_device(): whole = lax.all_gather(slopes, 'layer', axis=0, tiled=True)]
    unnamed x1 -> x60, local copies, waits for them, and re-layouts: 20.5 us -> 2.26 us
  transfers between devices with their start and end apart: 4 -> 51, of which waited for: 3 -> 21; matrix products, arithmetic and copies ran while one was open for 34% -> 12% of each run, Pallas kernels for 0% -> 19%
where the time goes in v3:
time: 244 us
  waiting for transfers between devices  78 us (32%)
  starting transfers between devices  68.3 us (28%)
  Pallas kernels  51 us (21%)
  local copies, waits for them, and re-layouts  15.1 us (6%)
  between operations  14.1 us (6%)
  matrix products  9.4 us (4%)
  other arithmetic  7.68 us (3%)
    ppermute x50, waiting for transfers between devices, send(): return lax.ppermute(x, AXES, moved(fn))  77.3 us
    ppermute x50, starting transfers between devices, send(): return lax.ppermute(x, AXES, moved(fn))  68.3 us
    pallas_call x3, Pallas kernels, reconstruct(): pl.pallas_call(functools.partial(reconstruct_kernel, tuple(pieces), len(a...  39.8 us
    pallas_call x2, Pallas kernels, fit(): pl.pallas_call(fit_kernel, grid=(count,), in_specs=[pl.BlockSpec((n, k),...  11.2 us
    dot_general x2, matrix products, nt(): lax.dot_general(a, b, (((1,), (1,)), ((), ())), preferred_element_type=jn...  9.4 us
  transfers between devices with their start and end apart: 51, of which 21 were waited for; matrix products, arithmetic and copies ran while one was open for 12% of the time, Pallas kernels for 19%

profile of v3, /device:TPU:24, one launch (start us, length us, event | category | flops | bytes accessed | tf_op | source)
XLA Modules:
  0.0 243.6 jit_solution(199132473695183318)
XLA Ops:
  12.5 8.3 %reduce-precision_convert_fusion = (bf16[1000,128]{1,0:T(8,128)(2,1)S(1)}, bf16[1000,128]{1,0:T(8,128)(2,1)S(1)}) fusion(bf16[1000,7950]{1,0:T(8,128)(2,1)} %refs_14_.1, s32[7950]{0:T(1024)S(1)} %fusion.34, s32[128]{0:T(128)S(1)} %fusion.40, pred[7950]{0:T(1024)(128)(4,1)S(1)} %broadcast_compare_fusion), kind=kOutput, calls=%fused_computation.15 | convolution fusion | flops 2037875200 | bytes 16452262 | tf_op jit(solution)/shard_map/dot_general | solution.py:85
  20.9 4.0 %collective-permute-start.1 = (f32[72,128]{1,0:T(8,128)S(1)}, f32[72,128]{1,0:T(8,128)S(1)}, u32[]{:S(2)}, u32[]{:S(2)}) collective-permute-start(f32[72,128]{1,0:T(8,128)S(1)} %add.159), channel_id=1, source_target_pairs={{0,64},{1,65},{2,66},{3,67},{4,68},{5,69},{6,70},{7,71},{8,72},{9,... | collective-permute-start | bytes 110600 | tf_op jit(solution)/shard_map/ppermute | solution.py:39
  38.1 4.9 %collective-permute-done.8.refs_6_ = bf16[64,4096]{1,0:T(8,128)(2,1)S(1)} collective-permute-done((bf16[64,4096]{1,0:T(8,128)(2,1)S(1)}, bf16[64,4096]{1,0:T(8,128)(2,1)S(1)}, u32[]{:S(2)}, u32[]{:S(2)}) %collective-permute-start.8) | collective-permute-done | bytes 524320 | tf_op jit(solution)/shard_map/ppermute | solution.py:39
  43.3 3.6 %collective-permute-done.10.refs_8_ = bf16[64,4096]{1,0:T(8,128)(2,1)S(1)} collective-permute-done((bf16[64,4096]{1,0:T(8,128)(2,1)S(1)}, bf16[64,4096]{1,0:T(8,128)(2,1)S(1)}, u32[]{:S(2)}, u32[]{:S(2)}) %collective-permute-start.10) | collective-permute-done | bytes 524320 | tf_op jit(solution)/shard_map/ppermute | solution.py:39
  47.1 5.5 %collective-permute-done.9.refs_7_ = bf16[64,3968]{1,0:T(8,128)(2,1)S(1)} collective-permute-done((bf16[64,3968]{1,0:T(8,128)(2,1)S(1)}, bf16[64,3968]{1,0:T(8,128)(2,1)S(1)}, u32[]{:S(2)}, u32[]{:S(2)}) %collective-permute-start.9) | collective-permute-done | bytes 507936 | tf_op jit(solution)/shard_map/ppermute | solution.py:39
  58.3 3.2 %collective-permute-start.14 = (bf16[128,4096]{1,0:T(8,128)(2,1)}, bf16[128,4096]{1,0:T(8,128)(2,1)}, u32[]{:S(2)}, u32[]{:S(2)}) collective-permute-start(bf16[128,4096]{1,0:T(8,128)(2,1)} %constant_dynamic-update-slice_fusion), channel_id=1, source_target_pairs={{0,4},{1,5},{2,6},{3,7},{4,8},{5,9},{6,10},{7,11},{8,12},{9,13},{1... | collective-permute-start | bytes 3145736 | tf_op jit(solution)/shard_map/ppermute | solution.py:39
  61.5 4.9 %collective-permute-done.12.refs_4_ = bf16[64,4096]{1,0:T(8,128)(2,1)S(1)} collective-permute-done((bf16[64,4096]{1,0:T(8,128)(2,1)S(1)}, bf16[64,4096]{1,0:T(8,128)(2,1)S(1)}, u32[]{:S(2)}, u32[]{:S(2)}) %collective-permute-start.12) | collective-permute-done | bytes 524320 | tf_op jit(solution)/shard_map/ppermute | solution.py:39
  73.5 13.2 %shard_map.55 = (f32[160,1000]{1,0:T(8,128)}, bf16[160,1000]{1,0:T(8,128)(2,1)S(1)}) custom-call(bf16[64,4096]{1,0:T(8,128)(2,1)} %copy-done.2, bf16[64,3968]{1,0:T(8,128)(2,1)S(1)} %pad_add_fusion.refs_1_, bf16[64,4096]{1,0:T(8,128)(2,1)} %copy-done.3, bf16[64,3968]{1,0:T(8,128)(2,1)S(1)} %collective-permute-done.5.refs_3_, bf16[64,4096]{1,0:T(8,128)(2,1)} %copy-done.4, ...), custom_call_target="tpu_custom_call" | custom-call | flops 10240000000 | bytes 25165824 | tf_op jit(solution)/shard_map/pallas_call | solution.py:139
  86.8 12.4 %collective-permute-done.18.refs_5_ = bf16[64,3968]{1,0:T(8,128)(2,1)S(1)} collective-permute-done((bf16[64,3968]{1,0:T(8,128)(2,1)S(1)}, bf16[64,3968]{1,0:T(8,128)(2,1)S(1)}, u32[]{:S(2)}, u32[]{:S(2)}) %collective-permute-start.18) | collective-permute-done | bytes 507936 | tf_op jit(solution)/shard_map/ppermute | solution.py:39
  104.9 13.8 %shard_map.56 = (f32[192,1000]{1,0:T(8,128)}, bf16[192,1000]{1,0:T(8,128)(2,1)S(1)}) custom-call(bf16[128,4096]{1,0:T(8,128)(2,1)} %collective-permute-done.14.refs_0_, bf16[128,3968]{1,0:T(8,128)(2,1)} %collective-permute-done.15.refs_1_, bf16[128,3968]{1,0:T(8,128)(2,1)} %collective-permute-done.16.refs_2_, ...), custom_call_target="tpu_custom_call" | custom-call | flops 12288000000 | bytes 25165824 | tf_op jit(solution)/shard_map/pallas_call | solution.py:139
  127.1 4.2 %collective-permute-start.26 = (bf16[11,8,1000]{2,1,0:T(8,128)(2,1)S(1)}, bf16[11,8,1000]{2,1,0:T(8,128)(2,1)S(1)}, u32[]{:S(2)}, u32[]{:S(2)}) collective-permute-start(bf16[11,8,1000]{2,1,0:T(8,128)(2,1)S(1)} %get-tuple-element.42), channel_id=1, source_target_pairs={{0,96},{1,97},{2,98},{3,99},{4,100},{5,101},{6,102},{7,103},{8,104... | collective-permute-start | bytes 528008 | tf_op jit(solution)/shard_map/ppermute | solution.py:39
  137.0 3.2 %collective-permute-start.31 = (bf16[128,2048]{1,0:T(8,128)(2,1)}, bf16[128,2048]{1,0:T(8,128)(2,1)}, u32[]{:S(2)}, u32[]{:S(2)}) collective-permute-start(bf16[128,2048]{1,0:T(8,128)(2,1)} %slice.193), channel_id=1, source_target_pairs={{0,4},{1,5},{2,6},{3,7},{4,8},{5,9},{6,10},{7,11},{8,12},{9,13},{1... | collective-permute-start | bytes 1572872 | tf_op jit(solution)/shard_map/ppermute | solution.py:39
  142.2 3.2 %collective-permute-start.30 = (bf16[128,1920]{1,0:T(8,128)(2,1)}, bf16[128,1920]{1,0:T(8,128)(2,1)S(1)}, u32[]{:S(2)}, u32[]{:S(2)}) collective-permute-start(bf16[128,1920]{1,0:T(8,128)(2,1)} %slice.192), channel_id=1, source_target_pairs={{0,3},{1,0},{2,1},{3,2},{4,7},{5,4},{6,5},{7,6},{8,11},{9,8},{10,9... | collective-permute-start | bytes 1474568 | tf_op jit(solution)/shard_map/ppermute | solution.py:39
  147.5 5.0 %collective-permute-done.27 = bf16[11,8,1000]{2,1,0:T(8,128)(2,1)} collective-permute-done((bf16[11,8,1000]{2,1,0:T(8,128)(2,1)S(1)}, bf16[11,8,1000]{2,1,0:T(8,128)(2,1)}, u32[]{:S(2)}, u32[]{:S(2)}) %collective-permute-start.27) | collective-permute-done | bytes 176032 | tf_op jit(solution)/shard_map/ppermute | solution.py:39
  153.7 6.6 %collective-permute-done.34.refs_10_ = bf16[64,2048]{1,0:T(8,128)(2,1)S(1)} collective-permute-done((bf16[64,2048]{1,0:T(8,128)(2,1)}, bf16[64,2048]{1,0:T(8,128)(2,1)S(1)}, u32[]{:S(2)}, u32[]{:S(2)}) %collective-permute-start.34) | collective-permute-done | bytes 262176 | tf_op jit(solution)/shard_map/ppermute | solution.py:39
  160.3 12.8 %shard_map.57 = (f32[160,1000]{1,0:T(8,128)}, bf16[160,1000]{1,0:T(8,128)(2,1)S(1)}) custom-call(bf16[64,4096]{1,0:T(8,128)(2,1)} %copy-done.6, bf16[128,2048]{1,0:T(8,128)(2,1)} %collective-permute-done.29.refs_1_, bf16[128,1920]{1,0:T(8,128)(2,1)S(1)} %collective-permute-done.30.refs_2_, bf16[64,4096]{1,0:T(8,128)(2,1)} %copy-done.7, ...), custom_call_target="tpu_custom_call" | custom-call | flops 10240000000 | bytes 25165824 | tf_op jit(solution)/shard_map/pallas_call | solution.py:139
  176.1 3.2 %collective-permute-start.38 = (bf16[5,8,1000]{2,1,0:T(8,128)(2,1)S(1)}, bf16[5,8,1000]{2,1,0:T(8,128)(2,1)S(1)}, u32[]{:S(2)}, u32[]{:S(2)}) collective-permute-start(bf16[5,8,1000]{2,1,0:T(8,128)(2,1)S(1)} %get-tuple-element.51), channel_id=1, source_target_pairs={{0,96},{1,97},{2,98},{3,99},{4,100},{5,101},{6,102},{7,103},{8,104... | collective-permute-start | bytes 240008 | tf_op jit(solution)/shard_map/ppermute | solution.py:39
  185.5 5.6 %shard_map.58 = bf16[4,128,975]{2,1,0:T(8,128)(2,1)S(1)} custom-call(bf16[128,1000]{1,0:T(8,128)(2,1)S(1)} %select_bitcast_fusion.p, bf16[8,975,1000]{2,1,0:T(8,128)(2,1)} %all-gather.4.cloned.1.call-done.f), custom_call_target="tpu_custom_call" | custom-call | flops 2995200000 | bytes 7800000 | tf_op jit(solution)/shard_map/pallas_call | solution.py:172
  191.2 3.2 %collective-permute-start.40 = (bf16[4,32,975]{2,1,0:T(8,128)(2,1)S(1)}, bf16[4,32,975]{2,1,0:T(8,128)(2,1)S(1)}, u32[]{:S(2)}, u32[]{:S(2)}) collective-permute-start(bf16[4,32,975]{2,1,0:T(8,128)(2,1)S(1)} %get-tuple-element.44), channel_id=1, source_target_pairs={{0,4},{1,5},{2,6},{3,7},{4,8},{5,9},{6,10},{7,11},{8,12},{9,13},{1... | collective-permute-start | bytes 748808 | tf_op jit(solution)/shard_map/ppermute | solution.py:39
  195.9 5.6 %shard_map.59 = bf16[4,128,975]{2,1,0:T(8,128)(2,1)S(1)} custom-call(bf16[128,1000]{1,0:T(8,128)(2,1)S(1)} %select_bitcast_fusion.p, bf16[8,975,1000]{2,1,0:T(8,128)(2,1)} %all-gather.4.cloned.1.call-done.f), custom_call_target="tpu_custom_call" | custom-call | flops 2995200000 | bytes 7800000 | tf_op jit(solution)/shard_map/pallas_call | solution.py:172
  208.6 5.2 %collective-permute-done.44 = bf16[4,32,975]{2,1,0:T(8,128)(2,1)S(1)} collective-permute-done((bf16[4,32,975]{2,1,0:T(8,128)(2,1)S(1)}, bf16[4,32,975]{2,1,0:T(8,128)(2,1)S(1)}, u32[]{:S(2)}, u32[]{:S(2)}) %collective-permute-start.44) | collective-permute-done | bytes 249632 | tf_op jit(solution)/shard_map/ppermute | solution.py:39
  214.7 3.2 %collective-permute-start.47 = (bf16[8,8,975]{2,0,1:T(8,128)(2,1)S(1)}, bf16[8,8,975]{2,0,1:T(8,128)(2,1)S(1)}, u32[]{:S(2)}, u32[]{:S(2)}) collective-permute-start(bf16[8,8,975]{2,0,1:T(8,128)(2,1)S(1)} %get-tuple-element.55), channel_id=1, source_target_pairs={{0,3},{1,0},{2,1},{3,2},{4,7},{5,4},{6,5},{7,6},{8,11},{9,8},{10,9... | collective-permute-start | bytes 374408 | tf_op jit(solution)/shard_map/ppermute | solution.py:39
  224.7 4.0 %collective-permute-start.49 = (bf16[8,7800]{1,0:T(8,128)(2,1)S(1)}, bf16[8,7800]{1,0:T(8,128)(2,1)S(1)}, u32[]{:S(2)}, u32[]{:S(2)}) collective-permute-start(bf16[8,7800]{1,0:T(8,128)(2,1)S(1)} %reshape.72), channel_id=1, source_target_pairs={{0,0},{1,8},{2,16},{3,24},{4,32},{5,40},{6,48},{7,56},{8,64},{9,72... | collective-permute-start | bytes 374408 | tf_op jit(solution)/shard_map/ppermute | solution.py:39
  228.7 7.3 %collective-permute-done.49 = bf16[8,7800]{1,0:T(8,128)(2,1)S(1)} collective-permute-done((bf16[8,7800]{1,0:T(8,128)(2,1)S(1)}, bf16[8,7800]{1,0:T(8,128)(2,1)S(1)}, u32[]{:S(2)}, u32[]{:S(2)}) %collective-permute-start.49) | collective-permute-done | bytes 124832 | tf_op jit(solution)/shard_map/ppermute | solution.py:39
  (192 shorter events, 83.5 us)
Async XLA Ops:
  6.5 179.0 %all-gather.4.cloned.1.call-start = ((), (), s32[]{:S(2)}) async-start(), calls=%async_computation | async-start | bytes 17989632 | tf_op jit(solution)/shard_map/all_gather | solution.py:220
  7.8 24.4 %collective-permute-start.4 = (bf16[64,4096]{1,0:T(8,128)(2,1)S(1)}, bf16[64,4096]{1,0:T(8,128)(2,1)S(1)}, u32[]{:S(2)}, u32[]{:S(2)}) collective-permute-start(bf16[64,4096]{1,0:T(8,128)(2,1)S(1)} %slice_multiply_fusion.refs_0_), channel_id=1, source_target_pairs={{0,1},{1,2},{2,3},{3,0},{4,5},{5,6},{6,7},{7,4},{8,9},{9,10},{10,1... | collective-permute-start | bytes 1572872 | tf_op jit(solution)/shard_map/ppermute | solution.py:39
  9.4 26.5 %collective-permute-start.6 = (bf16[64,4096]{1,0:T(8,128)(2,1)S(1)}, bf16[64,4096]{1,0:T(8,128)(2,1)S(1)}, u32[]{:S(2)}, u32[]{:S(2)}) collective-permute-start(bf16[64,4096]{1,0:T(8,128)(2,1)S(1)} %slice_multiply_fusion.refs_0_), channel_id=1, source_target_pairs={{0,3},{1,0},{2,1},{3,2},{4,7},{5,4},{6,5},{7,6},{8,11},{9,8},{10,9... | collective-permute-start | bytes 1572872 | tf_op jit(solution)/shard_map/ppermute | solution.py:39
  31.7 24.6 %collective-permute-start.11 = (bf16[64,3968]{1,0:T(8,128)(2,1)S(1)}, bf16[64,3968]{1,0:T(8,128)(2,1)}, u32[]{:S(2)}, u32[]{:S(2)}) collective-permute-start(bf16[64,3968]{1,0:T(8,128)(2,1)S(1)} %pad_add_fusion.refs_1_), channel_id=1, source_target_pairs={{0,12},{1,13},{2,14},{3,15},{4,0},{5,1},{6,2},{7,3},{8,4},{9,5},{1... | collective-permute-start | bytes 1523720 | tf_op jit(solution)/shard_map/ppermute | solution.py:39
  32.3 20.3 %collective-permute-start.9 = (bf16[64,3968]{1,0:T(8,128)(2,1)S(1)}, bf16[64,3968]{1,0:T(8,128)(2,1)S(1)}, u32[]{:S(2)}, u32[]{:S(2)}) collective-permute-start(bf16[64,3968]{1,0:T(8,128)(2,1)S(1)} %pad_add_fusion.refs_1_), channel_id=1, source_target_pairs={{0,4},{1,5},{2,6},{3,7},{4,8},{5,9},{6,10},{7,11},{8,12},{9,13},{1... | collective-permute-start | bytes 1523720 | tf_op jit(solution)/shard_map/ppermute | solution.py:39
  35.9 22.4 %collective-permute-start.7 = (bf16[64,3968]{1,0:T(8,128)(2,1)S(1)}, bf16[64,3968]{1,0:T(8,128)(2,1)S(1)}, u32[]{:S(2)}, u32[]{:S(2)}) collective-permute-start(bf16[64,3968]{1,0:T(8,128)(2,1)S(1)} %pad_add_fusion.refs_1_), channel_id=1, source_target_pairs={{0,3},{1,0},{2,1},{3,2},{4,7},{5,4},{6,5},{7,6},{8,11},{9,8},{10,9... | collective-permute-start | bytes 1523720 | tf_op jit(solution)/shard_map/ppermute | solution.py:39
  43.0 18.5 %collective-permute-start.5 = (bf16[64,3968]{1,0:T(8,128)(2,1)S(1)}, bf16[64,3968]{1,0:T(8,128)(2,1)S(1)}, u32[]{:S(2)}, u32[]{:S(2)}) collective-permute-start(bf16[64,3968]{1,0:T(8,128)(2,1)S(1)} %pad_add_fusion.refs_1_), channel_id=1, source_target_pairs={{0,1},{1,2},{2,3},{3,0},{4,5},{5,6},{6,7},{7,4},{8,9},{9,10},{10,1... | collective-permute-start | bytes 1523720 | tf_op jit(solution)/shard_map/ppermute | solution.py:39
  47.0 19.5 %collective-permute-start.12 = (bf16[64,4096]{1,0:T(8,128)(2,1)S(1)}, bf16[64,4096]{1,0:T(8,128)(2,1)S(1)}, u32[]{:S(2)}, u32[]{:S(2)}) collective-permute-start(bf16[64,4096]{1,0:T(8,128)(2,1)S(1)} %collective-permute-done.4.refs_2_), channel_id=1, source_target_pairs={{0,1},{1,2},{2,3},{3,0},{4,5},{5,6},{6,7},{7,4},{8,9},{9,10},{10,1... | collective-permute-start | bytes 1572872 | tf_op jit(solution)/shard_map/ppermute | solution.py:39
  58.3 43.2 %collective-permute-start.14 = (bf16[128,4096]{1,0:T(8,128)(2,1)}, bf16[128,4096]{1,0:T(8,128)(2,1)}, u32[]{:S(2)}, u32[]{:S(2)}) collective-permute-start(bf16[128,4096]{1,0:T(8,128)(2,1)} %constant_dynamic-update-slice_fusion), channel_id=1, source_target_pairs={{0,4},{1,5},{2,6},{3,7},{4,8},{5,9},{6,10},{7,11},{8,12},{9,13},{1... | collective-permute-start | bytes 3145736 | tf_op jit(solution)/shard_map/ppermute | solution.py:39
  61.5 40.0 %collective-permute-start.17 = (bf16[128,4096]{1,0:T(8,128)(2,1)}, bf16[128,4096]{1,0:T(8,128)(2,1)}, u32[]{:S(2)}, u32[]{:S(2)}) collective-permute-start(bf16[128,4096]{1,0:T(8,128)(2,1)} %constant_dynamic-update-slice_fusion), channel_id=1, source_target_pairs={{0,12},{1,13},{2,14},{3,15},{4,0},{5,1},{6,2},{7,3},{8,4},{9,5},{1... | collective-permute-start | bytes 3145736 | tf_op jit(solution)/shard_map/ppermute | solution.py:39
  66.4 35.5 %collective-permute-start.15 = (bf16[128,3968]{1,0:T(8,128)(2,1)}, bf16[128,3968]{1,0:T(8,128)(2,1)}, u32[]{:S(2)}, u32[]{:S(2)}) collective-permute-start(bf16[128,3968]{1,0:T(8,128)(2,1)} %constant_dynamic-update-slice_fusion.2), channel_id=1, source_target_pairs={{0,1},{1,2},{2,3},{3,0},{4,5},{5,6},{6,7},{7,4},{8,9},{9,10},{10,1... | collective-permute-start | bytes 3047432 | tf_op jit(solution)/shard_map/ppermute | solution.py:39
  67.4 37.5 %collective-permute-start.16 = (bf16[128,3968]{1,0:T(8,128)(2,1)}, bf16[128,3968]{1,0:T(8,128)(2,1)}, u32[]{:S(2)}, u32[]{:S(2)}) collective-permute-start(bf16[128,3968]{1,0:T(8,128)(2,1)} %constant_dynamic-update-slice_fusion.2), channel_id=1, source_target_pairs={{0,3},{1,0},{2,1},{3,2},{4,7},{5,4},{6,5},{7,6},{8,11},{9,8},{10,9... | collective-permute-start | bytes 3047432 | tf_op jit(solution)/shard_map/ppermute | solution.py:39
  72.3 26.8 %collective-permute-start.18 = (bf16[64,3968]{1,0:T(8,128)(2,1)S(1)}, bf16[64,3968]{1,0:T(8,128)(2,1)S(1)}, u32[]{:S(2)}, u32[]{:S(2)}) collective-permute-start(bf16[64,3968]{1,0:T(8,128)(2,1)S(1)} %collective-permute-done.7.refs_5_), channel_id=1, source_target_pairs={{0,3},{1,0},{2,1},{3,2},{4,7},{5,4},{6,5},{7,6},{8,11},{9,8},{10,9... | collective-permute-start | bytes 1523720 | tf_op jit(solution)/shard_map/ppermute | solution.py:39
  99.1 19.7 %collective-permute-start.20 = (bf16[64,4096]{1,0:T(8,128)(2,1)S(1)}, bf16[64,4096]{1,0:T(8,128)(2,1)S(1)}, u32[]{:S(2)}, u32[]{:S(2)}) collective-permute-start(bf16[64,4096]{1,0:T(8,128)(2,1)S(1)} %copy-done.18), channel_id=1, source_target_pairs={{0,4},{1,5},{2,6},{3,7},{4,8},{5,9},{6,10},{7,11},{8,12},{9,13},{1... | collective-permute-start | bytes 1572872 | tf_op jit(solution)/shard_map/ppermute | solution.py:39
  101.5 17.3 %collective-permute-start.21 = (bf16[64,4096]{1,0:T(8,128)(2,1)S(1)}, bf16[64,4096]{1,0:T(8,128)(2,1)S(1)}, u32[]{:S(2)}, u32[]{:S(2)}) collective-permute-start(bf16[64,4096]{1,0:T(8,128)(2,1)S(1)} %copy-done.18), channel_id=1, source_target_pairs={{0,12},{1,13},{2,14},{3,15},{4,0},{5,1},{6,2},{7,3},{8,4},{9,5},{1... | collective-permute-start | bytes 1572872 | tf_op jit(solution)/shard_map/ppermute | solution.py:39
  101.6 17.2 %collective-permute-start.22 = (bf16[64,3968]{1,0:T(8,128)(2,1)S(1)}, bf16[64,3968]{1,0:T(8,128)(2,1)S(1)}, u32[]{:S(2)}, u32[]{:S(2)}) collective-permute-start(bf16[64,3968]{1,0:T(8,128)(2,1)S(1)} %collective-permute-done.13.refs_7_), channel_id=1, source_target_pairs={{0,1},{1,2},{2,3},{3,0},{4,5},{5,6},{6,7},{7,4},{8,9},{9,10},{10,1... | collective-permute-start | bytes 1523720 | tf_op jit(solution)/shard_map/ppermute | solution.py:39
  101.9 16.9 %collective-permute-start.23 = (bf16[64,3968]{1,0:T(8,128)(2,1)S(1)}, bf16[64,3968]{1,0:T(8,128)(2,1)S(1)}, u32[]{:S(2)}, u32[]{:S(2)}) collective-permute-start(bf16[64,3968]{1,0:T(8,128)(2,1)S(1)} %collective-permute-done.13.refs_7_), channel_id=1, source_target_pairs={{0,3},{1,0},{2,1},{3,2},{4,7},{5,4},{6,5},{7,6},{8,11},{9,8},{10,9... | collective-permute-start | bytes 1523720 | tf_op jit(solution)/shard_map/ppermute | solution.py:39
  120.0 20.2 %collective-permute-start.28 = (bf16[64,2048]{1,0:T(8,128)(2,1)S(1)}, bf16[64,2048]{1,0:T(8,128)(2,1)S(1)}, u32[]{:S(2)}, u32[]{:S(2)}) collective-permute-start(bf16[64,2048]{1,0:T(8,128)(2,1)S(1)} %slice.150), channel_id=1, source_target_pairs={{0,4},{1,5},{2,6},{3,7},{4,8},{5,9},{6,10},{7,11},{8,12},{9,13},{1... | collective-permute-start | bytes 786440 | tf_op jit(solution)/shard_map/ppermute | solution.py:39
  123.2 17.0 %collective-permute-start.33 = (bf16[64,2048]{1,0:T(8,128)(2,1)S(1)}, bf16[64,2048]{1,0:T(8,128)(2,1)S(1)}, u32[]{:S(2)}, u32[]{:S(2)}) collective-permute-start(bf16[64,2048]{1,0:T(8,128)(2,1)S(1)} %slice.161), channel_id=1, source_target_pairs={{0,12},{1,13},{2,14},{3,15},{4,0},{5,1},{6,2},{7,3},{8,4},{9,5},{1... | collective-permute-start | bytes 786440 | tf_op jit(solution)/shard_map/ppermute | solution.py:39
  127.1 18.3 %collective-permute-start.26 = (bf16[11,8,1000]{2,1,0:T(8,128)(2,1)S(1)}, bf16[11,8,1000]{2,1,0:T(8,128)(2,1)S(1)}, u32[]{:S(2)}, u32[]{:S(2)}) collective-permute-start(bf16[11,8,1000]{2,1,0:T(8,128)(2,1)S(1)} %get-tuple-element.42), channel_id=1, source_target_pairs={{0,96},{1,97},{2,98},{3,99},{4,100},{5,101},{6,102},{7,103},{8,104... | collective-permute-start | bytes 528008 | tf_op jit(solution)/shard_map/ppermute | solution.py:39
  137.0 23.3 %collective-permute-start.31 = (bf16[128,2048]{1,0:T(8,128)(2,1)}, bf16[128,2048]{1,0:T(8,128)(2,1)}, u32[]{:S(2)}, u32[]{:S(2)}) collective-permute-start(bf16[128,2048]{1,0:T(8,128)(2,1)} %slice.193), channel_id=1, source_target_pairs={{0,4},{1,5},{2,6},{3,7},{4,8},{5,9},{6,10},{7,11},{8,12},{9,13},{1... | collective-permute-start | bytes 1572872 | tf_op jit(solution)/shard_map/ppermute | solution.py:39
  140.2 20.1 %collective-permute-start.32 = (bf16[128,2048]{1,0:T(8,128)(2,1)}, bf16[128,2048]{1,0:T(8,128)(2,1)}, u32[]{:S(2)}, u32[]{:S(2)}) collective-permute-start(bf16[128,2048]{1,0:T(8,128)(2,1)} %slice.194), channel_id=1, source_target_pairs={{0,12},{1,13},{2,14},{3,15},{4,0},{5,1},{6,2},{7,3},{8,4},{9,5},{1... | collective-permute-start | bytes 1572872 | tf_op jit(solution)/shard_map/ppermute | solution.py:39
  140.2 20.1 %collective-permute-start.29 = (bf16[128,2048]{1,0:T(8,128)(2,1)}, bf16[128,2048]{1,0:T(8,128)(2,1)}, u32[]{:S(2)}, u32[]{:S(2)}) collective-permute-start(bf16[128,2048]{1,0:T(8,128)(2,1)} %slice.191), channel_id=1, source_target_pairs={{0,1},{1,2},{2,3},{3,0},{4,5},{5,6},{6,7},{7,4},{8,9},{9,10},{10,1... | collective-permute-start | bytes 1572872 | tf_op jit(solution)/shard_map/ppermute | solution.py:39
  142.2 18.1 %collective-permute-start.30 = (bf16[128,1920]{1,0:T(8,128)(2,1)}, bf16[128,1920]{1,0:T(8,128)(2,1)S(1)}, u32[]{:S(2)}, u32[]{:S(2)}) collective-permute-start(bf16[128,1920]{1,0:T(8,128)(2,1)} %slice.192), channel_id=1, source_target_pairs={{0,3},{1,0},{2,1},{3,2},{4,7},{5,4},{6,5},{7,6},{8,11},{9,8},{10,9... | collective-permute-start | bytes 1474568 | tf_op jit(solution)/shard_map/ppermute | solution.py:39
  (47 other events, 497.2 us)
Sparse Core Ops, SparseCore 0:
  9.1 85.0 all-gather.3

commit v4 on v3

v4 whole, which is shorter than its diff:
```python
import functools

import jax
import jax.numpy as jnp
from jax import lax
from jax.experimental import pallas as pl
from jax.experimental.pallas import tpu as pltpu
from jax.sharding import PartitionSpec as P

SENSORS = 6
AXES = ("sens", "layer")
SIDE = 4
ROWS = 64
HALF = 4096
BWIDTH = 3968
EDGE = BWIDTH - 128
WIDE = HALF + BWIDTH
INSIDE = 14
PBLOCK = 256
VMEM = 52 * 2**20


def moved(fn):
    pairs = []
    for z in range(4):
        for c in range(2):
            for y in range(4):
                for x in range(4):
                    z2, c2, y2, x2 = fn(z, c, y, x)
                    pairs.append(
                        ((z * 2 + c) * 16 + y * 4 + x,
                         ((z2 % 4) * 2 + c2 % 2) * 16 + (y2 % 4) * 4 + x2 % 4)
                    )
    return pairs


def send(x, fn):
    return lax.ppermute(x, AXES, moved(fn))


def swap_core(v):
    return send(v, lambda z, c, y, x: (z, c + 1, y, x))


def right(v):
    return send(v, lambda z, c, y, x: (z, c, y, x + 1))


def left(v):
    return send(v, lambda z, c, y, x: (z, c, y, x - 1))


def up(v):
    return send(v, lambda z, c, y, x: (z, c, y + 1, x))


def down(v):
    return send(v, lambda z, c, y, x: (z, c, y - 1, x))


def hop_z(d):
    return lambda z, c, y, x: (z + d, c, y, x)


def hop_one(d):
    return lambda z, c, y, x: (z, c, y + d * (1 - c), x + d * c)


def hop_two(d):
    return lambda z, c, y, x: (z, c, y + d * c, x + d * (1 - c))


def home(z, c, y, x):
    layer = y * 4 + x
    sens, layer = layer // 2, 8 * (layer % 2) + z * 2 + c
    return (sens // 2, sens % 2, layer // 4, layer % 4)


def after(value, *others):
    return lax.optimization_barrier((value, *others))


def nt(a, b, **kw):
    return lax.dot_general(
        a, b, (((1,), (1,)), ((), ())), preferred_element_type=jnp.float32, **kw
    )


def reconstruct_kernel(pieces, places, count, *refs):
    arrays = refs[:count]
    position, means, ra, rb, rw, own, other, held, offsets, sems = refs[count:]

    @pl.when(pl.program_id(0) == 0)
    def _():
        copies = []
        for i, (a, row, rows, cols, to_row, to_col) in enumerate(pieces):
            copies.append(
                pltpu.make_async_copy(
                    arrays[a].at[pl.ds(row, rows), pl.ds(0, cols)],
                    held.at[pl.ds(to_row, rows), pl.ds(to_col, cols)],
                    sems.at[i],
                )
            )
        for k, (ry, rx) in enumerate(places):
            source = lax.rem(position[1] + ry, SIDE) * SIDE + lax.rem(position[2] + rx, SIDE)
            copies.append(
                pltpu.make_async_copy(
                    means.at[source],
                    offsets.at[pl.ds(k * ROWS, ROWS)],
                    sems.at[len(pieces) + k],
                )
            )
        for copy in copies:
            copy.start()
        for copy in copies:
            copy.wait()

    lane = lax.broadcasted_iota(jnp.int32, (ra.shape[0], 128), 1)
    edge = rb[:, EDGE:BWIDTH].astype(jnp.float32)
    edge = jnp.where(lane < INSIDE, edge, 0.0).astype(jnp.bfloat16)
    val = nt(held[:, :HALF], ra[...]) + nt(held[:, HALF : HALF + EDGE], rb[:, :EDGE])
    val = val + nt(held[:, HALF + EDGE :], edge) + nt(offsets[...], rw[...])
    n = val.shape[0]
    pairs = val.reshape(n // 16, 2, 8, val.shape[1])
    first = pairs[:, 0].reshape(n // 2, val.shape[1])
    second = pairs[:, 1].reshape(n // 2, val.shape[1])
    swapped = position[0] == 1
    own[...] = jnp.where(swapped, second, first)
    other[...] = jnp.where(swapped, first, second).astype(jnp.bfloat16)


def reconstruct(sources, position, means, r, rw):
    arrays, pieces = [], []
    for k, source in enumerate(sources.values()):
        for array, row, rows, cols, to_row, to_col in source:
            found = [i for i, a in enumerate(arrays) if a is array]
            if not found:
                arrays.append(array)
                found = [len(arrays) - 1]
            pieces.append((found[0], row, rows, cols, k * ROWS + to_row, to_col))
    n = ROWS * len(sources)
    p = r.shape[0]
    half = pl.BlockSpec((n // 2, PBLOCK), lambda j: (0, j))
    return pl.pallas_call(
        functools.partial(reconstruct_kernel, tuple(pieces), tuple(sources), len(arrays)),
        grid=(pl.cdiv(p, PBLOCK),),
        in_specs=[pl.BlockSpec(memory_space=pl.ANY)] * len(arrays)
        + [
            pl.BlockSpec(memory_space=pltpu.SMEM),
            pl.BlockSpec(memory_space=pl.ANY),
            pl.BlockSpec((PBLOCK, HALF), lambda j: (j, 0)),
            pl.BlockSpec((PBLOCK, HALF), lambda j: (j, 1)),
            pl.BlockSpec((PBLOCK, 128), lambda j: (j, 0)),
        ],
        out_specs=[half, half],
        out_shape=[
            jax.ShapeDtypeStruct((n // 2, p), jnp.float32),
            jax.ShapeDtypeStruct((n // 2, p), jnp.bfloat16),
        ],
        scratch_shapes=[
            pltpu.VMEM((n, WIDE), jnp.bfloat16),
            pltpu.VMEM((n, 128), jnp.bfloat16),
            pltpu.SemaphoreType.DMA((len(pieces) + len(sources),)),
        ],
        compiler_params=pltpu.CompilerParams(vmem_limit_bytes=VMEM),
        cost_estimate=pl.CostEstimate(flops=0, bytes_accessed=0, transcendentals=0),
    )(*arrays, position, means, r, r, rw)


def fit_kernel(p, f, out):
    out[0] = nt(p[...], f[0]).astype(jnp.bfloat16)


def fit(points, fitting, start, count):
    n, k = points.shape
    m = fitting.shape[1]
    return pl.pallas_call(
        fit_kernel,
        grid=(count,),
        in_specs=[
            pl.BlockSpec((n, k), lambda s: (0, 0)),
            pl.BlockSpec((1, m, k), lambda s: (s + start, 0, 0)),
        ],
        out_specs=pl.BlockSpec((1, n, m), lambda s: (s, 0, 0)),
        out_shape=jax.ShapeDtypeStruct((count, n, m), jnp.bfloat16),
        compiler_params=pltpu.CompilerParams(vmem_limit_bytes=VMEM),
        cost_estimate=pl.CostEstimate(
            flops=0, bytes_accessed=0, transcendentals=0
        ),
    )(points, fitting)


def picks_by_z(own, other, z):
    got = own + swap_core(other).astype(jnp.float32)
    got = got.reshape(-1, SIDE, 8, own.shape[1])

    def pick(d):
        return lax.dynamic_index_in_dim(got, (z + d) % SIDE, 1, keepdims=False)

    return [pick(0)] + [pick(d).astype(jnp.bfloat16) for d in (1, 3, 2)]


def sums_by_z(picked):
    pieces = picked[:1] + [send(v, hop_z(d)) for v, d in zip(picked[1:], (1, 3, 2))]
    return total(pieces).astype(jnp.bfloat16)


def owned(blocks, hop):
    pieces = [blocks[:, 0]]
    pieces += [send(blocks[:, d].astype(jnp.bfloat16), hop(d)) for d in (1, 3, 2)]
    return pieces


def total(pieces):
    out = pieces[0].astype(jnp.float32)
    for piece in pieces[1:]:
        out = out + piece.astype(jnp.float32)
    return out


def together(*pieces):
    return jnp.concatenate(
        [jnp.pad(p, ((0, 0), (0, HALF - p.shape[1]))) for p in pieces], axis=0
    )


def per_device(slopes, valid, sensor_map, reconstructor, fitting):
    s_idx = lax.axis_index("sens")
    l_idx = lax.axis_index("layer")
    z, c = s_idx // 2, s_idx % 2
    width = slopes.shape[1]
    width_p = reconstructor.shape[0]
    act = fitting.shape[0]
    position = jnp.stack([c, l_idx // SIDE, l_idx % SIDE]).astype(jnp.int32)

    everything = lax.all_gather(fitting, "sens", axis=0)

    live = valid.astype(jnp.bfloat16)[None, :]
    mine = jnp.pad(slopes * live, ((0, 0), (0, WIDE - width)))

    got_l, got_r = right(mine), left(mine)
    got_d, got_u = up(mine), down(mine)

    group = sensor_map * 2 + (lax.iota(jnp.int32, width) + s_idx * width) % 2
    lane = lax.iota(jnp.int32, 128)
    label = jnp.where(lane < 36, lane % 12, -1)
    member = ((group[None, :] == label[:, None]) & (valid[None, :] == 1)).astype(jnp.bfloat16)
    counted = jnp.concatenate([mine[:, :width], jnp.ones((8, width), jnp.bfloat16)], axis=0)
    stats = nt(counted, member)
    stats = jnp.broadcast_to(stats[None], (8, *stats.shape))
    stats = jnp.sum(lax.all_to_all(stats, "sens", 0, 0, tiled=True), axis=0)
    means = stats[:ROWS] / jnp.maximum(stats[ROWS : ROWS + 1], 1.0)
    high = lax.reduce_precision(means, 8, 7)
    low = (lane >= 12) & (lane < 24)
    means = jnp.where(low[None, :], means - high, high).astype(jnp.bfloat16)
    means = lax.all_gather(means, "layer", axis=0)

    send_u = together(got_l[:, :HALF], got_r[:, :HALF], got_d[:, :HALF])
    send_d = together(got_l[:, :HALF], got_r[:, :HALF], got_u[:, HALF:])
    send_r = together(got_d[:, HALF:], got_u[:, HALF:], got_l[:, :HALF])
    send_l = together(got_d[:, HALF:], got_u[:, HALF:], got_r[:, HALF:])
    member, send_u, send_d, send_r, send_l = after(member, send_u, send_d, send_r, send_l)
    one_d, one_u = up(send_u), down(send_d)
    one_l, one_r = right(send_r), left(send_l)
    rw = -nt(reconstructor, member)
    rw_high = lax.reduce_precision(rw, 8, 7)
    last = (lane >= 24) & (lane < 36)
    rw = jnp.where(last[None, :], rw - rw_high, rw_high).astype(jnp.bfloat16)

    def all_of(array):
        return [(array, 0, ROWS, WIDE, 0, 0)]

    def halves(array_a, index_a, array_b, index_b):
        return [
            (array_a, index_a * ROWS, ROWS, HALF, 0, 0),
            (array_b, index_b * ROWS, ROWS, BWIDTH, 0, HALF),
        ]

    own0, other0 = reconstruct(
        {
            (0, 0): all_of(mine),
            (0, 3): all_of(got_l),
            (0, 1): all_of(got_r),
            (3, 0): all_of(got_d),
            (1, 0): all_of(got_u),
        },
        position, means, reconstructor, rw,
    )

    own0, other0, one_d, one_u, one_l, one_r = after(own0, other0, one_d, one_u, one_l, one_r)
    far_x_a, far_x_b = one_l[2 * ROWS :], one_r[2 * ROWS :]
    far_y_a, far_y_b = one_d[2 * ROWS :], one_u[2 * ROWS :]
    two_d = together(far_x_a, one_d[:ROWS])
    two_u = together(far_x_a, one_u[ROWS : 2 * ROWS])
    two_l = together(far_y_b, one_l[:ROWS])
    two_r = together(far_y_b, one_r[ROWS : 2 * ROWS])
    two_d, two_u, two_l, two_r = after(two_d, two_u, two_l, two_r)
    get_d, get_u = up(two_d), down(two_u)
    get_l, get_r = right(two_l), left(two_r)

    own1, other1 = reconstruct(
        {
            (3, 3): halves(one_d, 0, one_l, 0),
            (3, 1): halves(one_d, 1, one_r, 0),
            (1, 3): halves(one_u, 0, one_l, 1),
            (1, 1): halves(one_u, 1, one_r, 1),
            (0, 2): halves(one_l, 2, one_r, 2),
            (2, 0): halves(one_d, 2, one_u, 2),
        },
        position, means, reconstructor, rw,
    )

    own1, other1, get_d, get_u, get_l, get_r = after(own1, other1, get_d, get_u, get_l, get_r)
    half = ROWS // 2
    end_d, end_u = up(get_d[:half]), down(get_u[half:ROWS])
    end_l, end_r = right(get_l[:half]), left(get_r[half:ROWS])

    picked = picks_by_z(
        jnp.concatenate([own0, own1], axis=0), jnp.concatenate([other0, other1], axis=0), z
    )
    *picked, end_d, end_u, end_l, end_r = after(*picked, end_d, end_u, end_l, end_r)
    near = sums_by_z(picked)

    own2, other2 = reconstruct(
        {
            (3, 2): halves(get_d, 0, get_l, 1),
            (1, 2): halves(get_u, 0, get_r, 1),
            (2, 3): halves(get_d, 1, get_l, 0),
            (2, 1): halves(get_u, 1, get_r, 0),
            (2, 2): [
                (end_d, 0, half, HALF, 0, 0),
                (end_u, 0, half, HALF, half, 0),
                (end_l, 0, half, BWIDTH, 0, HALF),
                (end_r, 0, half, BWIDTH, half, HALF),
            ],
        },
        position, means, reconstructor, rw,
    )
    far = sums_by_z(picks_by_z(own2, other2, z))

    names = [
        (0, 0), (0, 3), (0, 1), (3, 0), (1, 0),
        (3, 3), (3, 1), (1, 3), (1, 1), (0, 2), (2, 0),
        (3, 2), (1, 2), (2, 3), (2, 1), (2, 2),
    ]
    points = jnp.concatenate([near, far], axis=0)
    y_first = jnp.stack([points[names.index((i, j))] for i in range(4) for j in range(4)])
    x_first = jnp.stack([points[names.index((i, j))] for j in range(4) for i in range(4)])
    rows = jnp.where(c == 0, y_first, x_first).reshape(16 * 8, width_p)
    half_a = owned(fit(rows, everything, 0, 4).reshape(4, SIDE, SIDE * 8, act), hop_one)
    half_b = owned(fit(rows, everything, 4, 4).reshape(4, SIDE, SIDE * 8, act), hop_one)
    both = jnp.concatenate([total(half_a), total(half_b)], axis=0)
    done = total(owned(both.reshape(8, SIDE, 8, act), hop_two)).astype(jnp.bfloat16)
    done = jnp.moveaxis(done, 0, 1).reshape(8, 8 * act)
    return send(done, home).astype(jnp.float32)


def solution(mesh):
    placed = (P("layer", "sens"), P("sens"), P("sens"), P("layer", "sens"), P("sens", "layer"))
    return jax.shard_map(
        per_device,
        mesh=mesh,
        in_specs=placed,
        out_specs=P(("sens", "layer"), None),
        check_vma=False,
    )
```

time: 244 us -> 255 us (1.045)
  blocking collectives: 0 us -> 49.8 us
  waiting for transfers between devices: 78 us -> 50.9 us
  starting transfers between devices: 68.3 us -> 51.9 us
  local copies, waits for them, and re-layouts: 15.1 us -> 18 us
    all_gather x0 -> x1, blocking collectives: none -> 49.8 us  [per_device(): means = lax.all_gather(means, 'layer', axis=0)]
    ppermute x50 -> x34, waiting for transfers between devices: 77.3 us -> 50.2 us  [send(): return lax.ppermute(x, AXES, moved(fn))]
    ppermute x50 -> x34, starting transfers between devices: 68.3 us -> 46.6 us  [send(): return lax.ppermute(x, AXES, moved(fn))]
    all_to_all x0 -> x1, starting transfers between devices: none -> 5.31 us  [per_device(): stats = jnp.sum(lax.all_to_all(stats, 'sens', 0, 0, tiled=True), axis=0)]
    slice x10 -> x13, local copies, waits for them, and re-layouts: 8.43 us -> 13.4 us  [the longest x3 3.24 us: per_device(): send_u = together(got_l[:, :HALF], got_r[:, :HALF], got_d[:, :HALF])]
    concatenate x2 -> x0, local copies, waits for them, and re-layouts: 2.77 us -> none  [the longest x1 1.91 us: per_device(): pair_b = jnp.concatenate([b_down, b_up], axis=0)]
  transfers between devices with their start and end apart: 51 -> 36, of which waited for: 21 -> 16; matrix products, arithmetic and copies ran while one was open for 12% -> 14% of each run, Pallas kernels for 19% -> 17%
where the time goes in v4:
time: 255 us; the launch traced here: 253 us
  starting transfers between devices  51.9 us (20%)
  waiting for transfers between devices  50.9 us (20%)
  blocking collectives  49.8 us (20%)
  Pallas kernels  49.8 us (20%)
  local copies, waits for them, and re-layouts  18 us (7%)
  between operations  14 us (5%)
  other arithmetic  9.99 us (4%)
  matrix products  9.13 us (4%)
    ppermute x34, waiting for transfers between devices, send(): return lax.ppermute(x, AXES, moved(fn))  50.2 us
    all_gather x1, blocking collectives, per_device(): means = lax.all_gather(means, 'layer', axis=0)  49.8 us
    ppermute x34, starting transfers between devices, send(): return lax.ppermute(x, AXES, moved(fn))  46.6 us
    pallas_call x3, Pallas kernels, reconstruct(): pl.pallas_call(functools.partial(reconstruct_kernel, tuple(pieces), tuple...  38.6 us
    pallas_call x2, Pallas kernels, fit(): pl.pallas_call(fit_kernel, grid=(count,), in_specs=[pl.BlockSpec((n, k),...  11.2 us
    dot_general x2, matrix products, nt(): lax.dot_general(a, b, (((1,), (1,)), ((), ())), preferred_element_type=jn...  9.13 us
    all_to_all x1, starting transfers between devices, per_device(): stats = jnp.sum(lax.all_to_all(stats, 'sens', 0, 0, tiled=True), axis=0)  5.31 us
  transfers between devices with their start and end apart: 36, of which 16 were waited for; matrix products, arithmetic and copies ran while one was open for 14% of the time, Pallas kernels for 17%

profile of v4, /device:TPU:24, one launch (start us, length us, event | category | flops | bytes accessed | tf_op | source)
XLA Modules:
  0.0 253.5 jit_solution(85602859509674130)
XLA Ops:
  9.3 2.8 %collective-permute-start.1 = (bf16[64,8064]{1,0:T(8,128)(2,1)}, bf16[64,8064]{1,0:T(8,128)(2,1)}, u32[]{:S(2)}, u32[]{:S(2)}) collective-permute-start(bf16[64,8064]{1,0:T(8,128)(2,1)} %pad.18.refs_0_), channel_id=1, source_target_pairs={{0,3},{1,0},{2,1},{3,2},{4,7},{5,4},{6,5},{7,6},{8,11},{9,8},{10,9... | collective-permute-start | bytes 3096584 | tf_op jit(solution)/shard_map/ppermute | solution.py:38
  16.0 5.3 %all-to-all-start = ((f32[8,72,128]{2,1,0:T(8,128)}), f32[8,72,128]{2,1,0:T(8,128)S(1)}, u32[]{:S(2)}, u32[]{:S(2)}) async-start(f32[8,72,128]{2,1,0:T(8,128)} %broadcast_in_dim.21), calls=%async_computation | async-start | bytes 589824 | tf_op jit(solution)/shard_map/all_to_all | solution.py:251
  22.0 15.8 %collective-permute-done.3.refs_4_ = bf16[64,8064]{1,0:T(8,128)(2,1)} collective-permute-done((bf16[64,8064]{1,0:T(8,128)(2,1)}, bf16[64,8064]{1,0:T(8,128)(2,1)}, u32[]{:S(2)}, u32[]{:S(2)}) %collective-permute-start.3) | collective-permute-done | bytes 1032224 | tf_op jit(solution)/shard_map/ppermute | solution.py:38
  44.5 2.9 %pad_maximum_fusion.3 = (bf16[192,4096]{1,0:T(8,128)(2,1)}, bf16[192,4096]{1,0:T(8,128)(2,1)}, bf16[192,4096]{1,0:T(8,128)(2,1)}, bf16[192,4096]{1,0:T(8,128)(2,1)}) fusion(bf16[64,4096]{1,0:T(8,128)(2,1)S(1)} %slice.216, bf16[64,4096]{1,0:T(8,128)(2,1)S(1)} %pad.19, bf16[64,3968]{1,0:T(8,128)(2,1)S(1)} %slice.220, bf16[64,4096]{1,0:T(8,128)(2,1)S(1)} %slice.217, ...), kind=kLoop, calls=%fused_computation.15 | loop fusion | flops 17301504 | bytes 9404416 | tf_op jit(solution)/shard_map/concatenate | solution.py:222
  49.5 3.2 %collective-permute-start.7 = (bf16[192,4096]{1,0:T(8,128)(2,1)}, bf16[192,4096]{1,0:T(8,128)(2,1)}, u32[]{:S(2)}, u32[]{:S(2)}) collective-permute-start(bf16[192,4096]{1,0:T(8,128)(2,1)} %get-tuple-element.46), channel_id=1, source_target_pairs={{0,3},{1,0},{2,1},{3,2},{4,7},{5,4},{6,5},{7,6},{8,11},{9,8},{10,9... | collective-permute-start | bytes 4718600 | tf_op jit(solution)/shard_map/ppermute | solution.py:38
  52.8 49.8 %all-gather = bf16[1024,128]{1,0:T(8,128)(2,1)S(1)} all-gather(bf16[64,128]{1,0:T(8,128)(2,1)S(1)} %fusion.32), channel_id=2, replica_groups=mesh['sens'=8,'layer'=16] {'layer'}, dimensions={0}, use_global_device_ids=true | all-gather | bytes 278528 | tf_op jit(solution)/shard_map/all_gather | solution.py:256
  102.6 8.0 %fusion.11.refs_9_.refs_8_.refs_12_ = bf16[1000,128]{1,0:T(8,128)(2,1)S(1)} fusion(bf16[128,7950]{1,0:T(8,128)(2,1)S(1)} %fusion, bf16[1000,7950]{1,0:T(8,128)(2,1)} %refs_11_.1, pred[128]{0:T(512)(128)(4,1)S(1)} %compare_and_fusion.2), kind=kOutput, calls=%fused_computation.26 | convolution fusion | flops 2035840000 | bytes 18191328 | tf_op jit(solution)/shard_map/dot_general | solution.py:84
  110.7 12.4 %shard_map.55 = (f32[160,1000]{1,0:T(8,128)S(1)}, bf16[160,1000]{1,0:T(8,128)(2,1)S(1)}) custom-call(bf16[64,8064]{1,0:T(8,128)(2,1)} %pad.18.refs_0_, bf16[64,8064]{1,0:T(8,128)(2,1)} %collective-permute-done.refs_1_, bf16[64,8064]{1,0:T(8,128)(2,1)} %collective-permute-done.1.refs_2_, bf16[64,8064]{1,0:T(8,128)(2,1)} %collective-permute-done.2.refs_3_, ...), custom_call_target="tpu_custom_call" | custom-call | tf_op jit(solution)/shard_map/pallas_call | solution.py:144
  128.0 2.8 %collective-permute-start.11 = (bf16[128,4096]{1,0:T(8,128)(2,1)S(1)}, bf16[128,4096]{1,0:T(8,128)(2,1)S(1)}, u32[]{:S(2)}, u32[]{:S(2)}) collective-permute-start(bf16[128,4096]{1,0:T(8,128)(2,1)S(1)} %get-tuple-element.57), channel_id=1, source_target_pairs={{0,3},{1,0},{2,1},{3,2},{4,7},{5,4},{6,5},{7,6},{8,11},{9,8},{10,9... | collective-permute-start | bytes 3145736 | tf_op jit(solution)/shard_map/ppermute | solution.py:38
  132.8 13.5 %shard_map.56 = (f32[192,1000]{1,0:T(8,128)S(1)}, bf16[192,1000]{1,0:T(8,128)(2,1)S(1)}) custom-call(bf16[192,4096]{1,0:T(8,128)(2,1)} %collective-permute-done.4.refs_0_, bf16[192,4096]{1,0:T(8,128)(2,1)} %collective-permute-done.6.refs_1_, bf16[192,4096]{1,0:T(8,128)(2,1)} %collective-permute-done.7.refs_2_, ...), custom_call_target="tpu_custom_call" | custom-call | tf_op jit(solution)/shard_map/pallas_call | solution.py:144
  149.0 2.6 %collective-permute-done.9.refs_2_ = bf16[128,4096]{1,0:T(8,128)(2,1)S(1)} collective-permute-done((bf16[128,4096]{1,0:T(8,128)(2,1)S(1)}, bf16[128,4096]{1,0:T(8,128)(2,1)S(1)}, u32[]{:S(2)}, u32[]{:S(2)}) %collective-permute-start.9) | collective-permute-done | bytes 1048608 | tf_op jit(solution)/shard_map/ppermute | solution.py:38
  158.0 3.3 %collective-permute-start.16 = (bf16[32,4096]{1,0:T(8,128)(2,1)S(1)}, bf16[32,4096]{1,0:T(8,128)(2,1)S(1)}, u32[]{:S(2)}, u32[]{:S(2)}) collective-permute-start(bf16[32,4096]{1,0:T(8,128)(2,1)S(1)} %slice.184), channel_id=1, source_target_pairs={{0,3},{1,0},{2,1},{3,2},{4,7},{5,4},{6,5},{7,6},{8,11},{9,8},{10,9... | collective-permute-start | bytes 786440 | tf_op jit(solution)/shard_map/ppermute | solution.py:38
  167.7 2.3 collective-permute-start.18
  171.5 12.8 %shard_map.57 = (f32[160,1000]{1,0:T(8,128)}, bf16[160,1000]{1,0:T(8,128)(2,1)S(1)}) custom-call(bf16[128,4096]{1,0:T(8,128)(2,1)} %copy-done.2, bf16[128,4096]{1,0:T(8,128)(2,1)} %copy-done, bf16[128,4096]{1,0:T(8,128)(2,1)} %copy-done.3, bf16[128,4096]{1,0:T(8,128)(2,1)} %copy-done.1, bf16[32,4096]{1,0:T(8,128)(2,1)S(1)} %collective-permute-done.13.refs_4_, ...), custom_call_target="tpu_custom_call" | custom-call | tf_op jit(solution)/shard_map/pallas_call | solution.py:144
  193.0 2.4 collective-permute-done.23
  195.6 5.6 %shard_map.58 = bf16[4,128,975]{2,1,0:T(8,128)(2,1)S(1)} custom-call(bf16[128,1000]{1,0:T(8,128)(2,1)S(1)} %select_bitcast_fusion.p, bf16[8,975,1000]{2,1,0:T(8,128)(2,1)} %all-gather.5.cloned.1.call-done.f), custom_call_target="tpu_custom_call" | custom-call | tf_op jit(solution)/shard_map/pallas_call | solution.py:177
  204.6 5.6 %shard_map.59 = bf16[4,128,975]{2,1,0:T(8,128)(2,1)S(1)} custom-call(bf16[128,1000]{1,0:T(8,128)(2,1)S(1)} %select_bitcast_fusion.p, bf16[8,975,1000]{2,1,0:T(8,128)(2,1)} %all-gather.5.cloned.1.call-done.f), custom_call_target="tpu_custom_call" | custom-call | tf_op jit(solution)/shard_map/pallas_call | solution.py:177
  213.0 2.0 collective-permute-start.29
  215.2 2.1 collective-permute-done.27
  217.3 5.2 %collective-permute-done.28 = bf16[4,32,975]{2,1,0:T(8,128)(2,1)S(1)} collective-permute-done((bf16[4,32,975]{2,1,0:T(8,128)(2,1)S(1)}, bf16[4,32,975]{2,1,0:T(8,128)(2,1)S(1)}, u32[]{:S(2)}, u32[]{:S(2)}) %collective-permute-start.28) | collective-permute-done | bytes 249632 | tf_op jit(solution)/shard_map/ppermute | solution.py:38
  223.4 3.8 %collective-permute-start.31 = (bf16[8,8,975]{2,0,1:T(8,128)(2,1)S(1)}, bf16[8,8,975]{2,0,1:T(8,128)(2,1)S(1)}, u32[]{:S(2)}, u32[]{:S(2)}) collective-permute-start(bf16[8,8,975]{2,0,1:T(8,128)(2,1)S(1)} %get-tuple-element.97), channel_id=1, source_target_pairs={{0,3},{1,0},{2,1},{3,2},{4,7},{5,4},{6,5},{7,6},{8,11},{9,8},{10,9... | collective-permute-start | bytes 374408 | tf_op jit(solution)/shard_map/ppermute | solution.py:38
  230.1 3.6 %collective-permute-done.32 = bf16[8,8,975]{2,0,1:T(8,128)(2,1)S(1)} collective-permute-done((bf16[8,8,975]{2,0,1:T(8,128)(2,1)S(1)}, bf16[8,8,975]{2,0,1:T(8,128)(2,1)S(1)}, u32[]{:S(2)}, u32[]{:S(2)}) %collective-permute-start.32) | collective-permute-done | bytes 124832 | tf_op jit(solution)/shard_map/ppermute | solution.py:38
  234.0 3.4 %collective-permute-start.33 = (bf16[8,7800]{1,0:T(8,128)(2,1)S(1)}, bf16[8,7800]{1,0:T(8,128)(2,1)S(1)}, u32[]{:S(2)}, u32[]{:S(2)}) collective-permute-start(bf16[8,7800]{1,0:T(8,128)(2,1)S(1)} %reshape.72), channel_id=1, source_target_pairs={{0,0},{1,8},{2,16},{3,24},{4,32},{5,40},{6,48},{7,56},{8,64},{9,72... | collective-permute-start | bytes 374408 | tf_op jit(solution)/shard_map/ppermute | solution.py:38
  237.3 8.6 %collective-permute-done.33 = bf16[8,7800]{1,0:T(8,128)(2,1)S(1)} collective-permute-done((bf16[8,7800]{1,0:T(8,128)(2,1)S(1)}, bf16[8,7800]{1,0:T(8,128)(2,1)S(1)}, u32[]{:S(2)}, u32[]{:S(2)}) %collective-permute-start.33) | collective-permute-done | bytes 124832 | tf_op jit(solution)/shard_map/ppermute | solution.py:38
  (143 shorter events, 59.8 us)
Async XLA Ops:
  6.5 189.1 %all-gather.5.cloned.1.call-start = ((), (), s32[]{:S(2)}) async-start(), calls=%async_computation.1 | async-start | bytes 17989632 | tf_op jit(solution)/shard_map/all_gather | solution.py:236
  9.3 32.0 %collective-permute-start.1 = (bf16[64,8064]{1,0:T(8,128)(2,1)}, bf16[64,8064]{1,0:T(8,128)(2,1)}, u32[]{:S(2)}, u32[]{:S(2)}) collective-permute-start(bf16[64,8064]{1,0:T(8,128)(2,1)} %pad.18.refs_0_), channel_id=1, source_target_pairs={{0,3},{1,0},{2,1},{3,2},{4,7},{5,4},{6,5},{7,6},{8,11},{9,8},{10,9... | collective-permute-start | bytes 3096584 | tf_op jit(solution)/shard_map/ppermute | solution.py:38
  12.0 26.9 %collective-permute-start.2 = (bf16[64,8064]{1,0:T(8,128)(2,1)}, bf16[64,8064]{1,0:T(8,128)(2,1)}, u32[]{:S(2)}, u32[]{:S(2)}) collective-permute-start(bf16[64,8064]{1,0:T(8,128)(2,1)} %pad.18.refs_0_), channel_id=1, source_target_pairs={{0,4},{1,5},{2,6},{3,7},{4,8},{5,9},{6,10},{7,11},{8,12},{9,13},{1... | collective-permute-start | bytes 3096584 | tf_op jit(solution)/shard_map/ppermute | solution.py:38
  12.3 25.6 %collective-permute-start.3 = (bf16[64,8064]{1,0:T(8,128)(2,1)}, bf16[64,8064]{1,0:T(8,128)(2,1)}, u32[]{:S(2)}, u32[]{:S(2)}) collective-permute-start(bf16[64,8064]{1,0:T(8,128)(2,1)} %pad.18.refs_0_), channel_id=1, source_target_pairs={{0,12},{1,13},{2,14},{3,15},{4,0},{5,1},{6,2},{7,3},{8,4},{9,5},{1... | collective-permute-start | bytes 3096584 | tf_op jit(solution)/shard_map/ppermute | solution.py:38
  14.1 29.4 %collective-permute-start = (bf16[64,8064]{1,0:T(8,128)(2,1)}, bf16[64,8064]{1,0:T(8,128)(2,1)}, u32[]{:S(2)}, u32[]{:S(2)}) collective-permute-start(bf16[64,8064]{1,0:T(8,128)(2,1)} %pad.18.refs_0_), channel_id=1, source_target_pairs={{0,1},{1,2},{2,3},{3,0},{4,5},{5,6},{6,7},{7,4},{8,9},{9,10},{10,1... | collective-permute-start | bytes 3096584 | tf_op jit(solution)/shard_map/ppermute | solution.py:38
  16.0 36.8 %all-to-all-start = ((f32[8,72,128]{2,1,0:T(8,128)}), f32[8,72,128]{2,1,0:T(8,128)S(1)}, u32[]{:S(2)}, u32[]{:S(2)}) async-start(f32[8,72,128]{2,1,0:T(8,128)} %broadcast_in_dim.21), calls=%async_computation | async-start | bytes 589824 | tf_op jit(solution)/shard_map/all_to_all | solution.py:251
  47.4 75.6 %collective-permute-start.4 = (bf16[192,4096]{1,0:T(8,128)(2,1)}, bf16[192,4096]{1,0:T(8,128)(2,1)}, u32[]{:S(2)}, u32[]{:S(2)}) collective-permute-start(bf16[192,4096]{1,0:T(8,128)(2,1)} %get-tuple-element.43), channel_id=1, source_target_pairs={{0,4},{1,5},{2,6},{3,7},{4,8},{5,9},{6,10},{7,11},{8,12},{9,13},{1... | collective-permute-start | bytes 4718600 | tf_op jit(solution)/shard_map/ppermute | solution.py:38
  47.7 75.3 %collective-permute-start.5 = (bf16[192,4096]{1,0:T(8,128)(2,1)}, bf16[192,4096]{1,0:T(8,128)(2,1)}, u32[]{:S(2)}, u32[]{:S(2)}) collective-permute-start(bf16[192,4096]{1,0:T(8,128)(2,1)} %get-tuple-element.44), channel_id=1, source_target_pairs={{0,12},{1,13},{2,14},{3,15},{4,0},{5,1},{6,2},{7,3},{8,4},{9,5},{1... | collective-permute-start | bytes 4718600 | tf_op jit(solution)/shard_map/ppermute | solution.py:38
  49.4 73.6 %collective-permute-start.6 = (bf16[192,4096]{1,0:T(8,128)(2,1)}, bf16[192,4096]{1,0:T(8,128)(2,1)}, u32[]{:S(2)}, u32[]{:S(2)}) collective-permute-start(bf16[192,4096]{1,0:T(8,128)(2,1)} %get-tuple-element.45), channel_id=1, source_target_pairs={{0,1},{1,2},{2,3},{3,0},{4,5},{5,6},{6,7},{7,4},{8,9},{9,10},{10,1... | collective-permute-start | bytes 4718600 | tf_op jit(solution)/shard_map/ppermute | solution.py:38
  49.5 73.6 %collective-permute-start.7 = (bf16[192,4096]{1,0:T(8,128)(2,1)}, bf16[192,4096]{1,0:T(8,128)(2,1)}, u32[]{:S(2)}, u32[]{:S(2)}) collective-permute-start(bf16[192,4096]{1,0:T(8,128)(2,1)} %get-tuple-element.46), channel_id=1, source_target_pairs={{0,3},{1,0},{2,1},{3,2},{4,7},{5,4},{6,5},{7,6},{8,11},{9,8},{10,9... | collective-permute-start | bytes 4718600 | tf_op jit(solution)/shard_map/ppermute | solution.py:38
  127.5 20.1 %collective-permute-start.10 = (bf16[128,4096]{1,0:T(8,128)(2,1)S(1)}, bf16[128,4096]{1,0:T(8,128)(2,1)S(1)}, u32[]{:S(2)}, u32[]{:S(2)}) collective-permute-start(bf16[128,4096]{1,0:T(8,128)(2,1)S(1)} %get-tuple-element.56), channel_id=1, source_target_pairs={{0,1},{1,2},{2,3},{3,0},{4,5},{5,6},{6,7},{7,4},{8,9},{9,10},{10,1... | collective-permute-start | bytes 3145736 | tf_op jit(solution)/shard_map/ppermute | solution.py:38
  128.0 19.6 %collective-permute-start.11 = (bf16[128,4096]{1,0:T(8,128)(2,1)S(1)}, bf16[128,4096]{1,0:T(8,128)(2,1)S(1)}, u32[]{:S(2)}, u32[]{:S(2)}) collective-permute-start(bf16[128,4096]{1,0:T(8,128)(2,1)S(1)} %get-tuple-element.57), channel_id=1, source_target_pairs={{0,3},{1,0},{2,1},{3,2},{4,7},{5,4},{6,5},{7,6},{8,11},{9,8},{10,9... | collective-permute-start | bytes 3145736 | tf_op jit(solution)/shard_map/ppermute | solution.py:38
  130.8 18.2 %collective-permute-start.8 = (bf16[128,4096]{1,0:T(8,128)(2,1)S(1)}, bf16[128,4096]{1,0:T(8,128)(2,1)S(1)}, u32[]{:S(2)}, u32[]{:S(2)}) collective-permute-start(bf16[128,4096]{1,0:T(8,128)(2,1)S(1)} %get-tuple-element.54), channel_id=1, source_target_pairs={{0,4},{1,5},{2,6},{3,7},{4,8},{5,9},{6,10},{7,11},{8,12},{9,13},{1... | collective-permute-start | bytes 3145736 | tf_op jit(solution)/shard_map/ppermute | solution.py:38
  132.4 19.2 %collective-permute-start.9 = (bf16[128,4096]{1,0:T(8,128)(2,1)S(1)}, bf16[128,4096]{1,0:T(8,128)(2,1)S(1)}, u32[]{:S(2)}, u32[]{:S(2)}) collective-permute-start(bf16[128,4096]{1,0:T(8,128)(2,1)S(1)} %get-tuple-element.55), channel_id=1, source_target_pairs={{0,12},{1,13},{2,14},{3,15},{4,0},{5,1},{6,2},{7,3},{8,4},{9,5},{1... | collective-permute-start | bytes 3145736 | tf_op jit(solution)/shard_map/ppermute | solution.py:38
  153.8 9.6 %collective-permute-start.13 = (bf16[32,4096]{1,0:T(8,128)(2,1)S(1)}, bf16[32,4096]{1,0:T(8,128)(2,1)S(1)}, u32[]{:S(2)}, u32[]{:S(2)}) collective-permute-start(bf16[32,4096]{1,0:T(8,128)(2,1)S(1)} %slice.181), channel_id=1, source_target_pairs={{0,4},{1,5},{2,6},{3,7},{4,8},{5,9},{6,10},{7,11},{8,12},{9,13},{1... | collective-permute-start | bytes 786440 | tf_op jit(solution)/shard_map/ppermute | solution.py:38
  155.4 9.7 %collective-permute-start.14 = (bf16[32,4096]{1,0:T(8,128)(2,1)S(1)}, bf16[32,4096]{1,0:T(8,128)(2,1)S(1)}, u32[]{:S(2)}, u32[]{:S(2)}) collective-permute-start(bf16[32,4096]{1,0:T(8,128)(2,1)S(1)} %slice.182), channel_id=1, source_target_pairs={{0,12},{1,13},{2,14},{3,15},{4,0},{5,1},{6,2},{7,3},{8,4},{9,5},{1... | collective-permute-start | bytes 786440 | tf_op jit(solution)/shard_map/ppermute | solution.py:38
  166.7 17.7 %collective-permute-start.17 = (bf16[11,8,1000]{2,1,0:T(8,128)(2,1)}, bf16[11,8,1000]{2,1,0:T(8,128)(2,1)}, u32[]{:S(2)}, u32[]{:S(2)}) collective-permute-start(bf16[11,8,1000]{2,1,0:T(8,128)(2,1)} %get-tuple-element.66), channel_id=1, source_target_pairs={{0,32},{1,33},{2,34},{3,35},{4,36},{5,37},{6,38},{7,39},{8,40},{9,... | collective-permute-start | bytes 528008 | tf_op jit(solution)/shard_map/ppermute | solution.py:38
  167.7 16.7 %collective-permute-start.18 = (bf16[11,8,1000]{2,1,0:T(8,128)(2,1)S(1)}, bf16[11,8,1000]{2,1,0:T(8,128)(2,1)}, u32[]{:S(2)}, u32[]{:S(2)}) collective-permute-start(bf16[11,8,1000]{2,1,0:T(8,128)(2,1)S(1)} %get-tuple-element.67), channel_id=1, source_target_pairs={{0,96},{1,97},{2,98},{3,99},{4,100},{5,101},{6,102},{7,103},{8,104... | collective-permute-start | bytes 528008 | tf_op jit(solution)/shard_map/ppermute | solution.py:38
  170.0 14.4 %collective-permute-start.19 = (bf16[11,8,1000]{2,1,0:T(8,128)(2,1)S(1)}, bf16[11,8,1000]{2,1,0:T(8,128)(2,1)}, u32[]{:S(2)}, u32[]{:S(2)}) collective-permute-start(bf16[11,8,1000]{2,1,0:T(8,128)(2,1)S(1)} %get-tuple-element.68), channel_id=1, source_target_pairs={{0,64},{1,65},{2,66},{3,67},{4,68},{5,69},{6,70},{7,71},{8,72},{9,... | collective-permute-start | bytes 528008 | tf_op jit(solution)/shard_map/ppermute | solution.py:38
  201.3 11.7 %collective-permute-start.24 = (bf16[4,32,975]{2,1,0:T(8,128)(2,1)S(1)}, bf16[4,32,975]{2,1,0:T(8,128)(2,1)S(1)}, u32[]{:S(2)}, u32[]{:S(2)}) collective-permute-start(bf16[4,32,975]{2,1,0:T(8,128)(2,1)S(1)} %get-tuple-element.82), channel_id=1, source_target_pairs={{0,4},{1,5},{2,6},{3,7},{4,8},{5,9},{6,10},{7,11},{8,12},{9,13},{1... | collective-permute-start | bytes 748808 | tf_op jit(solution)/shard_map/ppermute | solution.py:38
  203.1 11.9 %collective-permute-start.25 = (bf16[4,32,975]{2,1,0:T(8,128)(2,1)S(1)}, bf16[4,32,975]{2,1,0:T(8,128)(2,1)S(1)}, u32[]{:S(2)}, u32[]{:S(2)}) collective-permute-start(bf16[4,32,975]{2,1,0:T(8,128)(2,1)S(1)} %get-tuple-element.83), channel_id=1, source_target_pairs={{0,12},{1,13},{2,14},{3,15},{4,0},{5,1},{6,2},{7,3},{8,4},{9,5},{1... | collective-permute-start | bytes 748808 | tf_op jit(solution)/shard_map/ppermute | solution.py:38
  203.4 11.6 %collective-permute-start.26 = (bf16[4,32,975]{2,1,0:T(8,128)(2,1)S(1)}, bf16[4,32,975]{2,1,0:T(8,128)(2,1)S(1)}, u32[]{:S(2)}, u32[]{:S(2)}) collective-permute-start(bf16[4,32,975]{2,1,0:T(8,128)(2,1)S(1)} %get-tuple-element.84), channel_id=1, source_target_pairs={{0,8},{1,9},{2,10},{3,11},{4,12},{5,13},{6,14},{7,15},{8,0},{9,1},... | collective-permute-start | bytes 748808 | tf_op jit(solution)/shard_map/ppermute | solution.py:38
  212.1 10.4 %collective-permute-start.28 = (bf16[4,32,975]{2,1,0:T(8,128)(2,1)S(1)}, bf16[4,32,975]{2,1,0:T(8,128)(2,1)S(1)}, u32[]{:S(2)}, u32[]{:S(2)}) collective-permute-start(bf16[4,32,975]{2,1,0:T(8,128)(2,1)S(1)} %get-tuple-element.87), channel_id=1, source_target_pairs={{0,12},{1,13},{2,14},{3,15},{4,0},{5,1},{6,2},{7,3},{8,4},{9,5},{1... | collective-permute-start | bytes 748808 | tf_op jit(solution)/shard_map/ppermute | solution.py:38
  234.0 12.0 %collective-permute-start.33 = (bf16[8,7800]{1,0:T(8,128)(2,1)S(1)}, bf16[8,7800]{1,0:T(8,128)(2,1)S(1)}, u32[]{:S(2)}, u32[]{:S(2)}) collective-permute-start(bf16[8,7800]{1,0:T(8,128)(2,1)S(1)} %reshape.72), channel_id=1, source_target_pairs={{0,0},{1,8},{2,16},{3,24},{4,32},{5,40},{6,48},{7,56},{8,64},{9,72... | collective-permute-start | bytes 374408 | tf_op jit(solution)/shard_map/ppermute | solution.py:38
  (20 other events, 116.4 us)
Sparse Core Ops, SparseCore 0:
  9.0 86.1 all-gather.4

commit v5 on v0

v5 whole, which is shorter than its diff:
```python
import functools

import jax
import jax.numpy as jnp
from jax import lax
from jax.experimental import pallas as pl
from jax.experimental.pallas import tpu as pltpu
from jax.sharding import PartitionSpec as P

SENSORS = 6
AXES = ("sens", "layer")
SIDE = 4
ROWS = 64
PART = 32
HALF = 4096
EDGE = 3840
MEANS = 3968
WIDE = 8064
INSIDE = 14
PBLOCK = 256
VMEM = 52 * 2**20


def moved(fn):
    pairs = []
    for z in range(4):
        for c in range(2):
            for y in range(4):
                for x in range(4):
                    z2, c2, y2, x2 = fn(z, c, y, x)
                    pairs.append(
                        ((z * 2 + c) * 16 + y * 4 + x,
                         ((z2 % 4) * 2 + c2 % 2) * 16 + (y2 % 4) * 4 + x2 % 4)
                    )
    return pairs


def send(x, fn):
    return lax.ppermute(x, AXES, moved(fn))


def swap_core(v):
    return send(v, lambda z, c, y, x: (z, c + 1, y, x))


def right(v):
    return send(v, lambda z, c, y, x: (z, c, y, x + 1))


def left(v):
    return send(v, lambda z, c, y, x: (z, c, y, x - 1))


def up(v):
    return send(v, lambda z, c, y, x: (z, c, y + 1, x))


def down(v):
    return send(v, lambda z, c, y, x: (z, c, y - 1, x))


def hop_z(d):
    return lambda z, c, y, x: (z + d, c, y, x)


def hop_one(d):
    return lambda z, c, y, x: (z, c, y + d * (1 - c), x + d * c)


def hop_two(d):
    return lambda z, c, y, x: (z, c, y + d * c, x + d * (1 - c))


def ring_z(v):
    return send(v, lambda z, c, y, x: (z + 1 - 2 * c, c, y, x))


def after(value, *others):
    return lax.optimization_barrier((value, *others))


def nt(a, b, **kw):
    return lax.dot_general(
        a, b, (((1,), (1,)), ((), ())), preferred_element_type=jnp.float32, **kw
    )


def reconstruct_kernel(pieces, count, index, *refs):
    arrays = refs[:count]
    if index == 0:
        position, ra, rb, rw, own, other, tail, held, sems = refs[count:]
    else:
        position, ra, rb, rw, tail, own, other, held, sems = refs[count:]

    def copies(side):
        out = []
        for i, (a, row, rows, ry, rx, inner, half) in enumerate(pieces):
            if half != side:
                continue
            if index == 0:
                y = lax.rem(position[1] + ry, SIDE)
                x = lax.rem(position[2] + rx, SIDE)
                to_row = pl.multiple_of((y * SIDE + x) * PART, PART) + inner
                source = arrays[a].at[pl.ds(row, rows)]
                width = HALF
            else:
                to_row = row
                width = HALF if half == 0 else WIDE - HALF
                source = arrays[a].at[pl.ds(row, rows), pl.ds(half * HALF, width)]
            target = held.at[pl.ds(to_row, rows), pl.ds(half * HALF, width)]
            out.append(pltpu.make_async_copy(source, target, sems.at[i]))
        return out

    @pl.when(pl.program_id(0) == 0)
    def _():
        for copy in copies(0) + copies(1):
            copy.start()
        for copy in copies(0):
            copy.wait()

    val = nt(held[:, :HALF], ra[...])

    @pl.when(pl.program_id(0) == 0)
    def _():
        for copy in copies(1):
            copy.wait()

    lane = lax.broadcasted_iota(jnp.int32, (ra.shape[0], 128), 1)
    edge = rb[:, EDGE:MEANS].astype(jnp.float32)
    edge = jnp.where(lane < INSIDE, edge, 0.0).astype(jnp.bfloat16)
    val = val + nt(held[:, HALF : HALF + EDGE], rb[:, :EDGE])
    val = val + nt(held[:, HALF + EDGE : HALF + MEANS], edge)
    if index == 0:
        means = held[:, HALF + MEANS :]
        tail[...] = means
    else:
        means = tail[...]
    val = val + nt(means, rw[...])
    n = val.shape[0]
    pairs = val.reshape(SIDE, 2, 2 * PART, val.shape[1])
    first = pairs[:, 0].reshape(n // 2, val.shape[1])
    second = pairs[:, 1].reshape(n // 2, val.shape[1])
    swapped = position[0] == 1
    own[...] = jnp.where(swapped, second, first)
    other[...] = jnp.where(swapped, first, second).astype(jnp.bfloat16)


def reconstruct(index, arrays, pieces, position, r, rw, tail=None):
    n = 16 * PART
    p = r.shape[0]
    half = pl.BlockSpec((n // 2, PBLOCK), lambda j: (0, j))
    whole = pl.BlockSpec((n, 128), lambda j: (0, 0))
    in_specs = [pl.BlockSpec(memory_space=pl.ANY)] * len(arrays) + [
        pl.BlockSpec(memory_space=pltpu.SMEM),
        pl.BlockSpec((PBLOCK, HALF), lambda j: (j, 0)),
        pl.BlockSpec((PBLOCK, HALF), lambda j: (j, 1)),
        pl.BlockSpec((PBLOCK, 128), lambda j: (j, index)),
    ]
    args = [*arrays, position, r, r, rw]
    out_specs = [half, half]
    out_shape = [
        jax.ShapeDtypeStruct((n // 2, p), jnp.float32),
        jax.ShapeDtypeStruct((n // 2, p), jnp.bfloat16),
    ]
    if index == 0:
        out_specs.append(whole)
        out_shape.append(jax.ShapeDtypeStruct((n, 128), jnp.bfloat16))
    else:
        in_specs.append(whole)
        args.append(tail)
    return pl.pallas_call(
        functools.partial(reconstruct_kernel, tuple(pieces), len(arrays), index),
        grid=(pl.cdiv(p, PBLOCK),),
        in_specs=in_specs,
        out_specs=out_specs,
        out_shape=out_shape,
        scratch_shapes=[
            pltpu.VMEM((n, 2 * HALF), jnp.bfloat16),
            pltpu.SemaphoreType.DMA((len(pieces),)),
        ],
        compiler_params=pltpu.CompilerParams(vmem_limit_bytes=VMEM),
        cost_estimate=pl.CostEstimate(flops=0, bytes_accessed=0, transcendentals=0),
    )(*args)


def fit_kernel(p, f0, f1, f2, f3, out, held, sems):
    sources = (f0, f1, f2, f3)
    copies = [
        pltpu.make_async_copy(f, held.at[i], sems.at[i]) for i, f in enumerate(sources)
    ]
    for copy in copies:
        copy.start()
    for i, copy in enumerate(copies):
        copy.wait()
        out[i] = nt(p[...], held[i]).astype(jnp.bfloat16)


def fit(points, blocks):
    n, k = points.shape
    m = blocks[0].shape[0]
    return pl.pallas_call(
        fit_kernel,
        in_specs=[pl.BlockSpec(memory_space=pltpu.VMEM)]
        + [pl.BlockSpec(memory_space=pl.ANY)] * 4,
        out_specs=pl.BlockSpec(memory_space=pltpu.VMEM),
        out_shape=jax.ShapeDtypeStruct((4, n, m), jnp.bfloat16),
        scratch_shapes=[
            pltpu.VMEM((4, m, k), jnp.bfloat16),
            pltpu.SemaphoreType.DMA((4,)),
        ],
        compiler_params=pltpu.CompilerParams(vmem_limit_bytes=VMEM),
        cost_estimate=pl.CostEstimate(flops=0, bytes_accessed=0, transcendentals=0),
    )(points, *blocks)


def picks_by_z(own, other, z):
    got = own + swap_core(other).astype(jnp.float32)
    got = got.reshape(SIDE, 2, PART, own.shape[1])

    def pick(d):
        return lax.dynamic_index_in_dim(got, (z + d) % SIDE, 0, keepdims=False)

    return [pick(0)] + [pick(d).astype(jnp.bfloat16) for d in (1, 3, 2)]


def sums_by_z(picked):
    pieces = picked[:1] + [send(v, hop_z(d)) for v, d in zip(picked[1:], (1, 3, 2))]
    return total(pieces).astype(jnp.bfloat16)


def owned(blocks, here, hop):
    def pick(d):
        return lax.dynamic_index_in_dim(blocks, (here + d) % SIDE, 1, keepdims=False)

    return [pick(0)] + [send(pick(d).astype(jnp.bfloat16), hop(d)) for d in (1, 3, 2)]


def total(pieces):
    out = pieces[0].astype(jnp.float32)
    for piece in pieces[1:]:
        out = out + piece.astype(jnp.float32)
    return out


def together(*pieces):
    return jnp.concatenate(pieces, axis=0)


def per_device(slopes, valid, sensor_map, reconstructor, fitting):
    s_idx = lax.axis_index("sens")
    l_idx = lax.axis_index("layer")
    z, c = s_idx // 2, s_idx % 2
    y, x = l_idx // SIDE, l_idx % SIDE
    width = slopes.shape[1]
    width_p = reconstructor.shape[0]
    act = fitting.shape[0]
    position = jnp.stack([c, y, x]).astype(jnp.int32)

    live = valid.astype(jnp.bfloat16)[None, :]
    masked = slopes * live
    late = lax.all_gather(
        jnp.pad(masked[PART:], ((0, 0), (0, WIDE - width))), "layer", axis=0, tiled=True
    )

    own_a = masked[:PART, :HALF]
    a_l, a_r = right(own_a), left(own_a)
    a_d, a_u = up(own_a), down(own_a)
    fits = [fitting, ring_z(fitting)]

    group = sensor_map * 2 + (lax.iota(jnp.int32, width) + s_idx * width) % 2
    lane = lax.iota(jnp.int32, 128)
    label = jnp.where(lane % 64 < 36, lane % 64 % 12, -1)
    member = ((group[None, :] == label[:, None]) & (valid[None, :] == 1)).astype(jnp.bfloat16)
    counted = jnp.concatenate([masked, jnp.ones((8, width), jnp.bfloat16)], axis=0)
    stats = nt(counted, member)
    stats = jnp.broadcast_to(stats[None], (8, *stats.shape))
    stats = jnp.sum(lax.all_to_all(stats, "sens", 0, 0, tiled=True), axis=0)
    means = stats[:ROWS] / jnp.maximum(stats[ROWS : ROWS + 1], 1.0)
    means = jnp.where((lane < 64)[None, :], means[:PART], means[PART:])
    high = lax.reduce_precision(means, 8, 7)
    low = (lane % 64 >= 12) & (lane % 64 < 24)
    means = jnp.where(low[None, :], means - high, high).astype(jnp.bfloat16)
    own_b = jnp.pad(masked[:PART, HALF:], ((0, 0), (0, 2 * HALF - width)))
    own_b = own_b + jnp.pad(means, ((0, 0), (MEANS, 0)))
    b_l, b_r = right(own_b), left(own_b)
    b_d, b_u = up(own_b), down(own_b)

    send_u = together(a_l, a_r, a_d)
    send_d = together(a_l, a_r, b_u)
    send_r = together(b_d, b_u, a_l)
    send_l = together(b_d, b_u, b_r)
    member, send_u, send_d, send_r, send_l, a_u, b_l, fits[1] = after(
        member, send_u, send_d, send_r, send_l, a_u, b_l, fits[1]
    )
    fits.append(ring_z(fits[-1]))
    one_d, one_u = up(send_u), down(send_d)
    one_l, one_r = right(send_r), left(send_l)
    rw = -nt(reconstructor, member)
    rw_high = lax.reduce_precision(rw, 8, 7)
    last = (lane % 64 >= 24) & (lane % 64 < 36)
    rw = jnp.where(last[None, :], rw - rw_high, rw_high)
    early = (lane < 64)[None, :]
    rw = jnp.concatenate([jnp.where(early, rw, 0.0), jnp.where(early, 0.0, rw)], axis=1)
    rw = rw.astype(jnp.bfloat16)

    fits[2], one_d, one_u, one_l, one_r, rw = after(fits[2], one_d, one_u, one_l, one_r, rw)
    fits.append(ring_z(fits[-1]))
    far_x_a, far_y_b = one_l[2 * PART :], one_u[2 * PART :]
    two_d = together(far_x_a, one_d[:PART])
    two_u = together(far_x_a, one_u[PART : 2 * PART])
    two_l = together(far_y_b, one_l[:PART])
    two_r = together(far_y_b, one_r[PART : 2 * PART])
    two_d, two_u, two_l, two_r = after(two_d, two_u, two_l, two_r)
    get_d, get_u = up(two_d), down(two_u)
    get_l, get_r = right(two_l), left(two_r)

    half = PART // 2
    ends = after(get_d[:half], get_u[half:PART], get_l[:half], get_r[half:PART])
    end_d, end_u = up(ends[0]), down(ends[1])
    end_l, end_r = right(ends[2]), left(ends[3])

    arrays = [own_a, own_b, a_l, b_l, a_r, b_r, a_d, b_d, a_u, b_u, one_d, one_u, one_l, one_r]
    arrays += [get_d, get_u, get_l, get_r, end_d, end_u, end_l, end_r]

    def piece(array, block, rows, ry, rx, inner, side):
        index = [i for i, a in enumerate(arrays) if a is array][0]
        return (index, block * rows, rows, ry, rx, inner, side)

    pieces = []
    for ry, rx, (array_a, block_a), (array_b, block_b) in (
        (0, 0, (own_a, 0), (own_b, 0)),
        (0, 3, (a_l, 0), (b_l, 0)),
        (0, 1, (a_r, 0), (b_r, 0)),
        (3, 0, (a_d, 0), (b_d, 0)),
        (1, 0, (a_u, 0), (b_u, 0)),
        (3, 3, (one_d, 0), (one_l, 0)),
        (3, 1, (one_d, 1), (one_r, 0)),
        (1, 3, (one_u, 0), (one_l, 1)),
        (1, 1, (one_u, 1), (one_r, 1)),
        (0, 2, (one_l, 2), (one_r, 2)),
        (2, 0, (one_d, 2), (one_u, 2)),
        (3, 2, (get_d, 0), (get_l, 1)),
        (1, 2, (get_u, 0), (get_r, 1)),
        (2, 3, (get_d, 1), (get_l, 0)),
        (2, 1, (get_u, 1), (get_r, 0)),
    ):
        pieces.append(piece(array_a, block_a, PART, ry, rx, 0, 0))
        pieces.append(piece(array_b, block_b, PART, ry, rx, 0, 1))
    pieces.append(piece(end_d, 0, half, 2, 2, 0, 0))
    pieces.append(piece(end_u, 0, half, 2, 2, half, 0))
    pieces.append(piece(end_l, 0, half, 2, 2, 0, 1))
    pieces.append(piece(end_r, 0, half, 2, 2, half, 1))
    own, other, tail = reconstruct(0, arrays, pieces, position, reconstructor, rw)
    own, other, *fits = after(own, other, *fits)
    picked = picks_by_z(own, other, z)
    swapped = [swap_core(f) for f in fits]
    swapped[0], swapped[1], *picked, late = after(swapped[0], swapped[1], *picked, late)
    near = sums_by_z(picked)

    own, other = reconstruct(
        1, [late], [(0, 0, 16 * PART, 0, 0, 0, side) for side in (0, 1)],
        position, reconstructor, rw, tail,
    )
    far = sums_by_z(picks_by_z(own, other, z))
    points = jnp.concatenate([near, far], axis=1)

    rows = points.reshape(SIDE, SIDE, 8, width_p)
    rows = jnp.where(c == 0, rows, jnp.swapaxes(rows, 0, 1)).reshape(2 * ROWS, width_p)
    one = jnp.where(c == 0, y, x)
    two = jnp.where(c == 0, x, y)
    half_a = owned(fit(rows, fits).reshape(4, SIDE, SIDE * 8, act), one, hop_one)
    half_b = owned(fit(rows, swapped).reshape(4, SIDE, SIDE * 8, act), one, hop_one)
    both = jnp.concatenate([total(half_a), total(half_b)], axis=0)
    done = total(owned(both.reshape(8, SIDE, 8, act), two, hop_two))

    sens = lax.iota(jnp.int32, 8)
    step = jnp.where(sens % 2 == 0, z - sens // 2, sens // 2 - z) % SIDE
    found = jnp.where(sens % 2 == c, 0, 4) + step
    done = jnp.take(done, found, axis=0)
    return jnp.moveaxis(done, 0, 1).reshape(8, 8 * act)


def solution(mesh):
    placed = (P("layer", "sens"), P("sens"), P("sens"), P("layer", "sens"), P("sens", "layer"))
    return jax.shard_map(
        per_device,
        mesh=mesh,
        in_specs=placed,
        out_specs=P(("sens", "layer"), None),
        check_vma=False,
    )
```

time: 285 us -> 240 us (0.84)
  matrix products: 59.2 us -> 9.29 us
  starting transfers between devices: 9.18 us -> 56.7 us
  Pallas kernels: 0 us -> 45.9 us
  blocking collectives: 39.9 us -> 0 us
  local copies, waits for them, and re-layouts: 48.2 us -> 11.3 us
  waiting for transfers between devices: 110 us -> 92.9 us
  other arithmetic: 2.25 us -> 9.12 us
    all_gather x2 -> x1, waiting for transfers between devices: 104 us -> 0.02 us  [per_device(): lax.all_gather(jnp.pad(masked[PART:], ((0, 0), (0, WIDE - width))), 'laye...]
    ppermute x0 -> x44, waiting for transfers between devices: none -> 90.6 us  [send(): return lax.ppermute(x, AXES, moved(fn))]
    ppermute x0 -> x44, starting transfers between devices: none -> 51.4 us  [send(): return lax.ppermute(x, AXES, moved(fn))]
    dot_general x5 -> x2, matrix products: 59.2 us -> 9.29 us  [nt(): lax.dot_general(a, b, (((1,), (1,)), ((), ())), preferred_element_type=jn...]
    pallas_call x0 -> x4, Pallas kernels: none -> 45.9 us  [the longest x2 36.5 us: reconstruct(): pl.pallas_call(functools.partial(reconstruct_kernel, tuple(pieces), len(a...]
    all_to_all x2 -> x0, blocking collectives: 39.9 us -> none  [the longest x1 29.5 us: summed_on_arrival(): lax.all_to_all(blocks, axis, split_axis=0, concat_axis=0, tiled=True)]
    all_gather x1 -> x0, local copies, waits for them, and re-layouts: 22.4 us -> none  [per_device(): whole = lax.all_gather(slopes, 'layer', axis=0, tiled=True)]
    unnamed x1 -> x36, local copies, waits for them, and re-layouts: 20.5 us -> 3.26 us
  transfers between devices with their start and end apart: 4 -> 46, of which waited for: 3 -> 25; matrix products, arithmetic and copies ran while one was open for 34% -> 9% of each run, Pallas kernels for 0% -> 11%
where the time goes in v5:
time: 240 us; the launch traced here: 239 us
  waiting for transfers between devices  92.9 us (39%)
  starting transfers between devices  56.7 us (24%)
  Pallas kernels  45.9 us (19%)
  between operations  13.9 us (6%)
  local copies, waits for them, and re-layouts  11.3 us (5%)
  matrix products  9.29 us (4%)
  other arithmetic  9.12 us (4%)
    ppermute x44, waiting for transfers between devices, send(): return lax.ppermute(x, AXES, moved(fn))  90.6 us
    ppermute x44, starting transfers between devices, send(): return lax.ppermute(x, AXES, moved(fn))  51.4 us
    pallas_call x2, Pallas kernels, reconstruct(): pl.pallas_call(functools.partial(reconstruct_kernel, tuple(pieces), len(a...  36.5 us
    pallas_call x2, Pallas kernels, fit(): pl.pallas_call(fit_kernel, in_specs=[pl.BlockSpec(memory_space=pltpu.VMEM...  9.38 us
    dot_general x2, matrix products, nt(): lax.dot_general(a, b, (((1,), (1,)), ((), ())), preferred_element_type=jn...  9.29 us
    all_to_all x1, starting transfers between devices, per_device(): stats = jnp.sum(lax.all_to_all(stats, 'sens', 0, 0, tiled=True), axis=0)  5.32 us
  transfers between devices with their start and end apart: 46, of which 25 were waited for; matrix products, arithmetic and copies ran while one was open for 9% of the time, Pallas kernels for 11%

profile of v5, /device:TPU:24, one launch (start us, length us, event | category | flops | bytes accessed | tf_op | source)
XLA Modules:
  0.0 239.1 jit_solution(13460916317338598362)
XLA Ops:
  11.5 5.3 %all-to-all-start = ((f32[8,72,128]{2,1,0:T(8,128)}), f32[8,72,128]{2,1,0:T(8,128)S(1)}, u32[]{:S(2)}, u32[]{:S(2)}) async-start(f32[8,72,128]{2,1,0:T(8,128)} %broadcast_in_dim.85), calls=%async_computation | async-start | bytes 589824 | tf_op jit(solution)/shard_map/all_to_all | solution.py:277
  25.6 2.5 %collective-permute-done.refs_2_ = bf16[32,4096]{1,0:T(8,128)(2,1)S(1)} collective-permute-done((bf16[32,4096]{1,0:T(8,128)(2,1)S(1)}, bf16[32,4096]{1,0:T(8,128)(2,1)S(1)}, u32[]{:S(2)}, u32[]{:S(2)}) %collective-permute-start) | collective-permute-done | bytes 262176 | tf_op jit(solution)/shard_map/ppermute | solution.py:39
  29.8 3.7 %collective-permute-start.5 = (bf16[32,4096]{1,0:T(8,128)(2,1)S(1)}, bf16[32,4096]{1,0:T(8,128)(2,1)S(1)}, u32[]{:S(2)}, u32[]{:S(2)}) collective-permute-start(bf16[32,4096]{1,0:T(8,128)(2,1)S(1)} %pad_add_fusion.refs_1_), channel_id=1, source_target_pairs={{0,3},{1,0},{2,1},{3,2},{4,7},{5,4},{6,5},{7,6},{8,11},{9,8},{10,9... | collective-permute-start | bytes 786440 | tf_op jit(solution)/shard_map/ppermute | solution.py:39
  35.3 5.1 %collective-permute-done.3.refs_9_ = bf16[32,4096]{1,0:T(8,128)(2,1)S(1)} collective-permute-done((bf16[32,4096]{1,0:T(8,128)(2,1)S(1)}, bf16[32,4096]{1,0:T(8,128)(2,1)S(1)}, u32[]{:S(2)}, u32[]{:S(2)}) %collective-permute-start.3) | collective-permute-done | bytes 262176 | tf_op jit(solution)/shard_map/ppermute | solution.py:39
  44.9 3.2 %collective-permute-done.7.refs_3_ = bf16[32,4096]{1,0:T(8,128)(2,1)S(1)} collective-permute-done((bf16[32,4096]{1,0:T(8,128)(2,1)S(1)}, bf16[32,4096]{1,0:T(8,128)(2,1)S(1)}, u32[]{:S(2)}, u32[]{:S(2)}) %collective-permute-start.7) | collective-permute-done | bytes 262176 | tf_op jit(solution)/shard_map/ppermute | solution.py:39
  51.7 2.5 %collective-permute-start.13 = (bf16[96,4096]{1,0:T(8,128)(2,1)S(1)}, bf16[96,4096]{1,0:T(8,128)(2,1)S(1)}, u32[]{:S(2)}, u32[]{:S(2)}) collective-permute-start(bf16[96,4096]{1,0:T(8,128)(2,1)S(1)} %get-tuple-element.51), channel_id=1, source_target_pairs={{0,3},{1,0},{2,1},{3,2},{4,7},{5,4},{6,5},{7,6},{8,11},{9,8},{10,9... | collective-permute-start | bytes 2359304 | tf_op jit(solution)/shard_map/ppermute | solution.py:39
  54.2 8.2 %select_convert_fusion.1 = (bf16[1000,128]{1,0:T(8,128)(2,1)S(1)}, bf16[1000,128]{1,0:T(8,128)(2,1)S(1)}) fusion(pred[128]{0:T(512)(128)(4,1)S(1)} %get-tuple-element.115, bf16[128,7950]{1,0:T(8,128)(2,1)S(1)} %fusion, bf16[1000,7950]{1,0:T(8,128)(2,1)} %refs_3_.1, pred[128]{0:T(512)(128)(4,1)S(1)} %compare_and_fusion.2), kind=kOutput, calls=%fused_computation.33 | convolution fusion | flops 2035968000 | bytes 18447456 | tf_op jit(solution)/shard_map/dot_general | solution.py:83
  63.2 21.3 %collective-permute-done.10.refs_10_ = bf16[96,4096]{1,0:T(8,128)(2,1)S(1)} collective-permute-done((bf16[96,4096]{1,0:T(8,128)(2,1)S(1)}, bf16[96,4096]{1,0:T(8,128)(2,1)S(1)}, u32[]{:S(2)}, u32[]{:S(2)}) %collective-permute-start.10) | collective-permute-done | bytes 786464 | tf_op jit(solution)/shard_map/ppermute | solution.py:39
  84.6 2.8 %collective-permute-done.11.refs_11_ = bf16[96,4096]{1,0:T(8,128)(2,1)S(1)} collective-permute-done((bf16[96,4096]{1,0:T(8,128)(2,1)S(1)}, bf16[96,4096]{1,0:T(8,128)(2,1)S(1)}, u32[]{:S(2)}, u32[]{:S(2)}) %collective-permute-start.11) | collective-permute-done | bytes 786464 | tf_op jit(solution)/shard_map/ppermute | solution.py:39
  92.4 2.7 %collective-permute-start.17 = (bf16[64,4096]{1,0:T(8,128)(2,1)S(1)}, bf16[64,4096]{1,0:T(8,128)(2,1)S(1)}, u32[]{:S(2)}, u32[]{:S(2)}) collective-permute-start(bf16[64,4096]{1,0:T(8,128)(2,1)S(1)} %get-tuple-element.60), channel_id=1, source_target_pairs={{0,3},{1,0},{2,1},{3,2},{4,7},{5,4},{6,5},{7,6},{8,11},{9,8},{10,9... | collective-permute-start | bytes 1572872 | tf_op jit(solution)/shard_map/ppermute | solution.py:39
  95.1 17.0 %collective-permute-done.14.refs_14_ = bf16[64,4096]{1,0:T(8,128)(2,1)S(1)} collective-permute-done((bf16[64,4096]{1,0:T(8,128)(2,1)S(1)}, bf16[64,4096]{1,0:T(8,128)(2,1)S(1)}, u32[]{:S(2)}, u32[]{:S(2)}) %collective-permute-start.14) | collective-permute-done | bytes 524320 | tf_op jit(solution)/shard_map/ppermute | solution.py:39
  119.4 2.8 %collective-permute-start.21 = (bf16[16,4096]{1,0:T(8,128)(2,1)}, bf16[16,4096]{1,0:T(8,128)(2,1)S(1)}, u32[]{:S(2)}, u32[]{:S(2)}) collective-permute-start(bf16[16,4096]{1,0:T(8,128)(2,1)} %slice.79), channel_id=1, source_target_pairs={{0,3},{1,0},{2,1},{3,2},{4,7},{5,4},{6,5},{7,6},{8,11},{9,8},{10,9... | collective-permute-start | bytes 393224 | tf_op jit(solution)/shard_map/ppermute | solution.py:39
  125.4 17.7 %shard_map.55 = (f32[256,1000]{1,0:T(8,128)}, bf16[256,1000]{1,0:T(8,128)(2,1)}, bf16[512,128]{1,0:T(8,128)(2,1)S(1)}) custom-call(bf16[32,4096]{1,0:T(8,128)(2,1)S(1)} %slice.70.refs_0_, bf16[32,4096]{1,0:T(8,128)(2,1)S(1)} %pad_add_fusion.refs_1_, bf16[32,4096]{1,0:T(8,128)(2,1)S(1)} %collective-permute-done.refs_2_, ...), custom_call_target="tpu_custom_call" | custom-call | tf_op jit(solution)/shard_map/pallas_call | solution.py:171
  143.9 7.0 %collective-permute-done.25 = bf16[256,1000]{1,0:T(8,128)(2,1)S(1)} collective-permute-done((bf16[256,1000]{1,0:T(8,128)(2,1)}, bf16[256,1000]{1,0:T(8,128)(2,1)S(1)}, u32[]{:S(2)}, u32[]{:S(2)}) %collective-permute-start.25) | collective-permute-done | bytes 512032 | tf_op jit(solution)/shard_map/ppermute | solution.py:39
  153.1 18.8 %shard_map.56 = (f32[256,1000]{1,0:T(8,128)}, bf16[256,1000]{1,0:T(8,128)(2,1)S(1)}) custom-call(bf16[512,8064]{1,0:T(8,128)(2,1)} %all-gather.2.cloned.1.call-done.refs_0_, s32[3]{0:T(128)S(1)} %pad_add_fusion.1.refs_22_.refs_1_, bf16[1000,7950]{1,0:T(8,128)(2,1)} %refs_3_.1, bf16[1000,7950]{1,0:T(8,128)(2,1)} %refs_3_.1, bf16[1000,256]{1,0:T(8,128)(2,1)S(1)} %copy-done, ...), custom_call_target="tpu_custom_call" | custom-call | tf_op jit(solution)/shard_map/pallas_call | solution.py:171
  172.6 3.3 %collective-permute-start.27 = (bf16[2,32,1000]{2,1,0:T(8,128)(2,1)}, bf16[2,32,1000]{2,1,0:T(8,128)(2,1)S(1)}, u32[]{:S(2)}, u32[]{:S(2)}) collective-permute-start(bf16[2,32,1000]{2,1,0:T(8,128)(2,1)} %get-tuple-element.75), channel_id=1, source_target_pairs={{0,96},{1,97},{2,98},{3,99},{4,100},{5,101},{6,102},{7,103},{8,104... | collective-permute-start | bytes 384008 | tf_op jit(solution)/shard_map/ppermute | solution.py:39
  182.0 3.6 %collective-permute-start.31 = (bf16[2,32,1000]{2,1,0:T(8,128)(2,1)S(1)}, bf16[2,32,1000]{2,1,0:T(8,128)(2,1)S(1)}, u32[]{:S(2)}, u32[]{:S(2)}) collective-permute-start(bf16[2,32,1000]{2,1,0:T(8,128)(2,1)S(1)} %get-tuple-element.96), channel_id=1, source_target_pairs={{0,96},{1,97},{2,98},{3,99},{4,100},{5,101},{6,102},{7,103},{8,104... | collective-permute-start | bytes 384008 | tf_op jit(solution)/shard_map/ppermute | solution.py:39
  186.4 4.2 %collective-permute-done.31 = bf16[2,32,1000]{2,1,0:T(8,128)(2,1)S(1)} collective-permute-done((bf16[2,32,1000]{2,1,0:T(8,128)(2,1)S(1)}, bf16[2,32,1000]{2,1,0:T(8,128)(2,1)S(1)}, u32[]{:S(2)}, u32[]{:S(2)}) %collective-permute-start.31) | collective-permute-done | bytes 128032 | tf_op jit(solution)/shard_map/ppermute | solution.py:39
  192.2 4.7 %shard_map.57 = bf16[4,128,975]{2,1,0:T(8,128)(2,1)S(1)} custom-call(bf16[128,1000]{1,0:T(8,128)(2,1)S(1)} %bitcast.97, bf16[975,1000]{1,0:T(8,128)(2,1)} %f0, bf16[975,1000]{1,0:T(8,128)(2,1)} %collective-permute-done.8.f1, bf16[975,1000]{1,0:T(8,128)(2,1)} %collective-permute-done.9.f2, bf16[975,1000]{1,0:T(8,128)(2,1)} %collective-permute-done.22.f3), custom_call_target="tpu_custom_call" | custom-call | tf_op jit(solution)/shard_map/pallas_call | solution.py:201
  197.8 2.5 %collective-permute-start.33 = (bf16[4,32,975]{2,1,0:T(8,128)(2,1)}, bf16[4,32,975]{2,1,0:T(8,128)(2,1)}, u32[]{:S(2)}, u32[]{:S(2)}) collective-permute-start(bf16[4,32,975]{2,1,0:T(8,128)(2,1)} %get-tuple-element.88), channel_id=1, source_target_pairs={{0,4},{1,5},{2,6},{3,7},{4,8},{5,9},{6,10},{7,11},{8,12},{9,13},{1... | collective-permute-start | bytes 748808 | tf_op jit(solution)/shard_map/ppermute | solution.py:39
  203.1 4.7 %shard_map.58 = bf16[4,128,975]{2,1,0:T(8,128)(2,1)S(1)} custom-call(bf16[128,1000]{1,0:T(8,128)(2,1)S(1)} %bitcast.98, bf16[975,1000]{1,0:T(8,128)(2,1)} %copy-done.3, bf16[975,1000]{1,0:T(8,128)(2,1)} %collective-permute-done.24.f1, bf16[975,1000]{1,0:T(8,128)(2,1)} %copy-done.4, bf16[975,1000]{1,0:T(8,128)(2,1)} %collective-permute-done.37.f3), custom_call_target="tpu_custom_call" | custom-call | tf_op jit(solution)/shard_map/pallas_call | solution.py:201
  214.9 5.4 %collective-permute-done.39 = bf16[4,32,975]{2,1,0:T(8,128)(2,1)S(1)} collective-permute-done((bf16[4,32,975]{2,1,0:T(8,128)(2,1)S(1)}, bf16[4,32,975]{2,1,0:T(8,128)(2,1)S(1)}, u32[]{:S(2)}, u32[]{:S(2)}) %collective-permute-start.39) | collective-permute-done | bytes 249632 | tf_op jit(solution)/shard_map/ppermute | solution.py:39
  221.0 3.0 %collective-permute-start.42 = (bf16[8,8,975]{2,1,0:T(8,128)(2,1)S(1)}, bf16[8,8,975]{2,1,0:T(8,128)(2,1)S(1)}, u32[]{:S(2)}, u32[]{:S(2)}) collective-permute-start(bf16[8,8,975]{2,1,0:T(8,128)(2,1)S(1)} %get-tuple-element.86), channel_id=1, source_target_pairs={{0,3},{1,0},{2,1},{3,2},{4,7},{5,4},{6,5},{7,6},{8,11},{9,8},{10,9... | collective-permute-start | bytes 374408 | tf_op jit(solution)/shard_map/ppermute | solution.py:39
  226.9 3.6 %collective-permute-done.43 = bf16[8,8,975]{2,1,0:T(8,128)(2,1)S(1)} collective-permute-done((bf16[8,8,975]{2,1,0:T(8,128)(2,1)S(1)}, bf16[8,8,975]{2,1,0:T(8,128)(2,1)S(1)}, u32[]{:S(2)}, u32[]{:S(2)}) %collective-permute-start.43) | collective-permute-done | bytes 124832 | tf_op jit(solution)/shard_map/ppermute | solution.py:39
  (165 shorter events, 69.5 us)
Async XLA Ops:
  6.5 146.6 %all-gather.2.cloned.1.call-start = ((), (), s32[]{:S(2)}) async-start(), calls=%async_computation.1 | async-start | bytes 8773632 | tf_op jit(solution)/shard_map/all_gather | solution.py:261
  11.5 13.2 %all-to-all-start = ((f32[8,72,128]{2,1,0:T(8,128)}), f32[8,72,128]{2,1,0:T(8,128)S(1)}, u32[]{:S(2)}, u32[]{:S(2)}) async-start(f32[8,72,128]{2,1,0:T(8,128)} %broadcast_in_dim.85), calls=%async_computation | async-start | bytes 589824 | tf_op jit(solution)/shard_map/all_to_all | solution.py:277
  16.8 11.3 %collective-permute-start = (bf16[32,4096]{1,0:T(8,128)(2,1)S(1)}, bf16[32,4096]{1,0:T(8,128)(2,1)S(1)}, u32[]{:S(2)}, u32[]{:S(2)}) collective-permute-start(bf16[32,4096]{1,0:T(8,128)(2,1)S(1)} %slice.70.refs_0_), channel_id=1, source_target_pairs={{0,1},{1,2},{2,3},{3,0},{4,5},{5,6},{6,7},{7,4},{8,9},{9,10},{10,1... | collective-permute-start | bytes 786440 | tf_op jit(solution)/shard_map/ppermute | solution.py:39
  18.4 11.4 %collective-permute-start.1 = (bf16[32,4096]{1,0:T(8,128)(2,1)S(1)}, bf16[32,4096]{1,0:T(8,128)(2,1)S(1)}, u32[]{:S(2)}, u32[]{:S(2)}) collective-permute-start(bf16[32,4096]{1,0:T(8,128)(2,1)S(1)} %slice.70.refs_0_), channel_id=1, source_target_pairs={{0,3},{1,0},{2,1},{3,2},{4,7},{5,4},{6,5},{7,6},{8,11},{9,8},{10,9... | collective-permute-start | bytes 786440 | tf_op jit(solution)/shard_map/ppermute | solution.py:39
  20.1 14.3 %collective-permute-start.2 = (bf16[32,4096]{1,0:T(8,128)(2,1)S(1)}, bf16[32,4096]{1,0:T(8,128)(2,1)S(1)}, u32[]{:S(2)}, u32[]{:S(2)}) collective-permute-start(bf16[32,4096]{1,0:T(8,128)(2,1)S(1)} %slice.70.refs_0_), channel_id=1, source_target_pairs={{0,4},{1,5},{2,6},{3,7},{4,8},{5,9},{6,10},{7,11},{8,12},{9,13},{1... | collective-permute-start | bytes 786440 | tf_op jit(solution)/shard_map/ppermute | solution.py:39
  20.3 27.7 %collective-permute-start.8 = (bf16[975,1000]{1,0:T(8,128)(2,1)}, bf16[975,1000]{1,0:T(8,128)(2,1)}, u32[]{:S(2)}, u32[]{:S(2)}) collective-permute-start(bf16[975,1000]{1,0:T(8,128)(2,1)} %f0), channel_id=1, source_target_pairs={{0,32},{1,33},{2,34},{3,35},{4,36},{5,37},{6,38},{7,39},{8,40},{9,... | collective-permute-start | bytes 5850008 | tf_op jit(solution)/shard_map/ppermute | solution.py:39
  24.8 15.6 %collective-permute-start.3 = (bf16[32,4096]{1,0:T(8,128)(2,1)S(1)}, bf16[32,4096]{1,0:T(8,128)(2,1)S(1)}, u32[]{:S(2)}, u32[]{:S(2)}) collective-permute-start(bf16[32,4096]{1,0:T(8,128)(2,1)S(1)} %pad_add_fusion.refs_1_), channel_id=1, source_target_pairs={{0,12},{1,13},{2,14},{3,15},{4,0},{5,1},{6,2},{7,3},{8,4},{9,5},{1... | collective-permute-start | bytes 786440 | tf_op jit(solution)/shard_map/ppermute | solution.py:39
  28.1 14.1 %collective-permute-start.4 = (bf16[32,4096]{1,0:T(8,128)(2,1)S(1)}, bf16[32,4096]{1,0:T(8,128)(2,1)S(1)}, u32[]{:S(2)}, u32[]{:S(2)}) collective-permute-start(bf16[32,4096]{1,0:T(8,128)(2,1)S(1)} %pad_add_fusion.refs_1_), channel_id=1, source_target_pairs={{0,4},{1,5},{2,6},{3,7},{4,8},{5,9},{6,10},{7,11},{8,12},{9,13},{1... | collective-permute-start | bytes 786440 | tf_op jit(solution)/shard_map/ppermute | solution.py:39
  29.8 12.4 %collective-permute-start.5 = (bf16[32,4096]{1,0:T(8,128)(2,1)S(1)}, bf16[32,4096]{1,0:T(8,128)(2,1)S(1)}, u32[]{:S(2)}, u32[]{:S(2)}) collective-permute-start(bf16[32,4096]{1,0:T(8,128)(2,1)S(1)} %pad_add_fusion.refs_1_), channel_id=1, source_target_pairs={{0,3},{1,0},{2,1},{3,2},{4,7},{5,4},{6,5},{7,6},{8,11},{9,8},{10,9... | collective-permute-start | bytes 786440 | tf_op jit(solution)/shard_map/ppermute | solution.py:39
  48.0 40.4 %collective-permute-start.9 = (bf16[975,1000]{1,0:T(8,128)(2,1)}, bf16[975,1000]{1,0:T(8,128)(2,1)}, u32[]{:S(2)}, u32[]{:S(2)}) collective-permute-start(bf16[975,1000]{1,0:T(8,128)(2,1)} %collective-permute-done.8.f1), channel_id=1, source_target_pairs={{0,32},{1,33},{2,34},{3,35},{4,36},{5,37},{6,38},{7,39},{8,40},{9,... | collective-permute-start | bytes 5850008 | tf_op jit(solution)/shard_map/ppermute | solution.py:39
  48.9 35.7 %collective-permute-start.10 = (bf16[96,4096]{1,0:T(8,128)(2,1)S(1)}, bf16[96,4096]{1,0:T(8,128)(2,1)S(1)}, u32[]{:S(2)}, u32[]{:S(2)}) collective-permute-start(bf16[96,4096]{1,0:T(8,128)(2,1)S(1)} %get-tuple-element.48), channel_id=1, source_target_pairs={{0,4},{1,5},{2,6},{3,7},{4,8},{5,9},{6,10},{7,11},{8,12},{9,13},{1... | collective-permute-start | bytes 2359304 | tf_op jit(solution)/shard_map/ppermute | solution.py:39
  49.3 38.1 %collective-permute-start.11 = (bf16[96,4096]{1,0:T(8,128)(2,1)S(1)}, bf16[96,4096]{1,0:T(8,128)(2,1)S(1)}, u32[]{:S(2)}, u32[]{:S(2)}) collective-permute-start(bf16[96,4096]{1,0:T(8,128)(2,1)S(1)} %get-tuple-element.49), channel_id=1, source_target_pairs={{0,12},{1,13},{2,14},{3,15},{4,0},{5,1},{6,2},{7,3},{8,4},{9,5},{1... | collective-permute-start | bytes 2359304 | tf_op jit(solution)/shard_map/ppermute | solution.py:39
  51.0 37.4 %collective-permute-start.12 = (bf16[96,4096]{1,0:T(8,128)(2,1)S(1)}, bf16[96,4096]{1,0:T(8,128)(2,1)S(1)}, u32[]{:S(2)}, u32[]{:S(2)}) collective-permute-start(bf16[96,4096]{1,0:T(8,128)(2,1)S(1)} %get-tuple-element.50), channel_id=1, source_target_pairs={{0,1},{1,2},{2,3},{3,0},{4,5},{5,6},{6,7},{7,4},{8,9},{9,10},{10,1... | collective-permute-start | bytes 2359304 | tf_op jit(solution)/shard_map/ppermute | solution.py:39
  51.7 36.7 %collective-permute-start.13 = (bf16[96,4096]{1,0:T(8,128)(2,1)S(1)}, bf16[96,4096]{1,0:T(8,128)(2,1)S(1)}, u32[]{:S(2)}, u32[]{:S(2)}) collective-permute-start(bf16[96,4096]{1,0:T(8,128)(2,1)S(1)} %get-tuple-element.51), channel_id=1, source_target_pairs={{0,3},{1,0},{2,1},{3,2},{4,7},{5,4},{6,5},{7,6},{8,11},{9,8},{10,9... | collective-permute-start | bytes 2359304 | tf_op jit(solution)/shard_map/ppermute | solution.py:39
  88.4 54.8 %collective-permute-start.22 = (bf16[975,1000]{1,0:T(8,128)(2,1)}, bf16[975,1000]{1,0:T(8,128)(2,1)}, u32[]{:S(2)}, u32[]{:S(2)}) collective-permute-start(bf16[975,1000]{1,0:T(8,128)(2,1)} %collective-permute-done.9.f2), channel_id=1, source_target_pairs={{0,32},{1,33},{2,34},{3,35},{4,36},{5,37},{6,38},{7,39},{8,40},{9,... | collective-permute-start | bytes 5850008 | tf_op jit(solution)/shard_map/ppermute | solution.py:39
  89.6 22.5 %collective-permute-start.14 = (bf16[64,4096]{1,0:T(8,128)(2,1)S(1)}, bf16[64,4096]{1,0:T(8,128)(2,1)S(1)}, u32[]{:S(2)}, u32[]{:S(2)}) collective-permute-start(bf16[64,4096]{1,0:T(8,128)(2,1)S(1)} %get-tuple-element.57), channel_id=1, source_target_pairs={{0,4},{1,5},{2,6},{3,7},{4,8},{5,9},{6,10},{7,11},{8,12},{9,13},{1... | collective-permute-start | bytes 1572872 | tf_op jit(solution)/shard_map/ppermute | solution.py:39
  91.9 21.0 %collective-permute-start.15 = (bf16[64,4096]{1,0:T(8,128)(2,1)S(1)}, bf16[64,4096]{1,0:T(8,128)(2,1)S(1)}, u32[]{:S(2)}, u32[]{:S(2)}) collective-permute-start(bf16[64,4096]{1,0:T(8,128)(2,1)S(1)} %get-tuple-element.58), channel_id=1, source_target_pairs={{0,12},{1,13},{2,14},{3,15},{4,0},{5,1},{6,2},{7,3},{8,4},{9,5},{1... | collective-permute-start | bytes 1572872 | tf_op jit(solution)/shard_map/ppermute | solution.py:39
  91.9 23.0 %collective-permute-start.16 = (bf16[64,4096]{1,0:T(8,128)(2,1)S(1)}, bf16[64,4096]{1,0:T(8,128)(2,1)S(1)}, u32[]{:S(2)}, u32[]{:S(2)}) collective-permute-start(bf16[64,4096]{1,0:T(8,128)(2,1)S(1)} %get-tuple-element.59), channel_id=1, source_target_pairs={{0,1},{1,2},{2,3},{3,0},{4,5},{5,6},{6,7},{7,4},{8,9},{9,10},{10,1... | collective-permute-start | bytes 1572872 | tf_op jit(solution)/shard_map/ppermute | solution.py:39
  92.4 23.2 %collective-permute-start.17 = (bf16[64,4096]{1,0:T(8,128)(2,1)S(1)}, bf16[64,4096]{1,0:T(8,128)(2,1)S(1)}, u32[]{:S(2)}, u32[]{:S(2)}) collective-permute-start(bf16[64,4096]{1,0:T(8,128)(2,1)S(1)} %get-tuple-element.60), channel_id=1, source_target_pairs={{0,3},{1,0},{2,1},{3,2},{4,7},{5,4},{6,5},{7,6},{8,11},{9,8},{10,9... | collective-permute-start | bytes 1572872 | tf_op jit(solution)/shard_map/ppermute | solution.py:39
  172.1 29.7 %collective-permute-start.36 = (bf16[975,1000]{1,0:T(8,128)(2,1)}, bf16[975,1000]{1,0:T(8,128)(2,1)S(1)}, u32[]{:S(2)}, u32[]{:S(2)}) collective-permute-start(bf16[975,1000]{1,0:T(8,128)(2,1)} %collective-permute-done.9.f2), channel_id=1, source_target_pairs={{0,16},{1,17},{2,18},{3,19},{4,20},{5,21},{6,22},{7,23},{8,24},{9,... | collective-permute-start | bytes 5850008 | tf_op jit(solution)/shard_map/ppermute | solution.py:39
  172.5 29.3 %collective-permute-start.37 = (bf16[975,1000]{1,0:T(8,128)(2,1)}, bf16[975,1000]{1,0:T(8,128)(2,1)}, u32[]{:S(2)}, u32[]{:S(2)}) collective-permute-start(bf16[975,1000]{1,0:T(8,128)(2,1)} %collective-permute-done.22.f3), channel_id=1, source_target_pairs={{0,16},{1,17},{2,18},{3,19},{4,20},{5,21},{6,22},{7,23},{8,24},{9,... | collective-permute-start | bytes 5850008 | tf_op jit(solution)/shard_map/ppermute | solution.py:39
  197.8 12.8 %collective-permute-start.33 = (bf16[4,32,975]{2,1,0:T(8,128)(2,1)}, bf16[4,32,975]{2,1,0:T(8,128)(2,1)}, u32[]{:S(2)}, u32[]{:S(2)}) collective-permute-start(bf16[4,32,975]{2,1,0:T(8,128)(2,1)} %get-tuple-element.88), channel_id=1, source_target_pairs={{0,4},{1,5},{2,6},{3,7},{4,8},{5,9},{6,10},{7,11},{8,12},{9,13},{1... | collective-permute-start | bytes 748808 | tf_op jit(solution)/shard_map/ppermute | solution.py:39
  200.3 12.3 %collective-permute-start.34 = (bf16[4,32,975]{2,1,0:T(8,128)(2,1)}, bf16[4,32,975]{2,1,0:T(8,128)(2,1)}, u32[]{:S(2)}, u32[]{:S(2)}) collective-permute-start(bf16[4,32,975]{2,1,0:T(8,128)(2,1)} %get-tuple-element.90), channel_id=1, source_target_pairs={{0,12},{1,13},{2,14},{3,15},{4,0},{5,1},{6,2},{7,3},{8,4},{9,5},{1... | collective-permute-start | bytes 748808 | tf_op jit(solution)/shard_map/ppermute | solution.py:39
  200.3 12.3 %collective-permute-start.35 = (bf16[4,32,975]{2,1,0:T(8,128)(2,1)}, bf16[4,32,975]{2,1,0:T(8,128)(2,1)}, u32[]{:S(2)}, u32[]{:S(2)}) collective-permute-start(bf16[4,32,975]{2,1,0:T(8,128)(2,1)} %get-tuple-element.89), channel_id=1, source_target_pairs={{0,8},{1,9},{2,10},{3,11},{4,12},{5,13},{6,14},{7,15},{8,0},{9,1},... | collective-permute-start | bytes 748808 | tf_op jit(solution)/shard_map/ppermute | solution.py:39
  (40 other events, 261.1 us)
Sparse Core Ops, SparseCore 0:
  9.7 102.9 all-gather.1

commit v6 on v5

--- a/solution.py
+++ b/solution.py
@@ -11,7 +11,9 @@
 AXES = ("sens", "layer")
 SIDE = 4
 ROWS = 64
-PART = 32
+PART = 16
+LATE = ROWS - PART
+LANES = 24
 HALF = 4096
 EDGE = 3840
 MEANS = 3968
@@ -94,13 +96,13 @@
 
     def copies(side):
         out = []
-        for i, (a, row, rows, ry, rx, inner, half) in enumerate(pieces):
+        for i, (a, row, rows, ry, rx, half) in enumerate(pieces):
             if half != side:
                 continue
             if index == 0:
                 y = lax.rem(position[1] + ry, SIDE)
                 x = lax.rem(position[2] + rx, SIDE)
-                to_row = pl.multiple_of((y * SIDE + x) * PART, PART) + inner
+                to_row = pl.multiple_of((y * SIDE + x) * PART, PART)
                 source = arrays[a].at[pl.ds(row, rows)]
                 width = HALF
             else:
@@ -130,31 +132,41 @@
     edge = jnp.where(lane < INSIDE, edge, 0.0).astype(jnp.bfloat16)
     val = val + nt(held[:, HALF : HALF + EDGE], rb[:, :EDGE])
     val = val + nt(held[:, HALF + EDGE : HALF + MEANS], edge)
+    high, low = rw[:, :128].astype(jnp.float32), rw[:, 128:].astype(jnp.float32)
+
+    def moved_by(means, q):
+        chosen = (lane >= q * LANES) & (lane < (q + 1) * LANES)
+        one = jnp.where(chosen, high, 0.0).astype(jnp.bfloat16)
+        two = jnp.where(chosen, low, 0.0).astype(jnp.bfloat16)
+        return nt(means, one) + nt(means, two)
+
+    n, p = val.shape
     if index == 0:
         means = held[:, HALF + MEANS :]
         tail[...] = means
+        val = val + moved_by(means, 0)
     else:
         means = tail[...]
-    val = val + nt(means, rw[...])
-    n = val.shape[0]
-    pairs = val.reshape(SIDE, 2, 2 * PART, val.shape[1])
-    first = pairs[:, 0].reshape(n // 2, val.shape[1])
-    second = pairs[:, 1].reshape(n // 2, val.shape[1])
+        shift = [moved_by(means, q).reshape(16, 1, PART, p) for q in range(1, ROWS // PART)]
+        val = val.reshape(16, LATE // PART, PART, p) + jnp.concatenate(shift, axis=1)
+    pairs = val.reshape(SIDE, 2, n // 8, p)
+    first = pairs[:, 0].reshape(n // 2, p)
+    second = pairs[:, 1].reshape(n // 2, p)
     swapped = position[0] == 1
     own[...] = jnp.where(swapped, second, first)
     other[...] = jnp.where(swapped, first, second).astype(jnp.bfloat16)
 
 
 def reconstruct(index, arrays, pieces, position, r, rw, tail=None):
-    n = 16 * PART
+    n = 16 * (PART if index == 0 else LATE)
     p = r.shape[0]
     half = pl.BlockSpec((n // 2, PBLOCK), lambda j: (0, j))
-    whole = pl.BlockSpec((n, 128), lambda j: (0, 0))
+    whole = pl.BlockSpec((16 * PART, 128), lambda j: (0, 0))
     in_specs = [pl.BlockSpec(memory_space=pl.ANY)] * len(arrays) + [
         pl.BlockSpec(memory_space=pltpu.SMEM),
         pl.BlockSpec((PBLOCK, HALF), lambda j: (j, 0)),
         pl.BlockSpec((PBLOCK, HALF), lambda j: (j, 1)),
-        pl.BlockSpec((PBLOCK, 128), lambda j: (j, index)),
+        pl.BlockSpec((PBLOCK, 256), lambda j: (j, 0)),
     ]
     args = [*arrays, position, r, r, rw]
     out_specs = [half, half]
@@ -164,7 +176,7 @@
     ]
     if index == 0:
         out_specs.append(whole)
-        out_shape.append(jax.ShapeDtypeStruct((n, 128), jnp.bfloat16))
+        out_shape.append(jax.ShapeDtypeStruct((16 * PART, 128), jnp.bfloat16))
     else:
         in_specs.append(whole)
         args.append(tail)
@@ -215,7 +227,7 @@
 
 def picks_by_z(own, other, z):
     got = own + swap_core(other).astype(jnp.float32)
-    got = got.reshape(SIDE, 2, PART, own.shape[1])
+    got = got.reshape(SIDE, 2, -1, own.shape[1])
 
     def pick(d):
         return lax.dynamic_index_in_dim(got, (z + d) % SIDE, 0, keepdims=False)
@@ -269,17 +281,19 @@
 
     group = sensor_map * 2 + (lax.iota(jnp.int32, width) + s_idx * width) % 2
     lane = lax.iota(jnp.int32, 128)
-    label = jnp.where(lane % 64 < 36, lane % 64 % 12, -1)
+    label = jnp.where(lane < LANES * (ROWS // PART), lane % 12, -1)
     member = ((group[None, :] == label[:, None]) & (valid[None, :] == 1)).astype(jnp.bfloat16)
     counted = jnp.concatenate([masked, jnp.ones((8, width), jnp.bfloat16)], axis=0)
     stats = nt(counted, member)
     stats = jnp.broadcast_to(stats[None], (8, *stats.shape))
     stats = jnp.sum(lax.all_to_all(stats, "sens", 0, 0, tiled=True), axis=0)
     means = stats[:ROWS] / jnp.maximum(stats[ROWS : ROWS + 1], 1.0)
-    means = jnp.where((lane < 64)[None, :], means[:PART], means[PART:])
     high = lax.reduce_precision(means, 8, 7)
-    low = (lane % 64 >= 12) & (lane % 64 < 24)
-    means = jnp.where(low[None, :], means - high, high).astype(jnp.bfloat16)
+    means = jnp.where((lane % LANES < 12)[None, :], high, means - high)
+    means = sum(
+        jnp.where((lane // LANES == q)[None, :], means[q * PART : (q + 1) * PART], 0.0)
+        for q in range(ROWS // PART)
+    ).astype(jnp.bfloat16)
     own_b = jnp.pad(masked[:PART, HALF:], ((0, 0), (0, 2 * HALF - width)))
     own_b = own_b + jnp.pad(means, ((0, 0), (MEANS, 0)))
     b_l, b_r = right(own_b), left(own_b)
@@ -289,22 +303,13 @@
     send_d = together(a_l, a_r, b_u)
     send_r = together(b_d, b_u, a_l)
     send_l = together(b_d, b_u, b_r)
-    member, send_u, send_d, send_r, send_l, a_u, b_l, fits[1] = after(
-        member, send_u, send_d, send_r, send_l, a_u, b_l, fits[1]
-    )
-    fits.append(ring_z(fits[-1]))
+    member, send_u, send_d, send_r, send_l, a_u, b_l = after(
+        member, send_u, send_d, send_r, send_l, a_u, b_l
+    )
     one_d, one_u = up(send_u), down(send_d)
     one_l, one_r = right(send_r), left(send_l)
-    rw = -nt(reconstructor, member)
-    rw_high = lax.reduce_precision(rw, 8, 7)
-    last = (lane % 64 >= 24) & (lane % 64 < 36)
-    rw = jnp.where(last[None, :], rw - rw_high, rw_high)
-    early = (lane < 64)[None, :]
-    rw = jnp.concatenate([jnp.where(early, rw, 0.0), jnp.where(early, 0.0, rw)], axis=1)
-    rw = rw.astype(jnp.bfloat16)
-
-    fits[2], one_d, one_u, one_l, one_r, rw = after(fits[2], one_d, one_u, one_l, one_r, rw)
-    fits.append(ring_z(fits[-1]))
+
+    member, one_d, one_u, one_l, one_r = after(member, one_d, one_u, one_l, one_r)
     far_x_a, far_y_b = one_l[2 * PART :], one_u[2 * PART :]
     two_d = together(far_x_a, one_d[:PART])
     two_u = together(far_x_a, one_u[PART : 2 * PART])
@@ -313,18 +318,21 @@
     two_d, two_u, two_l, two_r = after(two_d, two_u, two_l, two_r)
     get_d, get_u = up(two_d), down(two_u)
     get_l, get_r = right(two_l), left(two_r)
-
-    half = PART // 2
-    ends = after(get_d[:half], get_u[half:PART], get_l[:half], get_r[half:PART])
-    end_d, end_u = up(ends[0]), down(ends[1])
-    end_l, end_r = right(ends[2]), left(ends[3])
+    rw = -nt(reconstructor, member)
+    rw_high = lax.reduce_precision(rw, 8, 7)
+    rw_low = jnp.where((lane % LANES < 12)[None, :], rw - rw_high, 0.0)
+    rw = jnp.concatenate([rw_high, rw_low], axis=1).astype(jnp.bfloat16)
+
+    fits[1], rw, *ends = after(fits[1], rw, get_d[:PART], get_l[:PART])
+    fits.append(ring_z(fits[-1]))
+    end_d, end_l = up(ends[0]), right(ends[1])
 
     arrays = [own_a, own_b, a_l, b_l, a_r, b_r, a_d, b_d, a_u, b_u, one_d, one_u, one_l, one_r]
-    arrays += [get_d, get_u, get_l, get_r, end_d, end_u, end_l, end_r]
-
-    def piece(array, block, rows, ry, rx, inner, side):
+    arrays += [get_d, get_u, get_l, get_r, end_d, end_l]
+
+    def piece(array, block, ry, rx, side):
         index = [i for i, a in enumerate(arrays) if a is array][0]
-        return (index, block * rows, rows, ry, rx, inner, side)
+        return (index, block * PART, PART, ry, rx, side)
 
     pieces = []
     for ry, rx, (array_a, block_a), (array_b, block_b) in (
@@ -343,22 +351,21 @@
         (1, 2, (get_u, 0), (get_r, 1)),
         (2, 3, (get_d, 1), (get_l, 0)),
         (2, 1, (get_u, 1), (get_r, 0)),
+        (2, 2, (end_d, 0), (end_l, 0)),
     ):
-        pieces.append(piece(array_a, block_a, PART, ry, rx, 0, 0))
-        pieces.append(piece(array_b, block_b, PART, ry, rx, 0, 1))
-    pieces.append(piece(end_d, 0, half, 2, 2, 0, 0))
-    pieces.append(piece(end_u, 0, half, 2, 2, half, 0))
-    pieces.append(piece(end_l, 0, half, 2, 2, 0, 1))
-    pieces.append(piece(end_r, 0, half, 2, 2, half, 1))
+        pieces.append(piece(array_a, block_a, ry, rx, 0))
+        pieces.append(piece(array_b, block_b, ry, rx, 1))
     own, other, tail = reconstruct(0, arrays, pieces, position, reconstructor, rw)
     own, other, *fits = after(own, other, *fits)
-    picked = picks_by_z(own, other, z)
-    swapped = [swap_core(f) for f in fits]
-    swapped[0], swapped[1], *picked, late = after(swapped[0], swapped[1], *picked, late)
-    near = sums_by_z(picked)
+    fits.append(ring_z(fits[-1]))
+    swapped = [swap_core(fits[0]), swap_core(fits[1])]
+    near = sums_by_z(picks_by_z(own, other, z))
+    near, fits[2], fits[3], *swapped = after(near, fits[2], fits[3], *swapped)
+    swapped += [swap_core(fits[2]), swap_core(fits[3])]
+    near, late, *swapped = after(near, late, *swapped)
 
     own, other = reconstruct(
-        1, [late], [(0, 0, 16 * PART, 0, 0, 0, side) for side in (0, 1)],
+        1, [late], [(0, 0, 16 * LATE, 0, 0, side) for side in (0, 1)],
         position, reconstructor, rw, tail,
     )
     far = sums_by_z(picks_by_z(own, other, z))

time: 240 us -> 236 us (0.983)
  waiting for transfers between devices: 92.9 us -> 105 us
  starting transfers between devices: 56.7 us -> 46.6 us
  local copies, waits for them, and re-layouts: 11.3 us -> 5.15 us
    ppermute x44 -> x42, starting transfers between devices: 51.4 us -> 41.2 us  [send(): return lax.ppermute(x, AXES, moved(fn))]
    ppermute x44 -> x42, waiting for transfers between devices: 90.6 us -> 96.9 us  [send(): return lax.ppermute(x, AXES, moved(fn))]
    all_to_all x1, waiting for transfers between devices: 2.29 us -> 7.83 us  [per_device(): stats = jnp.sum(lax.all_to_all(stats, 'sens', 0, 0, tiled=True), axis=0)]
    slice x4 -> x2, local copies, waits for them, and re-layouts: 2.77 us -> 0.02 us  [per_device(): fits[1], rw, *ends = after(fits[1], rw, get_d[:PART], get_l[:PART])]
    unnamed x36 -> x22, local copies, waits for them, and re-layouts: 3.26 us -> 0.74 us
  transfers between devices with their start and end apart: 46 -> 44, of which waited for: 25 -> 24; matrix products, arithmetic and copies ran while one was open for 9% -> 6% of each run, Pallas kernels for 11% -> 7%
where the time goes in v6:
time: 236 us; the launch traced here: 235 us
  waiting for transfers between devices  105 us (44%)
  starting transfers between devices  46.6 us (20%)
  Pallas kernels  46.6 us (20%)
  between operations  13.9 us (6%)
  matrix products  9.37 us (4%)
  other arithmetic  8.98 us (4%)
  local copies, waits for them, and re-layouts  5.15 us (2%)
    ppermute x42, waiting for transfers between devices, send(): return lax.ppermute(x, AXES, moved(fn))  96.9 us
    ppermute x42, starting transfers between devices, send(): return lax.ppermute(x, AXES, moved(fn))  41.2 us
    pallas_call x2, Pallas kernels, reconstruct(): pl.pallas_call(functools.partial(reconstruct_kernel, tuple(pieces), len(a...  37.2 us
    pallas_call x2, Pallas kernels, fit(): pl.pallas_call(fit_kernel, in_specs=[pl.BlockSpec(memory_space=pltpu.VMEM...  9.39 us
    dot_general x2, matrix products, nt(): lax.dot_general(a, b, (((1,), (1,)), ((), ())), preferred_element_type=jn...  9.37 us
    all_to_all x1, waiting for transfers between devices, per_device(): stats = jnp.sum(lax.all_to_all(stats, 'sens', 0, 0, tiled=True), axis=0)  7.83 us
    all_to_all x1, starting transfers between devices, per_device(): stats = jnp.sum(lax.all_to_all(stats, 'sens', 0, 0, tiled=True), axis=0)  5.4 us
  transfers between devices with their start and end apart: 44, of which 24 were waited for; matrix products, arithmetic and copies ran while one was open for 6% of the time, Pallas kernels for 7%

profile of v6, /device:TPU:24, one launch (start us, length us, event | category | flops | bytes accessed | tf_op | source)
XLA Modules:
  0.0 235.3 jit_solution(17433264268669380288)
XLA Ops:
  15.1 5.4 %all-to-all-start = ((f32[8,72,128]{2,1,0:T(8,128)}), f32[8,72,128]{2,1,0:T(8,128)S(1)}, u32[]{:S(2)}, u32[]{:S(2)}) async-start(f32[8,72,128]{2,1,0:T(8,128)} %broadcast_in_dim.91), calls=%async_computation | async-start | bytes 589824 | tf_op jit(solution)/shard_map/all_to_all | solution.py:289
  20.5 7.8 %all-to-all-done = f32[8,72,128]{2,1,0:T(8,128)S(1)} async-done(((f32[8,72,128]{2,1,0:T(8,128)}), f32[8,72,128]{2,1,0:T(8,128)S(1)}, u32[]{:S(2)}, u32[]{:S(2)}) %all-to-all-start) | async-done | bytes 294944 | tf_op jit(solution)/shard_map/all_to_all | solution.py:289
  35.1 3.7 %collective-permute-done.3.refs_9_ = bf16[16,4096]{1,0:T(8,128)(2,1)S(1)} collective-permute-done((bf16[16,4096]{1,0:T(8,128)(2,1)S(1)}, bf16[16,4096]{1,0:T(8,128)(2,1)S(1)}, u32[]{:S(2)}, u32[]{:S(2)}) %collective-permute-start.3) | collective-permute-done | bytes 131104 | tf_op jit(solution)/shard_map/ppermute | solution.py:41
  40.1 3.3 %collective-permute-done.6.refs_8_ = bf16[16,4096]{1,0:T(8,128)(2,1)S(1)} collective-permute-done((bf16[16,4096]{1,0:T(8,128)(2,1)S(1)}, bf16[16,4096]{1,0:T(8,128)(2,1)S(1)}, u32[]{:S(2)}, u32[]{:S(2)}) %collective-permute-start.6) | collective-permute-done | bytes 131104 | tf_op jit(solution)/shard_map/ppermute | solution.py:41
  49.8 4.7 %collective-permute-done.10.refs_12_ = bf16[48,4096]{1,0:T(8,128)(2,1)S(1)} collective-permute-done((bf16[48,4096]{1,0:T(8,128)(2,1)S(1)}, bf16[48,4096]{1,0:T(8,128)(2,1)S(1)}, u32[]{:S(2)}, u32[]{:S(2)}) %collective-permute-start.10) | collective-permute-done | bytes 393248 | tf_op jit(solution)/shard_map/ppermute | solution.py:41
  55.6 4.2 %collective-permute-done.8.refs_10_ = bf16[48,4096]{1,0:T(8,128)(2,1)S(1)} collective-permute-done((bf16[48,4096]{1,0:T(8,128)(2,1)S(1)}, bf16[48,4096]{1,0:T(8,128)(2,1)S(1)}, u32[]{:S(2)}, u32[]{:S(2)}) %collective-permute-start.8) | collective-permute-done | bytes 393248 | tf_op jit(solution)/shard_map/ppermute | solution.py:41
  59.9 4.6 %collective-permute-done.9.refs_11_ = bf16[48,4096]{1,0:T(8,128)(2,1)S(1)} collective-permute-done((bf16[48,4096]{1,0:T(8,128)(2,1)S(1)}, bf16[48,4096]{1,0:T(8,128)(2,1)S(1)}, u32[]{:S(2)}, u32[]{:S(2)}) %collective-permute-start.9) | collective-permute-done | bytes 393248 | tf_op jit(solution)/shard_map/ppermute | solution.py:41
  66.0 8.3 %reduce-precision_convert_fusion = (bf16[1000,128]{1,0:T(8,128)(2,1)S(1)}, bf16[1000,128]{1,0:T(8,128)(2,1)S(1)}) fusion(pred[128]{0:T(512)(128)(4,1)S(1)} %get-tuple-element.116, bf16[128,7950]{1,0:T(8,128)(2,1)S(1)} %fusion, bf16[1000,7950]{1,0:T(8,128)(2,1)} %refs_3_.1), kind=kOutput, calls=%fused_computation.13 | convolution fusion | flops 2035968000 | bytes 18447328 | tf_op jit(solution)/shard_map/dot_general | solution.py:85
  75.2 3.3 %collective-permute-done.12.refs_14_ = bf16[32,4096]{1,0:T(8,128)(2,1)S(1)} collective-permute-done((bf16[32,4096]{1,0:T(8,128)(2,1)S(1)}, bf16[32,4096]{1,0:T(8,128)(2,1)S(1)}, u32[]{:S(2)}, u32[]{:S(2)}) %collective-permute-start.12) | collective-permute-done | bytes 262176 | tf_op jit(solution)/shard_map/ppermute | solution.py:41
  84.9 8.4 %collective-permute-done.13.refs_15_ = bf16[32,4096]{1,0:T(8,128)(2,1)S(1)} collective-permute-done((bf16[32,4096]{1,0:T(8,128)(2,1)}, bf16[32,4096]{1,0:T(8,128)(2,1)S(1)}, u32[]{:S(2)}, u32[]{:S(2)}) %collective-permute-start.13) | collective-permute-done | bytes 262176 | tf_op jit(solution)/shard_map/ppermute | solution.py:41
  95.2 12.8 %shard_map.55 = (f32[128,1000]{1,0:T(8,128)}, bf16[128,1000]{1,0:T(8,128)(2,1)S(1)}, bf16[256,128]{1,0:T(8,128)(2,1)S(1)}) custom-call(bf16[16,4096]{1,0:T(8,128)(2,1)S(1)} %slice.70.refs_0_, bf16[16,4096]{1,0:T(8,128)(2,1)S(1)} %pad_add_fusion.refs_1_, bf16[16,4096]{1,0:T(8,128)(2,1)S(1)} %collective-permute-done.refs_2_, ...), custom_call_target="tpu_custom_call" | custom-call | tf_op jit(solution)/shard_map/pallas_call | solution.py:183
  108.8 4.2 %collective-permute-done.20 = bf16[128,1000]{1,0:T(8,128)(2,1)S(1)} collective-permute-done((bf16[128,1000]{1,0:T(8,128)(2,1)S(1)}, bf16[128,1000]{1,0:T(8,128)(2,1)S(1)}, u32[]{:S(2)}, u32[]{:S(2)}) %collective-permute-start.20) | collective-permute-done | bytes 256032 | tf_op jit(solution)/shard_map/ppermute | solution.py:41
  114.3 3.1 %collective-permute-start.22 = (bf16[2,16,1000]{2,1,0:T(8,128)(2,1)S(1)}, bf16[2,16,1000]{2,1,0:T(8,128)(2,1)S(1)}, u32[]{:S(2)}, u32[]{:S(2)}) collective-permute-start(bf16[2,16,1000]{2,1,0:T(8,128)(2,1)S(1)} %get-tuple-element.101), channel_id=1, source_target_pairs={{0,96},{1,97},{2,98},{3,99},{4,100},{5,101},{6,102},{7,103},{8,104... | collective-permute-start | bytes 192008 | tf_op jit(solution)/shard_map/ppermute | solution.py:41
  117.4 19.2 %collective-permute-done.21 = bf16[2,16,1000]{2,1,0:T(8,128)(2,1)S(1)} collective-permute-done((bf16[2,16,1000]{2,1,0:T(8,128)(2,1)S(1)}, bf16[2,16,1000]{2,1,0:T(8,128)(2,1)S(1)}, u32[]{:S(2)}, u32[]{:S(2)}) %collective-permute-start.21) | collective-permute-done | bytes 64032 | tf_op jit(solution)/shard_map/ppermute | solution.py:41
  137.2 5.1 %collective-permute-done.23 = bf16[2,16,1000]{2,1,0:T(8,128)(2,1)S(1)} collective-permute-done((bf16[2,16,1000]{2,1,0:T(8,128)(2,1)S(1)}, bf16[2,16,1000]{2,1,0:T(8,128)(2,1)S(1)}, u32[]{:S(2)}, u32[]{:S(2)}) %collective-permute-start.23) | collective-permute-done | bytes 64032 | tf_op jit(solution)/shard_map/ppermute | solution.py:41
  143.0 3.9 %collective-permute-done.27.f2 = bf16[975,1000]{1,0:T(8,128)(2,1)} collective-permute-done((bf16[975,1000]{1,0:T(8,128)(2,1)}, bf16[975,1000]{1,0:T(8,128)(2,1)}, u32[]{:S(2)}, u32[]{:S(2)}) %collective-permute-start.27) | collective-permute-done | bytes 1950032 | tf_op jit(solution)/shard_map/ppermute | solution.py:41
  149.8 24.4 %shard_map.56 = (f32[384,1000]{1,0:T(8,128)}, bf16[384,1000]{1,0:T(8,128)(2,1)S(1)}) custom-call(bf16[768,8064]{1,0:T(8,128)(2,1)} %all-gather.2.cloned.1.call-done.refs_0_, s32[3]{0:T(128)S(1)} %pad_add_fusion.1.refs_20_.refs_1_, bf16[1000,7950]{1,0:T(8,128)(2,1)} %refs_3_.1, bf16[1000,7950]{1,0:T(8,128)(2,1)} %refs_3_.1, bf16[1000,256]{1,0:T(8,128)(2,1)S(1)} %copy-done, ...), custom_call_target="tpu_custom_call" | custom-call | tf_op jit(solution)/shard_map/pallas_call | solution.py:183
  178.9 3.2 %collective-permute-start.31 = (bf16[2,48,1000]{2,1,0:T(8,128)(2,1)S(1)}, bf16[2,48,1000]{2,1,0:T(8,128)(2,1)S(1)}, u32[]{:S(2)}, u32[]{:S(2)}) collective-permute-start(bf16[2,48,1000]{2,1,0:T(8,128)(2,1)S(1)} %get-tuple-element.89), channel_id=1, source_target_pairs={{0,96},{1,97},{2,98},{3,99},{4,100},{5,101},{6,102},{7,103},{8,104... | collective-permute-start | bytes 576008 | tf_op jit(solution)/shard_map/ppermute | solution.py:41
  182.2 9.1 %collective-permute-done.30 = bf16[2,48,1000]{2,1,0:T(8,128)(2,1)S(1)} collective-permute-done((bf16[2,48,1000]{2,1,0:T(8,128)(2,1)S(1)}, bf16[2,48,1000]{2,1,0:T(8,128)(2,1)S(1)}, u32[]{:S(2)}, u32[]{:S(2)}) %collective-permute-start.30) | collective-permute-done | bytes 192032 | tf_op jit(solution)/shard_map/ppermute | solution.py:41
  191.5 4.7 %shard_map.57 = bf16[4,128,975]{2,1,0:T(8,128)(2,1)S(1)} custom-call(bf16[128,1000]{1,0:T(8,128)(2,1)S(1)} %bitcast.101, bf16[975,1000]{1,0:T(8,128)(2,1)} %f0, bf16[975,1000]{1,0:T(8,128)(2,1)} %collective-permute-done.16.f1, bf16[975,1000]{1,0:T(8,128)(2,1)} %collective-permute-done.19.f2, bf16[975,1000]{1,0:T(8,128)(2,1)} %collective-permute-done.24.f3), custom_call_target="tpu_custom_call" | custom-call | tf_op jit(solution)/shard_map/pallas_call | solution.py:213
  198.8 4.7 %shard_map.58 = bf16[4,128,975]{2,1,0:T(8,128)(2,1)S(1)} custom-call(bf16[128,1000]{1,0:T(8,128)(2,1)S(1)} %bitcast.102, bf16[975,1000]{1,0:T(8,128)(2,1)} %collective-permute-done.25.f0, bf16[975,1000]{1,0:T(8,128)(2,1)} %collective-permute-done.26.f1, bf16[975,1000]{1,0:T(8,128)(2,1)} %collective-permute-done.27.f2, ...), custom_call_target="tpu_custom_call" | custom-call | tf_op jit(solution)/shard_map/pallas_call | solution.py:213
  210.4 6.2 %collective-permute-done.37 = bf16[4,32,975]{2,1,0:T(8,128)(2,1)S(1)} collective-permute-done((bf16[4,32,975]{2,1,0:T(8,128)(2,1)S(1)}, bf16[4,32,975]{2,1,0:T(8,128)(2,1)S(1)}, u32[]{:S(2)}, u32[]{:S(2)}) %collective-permute-start.37) | collective-permute-done | bytes 249632 | tf_op jit(solution)/shard_map/ppermute | solution.py:41
  217.0 3.2 %collective-permute-start.40 = (bf16[8,8,975]{2,1,0:T(8,128)(2,1)S(1)}, bf16[8,8,975]{2,1,0:T(8,128)(2,1)S(1)}, u32[]{:S(2)}, u32[]{:S(2)}) collective-permute-start(bf16[8,8,975]{2,1,0:T(8,128)(2,1)S(1)} %get-tuple-element.91), channel_id=1, source_target_pairs={{0,3},{1,0},{2,1},{3,2},{4,7},{5,4},{6,5},{7,6},{8,11},{9,8},{10,9... | collective-permute-start | bytes 374408 | tf_op jit(solution)/shard_map/ppermute | solution.py:41
  220.3 2.9 %collective-permute-done.39 = bf16[8,8,975]{2,1,0:T(8,128)(2,1)S(1)} collective-permute-done((bf16[8,8,975]{2,1,0:T(8,128)(2,1)S(1)}, bf16[8,8,975]{2,1,0:T(8,128)(2,1)S(1)}, u32[]{:S(2)}, u32[]{:S(2)}) %collective-permute-start.39) | collective-permute-done | bytes 124832 | tf_op jit(solution)/shard_map/ppermute | solution.py:41
  (147 shorter events, 60.9 us)
Async XLA Ops:
  6.5 143.2 %all-gather.2.cloned.1.call-start = ((), (), s32[]{:S(2)}) async-start(), calls=%async_computation.1 | async-start | bytes 13160448 | tf_op jit(solution)/shard_map/all_gather | solution.py:273
  9.7 22.0 %collective-permute-start = (bf16[16,4096]{1,0:T(8,128)(2,1)S(1)}, bf16[16,4096]{1,0:T(8,128)(2,1)S(1)}, u32[]{:S(2)}, u32[]{:S(2)}) collective-permute-start(bf16[16,4096]{1,0:T(8,128)(2,1)S(1)} %slice.70.refs_0_), channel_id=1, source_target_pairs={{0,1},{1,2},{2,3},{3,0},{4,5},{5,6},{6,7},{7,4},{8,9},{9,10},{10,1... | collective-permute-start | bytes 393224 | tf_op jit(solution)/shard_map/ppermute | solution.py:41
  11.3 22.7 %collective-permute-start.1 = (bf16[16,4096]{1,0:T(8,128)(2,1)S(1)}, bf16[16,4096]{1,0:T(8,128)(2,1)S(1)}, u32[]{:S(2)}, u32[]{:S(2)}) collective-permute-start(bf16[16,4096]{1,0:T(8,128)(2,1)S(1)} %slice.70.refs_0_), channel_id=1, source_target_pairs={{0,3},{1,0},{2,1},{3,2},{4,7},{5,4},{6,5},{7,6},{8,11},{9,8},{10,9... | collective-permute-start | bytes 393224 | tf_op jit(solution)/shard_map/ppermute | solution.py:41
  13.0 21.6 %collective-permute-start.2 = (bf16[16,4096]{1,0:T(8,128)(2,1)S(1)}, bf16[16,4096]{1,0:T(8,128)(2,1)S(1)}, u32[]{:S(2)}, u32[]{:S(2)}) collective-permute-start(bf16[16,4096]{1,0:T(8,128)(2,1)S(1)} %slice.70.refs_0_), channel_id=1, source_target_pairs={{0,4},{1,5},{2,6},{3,7},{4,8},{5,9},{6,10},{7,11},{8,12},{9,13},{1... | collective-permute-start | bytes 393224 | tf_op jit(solution)/shard_map/ppermute | solution.py:41
  15.1 13.3 %all-to-all-start = ((f32[8,72,128]{2,1,0:T(8,128)}), f32[8,72,128]{2,1,0:T(8,128)S(1)}, u32[]{:S(2)}, u32[]{:S(2)}) async-start(f32[8,72,128]{2,1,0:T(8,128)} %broadcast_in_dim.91), calls=%async_computation | async-start | bytes 589824 | tf_op jit(solution)/shard_map/all_to_all | solution.py:289
  44.3 11.3 %collective-permute-start.11 = (bf16[48,4096]{1,0:T(8,128)(2,1)S(1)}, bf16[48,4096]{1,0:T(8,128)(2,1)S(1)}, u32[]{:S(2)}, u32[]{:S(2)}) collective-permute-start(bf16[48,4096]{1,0:T(8,128)(2,1)S(1)} %get-tuple-element.52), channel_id=1, source_target_pairs={{0,3},{1,0},{2,1},{3,2},{4,7},{5,4},{6,5},{7,6},{8,11},{9,8},{10,9... | collective-permute-start | bytes 1179656 | tf_op jit(solution)/shard_map/ppermute | solution.py:41
  46.7 13.2 %collective-permute-start.8 = (bf16[48,4096]{1,0:T(8,128)(2,1)S(1)}, bf16[48,4096]{1,0:T(8,128)(2,1)S(1)}, u32[]{:S(2)}, u32[]{:S(2)}) collective-permute-start(bf16[48,4096]{1,0:T(8,128)(2,1)S(1)} %get-tuple-element.49), channel_id=1, source_target_pairs={{0,4},{1,5},{2,6},{3,7},{4,8},{5,9},{6,10},{7,11},{8,12},{9,13},{1... | collective-permute-start | bytes 1179656 | tf_op jit(solution)/shard_map/ppermute | solution.py:41
  47.4 17.0 %collective-permute-start.9 = (bf16[48,4096]{1,0:T(8,128)(2,1)S(1)}, bf16[48,4096]{1,0:T(8,128)(2,1)S(1)}, u32[]{:S(2)}, u32[]{:S(2)}) collective-permute-start(bf16[48,4096]{1,0:T(8,128)(2,1)S(1)} %get-tuple-element.50), channel_id=1, source_target_pairs={{0,12},{1,13},{2,14},{3,15},{4,0},{5,1},{6,2},{7,3},{8,4},{9,5},{1... | collective-permute-start | bytes 1179656 | tf_op jit(solution)/shard_map/ppermute | solution.py:41
  48.7 30.5 %collective-permute-start.16 = (bf16[975,1000]{1,0:T(8,128)(2,1)}, bf16[975,1000]{1,0:T(8,128)(2,1)}, u32[]{:S(2)}, u32[]{:S(2)}) collective-permute-start(bf16[975,1000]{1,0:T(8,128)(2,1)} %f0), channel_id=1, source_target_pairs={{0,32},{1,33},{2,34},{3,35},{4,36},{5,37},{6,38},{7,39},{8,40},{9,... | collective-permute-start | bytes 5850008 | tf_op jit(solution)/shard_map/ppermute | solution.py:41
  66.0 12.5 %collective-permute-start.12 = (bf16[32,4096]{1,0:T(8,128)(2,1)S(1)}, bf16[32,4096]{1,0:T(8,128)(2,1)S(1)}, u32[]{:S(2)}, u32[]{:S(2)}) collective-permute-start(bf16[32,4096]{1,0:T(8,128)(2,1)S(1)} %get-tuple-element.57), channel_id=1, source_target_pairs={{0,4},{1,5},{2,6},{3,7},{4,8},{5,9},{6,10},{7,11},{8,12},{9,13},{1... | collective-permute-start | bytes 786440 | tf_op jit(solution)/shard_map/ppermute | solution.py:41
  66.0 13.2 %collective-permute-start.14 = (bf16[32,4096]{1,0:T(8,128)(2,1)S(1)}, bf16[32,4096]{1,0:T(8,128)(2,1)S(1)}, u32[]{:S(2)}, u32[]{:S(2)}) collective-permute-start(bf16[32,4096]{1,0:T(8,128)(2,1)S(1)} %get-tuple-element.59), channel_id=1, source_target_pairs={{0,1},{1,2},{2,3},{3,0},{4,5},{5,6},{6,7},{7,4},{8,9},{9,10},{10,1... | collective-permute-start | bytes 786440 | tf_op jit(solution)/shard_map/ppermute | solution.py:41
  79.2 28.8 %collective-permute-start.19 = (bf16[975,1000]{1,0:T(8,128)(2,1)}, bf16[975,1000]{1,0:T(8,128)(2,1)}, u32[]{:S(2)}, u32[]{:S(2)}) collective-permute-start(bf16[975,1000]{1,0:T(8,128)(2,1)} %collective-permute-done.16.f1), channel_id=1, source_target_pairs={{0,32},{1,33},{2,34},{3,35},{4,36},{5,37},{6,38},{7,39},{8,40},{9,... | collective-permute-start | bytes 5850008 | tf_op jit(solution)/shard_map/ppermute | solution.py:41
  79.5 13.7 %collective-permute-start.13 = (bf16[32,4096]{1,0:T(8,128)(2,1)}, bf16[32,4096]{1,0:T(8,128)(2,1)S(1)}, u32[]{:S(2)}, u32[]{:S(2)}) collective-permute-start(bf16[32,4096]{1,0:T(8,128)(2,1)} %get-tuple-element.58), channel_id=1, source_target_pairs={{0,12},{1,13},{2,14},{3,15},{4,0},{5,1},{6,2},{7,3},{8,4},{9,5},{1... | collective-permute-start | bytes 786440 | tf_op jit(solution)/shard_map/ppermute | solution.py:41
  82.3 12.2 %collective-permute-start.15 = (bf16[32,4096]{1,0:T(8,128)(2,1)}, bf16[32,4096]{1,0:T(8,128)(2,1)S(1)}, u32[]{:S(2)}, u32[]{:S(2)}) collective-permute-start(bf16[32,4096]{1,0:T(8,128)(2,1)} %get-tuple-element.60), channel_id=1, source_target_pairs={{0,3},{1,0},{2,1},{3,2},{4,7},{5,4},{6,5},{7,6},{8,11},{9,8},{10,9... | collective-permute-start | bytes 786440 | tf_op jit(solution)/shard_map/ppermute | solution.py:41
  82.3 12.2 %collective-permute-start.17 = (bf16[16,4096]{1,0:T(8,128)(2,1)S(1)}, bf16[16,4096]{1,0:T(8,128)(2,1)S(1)}, u32[]{:S(2)}, u32[]{:S(2)}) collective-permute-start(bf16[16,4096]{1,0:T(8,128)(2,1)S(1)} %slice.78), channel_id=1, source_target_pairs={{0,4},{1,5},{2,6},{3,7},{4,8},{5,9},{6,10},{7,11},{8,12},{9,13},{1... | collective-permute-start | bytes 393224 | tf_op jit(solution)/shard_map/ppermute | solution.py:41
  82.8 11.7 %collective-permute-start.18 = (bf16[16,4096]{1,0:T(8,128)(2,1)S(1)}, bf16[16,4096]{1,0:T(8,128)(2,1)S(1)}, u32[]{:S(2)}, u32[]{:S(2)}) collective-permute-start(bf16[16,4096]{1,0:T(8,128)(2,1)S(1)} %slice.79), channel_id=1, source_target_pairs={{0,1},{1,2},{2,3},{3,0},{4,5},{5,6},{6,7},{7,4},{8,9},{9,10},{10,1... | collective-permute-start | bytes 393224 | tf_op jit(solution)/shard_map/ppermute | solution.py:41
  108.0 34.4 %collective-permute-start.24 = (bf16[975,1000]{1,0:T(8,128)(2,1)}, bf16[975,1000]{1,0:T(8,128)(2,1)}, u32[]{:S(2)}, u32[]{:S(2)}) collective-permute-start(bf16[975,1000]{1,0:T(8,128)(2,1)} %collective-permute-done.19.f2), channel_id=1, source_target_pairs={{0,32},{1,33},{2,34},{3,35},{4,36},{5,37},{6,38},{7,39},{8,40},{9,... | collective-permute-start | bytes 5850008 | tf_op jit(solution)/shard_map/ppermute | solution.py:41
  108.2 34.2 %collective-permute-start.25 = (bf16[975,1000]{1,0:T(8,128)(2,1)}, bf16[975,1000]{1,0:T(8,128)(2,1)}, u32[]{:S(2)}, u32[]{:S(2)}) collective-permute-start(bf16[975,1000]{1,0:T(8,128)(2,1)} %f0), channel_id=1, source_target_pairs={{0,16},{1,17},{2,18},{3,19},{4,20},{5,21},{6,22},{7,23},{8,24},{9,... | collective-permute-start | bytes 5850008 | tf_op jit(solution)/shard_map/ppermute | solution.py:41
  108.2 34.2 %collective-permute-start.26 = (bf16[975,1000]{1,0:T(8,128)(2,1)}, bf16[975,1000]{1,0:T(8,128)(2,1)}, u32[]{:S(2)}, u32[]{:S(2)}) collective-permute-start(bf16[975,1000]{1,0:T(8,128)(2,1)} %collective-permute-done.16.f1), channel_id=1, source_target_pairs={{0,16},{1,17},{2,18},{3,19},{4,20},{5,21},{6,22},{7,23},{8,24},{9,... | collective-permute-start | bytes 5850008 | tf_op jit(solution)/shard_map/ppermute | solution.py:41
  114.1 22.5 %collective-permute-start.21 = (bf16[2,16,1000]{2,1,0:T(8,128)(2,1)S(1)}, bf16[2,16,1000]{2,1,0:T(8,128)(2,1)S(1)}, u32[]{:S(2)}, u32[]{:S(2)}) collective-permute-start(bf16[2,16,1000]{2,1,0:T(8,128)(2,1)S(1)} %get-tuple-element.99), channel_id=1, source_target_pairs={{0,32},{1,33},{2,34},{3,35},{4,36},{5,37},{6,38},{7,39},{8,40},{9,... | collective-permute-start | bytes 192008 | tf_op jit(solution)/shard_map/ppermute | solution.py:41
  114.3 23.0 %collective-permute-start.22 = (bf16[2,16,1000]{2,1,0:T(8,128)(2,1)S(1)}, bf16[2,16,1000]{2,1,0:T(8,128)(2,1)S(1)}, u32[]{:S(2)}, u32[]{:S(2)}) collective-permute-start(bf16[2,16,1000]{2,1,0:T(8,128)(2,1)S(1)} %get-tuple-element.101), channel_id=1, source_target_pairs={{0,96},{1,97},{2,98},{3,99},{4,100},{5,101},{6,102},{7,103},{8,104... | collective-permute-start | bytes 192008 | tf_op jit(solution)/shard_map/ppermute | solution.py:41
  178.9 12.4 %collective-permute-start.30 = (bf16[2,48,1000]{2,1,0:T(8,128)(2,1)S(1)}, bf16[2,48,1000]{2,1,0:T(8,128)(2,1)S(1)}, u32[]{:S(2)}, u32[]{:S(2)}) collective-permute-start(bf16[2,48,1000]{2,1,0:T(8,128)(2,1)S(1)} %get-tuple-element.87), channel_id=1, source_target_pairs={{0,32},{1,33},{2,34},{3,35},{4,36},{5,37},{6,38},{7,39},{8,40},{9,... | collective-permute-start | bytes 576008 | tf_op jit(solution)/shard_map/ppermute | solution.py:41
  178.9 12.4 %collective-permute-start.31 = (bf16[2,48,1000]{2,1,0:T(8,128)(2,1)S(1)}, bf16[2,48,1000]{2,1,0:T(8,128)(2,1)S(1)}, u32[]{:S(2)}, u32[]{:S(2)}) collective-permute-start(bf16[2,48,1000]{2,1,0:T(8,128)(2,1)S(1)} %get-tuple-element.89), channel_id=1, source_target_pairs={{0,96},{1,97},{2,98},{3,99},{4,100},{5,101},{6,102},{7,103},{8,104... | collective-permute-start | bytes 576008 | tf_op jit(solution)/shard_map/ppermute | solution.py:41
  197.1 11.7 %collective-permute-start.34 = (bf16[4,32,975]{2,1,0:T(8,128)(2,1)S(1)}, bf16[4,32,975]{2,1,0:T(8,128)(2,1)S(1)}, u32[]{:S(2)}, u32[]{:S(2)}) collective-permute-start(bf16[4,32,975]{2,1,0:T(8,128)(2,1)S(1)} %get-tuple-element.95), channel_id=1, source_target_pairs={{0,12},{1,13},{2,14},{3,15},{4,0},{5,1},{6,2},{7,3},{8,4},{9,5},{1... | collective-permute-start | bytes 748808 | tf_op jit(solution)/shard_map/ppermute | solution.py:41
  (31 other events, 280.5 us)
Sparse Core Ops, SparseCore 0:
  9.8 104.8 all-gather.1

commit v7 on v6

--- a/solution.py
+++ b/solution.py
@@ -303,13 +303,17 @@
     send_d = together(a_l, a_r, b_u)
     send_r = together(b_d, b_u, a_l)
     send_l = together(b_d, b_u, b_r)
-    member, send_u, send_d, send_r, send_l, a_u, b_l = after(
-        member, send_u, send_d, send_r, send_l, a_u, b_l
-    )
+    fits[1], send_u, send_d, send_r, send_l, a_u, b_l = after(
+        fits[1], send_u, send_d, send_r, send_l, a_u, b_l
+    )
+    fits.append(ring_z(fits[-1]))
     one_d, one_u = up(send_u), down(send_d)
     one_l, one_r = right(send_r), left(send_l)
 
-    member, one_d, one_u, one_l, one_r = after(member, one_d, one_u, one_l, one_r)
+    member, fits[2], one_d, one_u, one_l, one_r = after(
+        member, fits[2], one_d, one_u, one_l, one_r
+    )
+    fits.append(ring_z(fits[-1]))
     far_x_a, far_y_b = one_l[2 * PART :], one_u[2 * PART :]
     two_d = together(far_x_a, one_d[:PART])
     two_u = together(far_x_a, one_u[PART : 2 * PART])
@@ -323,9 +327,9 @@
     rw_low = jnp.where((lane % LANES < 12)[None, :], rw - rw_high, 0.0)
     rw = jnp.concatenate([rw_high, rw_low], axis=1).astype(jnp.bfloat16)
 
-    fits[1], rw, *ends = after(fits[1], rw, get_d[:PART], get_l[:PART])
-    fits.append(ring_z(fits[-1]))
+    rw, get_u, get_r, *ends = after(rw, get_u, get_r, get_d[:PART], get_l[:PART])
     end_d, end_l = up(ends[0]), right(ends[1])
+    end_d, end_l, *fits = after(end_d, end_l, *fits)
 
     arrays = [own_a, own_b, a_l, b_l, a_r, b_r, a_d, b_d, a_u, b_u, one_d, one_u, one_l, one_r]
     arrays += [get_d, get_u, get_l, get_r, end_d, end_l]
@@ -356,13 +360,10 @@
         pieces.append(piece(array_a, block_a, ry, rx, 0))
         pieces.append(piece(array_b, block_b, ry, rx, 1))
     own, other, tail = reconstruct(0, arrays, pieces, position, reconstructor, rw)
-    own, other, *fits = after(own, other, *fits)
-    fits.append(ring_z(fits[-1]))
-    swapped = [swap_core(fits[0]), swap_core(fits[1])]
+    swapped = [swap_core(f) for f in fits]
+    own, other, *swapped = after(own, other, *swapped)
     near = sums_by_z(picks_by_z(own, other, z))
-    near, fits[2], fits[3], *swapped = after(near, fits[2], fits[3], *swapped)
-    swapped += [swap_core(fits[2]), swap_core(fits[3])]
-    near, late, *swapped = after(near, late, *swapped)
+    near, late = after(near, late)
 
     own, other = reconstruct(
         1, [late], [(0, 0, 16 * LATE, 0, 0, side) for side in (0, 1)],

time: 236 us -> 219 us (0.928)
  waiting for transfers between devices: 105 us -> 79.2 us
  starting transfers between devices: 46.6 us -> 50.6 us
  other arithmetic: 8.98 us -> 12.2 us
    ppermute x42, waiting for transfers between devices: 96.9 us -> 74.4 us  [send(): return lax.ppermute(x, AXES, moved(fn))]
    ppermute x42, starting transfers between devices: 41.2 us -> 45.2 us  [send(): return lax.ppermute(x, AXES, moved(fn))]
    all_to_all x1, waiting for transfers between devices: 7.83 us -> 4.79 us  [per_device(): stats = jnp.sum(lax.all_to_all(stats, 'sens', 0, 0, tiled=True), axis=0)]
  transfers between devices with their start and end apart: 44 -> 44, of which waited for: 24 -> 22; matrix products, arithmetic and copies ran while one was open for 6% -> 9% of each run, Pallas kernels for 7% -> 8%
where the time goes in v7:
time: 219 us; the launch traced here: 217 us
  waiting for transfers between devices  79.2 us (36%)
  starting transfers between devices  50.6 us (23%)
  Pallas kernels  46.5 us (21%)
  between operations  14 us (6%)
  other arithmetic  12.2 us (6%)
  matrix products  9.26 us (4%)
  local copies, waits for them, and re-layouts  5.72 us (3%)
    ppermute x42, waiting for transfers between devices, send(): return lax.ppermute(x, AXES, moved(fn))  74.4 us
    ppermute x42, starting transfers between devices, send(): return lax.ppermute(x, AXES, moved(fn))  45.2 us
    pallas_call x2, Pallas kernels, reconstruct(): pl.pallas_call(functools.partial(reconstruct_kernel, tuple(pieces), len(a...  37.1 us
    pallas_call x2, Pallas kernels, fit(): pl.pallas_call(fit_kernel, in_specs=[pl.BlockSpec(memory_space=pltpu.VMEM...  9.39 us
    dot_general x2, matrix products, nt(): lax.dot_general(a, b, (((1,), (1,)), ((), ())), preferred_element_type=jn...  9.26 us
    all_to_all x1, starting transfers between devices, per_device(): stats = jnp.sum(lax.all_to_all(stats, 'sens', 0, 0, tiled=True), axis=0)  5.4 us
    all_to_all x1, waiting for transfers between devices, per_device(): stats = jnp.sum(lax.all_to_all(stats, 'sens', 0, 0, tiled=True), axis=0)  4.79 us
  transfers between devices with their start and end apart: 44, of which 22 were waited for; matrix products, arithmetic and copies ran while one was open for 9% of the time, Pallas kernels for 8%

profile of v7, /device:TPU:24, one launch (start us, length us, event | category | flops | bytes accessed | tf_op | source)
XLA Modules:
  0.0 217.4 jit_solution(10945892261738828529)
XLA Ops:
  15.7 5.4 %all-to-all-start = ((f32[8,72,128]{2,1,0:T(8,128)}), f32[8,72,128]{2,1,0:T(8,128)}, u32[]{:S(2)}, u32[]{:S(2)}) async-start(f32[8,72,128]{2,1,0:T(8,128)} %broadcast_in_dim.91), calls=%async_computation | async-start | bytes 589824 | tf_op jit(solution)/shard_map/all_to_all | solution.py:289
  24.4 4.8 %all-to-all-done = f32[8,72,128]{2,1,0:T(8,128)} async-done(((f32[8,72,128]{2,1,0:T(8,128)}), f32[8,72,128]{2,1,0:T(8,128)}, u32[]{:S(2)}, u32[]{:S(2)}) %all-to-all-start) | async-done | bytes 294944 | tf_op jit(solution)/shard_map/all_to_all | solution.py:289
  38.0 3.7 %collective-permute-done.4.refs_9_ = bf16[16,4096]{1,0:T(8,128)(2,1)S(1)} collective-permute-done((bf16[16,4096]{1,0:T(8,128)(2,1)S(1)}, bf16[16,4096]{1,0:T(8,128)(2,1)S(1)}, u32[]{:S(2)}, u32[]{:S(2)}) %collective-permute-start.4) | collective-permute-done | bytes 131104 | tf_op jit(solution)/shard_map/ppermute | solution.py:41
  44.0 3.8 %collective-permute-done.8.refs_3_ = bf16[16,4096]{1,0:T(8,128)(2,1)S(1)} collective-permute-done((bf16[16,4096]{1,0:T(8,128)(2,1)S(1)}, bf16[16,4096]{1,0:T(8,128)(2,1)S(1)}, u32[]{:S(2)}, u32[]{:S(2)}) %collective-permute-start.8) | collective-permute-done | bytes 131104 | tf_op jit(solution)/shard_map/ppermute | solution.py:41
  52.4 3.0 %collective-permute-start.13 = (bf16[48,4096]{1,0:T(8,128)(2,1)S(1)}, bf16[48,4096]{1,0:T(8,128)(2,1)S(1)}, u32[]{:S(2)}, u32[]{:S(2)}) collective-permute-start(bf16[48,4096]{1,0:T(8,128)(2,1)S(1)} %get-tuple-element.52), channel_id=1, source_target_pairs={{0,3},{1,0},{2,1},{3,2},{4,7},{5,4},{6,5},{7,6},{8,11},{9,8},{10,9... | collective-permute-start | bytes 1179656 | tf_op jit(solution)/shard_map/ppermute | solution.py:41
  56.8 12.8 %collective-permute-done.10.refs_10_ = bf16[48,4096]{1,0:T(8,128)(2,1)S(1)} collective-permute-done((bf16[48,4096]{1,0:T(8,128)(2,1)S(1)}, bf16[48,4096]{1,0:T(8,128)(2,1)S(1)}, u32[]{:S(2)}, u32[]{:S(2)}) %collective-permute-start.10) | collective-permute-done | bytes 393248 | tf_op jit(solution)/shard_map/ppermute | solution.py:41
  69.6 3.4 %collective-permute-done.11.refs_11_ = bf16[48,4096]{1,0:T(8,128)(2,1)S(1)} collective-permute-done((bf16[48,4096]{1,0:T(8,128)(2,1)S(1)}, bf16[48,4096]{1,0:T(8,128)(2,1)S(1)}, u32[]{:S(2)}, u32[]{:S(2)}) %collective-permute-start.11) | collective-permute-done | bytes 393248 | tf_op jit(solution)/shard_map/ppermute | solution.py:41
  73.1 3.4 %collective-permute-done.9.f2 = bf16[975,1000]{1,0:T(8,128)(2,1)} collective-permute-done((bf16[975,1000]{1,0:T(8,128)(2,1)S(1)}, bf16[975,1000]{1,0:T(8,128)(2,1)}, u32[]{:S(2)}, u32[]{:S(2)}) %collective-permute-start.9) | collective-permute-done | bytes 1950032 | tf_op jit(solution)/shard_map/ppermute | solution.py:41
  79.1 3.0 %collective-permute-start.16 = (bf16[32,4096]{1,0:T(8,128)(2,1)S(1)}, bf16[32,4096]{1,0:T(8,128)(2,1)S(1)}, u32[]{:S(2)}, u32[]{:S(2)}) collective-permute-start(bf16[32,4096]{1,0:T(8,128)(2,1)S(1)} %get-tuple-element.60), channel_id=1, source_target_pairs={{0,3},{1,0},{2,1},{3,2},{4,7},{5,4},{6,5},{7,6},{8,11},{9,8},{10,9... | collective-permute-start | bytes 786440 | tf_op jit(solution)/shard_map/ppermute | solution.py:41
  82.0 8.2 %reduce-precision_convert_fusion = (bf16[1000,128]{1,0:T(8,128)(2,1)S(1)}, bf16[1000,128]{1,0:T(8,128)(2,1)S(1)}) fusion(pred[128]{0:T(512)(128)(4,1)S(1)} %copy-done.15, bf16[128,7950]{1,0:T(8,128)(2,1)S(1)} %fusion, bf16[1000,7950]{1,0:T(8,128)(2,1)} %refs_3_.1), kind=kOutput, calls=%fused_computation.13 | convolution fusion | flops 2035968000 | bytes 18447328 | tf_op jit(solution)/shard_map/dot_general | solution.py:85
  91.1 2.7 %collective-permute-done.17.refs_16_ = bf16[32,4096]{1,0:T(8,128)(2,1)S(1)} collective-permute-done((bf16[32,4096]{1,0:T(8,128)(2,1)S(1)}, bf16[32,4096]{1,0:T(8,128)(2,1)S(1)}, u32[]{:S(2)}, u32[]{:S(2)}) %collective-permute-start.17) | collective-permute-done | bytes 262176 | tf_op jit(solution)/shard_map/ppermute | solution.py:41
  97.4 5.0 %collective-permute-done.18.refs_18_ = bf16[16,4096]{1,0:T(8,128)(2,1)S(1)} collective-permute-done((bf16[16,4096]{1,0:T(8,128)(2,1)S(1)}, bf16[16,4096]{1,0:T(8,128)(2,1)S(1)}, u32[]{:S(2)}, u32[]{:S(2)}) %collective-permute-start.18) | collective-permute-done | bytes 131104 | tf_op jit(solution)/shard_map/ppermute | solution.py:41
  102.4 3.9 %collective-permute-done.19.refs_19_ = bf16[16,4096]{1,0:T(8,128)(2,1)S(1)} collective-permute-done((bf16[16,4096]{1,0:T(8,128)(2,1)S(1)}, bf16[16,4096]{1,0:T(8,128)(2,1)S(1)}, u32[]{:S(2)}, u32[]{:S(2)}) %collective-permute-start.19) | collective-permute-done | bytes 131104 | tf_op jit(solution)/shard_map/ppermute | solution.py:41
  107.4 12.7 %shard_map.55 = (f32[128,1000]{1,0:T(8,128)}, bf16[128,1000]{1,0:T(8,128)(2,1)S(1)}, bf16[256,128]{1,0:T(8,128)(2,1)S(1)}) custom-call(bf16[16,4096]{1,0:T(8,128)(2,1)S(1)} %slice.70.refs_0_, bf16[16,4096]{1,0:T(8,128)(2,1)S(1)} %pad_add_fusion.refs_1_, bf16[16,4096]{1,0:T(8,128)(2,1)S(1)} %collective-permute-done.refs_2_, ...), custom_call_target="tpu_custom_call" | custom-call | tf_op jit(solution)/shard_map/pallas_call | solution.py:183
  123.1 3.2 %collective-permute-start.27 = (bf16[2,16,1000]{2,1,0:T(8,128)(2,1)S(1)}, bf16[2,16,1000]{2,1,0:T(8,128)(2,1)S(1)}, u32[]{:S(2)}, u32[]{:S(2)}) collective-permute-start(bf16[2,16,1000]{2,1,0:T(8,128)(2,1)S(1)} %get-tuple-element.101), channel_id=1, source_target_pairs={{0,96},{1,97},{2,98},{3,99},{4,100},{5,101},{6,102},{7,103},{8,104... | collective-permute-start | bytes 192008 | tf_op jit(solution)/shard_map/ppermute | solution.py:41
  128.5 3.5 %collective-permute-done.28 = bf16[2,16,1000]{2,1,0:T(8,128)(2,1)S(1)} collective-permute-done((bf16[2,16,1000]{2,1,0:T(8,128)(2,1)S(1)}, bf16[2,16,1000]{2,1,0:T(8,128)(2,1)S(1)}, u32[]{:S(2)}, u32[]{:S(2)}) %collective-permute-start.28) | collective-permute-done | bytes 64032 | tf_op jit(solution)/shard_map/ppermute | solution.py:41
  132.2 24.4 %shard_map.56 = (f32[384,1000]{1,0:T(8,128)}, bf16[384,1000]{1,0:T(8,128)(2,1)S(1)}) custom-call(bf16[768,8064]{1,0:T(8,128)(2,1)} %all-gather.2.cloned.1.call-done.refs_0_, s32[3]{0:T(128)S(1)} %pad_add_fusion.1.refs_20_.refs_1_, bf16[1000,7950]{1,0:T(8,128)(2,1)} %refs_3_.1, bf16[1000,7950]{1,0:T(8,128)(2,1)} %refs_3_.1, bf16[1000,256]{1,0:T(8,128)(2,1)S(1)} %copy-done, ...), custom_call_target="tpu_custom_call" | custom-call | tf_op jit(solution)/shard_map/pallas_call | solution.py:183
  161.4 3.2 %collective-permute-start.31 = (bf16[2,48,1000]{2,1,0:T(8,128)(2,1)S(1)}, bf16[2,48,1000]{2,1,0:T(8,128)(2,1)S(1)}, u32[]{:S(2)}, u32[]{:S(2)}) collective-permute-start(bf16[2,48,1000]{2,1,0:T(8,128)(2,1)S(1)} %get-tuple-element.89), channel_id=1, source_target_pairs={{0,96},{1,97},{2,98},{3,99},{4,100},{5,101},{6,102},{7,103},{8,104... | collective-permute-start | bytes 576008 | tf_op jit(solution)/shard_map/ppermute | solution.py:41
  164.6 9.1 %collective-permute-done.30 = bf16[2,48,1000]{2,1,0:T(8,128)(2,1)S(1)} collective-permute-done((bf16[2,48,1000]{2,1,0:T(8,128)(2,1)S(1)}, bf16[2,48,1000]{2,1,0:T(8,128)(2,1)S(1)}, u32[]{:S(2)}, u32[]{:S(2)}) %collective-permute-start.30) | collective-permute-done | bytes 192032 | tf_op jit(solution)/shard_map/ppermute | solution.py:41
  173.9 4.7 %shard_map.57 = bf16[4,128,975]{2,1,0:T(8,128)(2,1)S(1)} custom-call(bf16[128,1000]{1,0:T(8,128)(2,1)S(1)} %bitcast.101, bf16[975,1000]{1,0:T(8,128)(2,1)} %f0, bf16[975,1000]{1,0:T(8,128)(2,1)} %copy-done.1, bf16[975,1000]{1,0:T(8,128)(2,1)} %collective-permute-done.9.f2, bf16[975,1000]{1,0:T(8,128)(2,1)} %collective-permute-done.20.f3), custom_call_target="tpu_custom_call" | custom-call | tf_op jit(solution)/shard_map/pallas_call | solution.py:213
  181.9 4.7 %shard_map.58 = bf16[4,128,975]{2,1,0:T(8,128)(2,1)S(1)} custom-call(bf16[128,1000]{1,0:T(8,128)(2,1)S(1)} %bitcast.102, bf16[975,1000]{1,0:T(8,128)(2,1)} %collective-permute-done.21.f0, bf16[975,1000]{1,0:T(8,128)(2,1)} %collective-permute-done.22.f1, bf16[975,1000]{1,0:T(8,128)(2,1)} %collective-permute-done.23.f2, ...), custom_call_target="tpu_custom_call" | custom-call | tf_op jit(solution)/shard_map/pallas_call | solution.py:213
  193.1 5.6 %collective-permute-done.37 = bf16[4,32,975]{2,1,0:T(8,128)(2,1)S(1)} collective-permute-done((bf16[4,32,975]{2,1,0:T(8,128)(2,1)S(1)}, bf16[4,32,975]{2,1,0:T(8,128)(2,1)S(1)}, u32[]{:S(2)}, u32[]{:S(2)}) %collective-permute-start.37) | collective-permute-done | bytes 249632 | tf_op jit(solution)/shard_map/ppermute | solution.py:41
  199.1 3.2 %collective-permute-start.40 = (bf16[8,8,975]{2,1,0:T(8,128)(2,1)S(1)}, bf16[8,8,975]{2,1,0:T(8,128)(2,1)S(1)}, u32[]{:S(2)}, u32[]{:S(2)}) collective-permute-start(bf16[8,8,975]{2,1,0:T(8,128)(2,1)S(1)} %get-tuple-element.91), channel_id=1, source_target_pairs={{0,3},{1,0},{2,1},{3,2},{4,7},{5,4},{6,5},{7,6},{8,11},{9,8},{10,9... | collective-permute-start | bytes 374408 | tf_op jit(solution)/shard_map/ppermute | solution.py:41
  202.5 2.8 %collective-permute-done.39 = bf16[8,8,975]{2,1,0:T(8,128)(2,1)S(1)} collective-permute-done((bf16[8,8,975]{2,1,0:T(8,128)(2,1)S(1)}, bf16[8,8,975]{2,1,0:T(8,128)(2,1)S(1)}, u32[]{:S(2)}, u32[]{:S(2)}) %collective-permute-start.39) | collective-permute-done | bytes 124832 | tf_op jit(solution)/shard_map/ppermute | solution.py:41
  (161 shorter events, 63.4 us)
Async XLA Ops:
  6.5 125.6 %all-gather.2.cloned.1.call-start = ((), (), s32[]{:S(2)}) async-start(), calls=%async_computation.1 | async-start | bytes 13160448 | tf_op jit(solution)/shard_map/all_gather | solution.py:273
  9.7 24.6 %collective-permute-start = (bf16[16,4096]{1,0:T(8,128)(2,1)S(1)}, bf16[16,4096]{1,0:T(8,128)(2,1)S(1)}, u32[]{:S(2)}, u32[]{:S(2)}) collective-permute-start(bf16[16,4096]{1,0:T(8,128)(2,1)S(1)} %slice.70.refs_0_), channel_id=1, source_target_pairs={{0,1},{1,2},{2,3},{3,0},{4,5},{5,6},{6,7},{7,4},{8,9},{9,10},{10,1... | collective-permute-start | bytes 393224 | tf_op jit(solution)/shard_map/ppermute | solution.py:41
  11.3 24.5 %collective-permute-start.2 = (bf16[16,4096]{1,0:T(8,128)(2,1)S(1)}, bf16[16,4096]{1,0:T(8,128)(2,1)S(1)}, u32[]{:S(2)}, u32[]{:S(2)}) collective-permute-start(bf16[16,4096]{1,0:T(8,128)(2,1)S(1)} %slice.70.refs_0_), channel_id=1, source_target_pairs={{0,3},{1,0},{2,1},{3,2},{4,7},{5,4},{6,5},{7,6},{8,11},{9,8},{10,9... | collective-permute-start | bytes 393224 | tf_op jit(solution)/shard_map/ppermute | solution.py:41
  13.0 24.3 %collective-permute-start.3 = (bf16[16,4096]{1,0:T(8,128)(2,1)S(1)}, bf16[16,4096]{1,0:T(8,128)(2,1)S(1)}, u32[]{:S(2)}, u32[]{:S(2)}) collective-permute-start(bf16[16,4096]{1,0:T(8,128)(2,1)S(1)} %slice.70.refs_0_), channel_id=1, source_target_pairs={{0,4},{1,5},{2,6},{3,7},{4,8},{5,9},{6,10},{7,11},{8,12},{9,13},{1... | collective-permute-start | bytes 393224 | tf_op jit(solution)/shard_map/ppermute | solution.py:41
  15.7 13.5 %all-to-all-start = ((f32[8,72,128]{2,1,0:T(8,128)}), f32[8,72,128]{2,1,0:T(8,128)}, u32[]{:S(2)}, u32[]{:S(2)}) async-start(f32[8,72,128]{2,1,0:T(8,128)} %broadcast_in_dim.91), calls=%async_computation | async-start | bytes 589824 | tf_op jit(solution)/shard_map/all_to_all | solution.py:289
  21.1 29.0 %collective-permute-start.1 = (bf16[975,1000]{1,0:T(8,128)(2,1)}, bf16[975,1000]{1,0:T(8,128)(2,1)S(1)}, u32[]{:S(2)}, u32[]{:S(2)}) collective-permute-start(bf16[975,1000]{1,0:T(8,128)(2,1)} %f0), channel_id=1, source_target_pairs={{0,32},{1,33},{2,34},{3,35},{4,36},{5,37},{6,38},{7,39},{8,40},{9,... | collective-permute-start | bytes 5850008 | tf_op jit(solution)/shard_map/ppermute | solution.py:41
  50.1 26.3 %collective-permute-start.9 = (bf16[975,1000]{1,0:T(8,128)(2,1)S(1)}, bf16[975,1000]{1,0:T(8,128)(2,1)}, u32[]{:S(2)}, u32[]{:S(2)}) collective-permute-start(bf16[975,1000]{1,0:T(8,128)(2,1)S(1)} %collective-permute-done.1.f1), channel_id=1, source_target_pairs={{0,32},{1,33},{2,34},{3,35},{4,36},{5,37},{6,38},{7,39},{8,40},{9,... | collective-permute-start | bytes 5850008 | tf_op jit(solution)/shard_map/ppermute | solution.py:41
  50.1 19.5 %collective-permute-start.10 = (bf16[48,4096]{1,0:T(8,128)(2,1)S(1)}, bf16[48,4096]{1,0:T(8,128)(2,1)S(1)}, u32[]{:S(2)}, u32[]{:S(2)}) collective-permute-start(bf16[48,4096]{1,0:T(8,128)(2,1)S(1)} %get-tuple-element.49), channel_id=1, source_target_pairs={{0,4},{1,5},{2,6},{3,7},{4,8},{5,9},{6,10},{7,11},{8,12},{9,13},{1... | collective-permute-start | bytes 1179656 | tf_op jit(solution)/shard_map/ppermute | solution.py:41
  51.7 21.3 %collective-permute-start.11 = (bf16[48,4096]{1,0:T(8,128)(2,1)S(1)}, bf16[48,4096]{1,0:T(8,128)(2,1)S(1)}, u32[]{:S(2)}, u32[]{:S(2)}) collective-permute-start(bf16[48,4096]{1,0:T(8,128)(2,1)S(1)} %get-tuple-element.50), channel_id=1, source_target_pairs={{0,12},{1,13},{2,14},{3,15},{4,0},{5,1},{6,2},{7,3},{8,4},{9,5},{1... | collective-permute-start | bytes 1179656 | tf_op jit(solution)/shard_map/ppermute | solution.py:41
  52.1 20.9 %collective-permute-start.12 = (bf16[48,4096]{1,0:T(8,128)(2,1)S(1)}, bf16[48,4096]{1,0:T(8,128)(2,1)S(1)}, u32[]{:S(2)}, u32[]{:S(2)}) collective-permute-start(bf16[48,4096]{1,0:T(8,128)(2,1)S(1)} %get-tuple-element.51), channel_id=1, source_target_pairs={{0,1},{1,2},{2,3},{3,0},{4,5},{5,6},{6,7},{7,4},{8,9},{9,10},{10,1... | collective-permute-start | bytes 1179656 | tf_op jit(solution)/shard_map/ppermute | solution.py:41
  52.4 20.6 %collective-permute-start.13 = (bf16[48,4096]{1,0:T(8,128)(2,1)S(1)}, bf16[48,4096]{1,0:T(8,128)(2,1)S(1)}, u32[]{:S(2)}, u32[]{:S(2)}) collective-permute-start(bf16[48,4096]{1,0:T(8,128)(2,1)S(1)} %get-tuple-element.52), channel_id=1, source_target_pairs={{0,3},{1,0},{2,1},{3,2},{4,7},{5,4},{6,5},{7,6},{8,11},{9,8},{10,9... | collective-permute-start | bytes 1179656 | tf_op jit(solution)/shard_map/ppermute | solution.py:41
  76.4 29.8 %collective-permute-start.20 = (bf16[975,1000]{1,0:T(8,128)(2,1)}, bf16[975,1000]{1,0:T(8,128)(2,1)}, u32[]{:S(2)}, u32[]{:S(2)}) collective-permute-start(bf16[975,1000]{1,0:T(8,128)(2,1)} %collective-permute-done.9.f2), channel_id=1, source_target_pairs={{0,32},{1,33},{2,34},{3,35},{4,36},{5,37},{6,38},{7,39},{8,40},{9,... | collective-permute-start | bytes 5850008 | tf_op jit(solution)/shard_map/ppermute | solution.py:41
  76.7 14.4 %collective-permute-start.14 = (bf16[32,4096]{1,0:T(8,128)(2,1)S(1)}, bf16[32,4096]{1,0:T(8,128)(2,1)S(1)}, u32[]{:S(2)}, u32[]{:S(2)}) collective-permute-start(bf16[32,4096]{1,0:T(8,128)(2,1)S(1)} %get-tuple-element.57), channel_id=1, source_target_pairs={{0,4},{1,5},{2,6},{3,7},{4,8},{5,9},{6,10},{7,11},{8,12},{9,13},{1... | collective-permute-start | bytes 786440 | tf_op jit(solution)/shard_map/ppermute | solution.py:41
  78.3 15.4 %collective-permute-start.17 = (bf16[32,4096]{1,0:T(8,128)(2,1)S(1)}, bf16[32,4096]{1,0:T(8,128)(2,1)S(1)}, u32[]{:S(2)}, u32[]{:S(2)}) collective-permute-start(bf16[32,4096]{1,0:T(8,128)(2,1)S(1)} %get-tuple-element.61), channel_id=1, source_target_pairs={{0,1},{1,2},{2,3},{3,0},{4,5},{5,6},{6,7},{7,4},{8,9},{9,10},{10,1... | collective-permute-start | bytes 786440 | tf_op jit(solution)/shard_map/ppermute | solution.py:41
  78.6 15.3 %collective-permute-start.15 = (bf16[32,4096]{1,0:T(8,128)(2,1)S(1)}, bf16[32,4096]{1,0:T(8,128)(2,1)S(1)}, u32[]{:S(2)}, u32[]{:S(2)}) collective-permute-start(bf16[32,4096]{1,0:T(8,128)(2,1)S(1)} %get-tuple-element.59), channel_id=1, source_target_pairs={{0,12},{1,13},{2,14},{3,15},{4,0},{5,1},{6,2},{7,3},{8,4},{9,5},{1... | collective-permute-start | bytes 786440 | tf_op jit(solution)/shard_map/ppermute | solution.py:41
  79.1 14.9 %collective-permute-start.16 = (bf16[32,4096]{1,0:T(8,128)(2,1)S(1)}, bf16[32,4096]{1,0:T(8,128)(2,1)S(1)}, u32[]{:S(2)}, u32[]{:S(2)}) collective-permute-start(bf16[32,4096]{1,0:T(8,128)(2,1)S(1)} %get-tuple-element.60), channel_id=1, source_target_pairs={{0,3},{1,0},{2,1},{3,2},{4,7},{5,4},{6,5},{7,6},{8,11},{9,8},{10,9... | collective-permute-start | bytes 786440 | tf_op jit(solution)/shard_map/ppermute | solution.py:41
  106.2 13.9 %collective-permute-start.21 = (bf16[975,1000]{1,0:T(8,128)(2,1)}, bf16[975,1000]{1,0:T(8,128)(2,1)}, u32[]{:S(2)}, u32[]{:S(2)}) collective-permute-start(bf16[975,1000]{1,0:T(8,128)(2,1)} %f0), channel_id=1, source_target_pairs={{0,16},{1,17},{2,18},{3,19},{4,20},{5,21},{6,22},{7,23},{8,24},{9,... | collective-permute-start | bytes 5850008 | tf_op jit(solution)/shard_map/ppermute | solution.py:41
  106.3 13.9 %collective-permute-start.22 = (bf16[975,1000]{1,0:T(8,128)(2,1)}, bf16[975,1000]{1,0:T(8,128)(2,1)}, u32[]{:S(2)}, u32[]{:S(2)}) collective-permute-start(bf16[975,1000]{1,0:T(8,128)(2,1)} %copy-done.1), channel_id=1, source_target_pairs={{0,16},{1,17},{2,18},{3,19},{4,20},{5,21},{6,22},{7,23},{8,24},{9,... | collective-permute-start | bytes 5850008 | tf_op jit(solution)/shard_map/ppermute | solution.py:41
  106.8 13.4 %collective-permute-start.23 = (bf16[975,1000]{1,0:T(8,128)(2,1)}, bf16[975,1000]{1,0:T(8,128)(2,1)}, u32[]{:S(2)}, u32[]{:S(2)}) collective-permute-start(bf16[975,1000]{1,0:T(8,128)(2,1)} %collective-permute-done.9.f2), channel_id=1, source_target_pairs={{0,16},{1,17},{2,18},{3,19},{4,20},{5,21},{6,22},{7,23},{8,24},{9,... | collective-permute-start | bytes 5850008 | tf_op jit(solution)/shard_map/ppermute | solution.py:41
  106.9 13.3 %collective-permute-start.24 = (bf16[975,1000]{1,0:T(8,128)(2,1)}, bf16[975,1000]{1,0:T(8,128)(2,1)}, u32[]{:S(2)}, u32[]{:S(2)}) collective-permute-start(bf16[975,1000]{1,0:T(8,128)(2,1)} %collective-permute-done.20.f3), channel_id=1, source_target_pairs={{0,16},{1,17},{2,18},{3,19},{4,20},{5,21},{6,22},{7,23},{8,24},{9,... | collective-permute-start | bytes 5850008 | tf_op jit(solution)/shard_map/ppermute | solution.py:41
  161.3 12.4 %collective-permute-start.30 = (bf16[2,48,1000]{2,1,0:T(8,128)(2,1)S(1)}, bf16[2,48,1000]{2,1,0:T(8,128)(2,1)S(1)}, u32[]{:S(2)}, u32[]{:S(2)}) collective-permute-start(bf16[2,48,1000]{2,1,0:T(8,128)(2,1)S(1)} %get-tuple-element.87), channel_id=1, source_target_pairs={{0,32},{1,33},{2,34},{3,35},{4,36},{5,37},{6,38},{7,39},{8,40},{9,... | collective-permute-start | bytes 576008 | tf_op jit(solution)/shard_map/ppermute | solution.py:41
  161.4 12.4 %collective-permute-start.31 = (bf16[2,48,1000]{2,1,0:T(8,128)(2,1)S(1)}, bf16[2,48,1000]{2,1,0:T(8,128)(2,1)S(1)}, u32[]{:S(2)}, u32[]{:S(2)}) collective-permute-start(bf16[2,48,1000]{2,1,0:T(8,128)(2,1)S(1)} %get-tuple-element.89), channel_id=1, source_target_pairs={{0,96},{1,97},{2,98},{3,99},{4,100},{5,101},{6,102},{7,103},{8,104... | collective-permute-start | bytes 576008 | tf_op jit(solution)/shard_map/ppermute | solution.py:41
  179.2 12.0 %collective-permute-start.34 = (bf16[4,32,975]{2,1,0:T(8,128)(2,1)S(1)}, bf16[4,32,975]{2,1,0:T(8,128)(2,1)S(1)}, u32[]{:S(2)}, u32[]{:S(2)}) collective-permute-start(bf16[4,32,975]{2,1,0:T(8,128)(2,1)S(1)} %get-tuple-element.95), channel_id=1, source_target_pairs={{0,12},{1,13},{2,14},{3,15},{4,0},{5,1},{6,2},{7,3},{8,4},{9,5},{1... | collective-permute-start | bytes 748808 | tf_op jit(solution)/shard_map/ppermute | solution.py:41
  180.8 10.4 %collective-permute-start.35 = (bf16[4,32,975]{2,1,0:T(8,128)(2,1)S(1)}, bf16[4,32,975]{2,1,0:T(8,128)(2,1)S(1)}, u32[]{:S(2)}, u32[]{:S(2)}) collective-permute-start(bf16[4,32,975]{2,1,0:T(8,128)(2,1)S(1)} %get-tuple-element.94), channel_id=1, source_target_pairs={{0,8},{1,9},{2,10},{3,11},{4,12},{5,13},{6,14},{7,15},{8,0},{9,1},... | collective-permute-start | bytes 748808 | tf_op jit(solution)/shard_map/ppermute | solution.py:41
  (38 other events, 369.9 us)
Sparse Core Ops, SparseCore 0:
  9.8 113.2 all-gather.1

commit v8 on v0

v8 whole, which is shorter than its diff:
```python
import functools

import jax
import jax.numpy as jnp
from jax import lax
from jax.experimental import pallas as pl
from jax.experimental.pallas import tpu as pltpu
from jax.sharding import PartitionSpec as P

SENSORS = 6
AXES = ("sens", "layer")
SIDE = 4
ROWS = 64
VMEM = 52 * 2**20


def moved(fn):
    pairs = []
    for z in range(4):
        for c in range(2):
            for y in range(4):
                for x in range(4):
                    z2, c2, y2, x2 = fn(z, c, y, x)
                    pairs.append(
                        ((z * 2 + c) * 16 + y * 4 + x,
                         ((z2 % 4) * 2 + c2 % 2) * 16 + (y2 % 4) * 4 + x2 % 4)
                    )
    return pairs


def send(x, fn):
    return lax.ppermute(x, AXES, moved(fn))


def swap_core(v):
    return send(v, lambda z, c, y, x: (z, c + 1, y, x))


def ring_z(v):
    return send(v, lambda z, c, y, x: (z + 1 - 2 * c, c, y, x))


def hop_x(d):
    return lambda z, c, y, x: (z, c, y, x + d)


def hop_y(d):
    return lambda z, c, y, x: (z, c, y + d, x)


def hop_z(d):
    return lambda z, c, y, x: (z + d, c, y, x)


def hop_one(d):
    return lambda z, c, y, x: (z, c, y + d * (1 - c), x + d * c)


def hop_two(d):
    return lambda z, c, y, x: (z, c, y + d * c, x + d * (1 - c))


def after(value, *others):
    return lax.optimization_barrier((value, *others))


def nt(a, b, **kw):
    return lax.dot_general(
        a, b, (((1,), (1,)), ((), ())), preferred_element_type=jnp.float32, **kw
    )


def fit_kernel(p, *refs):
    count = len(refs) - 3
    sources, (out, held, sems) = refs[:count], refs[count:]
    copies = [
        pltpu.make_async_copy(f, held.at[i], sems.at[i]) for i, f in enumerate(sources)
    ]
    for copy in copies:
        copy.start()
    for i, copy in enumerate(copies):
        copy.wait()
        out[i] = nt(p[...], held[i]).astype(jnp.bfloat16)


def fit(points, blocks):
    n, k = points.shape
    m = blocks[0].shape[0]
    count = len(blocks)
    return pl.pallas_call(
        fit_kernel,
        in_specs=[pl.BlockSpec(memory_space=pltpu.VMEM)]
        + [pl.BlockSpec(memory_space=pl.ANY)] * count,
        out_specs=pl.BlockSpec(memory_space=pltpu.VMEM),
        out_shape=jax.ShapeDtypeStruct((count, n, m), jnp.bfloat16),
        scratch_shapes=[
            pltpu.VMEM((count, m, k), jnp.bfloat16),
            pltpu.SemaphoreType.DMA((count,)),
        ],
        compiler_params=pltpu.CompilerParams(vmem_limit_bytes=VMEM),
        cost_estimate=pl.CostEstimate(flops=0, bytes_accessed=0, transcendentals=0),
    )(points, *blocks)


def sums_by_sens(full, z, c):
    halves = full.reshape(SIDE, 2, 2 * ROWS, full.shape[1])

    def core(i):
        return lax.dynamic_index_in_dim(halves, i, 1, keepdims=False)

    got = core(c) + swap_core(core(1 - c).astype(jnp.bfloat16)).astype(jnp.float32)

    def pick(d):
        return lax.dynamic_index_in_dim(got, (z + d) % SIDE, 0, keepdims=False)

    pieces = [pick(0)] + [send(pick(d).astype(jnp.bfloat16), hop_z(d)) for d in (1, 3, 2)]
    return total(pieces).astype(jnp.bfloat16)


def owned(blocks, here, hop):
    def pick(d):
        return lax.dynamic_index_in_dim(blocks, (here + d) % SIDE, 1, keepdims=False)

    return [pick(0)] + [send(pick(d).astype(jnp.bfloat16), hop(d)) for d in (1, 3, 2)]


def total(pieces):
    out = pieces[0].astype(jnp.float32)
    for piece in pieces[1:]:
        out = out + piece.astype(jnp.float32)
    return out


def per_device(slopes, valid, sensor_map, reconstructor, fitting):
    s_idx = lax.axis_index("sens")
    l_idx = lax.axis_index("layer")
    z, c = s_idx // 2, s_idx % 2
    y, x = l_idx // SIDE, l_idx % SIDE
    width = slopes.shape[1]
    width_p = reconstructor.shape[0]
    act = fitting.shape[0]

    masked = slopes * valid.astype(jnp.bfloat16)[None, :]
    whole = lax.all_gather(masked, "layer", axis=0, tiled=True)
    fits = [fitting, ring_z(fitting)]

    group = sensor_map * 2 + (lax.iota(jnp.int32, width) + s_idx * width) % 2
    lane = lax.iota(jnp.int32, 128)
    label = jnp.where(lane < 36, lane % 12, -1)
    member = ((group[None, :] == label[:, None]) & (valid[None, :] == 1)).astype(jnp.bfloat16)
    counted = jnp.concatenate([masked, jnp.ones((8, width), jnp.bfloat16)], axis=0)
    stats = nt(counted, member)
    stats = jnp.broadcast_to(stats[None], (8, *stats.shape))
    stats = jnp.sum(lax.all_to_all(stats, "sens", 0, 0, tiled=True), axis=0)
    means = stats[:ROWS] / jnp.maximum(stats[ROWS : ROWS + 1], 1.0)
    high = lax.reduce_precision(means, 8, 7)
    low = (lane >= 12) & (lane < 24)
    means = jnp.where(low[None, :], means - high, high).astype(jnp.bfloat16)

    along = jnp.stack([means] + [send(means, hop_x(d)) for d in (1, 2, 3)])
    along = jnp.take(along, (x - jnp.arange(SIDE)) % SIDE, axis=0, mode="clip")
    means = jnp.stack([along] + [send(along, hop_y(d)) for d in (1, 2, 3)])
    means = jnp.take(means, (y - jnp.arange(SIDE)) % SIDE, axis=0, mode="clip")
    means = means.reshape(16 * ROWS, 128)
    fits[1], member, means = after(fits[1], member, means)
    fits.append(ring_z(fits[-1]))

    rw = -nt(reconstructor, member)
    rw_high = lax.reduce_precision(rw, 8, 7)
    last = (lane >= 24) & (lane < 36)
    rw = jnp.where(last[None, :], rw - rw_high, rw_high).astype(jnp.bfloat16)
    fits[2], rw = after(fits[2], rw)
    fits.append(ring_z(fits[-1]))
    shift = nt(means, rw)
    shift, *fits = after(shift, *fits)
    swapped = [swap_core(f) for f in fits]
    shift, whole, *swapped = after(shift, whole, *swapped)

    points = sums_by_sens(nt(whole, reconstructor) + shift, z, c)

    rows = points.reshape(SIDE, SIDE, 8, width_p)
    rows = jnp.where(c == 0, rows, jnp.swapaxes(rows, 0, 1)).reshape(2 * ROWS, width_p)
    one = jnp.where(c == 0, y, x)
    two = jnp.where(c == 0, x, y)
    first = fit(rows, fits + swapped[:1])
    first, rows = after(first, rows)
    half_a = owned(first.reshape(5, SIDE, SIDE * 8, act), one, hop_one)
    half_b = owned(fit(rows, swapped[1:]).reshape(3, SIDE, SIDE * 8, act), one, hop_one)
    both = jnp.concatenate([total(half_a), total(half_b)], axis=0)
    done = total(owned(both.reshape(8, SIDE, 8, act), two, hop_two))

    sens = lax.iota(jnp.int32, 8)
    step = jnp.where(sens % 2 == 0, z - sens // 2, sens // 2 - z) % SIDE
    found = jnp.where(sens % 2 == c, 0, 4) + step
    done = jnp.take(done, found, axis=0, mode="clip")
    return jnp.moveaxis(done, 0, 1).reshape(8, 8 * act)


def solution(mesh):
    placed = (P("layer", "sens"), P("sens"), P("sens"), P("layer", "sens"), P("sens", "layer"))
    return jax.shard_map(
        per_device,
        mesh=mesh,
        in_specs=placed,
        out_specs=P(("sens", "layer"), None),
        check_vma=False,
    )
```

time: 285 us -> 232 us (0.81)
  blocking collectives: 39.9 us -> 0 us
  local copies, waits for them, and re-layouts: 48.2 us -> 20.8 us
  starting transfers between devices: 9.18 us -> 33.5 us
  matrix products: 59.2 us -> 38.2 us
  Pallas kernels: 0 us -> 9.38 us
  other arithmetic: 2.25 us -> 7.87 us
  waiting for transfers between devices: 110 us -> 107 us
    all_gather x2 -> x1, waiting for transfers between devices: 104 us -> 11.5 us  [per_device(): whole = lax.all_gather(masked, 'layer', axis=0, tiled=True)]
    ppermute x0 -> x26, waiting for transfers between devices: none -> 90.5 us  [send(): return lax.ppermute(x, AXES, moved(fn))]
    all_to_all x2 -> x0, blocking collectives: 39.9 us -> none  [the longest x1 29.5 us: summed_on_arrival(): lax.all_to_all(blocks, axis, split_axis=0, concat_axis=0, tiled=True)]
    ppermute x0 -> x26, starting transfers between devices: none -> 28.2 us  [send(): return lax.ppermute(x, AXES, moved(fn))]
    all_gather x1 -> x0, local copies, waits for them, and re-layouts: 22.4 us -> none  [per_device(): whole = lax.all_gather(slopes, 'layer', axis=0, tiled=True)]
    dot_general x5 -> x4, matrix products: 59.2 us -> 38.2 us  [nt(): lax.dot_general(a, b, (((1,), (1,)), ((), ())), preferred_element_type=jn...]
    unnamed x1 -> x9, local copies, waits for them, and re-layouts: 20.5 us -> 0.87 us
    pallas_call x0 -> x2, Pallas kernels: none -> 9.38 us  [fit(): pl.pallas_call(fit_kernel, in_specs=[pl.BlockSpec(memory_space=pltpu.VMEM...]
  transfers between devices with their start and end apart: 4 -> 28, of which waited for: 3 -> 22; matrix products, arithmetic and copies ran while one was open for 34% -> 9% of each run, Pallas kernels for 0% -> 0%
where the time goes in v8:
time: 232 us; the launch traced here: 231 us
  waiting for transfers between devices  107 us (46%)
  matrix products  38.2 us (16%)
  starting transfers between devices  33.5 us (14%)
  local copies, waits for them, and re-layouts  20.8 us (9%)
  between operations  13.8 us (6%)
  Pallas kernels  9.38 us (4%)
  other arithmetic  7.87 us (3%)
    ppermute x26, waiting for transfers between devices, send(): return lax.ppermute(x, AXES, moved(fn))  90.5 us
    dot_general x4, matrix products, nt(): lax.dot_general(a, b, (((1,), (1,)), ((), ())), preferred_element_type=jn...  38.2 us
    ppermute x26, starting transfers between devices, send(): return lax.ppermute(x, AXES, moved(fn))  28.2 us
    all_gather x1, waiting for transfers between devices, per_device(): whole = lax.all_gather(masked, 'layer', axis=0, tiled=True)  11.5 us
    pallas_call x2, Pallas kernels, fit(): pl.pallas_call(fit_kernel, in_specs=[pl.BlockSpec(memory_space=pltpu.VMEM...  9.38 us
    dynamic_slice x2, local copies, waits for them, and re-layouts, core(): return lax.dynamic_index_in_dim(halves, i, 1, keepdims=False)  7.92 us
    reshape x1, local copies, waits for them, and re-layouts, sums_by_sens(): halves = full.reshape(SIDE, 2, 2 * ROWS, full.shape[1])  6.49 us
    all_to_all x1, starting transfers between devices, per_device(): stats = jnp.sum(lax.all_to_all(stats, 'sens', 0, 0, tiled=True), axis=0)  5.31 us
  transfers between devices with their start and end apart: 28, of which 22 were waited for; matrix products, arithmetic and copies ran while one was open for 9% of the time, Pallas kernels for 0%

profile of v8, /device:TPU:24, one launch (start us, length us, event | category | flops | bytes accessed | tf_op | source)
XLA Modules:
  0.0 230.7 jit_solution(3344607221401818486)
XLA Ops:
  12.8 5.3 %all-to-all-start = ((f32[8,72,128]{2,1,0:T(8,128)}), f32[8,72,128]{2,1,0:T(8,128)S(1)}, u32[]{:S(2)}, u32[]{:S(2)}) async-start(f32[8,72,128]{2,1,0:T(8,128)} %broadcast_in_dim.47), calls=%async_computation | async-start | bytes 589824 | tf_op jit(solution)/shard_map/all_to_all | solution.py:154
  21.0 5.2 %all-to-all-done = f32[8,72,128]{2,1,0:T(8,128)S(1)} async-done(((f32[8,72,128]{2,1,0:T(8,128)}), f32[8,72,128]{2,1,0:T(8,128)S(1)}, u32[]{:S(2)}, u32[]{:S(2)}) %all-to-all-start) | async-done | bytes 294944 | tf_op jit(solution)/shard_map/all_to_all | solution.py:154
  27.8 2.7 %collective-permute-start.2 = (bf16[64,128]{1,0:T(8,128)(2,1)S(1)}, bf16[64,128]{1,0:T(8,128)(2,1)S(1)}, u32[]{:S(2)}, u32[]{:S(2)}) collective-permute-start(bf16[64,128]{1,0:T(8,128)(2,1)S(1)} %fusion.26), channel_id=1, source_target_pairs={{0,2},{1,3},{2,0},{3,1},{4,6},{5,7},{6,4},{7,5},{8,10},{9,11},{10,... | collective-permute-start | bytes 49160 | tf_op jit(solution)/shard_map/ppermute | solution.py:32
  35.4 2.6 %collective-permute-start.5 = (bf16[4,64,128]{2,1,0:T(8,128)(2,1)S(1)}, bf16[4,64,128]{2,1,0:T(8,128)(2,1)S(1)}, u32[]{:S(2)}, u32[]{:S(2)}) collective-permute-start(bf16[4,64,128]{2,1,0:T(8,128)(2,1)S(1)} %gather_fusion), channel_id=1, source_target_pairs={{0,8},{1,9},{2,10},{3,11},{4,12},{5,13},{6,14},{7,15},{8,0},{9,1},... | collective-permute-start | bytes 196616 | tf_op jit(solution)/shard_map/ppermute | solution.py:32
  38.0 3.2 %collective-permute-done.4 = bf16[4,64,128]{2,1,0:T(8,128)(2,1)S(1)} collective-permute-done((bf16[4,64,128]{2,1,0:T(8,128)(2,1)S(1)}, bf16[4,64,128]{2,1,0:T(8,128)(2,1)S(1)}, u32[]{:S(2)}, u32[]{:S(2)}) %collective-permute-start.4) | collective-permute-done | bytes 65568 | tf_op jit(solution)/shard_map/ppermute | solution.py:32
  44.7 2.6 %collective-permute-done.refs_1_ = bf16[975,1000]{1,0:T(8,128)(2,1)} collective-permute-done((bf16[975,1000]{1,0:T(8,128)(2,1)}, bf16[975,1000]{1,0:T(8,128)(2,1)}, u32[]{:S(2)}, u32[]{:S(2)}) %collective-permute-start) | collective-permute-done | bytes 1950032 | tf_op jit(solution)/shard_map/ppermute | solution.py:32
  47.3 8.0 %fusion.8 = bf16[1000,128]{1,0:T(8,128)(2,1)S(1)} fusion(bf16[128,7950]{1,0:T(8,128)(2,1)S(1)} %fusion.1, bf16[1000,7950]{1,0:T(8,128)(2,1)} %param.8, pred[128]{0:T(512)(128)(4,1)S(1)} %compare_and_fusion.2), kind=kOutput, calls=%fused_computation.18 | convolution fusion | flops 2035840000 | bytes 18191328 | tf_op jit(solution)/shard_map/dot_general | solution.py:68
  55.4 18.4 %collective-permute-done.7.refs_2_ = bf16[975,1000]{1,0:T(8,128)(2,1)} collective-permute-done((bf16[975,1000]{1,0:T(8,128)(2,1)}, bf16[975,1000]{1,0:T(8,128)(2,1)}, u32[]{:S(2)}, u32[]{:S(2)}) %collective-permute-start.7) | collective-permute-done | bytes 1950032 | tf_op jit(solution)/shard_map/ppermute | solution.py:32
  73.8 2.6 %fusion.39 = f32[1024,1000]{0,1:T(8,128)} fusion(bf16[1024,128]{1,0:T(8,128)(2,1)S(1)} %bitcast.112, bf16[1000,128]{1,0:T(8,128)(2,1)S(1)} %fusion.8), kind=kOutput, calls=%fused_computation.101 | convolution fusion | flops 262144000 | bytes 4614144 | tf_op jit(solution)/shard_map/dot_general | solution.py:68
  76.4 23.7 %collective-permute-done.8.refs_3_ = bf16[975,1000]{1,0:T(8,128)(2,1)S(1)} collective-permute-done((bf16[975,1000]{1,0:T(8,128)(2,1)}, bf16[975,1000]{1,0:T(8,128)(2,1)S(1)}, u32[]{:S(2)}, u32[]{:S(2)}) %collective-permute-start.8) | collective-permute-done | bytes 1950032 | tf_op jit(solution)/shard_map/ppermute | solution.py:32
  101.2 3.3 %collective-permute-done.10.refs_0_ = bf16[975,1000]{1,0:T(8,128)(2,1)} collective-permute-done((bf16[975,1000]{1,0:T(8,128)(2,1)}, bf16[975,1000]{1,0:T(8,128)(2,1)}, u32[]{:S(2)}, u32[]{:S(2)}) %collective-permute-start.10) | collective-permute-done | bytes 1950032 | tf_op jit(solution)/shard_map/ppermute | solution.py:32
  104.6 5.7 %collective-permute-done.11.refs_1_ = bf16[975,1000]{1,0:T(8,128)(2,1)} collective-permute-done((bf16[975,1000]{1,0:T(8,128)(2,1)}, bf16[975,1000]{1,0:T(8,128)(2,1)}, u32[]{:S(2)}, u32[]{:S(2)}) %collective-permute-start.11) | collective-permute-done | bytes 1950032 | tf_op jit(solution)/shard_map/ppermute | solution.py:32
  110.3 2.9 %collective-permute-done.9.refs_4_ = bf16[975,1000]{1,0:T(8,128)(2,1)} collective-permute-done((bf16[975,1000]{1,0:T(8,128)(2,1)}, bf16[975,1000]{1,0:T(8,128)(2,1)}, u32[]{:S(2)}, u32[]{:S(2)}) %collective-permute-start.9) | collective-permute-done | bytes 1950032 | tf_op jit(solution)/shard_map/ppermute | solution.py:32
  113.1 11.5 %all-gather.2.cloned.1.call-done = bf16[1024,7950]{1,0:T(8,128)(2,1)} async-done(((bf16[64,7950]{1,0:T(8,128)(2,1)}), bf16[1024,7950]{1,0:T(8,128)(2,1)}) %all-gather.2.cloned.1.call-update) | async-done | bytes 16281616 | tf_op jit(solution)/shard_map/all_gather | solution.py:144
  124.6 25.2 %convolution_add_fusion = f32[1024,1000]{0,1:T(8,128)} fusion(f32[1024,1000]{0,1:T(8,128)} %fusion.39, bf16[1024,7950]{1,0:T(8,128)(2,1)} %all-gather.2.cloned.1.call-done, bf16[1000,7950]{1,0:T(8,128)(2,1)} %param.8), kind=kOutput, calls=%fused_computation.6 | convolution fusion | flops 16282624000 | bytes 40373600 | tf_op jit(solution)/shard_map/dot_general | solution.py:68
  149.8 6.5 %reshape.250 = f32[4,2,128,1000]{2,1,0,3:T(2,128)} reshape(f32[1024,1000]{0,1:T(8,128)} %convolution_add_fusion) | data formatting | bytes 8192000 | tf_op jit(solution)/shard_map/reshape | solution.py:106
  156.3 4.0 %constant_dynamic-slice_fusion = bf16[4,1,128,1000]{2,1,0,3:T(2,128)(2,1)S(1)} fusion(f32[4,2,128,1000]{2,1,0,3:T(2,128)} %reshape.250, s32[]{:T(128)S(6)} %select_n.271), kind=kLoop, calls=%fused_computation.66 | loop fusion | bytes 2048004 | tf_op jit(solution)/shard_map/jit(dynamic_index_in_dim)/dynamic_slice | solution.py:109
  160.6 3.9 %constant_dynamic-slice_fusion.1 = f32[4,1,128,1000]{2,1,0,3:T(1,128)S(1)} fusion(f32[4,2,128,1000]{2,1,0,3:T(2,128)} %reshape.250, s32[]{:T(128)S(6)} %select_n.270), kind=kLoop, calls=%fused_computation.67 | loop fusion | bytes 4096004 | tf_op jit(solution)/shard_map/jit(dynamic_index_in_dim)/dynamic_slice | solution.py:109
  170.1 4.5 %collective-permute-done.14 = bf16[128,1000]{0,1:T(8,128)(2,1)S(1)} collective-permute-done((bf16[128,1000]{0,1:T(8,128)(2,1)S(1)}, bf16[128,1000]{0,1:T(8,128)(2,1)S(1)}, u32[]{:S(2)}, u32[]{:S(2)}) %collective-permute-start.14) | collective-permute-done | bytes 256032 | tf_op jit(solution)/shard_map/ppermute | solution.py:32
  175.5 5.9 %collective-permute-done.16 = bf16[128,1000]{0,1:T(8,128)(2,1)} collective-permute-done((bf16[128,1000]{0,1:T(8,128)(2,1)S(1)}, bf16[128,1000]{0,1:T(8,128)(2,1)}, u32[]{:S(2)}, u32[]{:S(2)}) %collective-permute-start.16) | collective-permute-done | bytes 256032 | tf_op jit(solution)/shard_map/ppermute | solution.py:32
  182.7 5.5 %shard_map.55 = bf16[5,128,975]{2,1,0:T(8,128)(2,1)S(1)} custom-call(bf16[128,1000]{1,0:T(8,128)(2,1)S(1)} %bitcast.110, bf16[975,1000]{1,0:T(8,128)(2,1)} %refs_0_, bf16[975,1000]{1,0:T(8,128)(2,1)} %collective-permute-done.refs_1_, bf16[975,1000]{1,0:T(8,128)(2,1)} %collective-permute-done.7.refs_2_, bf16[975,1000]{1,0:T(8,128)(2,1)} %copy-done, ...), custom_call_target="tpu_custom_call" | custom-call | tf_op jit(solution)/shard_map/pallas_call | solution.py:90
  188.2 3.9 %shard_map.56 = bf16[3,128,975]{2,1,0:T(8,128)(2,1)S(1)} custom-call(bf16[128,1000]{1,0:T(8,128)(2,1)S(1)} %bitcast.111, bf16[975,1000]{1,0:T(8,128)(2,1)} %collective-permute-done.10.refs_0_, bf16[975,1000]{1,0:T(8,128)(2,1)} %collective-permute-done.11.refs_1_, bf16[975,1000]{1,0:T(8,128)(2,1)} %collective-permute-done.12.refs_2_), custom_call_target="tpu_custom_call" | custom-call | tf_op jit(solution)/shard_map/pallas_call | solution.py:90
  204.9 6.1 %collective-permute-done.18 = bf16[5,32,975]{2,1,0:T(8,128)(2,1)S(1)} collective-permute-done((bf16[5,32,975]{2,1,0:T(8,128)(2,1)S(1)}, bf16[5,32,975]{2,1,0:T(8,128)(2,1)S(1)}, u32[]{:S(2)}, u32[]{:S(2)}) %collective-permute-start.18) | collective-permute-done | bytes 312032 | tf_op jit(solution)/shard_map/ppermute | solution.py:32
  212.8 3.0 %collective-permute-start.24 = (bf16[8,8,975]{2,1,0:T(8,128)(2,1)S(1)}, bf16[8,8,975]{2,1,0:T(8,128)(2,1)S(1)}, u32[]{:S(2)}, u32[]{:S(2)}) collective-permute-start(bf16[8,8,975]{2,1,0:T(8,128)(2,1)S(1)} %get-tuple-element.48), channel_id=1, source_target_pairs={{0,3},{1,0},{2,1},{3,2},{4,7},{5,4},{6,5},{7,6},{8,11},{9,8},{10,9... | collective-permute-start | bytes 374408 | tf_op jit(solution)/shard_map/ppermute | solution.py:32
  (89 shorter events, 50.5 us)
Async XLA Ops:
  6.5 118.1 %all-gather.2.cloned.1.call-start = ((), (), s32[]{:S(2)}) async-start(), calls=%async_computation.1 | async-start | bytes 17547264 | tf_op jit(solution)/shard_map/all_gather | solution.py:144
  12.8 13.3 %all-to-all-start = ((f32[8,72,128]{2,1,0:T(8,128)}), f32[8,72,128]{2,1,0:T(8,128)S(1)}, u32[]{:S(2)}, u32[]{:S(2)}) async-start(f32[8,72,128]{2,1,0:T(8,128)} %broadcast_in_dim.47), calls=%async_computation | async-start | bytes 589824 | tf_op jit(solution)/shard_map/all_to_all | solution.py:154
  18.2 29.1 %collective-permute-start = (bf16[975,1000]{1,0:T(8,128)(2,1)}, bf16[975,1000]{1,0:T(8,128)(2,1)}, u32[]{:S(2)}, u32[]{:S(2)}) collective-permute-start(bf16[975,1000]{1,0:T(8,128)(2,1)} %refs_0_), channel_id=1, source_target_pairs={{0,32},{1,33},{2,34},{3,35},{4,36},{5,37},{6,38},{7,39},{8,40},{9,... | collective-permute-start | bytes 5850008 | tf_op jit(solution)/shard_map/ppermute | solution.py:32
  26.2 5.7 %collective-permute-start.1 = (bf16[64,128]{1,0:T(8,128)(2,1)S(1)}, bf16[64,128]{1,0:T(8,128)(2,1)S(1)}, u32[]{:S(2)}, u32[]{:S(2)}) collective-permute-start(bf16[64,128]{1,0:T(8,128)(2,1)S(1)} %fusion.26), channel_id=1, source_target_pairs={{0,1},{1,2},{2,3},{3,0},{4,5},{5,6},{6,7},{7,4},{8,9},{9,10},{10,1... | collective-permute-start | bytes 49160 | tf_op jit(solution)/shard_map/ppermute | solution.py:32
  35.1 6.1 %collective-permute-start.4 = (bf16[4,64,128]{2,1,0:T(8,128)(2,1)S(1)}, bf16[4,64,128]{2,1,0:T(8,128)(2,1)S(1)}, u32[]{:S(2)}, u32[]{:S(2)}) collective-permute-start(bf16[4,64,128]{2,1,0:T(8,128)(2,1)S(1)} %gather_fusion), channel_id=1, source_target_pairs={{0,4},{1,5},{2,6},{3,7},{4,8},{5,9},{6,10},{7,11},{8,12},{9,13},{1... | collective-permute-start | bytes 196616 | tf_op jit(solution)/shard_map/ppermute | solution.py:32
  35.4 7.5 %collective-permute-start.5 = (bf16[4,64,128]{2,1,0:T(8,128)(2,1)S(1)}, bf16[4,64,128]{2,1,0:T(8,128)(2,1)S(1)}, u32[]{:S(2)}, u32[]{:S(2)}) collective-permute-start(bf16[4,64,128]{2,1,0:T(8,128)(2,1)S(1)} %gather_fusion), channel_id=1, source_target_pairs={{0,8},{1,9},{2,10},{3,11},{4,12},{5,13},{6,14},{7,15},{8,0},{9,1},... | collective-permute-start | bytes 196616 | tf_op jit(solution)/shard_map/ppermute | solution.py:32
  38.0 6.0 %collective-permute-start.6 = (bf16[4,64,128]{2,1,0:T(8,128)(2,1)S(1)}, bf16[4,64,128]{2,1,0:T(8,128)(2,1)S(1)}, u32[]{:S(2)}, u32[]{:S(2)}) collective-permute-start(bf16[4,64,128]{2,1,0:T(8,128)(2,1)S(1)} %gather_fusion), channel_id=1, source_target_pairs={{0,12},{1,13},{2,14},{3,15},{4,0},{5,1},{6,2},{7,3},{8,4},{9,5},{1... | collective-permute-start | bytes 196616 | tf_op jit(solution)/shard_map/ppermute | solution.py:32
  47.3 26.5 %collective-permute-start.7 = (bf16[975,1000]{1,0:T(8,128)(2,1)}, bf16[975,1000]{1,0:T(8,128)(2,1)}, u32[]{:S(2)}, u32[]{:S(2)}) collective-permute-start(bf16[975,1000]{1,0:T(8,128)(2,1)} %collective-permute-done.refs_1_), channel_id=1, source_target_pairs={{0,32},{1,33},{2,34},{3,35},{4,36},{5,37},{6,38},{7,39},{8,40},{9,... | collective-permute-start | bytes 5850008 | tf_op jit(solution)/shard_map/ppermute | solution.py:32
  73.8 26.4 %collective-permute-start.8 = (bf16[975,1000]{1,0:T(8,128)(2,1)}, bf16[975,1000]{1,0:T(8,128)(2,1)S(1)}, u32[]{:S(2)}, u32[]{:S(2)}) collective-permute-start(bf16[975,1000]{1,0:T(8,128)(2,1)} %collective-permute-done.7.refs_2_), channel_id=1, source_target_pairs={{0,32},{1,33},{2,34},{3,35},{4,36},{5,37},{6,38},{7,39},{8,40},{9,... | collective-permute-start | bytes 5850008 | tf_op jit(solution)/shard_map/ppermute | solution.py:32
  100.2 10.1 %collective-permute-start.11 = (bf16[975,1000]{1,0:T(8,128)(2,1)}, bf16[975,1000]{1,0:T(8,128)(2,1)}, u32[]{:S(2)}, u32[]{:S(2)}) collective-permute-start(bf16[975,1000]{1,0:T(8,128)(2,1)} %collective-permute-done.7.refs_2_), channel_id=1, source_target_pairs={{0,16},{1,17},{2,18},{3,19},{4,20},{5,21},{6,22},{7,23},{8,24},{9,... | collective-permute-start | bytes 5850008 | tf_op jit(solution)/shard_map/ppermute | solution.py:32
  100.7 9.6 %collective-permute-start.12 = (bf16[975,1000]{1,0:T(8,128)(2,1)S(1)}, bf16[975,1000]{1,0:T(8,128)(2,1)}, u32[]{:S(2)}, u32[]{:S(2)}) collective-permute-start(bf16[975,1000]{1,0:T(8,128)(2,1)S(1)} %collective-permute-done.8.refs_3_), channel_id=1, source_target_pairs={{0,16},{1,17},{2,18},{3,19},{4,20},{5,21},{6,22},{7,23},{8,24},{9,... | collective-permute-start | bytes 5850008 | tf_op jit(solution)/shard_map/ppermute | solution.py:32
  100.7 12.4 %collective-permute-start.9 = (bf16[975,1000]{1,0:T(8,128)(2,1)}, bf16[975,1000]{1,0:T(8,128)(2,1)}, u32[]{:S(2)}, u32[]{:S(2)}) collective-permute-start(bf16[975,1000]{1,0:T(8,128)(2,1)} %refs_0_), channel_id=1, source_target_pairs={{0,16},{1,17},{2,18},{3,19},{4,20},{5,21},{6,22},{7,23},{8,24},{9,... | collective-permute-start | bytes 5850008 | tf_op jit(solution)/shard_map/ppermute | solution.py:32
  164.9 9.8 %collective-permute-start.14 = (bf16[128,1000]{0,1:T(8,128)(2,1)S(1)}, bf16[128,1000]{0,1:T(8,128)(2,1)S(1)}, u32[]{:S(2)}, u32[]{:S(2)}) collective-permute-start(bf16[128,1000]{0,1:T(8,128)(2,1)S(1)} %get-tuple-element.41), channel_id=1, source_target_pairs={{0,32},{1,33},{2,34},{3,35},{4,36},{5,37},{6,38},{7,39},{8,40},{9,... | collective-permute-start | bytes 768008 | tf_op jit(solution)/shard_map/ppermute | solution.py:32
  166.5 9.0 %collective-permute-start.15 = (bf16[128,1000]{0,1:T(8,128)(2,1)S(1)}, bf16[128,1000]{0,1:T(8,128)(2,1)S(1)}, u32[]{:S(2)}, u32[]{:S(2)}) collective-permute-start(bf16[128,1000]{0,1:T(8,128)(2,1)S(1)} %get-tuple-element.43), channel_id=1, source_target_pairs={{0,96},{1,97},{2,98},{3,99},{4,100},{5,101},{6,102},{7,103},{8,104... | collective-permute-start | bytes 768008 | tf_op jit(solution)/shard_map/ppermute | solution.py:32
  168.2 13.2 %collective-permute-start.16 = (bf16[128,1000]{0,1:T(8,128)(2,1)S(1)}, bf16[128,1000]{0,1:T(8,128)(2,1)}, u32[]{:S(2)}, u32[]{:S(2)}) collective-permute-start(bf16[128,1000]{0,1:T(8,128)(2,1)S(1)} %get-tuple-element.42), channel_id=1, source_target_pairs={{0,64},{1,65},{2,66},{3,67},{4,68},{5,69},{6,70},{7,71},{8,72},{9,... | collective-permute-start | bytes 768008 | tf_op jit(solution)/shard_map/ppermute | solution.py:32
  192.9 6.3 %collective-permute-start.20 = (bf16[3,32,975]{2,1,0:T(8,128)(2,1)S(1)}, bf16[3,32,975]{2,1,0:T(8,128)(2,1)S(1)}, u32[]{:S(2)}, u32[]{:S(2)}) collective-permute-start(bf16[3,32,975]{2,1,0:T(8,128)(2,1)S(1)} %get-tuple-element.50), channel_id=1, source_target_pairs={{0,4},{1,5},{2,6},{3,7},{4,8},{5,9},{6,10},{7,11},{8,12},{9,13},{1... | collective-permute-start | bytes 561608 | tf_op jit(solution)/shard_map/ppermute | solution.py:32
  193.5 9.3 %collective-permute-start.21 = (bf16[3,32,975]{2,1,0:T(8,128)(2,1)}, bf16[3,32,975]{2,1,0:T(8,128)(2,1)}, u32[]{:S(2)}, u32[]{:S(2)}) collective-permute-start(bf16[3,32,975]{2,1,0:T(8,128)(2,1)} %get-tuple-element.52), channel_id=1, source_target_pairs={{0,12},{1,13},{2,14},{3,15},{4,0},{5,1},{6,2},{7,3},{8,4},{9,5},{1... | collective-permute-start | bytes 561608 | tf_op jit(solution)/shard_map/ppermute | solution.py:32
  194.9 7.8 %collective-permute-start.22 = (bf16[3,32,975]{2,1,0:T(8,128)(2,1)}, bf16[3,32,975]{2,1,0:T(8,128)(2,1)}, u32[]{:S(2)}, u32[]{:S(2)}) collective-permute-start(bf16[3,32,975]{2,1,0:T(8,128)(2,1)} %get-tuple-element.51), channel_id=1, source_target_pairs={{0,8},{1,9},{2,10},{3,11},{4,12},{5,13},{6,14},{7,15},{8,0},{9,1},... | collective-permute-start | bytes 561608 | tf_op jit(solution)/shard_map/ppermute | solution.py:32
  197.2 7.8 %collective-permute-start.17 = (bf16[5,32,975]{2,1,0:T(8,128)(2,1)}, bf16[5,32,975]{2,1,0:T(8,128)(2,1)S(1)}, u32[]{:S(2)}, u32[]{:S(2)}) collective-permute-start(bf16[5,32,975]{2,1,0:T(8,128)(2,1)} %get-tuple-element.44), channel_id=1, source_target_pairs={{0,4},{1,5},{2,6},{3,7},{4,8},{5,9},{6,10},{7,11},{8,12},{9,13},{1... | collective-permute-start | bytes 936008 | tf_op jit(solution)/shard_map/ppermute | solution.py:32
  199.3 11.8 %collective-permute-start.18 = (bf16[5,32,975]{2,1,0:T(8,128)(2,1)S(1)}, bf16[5,32,975]{2,1,0:T(8,128)(2,1)S(1)}, u32[]{:S(2)}, u32[]{:S(2)}) collective-permute-start(bf16[5,32,975]{2,1,0:T(8,128)(2,1)S(1)} %get-tuple-element.46), channel_id=1, source_target_pairs={{0,12},{1,13},{2,14},{3,15},{4,0},{5,1},{6,2},{7,3},{8,4},{9,5},{1... | collective-permute-start | bytes 936008 | tf_op jit(solution)/shard_map/ppermute | solution.py:32
  200.0 11.1 %collective-permute-start.19 = (bf16[5,32,975]{2,1,0:T(8,128)(2,1)S(1)}, bf16[5,32,975]{2,1,0:T(8,128)(2,1)}, u32[]{:S(2)}, u32[]{:S(2)}) collective-permute-start(bf16[5,32,975]{2,1,0:T(8,128)(2,1)S(1)} %get-tuple-element.45), channel_id=1, source_target_pairs={{0,8},{1,9},{2,10},{3,11},{4,12},{5,13},{6,14},{7,15},{8,0},{9,1},... | collective-permute-start | bytes 936008 | tf_op jit(solution)/shard_map/ppermute | solution.py:32
  212.4 6.2 %collective-permute-start.23 = (bf16[8,8,975]{2,1,0:T(8,128)(2,1)S(1)}, bf16[8,8,975]{2,1,0:T(8,128)(2,1)S(1)}, u32[]{:S(2)}, u32[]{:S(2)}) collective-permute-start(bf16[8,8,975]{2,1,0:T(8,128)(2,1)S(1)} %get-tuple-element.47), channel_id=1, source_target_pairs={{0,1},{1,2},{2,3},{3,0},{4,5},{5,6},{6,7},{7,4},{8,9},{9,10},{10,1... | collective-permute-start | bytes 374408 | tf_op jit(solution)/shard_map/ppermute | solution.py:32
  212.8 6.9 %collective-permute-start.24 = (bf16[8,8,975]{2,1,0:T(8,128)(2,1)S(1)}, bf16[8,8,975]{2,1,0:T(8,128)(2,1)S(1)}, u32[]{:S(2)}, u32[]{:S(2)}) collective-permute-start(bf16[8,8,975]{2,1,0:T(8,128)(2,1)S(1)} %get-tuple-element.48), channel_id=1, source_target_pairs={{0,3},{1,0},{2,1},{3,2},{4,7},{5,4},{6,5},{7,6},{8,11},{9,8},{10,9... | collective-permute-start | bytes 374408 | tf_op jit(solution)/shard_map/ppermute | solution.py:32
  215.7 6.5 %collective-permute-start.25 = (bf16[8,8,975]{2,1,0:T(8,128)(2,1)S(1)}, bf16[8,8,975]{2,1,0:T(8,128)(2,1)S(1)}, u32[]{:S(2)}, u32[]{:S(2)}) collective-permute-start(bf16[8,8,975]{2,1,0:T(8,128)(2,1)S(1)} %get-tuple-element.49), channel_id=1, source_target_pairs={{0,2},{1,3},{2,0},{3,1},{4,6},{5,7},{6,4},{7,5},{8,10},{9,11},{10,... | collective-permute-start | bytes 374408 | tf_op jit(solution)/shard_map/ppermute | solution.py:32
  (8 other events, 74.8 us)
Sparse Core Ops, SparseCore 0:
  9.8 114.7 all-gather.1

commit v9 on v7

--- a/solution.py
+++ b/solution.py
@@ -195,8 +195,9 @@
     )(*args)
 
 
-def fit_kernel(p, f0, f1, f2, f3, out, held, sems):
-    sources = (f0, f1, f2, f3)
+def fit_kernel(p, *refs):
+    count = len(refs) - 3
+    sources, (out, held, sems) = refs[:count], refs[count:]
     copies = [
         pltpu.make_async_copy(f, held.at[i], sems.at[i]) for i, f in enumerate(sources)
     ]
@@ -210,15 +211,16 @@
 def fit(points, blocks):
     n, k = points.shape
     m = blocks[0].shape[0]
+    count = len(blocks)
     return pl.pallas_call(
         fit_kernel,
         in_specs=[pl.BlockSpec(memory_space=pltpu.VMEM)]
-        + [pl.BlockSpec(memory_space=pl.ANY)] * 4,
+        + [pl.BlockSpec(memory_space=pl.ANY)] * count,
         out_specs=pl.BlockSpec(memory_space=pltpu.VMEM),
-        out_shape=jax.ShapeDtypeStruct((4, n, m), jnp.bfloat16),
+        out_shape=jax.ShapeDtypeStruct((count, n, m), jnp.bfloat16),
         scratch_shapes=[
-            pltpu.VMEM((4, m, k), jnp.bfloat16),
-            pltpu.SemaphoreType.DMA((4,)),
+            pltpu.VMEM((count, m, k), jnp.bfloat16),
+            pltpu.SemaphoreType.DMA((count,)),
         ],
         compiler_params=pltpu.CompilerParams(vmem_limit_bytes=VMEM),
         cost_estimate=pl.CostEstimate(flops=0, bytes_accessed=0, transcendentals=0),
@@ -362,13 +364,15 @@
     own, other, tail = reconstruct(0, arrays, pieces, position, reconstructor, rw)
     swapped = [swap_core(f) for f in fits]
     own, other, *swapped = after(own, other, *swapped)
-    near = sums_by_z(picks_by_z(own, other, z))
-    near, late = after(near, late)
+    picked = picks_by_z(own, other, z)
+    *picked, late = after(*picked, late)
+    near = sums_by_z(picked)
 
     own, other = reconstruct(
         1, [late], [(0, 0, 16 * LATE, 0, 0, side) for side in (0, 1)],
         position, reconstructor, rw, tail,
     )
+    own, other, near = after(own, other, near)
     far = sums_by_z(picks_by_z(own, other, z))
     points = jnp.concatenate([near, far], axis=1)
 
@@ -384,7 +388,7 @@
     sens = lax.iota(jnp.int32, 8)
     step = jnp.where(sens % 2 == 0, z - sens // 2, sens // 2 - z) % SIDE
     found = jnp.where(sens % 2 == c, 0, 4) + step
-    done = jnp.take(done, found, axis=0)
+    done = jnp.take(done, found, axis=0, mode="clip")
     return jnp.moveaxis(done, 0, 1).reshape(8, 8 * act)
 
 

time: 219 us -> 215 us (0.982)
  waiting for transfers between devices: 79.2 us -> 72.6 us
  starting transfers between devices: 50.6 us -> 53.2 us
    ppermute x42, waiting for transfers between devices: 74.4 us -> 67.7 us  [send(): return lax.ppermute(x, AXES, moved(fn))]
    ppermute x42, starting transfers between devices: 45.2 us -> 47.8 us  [send(): return lax.ppermute(x, AXES, moved(fn))]
  transfers between devices with their start and end apart: 44 -> 44, of which waited for: 22 -> 23; matrix products, arithmetic and copies ran while one was open for 9% -> 9% of each run, Pallas kernels for 8% -> 20%
where the time goes in v9:
time: 215 us; the launch traced here: 213 us
  waiting for transfers between devices  72.6 us (34%)
  starting transfers between devices  53.2 us (25%)
  Pallas kernels  46.5 us (22%)
  between operations  14 us (7%)
  other arithmetic  12.1 us (6%)
  matrix products  9.26 us (4%)
  local copies, waits for them, and re-layouts  5.74 us (3%)
    ppermute x42, waiting for transfers between devices, send(): return lax.ppermute(x, AXES, moved(fn))  67.7 us
    ppermute x42, starting transfers between devices, send(): return lax.ppermute(x, AXES, moved(fn))  47.8 us
    pallas_call x2, Pallas kernels, reconstruct(): pl.pallas_call(functools.partial(reconstruct_kernel, tuple(pieces), len(a...  37.1 us
    pallas_call x2, Pallas kernels, fit(): pl.pallas_call(fit_kernel, in_specs=[pl.BlockSpec(memory_space=pltpu.VMEM...  9.38 us
    dot_general x2, matrix products, nt(): lax.dot_general(a, b, (((1,), (1,)), ((), ())), preferred_element_type=jn...  9.26 us
    all_to_all x1, starting transfers between devices, per_device(): stats = jnp.sum(lax.all_to_all(stats, 'sens', 0, 0, tiled=True), axis=0)  5.4 us
    all_to_all x1, waiting for transfers between devices, per_device(): stats = jnp.sum(lax.all_to_all(stats, 'sens', 0, 0, tiled=True), axis=0)  4.79 us
  transfers between devices with their start and end apart: 44, of which 23 were waited for; matrix products, arithmetic and copies ran while one was open for 9% of the time, Pallas kernels for 20%

profile of v9, /device:TPU:24, one launch (start us, length us, event | category | flops | bytes accessed | tf_op | source)
XLA Modules:
  0.0 213.4 jit_solution(8923382604224788045)
XLA Ops:
  15.7 5.4 %all-to-all-start = ((f32[8,72,128]{2,1,0:T(8,128)}), f32[8,72,128]{2,1,0:T(8,128)}, u32[]{:S(2)}, u32[]{:S(2)}) async-start(f32[8,72,128]{2,1,0:T(8,128)} %broadcast_in_dim.79), calls=%async_computation | async-start | bytes 589824 | tf_op jit(solution)/shard_map/all_to_all | solution.py:291
  24.4 4.8 %all-to-all-done = f32[8,72,128]{2,1,0:T(8,128)} async-done(((f32[8,72,128]{2,1,0:T(8,128)}), f32[8,72,128]{2,1,0:T(8,128)}, u32[]{:S(2)}, u32[]{:S(2)}) %all-to-all-start) | async-done | bytes 294944 | tf_op jit(solution)/shard_map/all_to_all | solution.py:291
  38.0 3.7 %collective-permute-done.4.refs_9_ = bf16[16,4096]{1,0:T(8,128)(2,1)S(1)} collective-permute-done((bf16[16,4096]{1,0:T(8,128)(2,1)S(1)}, bf16[16,4096]{1,0:T(8,128)(2,1)S(1)}, u32[]{:S(2)}, u32[]{:S(2)}) %collective-permute-start.4) | collective-permute-done | bytes 131104 | tf_op jit(solution)/shard_map/ppermute | solution.py:41
  44.0 3.8 %collective-permute-done.8.refs_3_ = bf16[16,4096]{1,0:T(8,128)(2,1)S(1)} collective-permute-done((bf16[16,4096]{1,0:T(8,128)(2,1)S(1)}, bf16[16,4096]{1,0:T(8,128)(2,1)S(1)}, u32[]{:S(2)}, u32[]{:S(2)}) %collective-permute-start.8) | collective-permute-done | bytes 131104 | tf_op jit(solution)/shard_map/ppermute | solution.py:41
  52.4 3.0 %collective-permute-start.13 = (bf16[48,4096]{1,0:T(8,128)(2,1)S(1)}, bf16[48,4096]{1,0:T(8,128)(2,1)S(1)}, u32[]{:S(2)}, u32[]{:S(2)}) collective-permute-start(bf16[48,4096]{1,0:T(8,128)(2,1)S(1)} %get-tuple-element.58), channel_id=1, source_target_pairs={{0,3},{1,0},{2,1},{3,2},{4,7},{5,4},{6,5},{7,6},{8,11},{9,8},{10,9... | collective-permute-start | bytes 1179656 | tf_op jit(solution)/shard_map/ppermute | solution.py:41
  56.8 12.8 %collective-permute-done.10.refs_10_ = bf16[48,4096]{1,0:T(8,128)(2,1)S(1)} collective-permute-done((bf16[48,4096]{1,0:T(8,128)(2,1)S(1)}, bf16[48,4096]{1,0:T(8,128)(2,1)S(1)}, u32[]{:S(2)}, u32[]{:S(2)}) %collective-permute-start.10) | collective-permute-done | bytes 393248 | tf_op jit(solution)/shard_map/ppermute | solution.py:41
  69.6 3.4 %collective-permute-done.11.refs_11_ = bf16[48,4096]{1,0:T(8,128)(2,1)S(1)} collective-permute-done((bf16[48,4096]{1,0:T(8,128)(2,1)S(1)}, bf16[48,4096]{1,0:T(8,128)(2,1)S(1)}, u32[]{:S(2)}, u32[]{:S(2)}) %collective-permute-start.11) | collective-permute-done | bytes 393248 | tf_op jit(solution)/shard_map/ppermute | solution.py:41
  73.1 3.4 %collective-permute-done.9.refs_2_ = bf16[975,1000]{1,0:T(8,128)(2,1)} collective-permute-done((bf16[975,1000]{1,0:T(8,128)(2,1)S(1)}, bf16[975,1000]{1,0:T(8,128)(2,1)}, u32[]{:S(2)}, u32[]{:S(2)}) %collective-permute-start.9) | collective-permute-done | bytes 1950032 | tf_op jit(solution)/shard_map/ppermute | solution.py:41
  79.1 3.0 %collective-permute-start.16 = (bf16[32,4096]{1,0:T(8,128)(2,1)S(1)}, bf16[32,4096]{1,0:T(8,128)(2,1)S(1)}, u32[]{:S(2)}, u32[]{:S(2)}) collective-permute-start(bf16[32,4096]{1,0:T(8,128)(2,1)S(1)} %get-tuple-element.66), channel_id=1, source_target_pairs={{0,3},{1,0},{2,1},{3,2},{4,7},{5,4},{6,5},{7,6},{8,11},{9,8},{10,9... | collective-permute-start | bytes 786440 | tf_op jit(solution)/shard_map/ppermute | solution.py:41
  82.0 8.2 %reduce-precision_convert_fusion = (bf16[1000,128]{1,0:T(8,128)(2,1)S(1)}, bf16[1000,128]{1,0:T(8,128)(2,1)S(1)}) fusion(pred[128]{0:T(512)(128)(4,1)S(1)} %copy-done.15, bf16[128,7950]{1,0:T(8,128)(2,1)S(1)} %fusion, bf16[1000,7950]{1,0:T(8,128)(2,1)} %refs_3_.1), kind=kOutput, calls=%fused_computation.13 | convolution fusion | flops 2035968000 | bytes 18447328 | tf_op jit(solution)/shard_map/dot_general | solution.py:85
  91.1 2.7 %collective-permute-done.17.refs_16_ = bf16[32,4096]{1,0:T(8,128)(2,1)S(1)} collective-permute-done((bf16[32,4096]{1,0:T(8,128)(2,1)S(1)}, bf16[32,4096]{1,0:T(8,128)(2,1)S(1)}, u32[]{:S(2)}, u32[]{:S(2)}) %collective-permute-start.17) | collective-permute-done | bytes 262176 | tf_op jit(solution)/shard_map/ppermute | solution.py:41
  97.4 5.0 %collective-permute-done.18.refs_18_ = bf16[16,4096]{1,0:T(8,128)(2,1)S(1)} collective-permute-done((bf16[16,4096]{1,0:T(8,128)(2,1)S(1)}, bf16[16,4096]{1,0:T(8,128)(2,1)S(1)}, u32[]{:S(2)}, u32[]{:S(2)}) %collective-permute-start.18) | collective-permute-done | bytes 131104 | tf_op jit(solution)/shard_map/ppermute | solution.py:41
  102.4 3.9 %collective-permute-done.19.refs_19_ = bf16[16,4096]{1,0:T(8,128)(2,1)S(1)} collective-permute-done((bf16[16,4096]{1,0:T(8,128)(2,1)S(1)}, bf16[16,4096]{1,0:T(8,128)(2,1)S(1)}, u32[]{:S(2)}, u32[]{:S(2)}) %collective-permute-start.19) | collective-permute-done | bytes 131104 | tf_op jit(solution)/shard_map/ppermute | solution.py:41
  107.4 12.7 %shard_map.55 = (f32[128,1000]{1,0:T(8,128)}, bf16[128,1000]{1,0:T(8,128)(2,1)S(1)}, bf16[256,128]{1,0:T(8,128)(2,1)S(1)}) custom-call(bf16[16,4096]{1,0:T(8,128)(2,1)S(1)} %slice.70.refs_0_, bf16[16,4096]{1,0:T(8,128)(2,1)S(1)} %pad_add_fusion.refs_1_, bf16[16,4096]{1,0:T(8,128)(2,1)S(1)} %collective-permute-done.refs_2_, ...), custom_call_target="tpu_custom_call" | custom-call | tf_op jit(solution)/shard_map/pallas_call | solution.py:183
  123.2 3.1 %collective-permute-start.27 = (bf16[2,16,1000]{2,1,0:T(8,128)(2,1)S(1)}, bf16[2,16,1000]{2,1,0:T(8,128)(2,1)S(1)}, u32[]{:S(2)}, u32[]{:S(2)}) collective-permute-start(bf16[2,16,1000]{2,1,0:T(8,128)(2,1)S(1)} %get-tuple-element.90), channel_id=1, source_target_pairs={{0,96},{1,97},{2,98},{3,99},{4,100},{5,101},{6,102},{7,103},{8,104... | collective-permute-start | bytes 192008 | tf_op jit(solution)/shard_map/ppermute | solution.py:41
  126.5 24.4 %shard_map.56 = (f32[384,1000]{1,0:T(8,128)}, bf16[384,1000]{1,0:T(8,128)(2,1)S(1)}) custom-call(bf16[768,8064]{1,0:T(8,128)(2,1)} %all-gather.2.cloned.1.call-done.refs_0_, s32[3]{0:T(128)S(1)} %pad_add_fusion.1.refs_20_.refs_1_, bf16[1000,7950]{1,0:T(8,128)(2,1)} %refs_3_.1, bf16[1000,7950]{1,0:T(8,128)(2,1)} %refs_3_.1, bf16[1000,256]{1,0:T(8,128)(2,1)S(1)} %copy-done, ...), custom_call_target="tpu_custom_call" | custom-call | tf_op jit(solution)/shard_map/pallas_call | solution.py:183
  161.2 2.7 %collective-permute-done.30 = bf16[2,48,1000]{2,1,0:T(8,128)(2,1)S(1)} collective-permute-done((bf16[2,48,1000]{2,1,0:T(8,128)(2,1)S(1)}, bf16[2,48,1000]{2,1,0:T(8,128)(2,1)S(1)}, u32[]{:S(2)}, u32[]{:S(2)}) %collective-permute-start.30) | collective-permute-done | bytes 192032 | tf_op jit(solution)/shard_map/ppermute | solution.py:41
  164.8 3.7 %collective-permute-done.32 = bf16[2,48,1000]{2,1,0:T(8,128)(2,1)S(1)} collective-permute-done((bf16[2,48,1000]{2,1,0:T(8,128)(2,1)S(1)}, bf16[2,48,1000]{2,1,0:T(8,128)(2,1)S(1)}, u32[]{:S(2)}, u32[]{:S(2)}) %collective-permute-start.32) | collective-permute-done | bytes 192032 | tf_op jit(solution)/shard_map/ppermute | solution.py:41
  168.7 4.7 %shard_map.57 = bf16[4,128,975]{2,1,0:T(8,128)(2,1)S(1)} custom-call(bf16[128,1000]{1,0:T(8,128)(2,1)S(1)} %bitcast.94, bf16[975,1000]{1,0:T(8,128)(2,1)} %refs_0_, bf16[975,1000]{1,0:T(8,128)(2,1)} %copy-done.1, bf16[975,1000]{1,0:T(8,128)(2,1)} %collective-permute-done.9.refs_2_, bf16[975,1000]{1,0:T(8,128)(2,1)} %collective-permute-done.20.refs_3_), custom_call_target="tpu_custom_call" | custom-call | tf_op jit(solution)/shard_map/pallas_call | solution.py:215
  177.7 4.7 %shard_map.58 = bf16[4,128,975]{2,1,0:T(8,128)(2,1)S(1)} custom-call(bf16[128,1000]{1,0:T(8,128)(2,1)S(1)} %bitcast.95, bf16[975,1000]{1,0:T(8,128)(2,1)} %collective-permute-done.21.refs_0_, bf16[975,1000]{1,0:T(8,128)(2,1)} %collective-permute-done.22.refs_1_, bf16[975,1000]{1,0:T(8,128)(2,1)} %collective-permute-done.23.refs_2_, ...), custom_call_target="tpu_custom_call" | custom-call | tf_op jit(solution)/shard_map/pallas_call | solution.py:215
  188.9 5.9 %collective-permute-done.37 = bf16[4,32,975]{2,1,0:T(8,128)(2,1)S(1)} collective-permute-done((bf16[4,32,975]{2,1,0:T(8,128)(2,1)S(1)}, bf16[4,32,975]{2,1,0:T(8,128)(2,1)S(1)}, u32[]{:S(2)}, u32[]{:S(2)}) %collective-permute-start.37) | collective-permute-done | bytes 249632 | tf_op jit(solution)/shard_map/ppermute | solution.py:41
  195.2 3.2 %collective-permute-start.40 = (bf16[8,8,975]{2,1,0:T(8,128)(2,1)S(1)}, bf16[8,8,975]{2,1,0:T(8,128)(2,1)S(1)}, u32[]{:S(2)}, u32[]{:S(2)}) collective-permute-start(bf16[8,8,975]{2,1,0:T(8,128)(2,1)S(1)} %get-tuple-element.103), channel_id=1, source_target_pairs={{0,3},{1,0},{2,1},{3,2},{4,7},{5,4},{6,5},{7,6},{8,11},{9,8},{10,9... | collective-permute-start | bytes 374408 | tf_op jit(solution)/shard_map/ppermute | solution.py:41
  198.4 2.9 %collective-permute-done.39 = bf16[8,8,975]{2,1,0:T(8,128)(2,1)S(1)} collective-permute-done((bf16[8,8,975]{2,1,0:T(8,128)(2,1)S(1)}, bf16[8,8,975]{2,1,0:T(8,128)(2,1)S(1)}, u32[]{:S(2)}, u32[]{:S(2)}) %collective-permute-start.39) | collective-permute-done | bytes 124832 | tf_op jit(solution)/shard_map/ppermute | solution.py:41
  202.3 2.5 %collective-permute-done.41 = bf16[8,8,975]{2,1,0:T(8,128)(2,1)S(1)} collective-permute-done((bf16[8,8,975]{2,1,0:T(8,128)(2,1)S(1)}, bf16[8,8,975]{2,1,0:T(8,128)(2,1)S(1)}, u32[]{:S(2)}, u32[]{:S(2)}) %collective-permute-start.41) | collective-permute-done | bytes 124832 | tf_op jit(solution)/shard_map/ppermute | solution.py:41
  (160 shorter events, 66.0 us)
Async XLA Ops:
  6.5 116.6 %all-gather.2.cloned.1.call-start = ((), (), s32[]{:S(2)}) async-start(), calls=%async_computation.1 | async-start | bytes 13160448 | tf_op jit(solution)/shard_map/all_gather | solution.py:275
  9.7 24.6 %collective-permute-start = (bf16[16,4096]{1,0:T(8,128)(2,1)S(1)}, bf16[16,4096]{1,0:T(8,128)(2,1)S(1)}, u32[]{:S(2)}, u32[]{:S(2)}) collective-permute-start(bf16[16,4096]{1,0:T(8,128)(2,1)S(1)} %slice.70.refs_0_), channel_id=1, source_target_pairs={{0,1},{1,2},{2,3},{3,0},{4,5},{5,6},{6,7},{7,4},{8,9},{9,10},{10,1... | collective-permute-start | bytes 393224 | tf_op jit(solution)/shard_map/ppermute | solution.py:41
  11.3 24.5 %collective-permute-start.2 = (bf16[16,4096]{1,0:T(8,128)(2,1)S(1)}, bf16[16,4096]{1,0:T(8,128)(2,1)S(1)}, u32[]{:S(2)}, u32[]{:S(2)}) collective-permute-start(bf16[16,4096]{1,0:T(8,128)(2,1)S(1)} %slice.70.refs_0_), channel_id=1, source_target_pairs={{0,3},{1,0},{2,1},{3,2},{4,7},{5,4},{6,5},{7,6},{8,11},{9,8},{10,9... | collective-permute-start | bytes 393224 | tf_op jit(solution)/shard_map/ppermute | solution.py:41
  13.0 24.3 %collective-permute-start.3 = (bf16[16,4096]{1,0:T(8,128)(2,1)S(1)}, bf16[16,4096]{1,0:T(8,128)(2,1)S(1)}, u32[]{:S(2)}, u32[]{:S(2)}) collective-permute-start(bf16[16,4096]{1,0:T(8,128)(2,1)S(1)} %slice.70.refs_0_), channel_id=1, source_target_pairs={{0,4},{1,5},{2,6},{3,7},{4,8},{5,9},{6,10},{7,11},{8,12},{9,13},{1... | collective-permute-start | bytes 393224 | tf_op jit(solution)/shard_map/ppermute | solution.py:41
  15.7 13.5 %all-to-all-start = ((f32[8,72,128]{2,1,0:T(8,128)}), f32[8,72,128]{2,1,0:T(8,128)}, u32[]{:S(2)}, u32[]{:S(2)}) async-start(f32[8,72,128]{2,1,0:T(8,128)} %broadcast_in_dim.79), calls=%async_computation | async-start | bytes 589824 | tf_op jit(solution)/shard_map/all_to_all | solution.py:291
  21.1 29.0 %collective-permute-start.1 = (bf16[975,1000]{1,0:T(8,128)(2,1)}, bf16[975,1000]{1,0:T(8,128)(2,1)S(1)}, u32[]{:S(2)}, u32[]{:S(2)}) collective-permute-start(bf16[975,1000]{1,0:T(8,128)(2,1)} %refs_0_), channel_id=1, source_target_pairs={{0,32},{1,33},{2,34},{3,35},{4,36},{5,37},{6,38},{7,39},{8,40},{9,... | collective-permute-start | bytes 5850008 | tf_op jit(solution)/shard_map/ppermute | solution.py:41
  50.1 26.3 %collective-permute-start.9 = (bf16[975,1000]{1,0:T(8,128)(2,1)S(1)}, bf16[975,1000]{1,0:T(8,128)(2,1)}, u32[]{:S(2)}, u32[]{:S(2)}) collective-permute-start(bf16[975,1000]{1,0:T(8,128)(2,1)S(1)} %collective-permute-done.1.refs_1_), channel_id=1, source_target_pairs={{0,32},{1,33},{2,34},{3,35},{4,36},{5,37},{6,38},{7,39},{8,40},{9,... | collective-permute-start | bytes 5850008 | tf_op jit(solution)/shard_map/ppermute | solution.py:41
  50.1 19.5 %collective-permute-start.10 = (bf16[48,4096]{1,0:T(8,128)(2,1)S(1)}, bf16[48,4096]{1,0:T(8,128)(2,1)S(1)}, u32[]{:S(2)}, u32[]{:S(2)}) collective-permute-start(bf16[48,4096]{1,0:T(8,128)(2,1)S(1)} %get-tuple-element.55), channel_id=1, source_target_pairs={{0,4},{1,5},{2,6},{3,7},{4,8},{5,9},{6,10},{7,11},{8,12},{9,13},{1... | collective-permute-start | bytes 1179656 | tf_op jit(solution)/shard_map/ppermute | solution.py:41
  51.7 21.3 %collective-permute-start.11 = (bf16[48,4096]{1,0:T(8,128)(2,1)S(1)}, bf16[48,4096]{1,0:T(8,128)(2,1)S(1)}, u32[]{:S(2)}, u32[]{:S(2)}) collective-permute-start(bf16[48,4096]{1,0:T(8,128)(2,1)S(1)} %get-tuple-element.56), channel_id=1, source_target_pairs={{0,12},{1,13},{2,14},{3,15},{4,0},{5,1},{6,2},{7,3},{8,4},{9,5},{1... | collective-permute-start | bytes 1179656 | tf_op jit(solution)/shard_map/ppermute | solution.py:41
  52.1 20.9 %collective-permute-start.12 = (bf16[48,4096]{1,0:T(8,128)(2,1)S(1)}, bf16[48,4096]{1,0:T(8,128)(2,1)S(1)}, u32[]{:S(2)}, u32[]{:S(2)}) collective-permute-start(bf16[48,4096]{1,0:T(8,128)(2,1)S(1)} %get-tuple-element.57), channel_id=1, source_target_pairs={{0,1},{1,2},{2,3},{3,0},{4,5},{5,6},{6,7},{7,4},{8,9},{9,10},{10,1... | collective-permute-start | bytes 1179656 | tf_op jit(solution)/shard_map/ppermute | solution.py:41
  52.4 20.6 %collective-permute-start.13 = (bf16[48,4096]{1,0:T(8,128)(2,1)S(1)}, bf16[48,4096]{1,0:T(8,128)(2,1)S(1)}, u32[]{:S(2)}, u32[]{:S(2)}) collective-permute-start(bf16[48,4096]{1,0:T(8,128)(2,1)S(1)} %get-tuple-element.58), channel_id=1, source_target_pairs={{0,3},{1,0},{2,1},{3,2},{4,7},{5,4},{6,5},{7,6},{8,11},{9,8},{10,9... | collective-permute-start | bytes 1179656 | tf_op jit(solution)/shard_map/ppermute | solution.py:41
  76.4 29.8 %collective-permute-start.20 = (bf16[975,1000]{1,0:T(8,128)(2,1)}, bf16[975,1000]{1,0:T(8,128)(2,1)}, u32[]{:S(2)}, u32[]{:S(2)}) collective-permute-start(bf16[975,1000]{1,0:T(8,128)(2,1)} %collective-permute-done.9.refs_2_), channel_id=1, source_target_pairs={{0,32},{1,33},{2,34},{3,35},{4,36},{5,37},{6,38},{7,39},{8,40},{9,... | collective-permute-start | bytes 5850008 | tf_op jit(solution)/shard_map/ppermute | solution.py:41
  76.7 14.4 %collective-permute-start.14 = (bf16[32,4096]{1,0:T(8,128)(2,1)S(1)}, bf16[32,4096]{1,0:T(8,128)(2,1)S(1)}, u32[]{:S(2)}, u32[]{:S(2)}) collective-permute-start(bf16[32,4096]{1,0:T(8,128)(2,1)S(1)} %get-tuple-element.63), channel_id=1, source_target_pairs={{0,4},{1,5},{2,6},{3,7},{4,8},{5,9},{6,10},{7,11},{8,12},{9,13},{1... | collective-permute-start | bytes 786440 | tf_op jit(solution)/shard_map/ppermute | solution.py:41
  78.3 15.4 %collective-permute-start.17 = (bf16[32,4096]{1,0:T(8,128)(2,1)S(1)}, bf16[32,4096]{1,0:T(8,128)(2,1)S(1)}, u32[]{:S(2)}, u32[]{:S(2)}) collective-permute-start(bf16[32,4096]{1,0:T(8,128)(2,1)S(1)} %get-tuple-element.67), channel_id=1, source_target_pairs={{0,1},{1,2},{2,3},{3,0},{4,5},{5,6},{6,7},{7,4},{8,9},{9,10},{10,1... | collective-permute-start | bytes 786440 | tf_op jit(solution)/shard_map/ppermute | solution.py:41
  78.6 15.3 %collective-permute-start.15 = (bf16[32,4096]{1,0:T(8,128)(2,1)S(1)}, bf16[32,4096]{1,0:T(8,128)(2,1)S(1)}, u32[]{:S(2)}, u32[]{:S(2)}) collective-permute-start(bf16[32,4096]{1,0:T(8,128)(2,1)S(1)} %get-tuple-element.65), channel_id=1, source_target_pairs={{0,12},{1,13},{2,14},{3,15},{4,0},{5,1},{6,2},{7,3},{8,4},{9,5},{1... | collective-permute-start | bytes 786440 | tf_op jit(solution)/shard_map/ppermute | solution.py:41
  79.1 14.9 %collective-permute-start.16 = (bf16[32,4096]{1,0:T(8,128)(2,1)S(1)}, bf16[32,4096]{1,0:T(8,128)(2,1)S(1)}, u32[]{:S(2)}, u32[]{:S(2)}) collective-permute-start(bf16[32,4096]{1,0:T(8,128)(2,1)S(1)} %get-tuple-element.66), channel_id=1, source_target_pairs={{0,3},{1,0},{2,1},{3,2},{4,7},{5,4},{6,5},{7,6},{8,11},{9,8},{10,9... | collective-permute-start | bytes 786440 | tf_op jit(solution)/shard_map/ppermute | solution.py:41
  106.2 13.9 %collective-permute-start.21 = (bf16[975,1000]{1,0:T(8,128)(2,1)}, bf16[975,1000]{1,0:T(8,128)(2,1)}, u32[]{:S(2)}, u32[]{:S(2)}) collective-permute-start(bf16[975,1000]{1,0:T(8,128)(2,1)} %refs_0_), channel_id=1, source_target_pairs={{0,16},{1,17},{2,18},{3,19},{4,20},{5,21},{6,22},{7,23},{8,24},{9,... | collective-permute-start | bytes 5850008 | tf_op jit(solution)/shard_map/ppermute | solution.py:41
  106.3 13.9 %collective-permute-start.22 = (bf16[975,1000]{1,0:T(8,128)(2,1)}, bf16[975,1000]{1,0:T(8,128)(2,1)}, u32[]{:S(2)}, u32[]{:S(2)}) collective-permute-start(bf16[975,1000]{1,0:T(8,128)(2,1)} %copy-done.1), channel_id=1, source_target_pairs={{0,16},{1,17},{2,18},{3,19},{4,20},{5,21},{6,22},{7,23},{8,24},{9,... | collective-permute-start | bytes 5850008 | tf_op jit(solution)/shard_map/ppermute | solution.py:41
  106.8 13.4 %collective-permute-start.23 = (bf16[975,1000]{1,0:T(8,128)(2,1)}, bf16[975,1000]{1,0:T(8,128)(2,1)}, u32[]{:S(2)}, u32[]{:S(2)}) collective-permute-start(bf16[975,1000]{1,0:T(8,128)(2,1)} %collective-permute-done.9.refs_2_), channel_id=1, source_target_pairs={{0,16},{1,17},{2,18},{3,19},{4,20},{5,21},{6,22},{7,23},{8,24},{9,... | collective-permute-start | bytes 5850008 | tf_op jit(solution)/shard_map/ppermute | solution.py:41
  106.9 13.3 %collective-permute-start.24 = (bf16[975,1000]{1,0:T(8,128)(2,1)}, bf16[975,1000]{1,0:T(8,128)(2,1)}, u32[]{:S(2)}, u32[]{:S(2)}) collective-permute-start(bf16[975,1000]{1,0:T(8,128)(2,1)} %collective-permute-done.20.refs_3_), channel_id=1, source_target_pairs={{0,16},{1,17},{2,18},{3,19},{4,20},{5,21},{6,22},{7,23},{8,24},{9,... | collective-permute-start | bytes 5850008 | tf_op jit(solution)/shard_map/ppermute | solution.py:41
  123.1 27.7 %collective-permute-start.26 = (bf16[2,16,1000]{2,1,0:T(8,128)(2,1)S(1)}, bf16[2,16,1000]{2,1,0:T(8,128)(2,1)S(1)}, u32[]{:S(2)}, u32[]{:S(2)}) collective-permute-start(bf16[2,16,1000]{2,1,0:T(8,128)(2,1)S(1)} %get-tuple-element.89), channel_id=1, source_target_pairs={{0,32},{1,33},{2,34},{3,35},{4,36},{5,37},{6,38},{7,39},{8,40},{9,... | collective-permute-start | bytes 192008 | tf_op jit(solution)/shard_map/ppermute | solution.py:41
  123.2 27.6 %collective-permute-start.27 = (bf16[2,16,1000]{2,1,0:T(8,128)(2,1)S(1)}, bf16[2,16,1000]{2,1,0:T(8,128)(2,1)S(1)}, u32[]{:S(2)}, u32[]{:S(2)}) collective-permute-start(bf16[2,16,1000]{2,1,0:T(8,128)(2,1)S(1)} %get-tuple-element.90), channel_id=1, source_target_pairs={{0,96},{1,97},{2,98},{3,99},{4,100},{5,101},{6,102},{7,103},{8,104... | collective-permute-start | bytes 192008 | tf_op jit(solution)/shard_map/ppermute | solution.py:41
  126.4 24.5 %collective-permute-start.28 = (bf16[2,16,1000]{2,1,0:T(8,128)(2,1)S(1)}, bf16[2,16,1000]{2,1,0:T(8,128)(2,1)S(1)}, u32[]{:S(2)}, u32[]{:S(2)}) collective-permute-start(bf16[2,16,1000]{2,1,0:T(8,128)(2,1)S(1)} %get-tuple-element.91), channel_id=1, source_target_pairs={{0,64},{1,65},{2,66},{3,67},{4,68},{5,69},{6,70},{7,71},{8,72},{9,... | collective-permute-start | bytes 192008 | tf_op jit(solution)/shard_map/ppermute | solution.py:41
  173.5 11.0 %collective-permute-start.33 = (bf16[4,32,975]{2,1,0:T(8,128)(2,1)S(1)}, bf16[4,32,975]{2,1,0:T(8,128)(2,1)S(1)}, u32[]{:S(2)}, u32[]{:S(2)}) collective-permute-start(bf16[4,32,975]{2,1,0:T(8,128)(2,1)S(1)} %get-tuple-element.105), channel_id=1, source_target_pairs={{0,4},{1,5},{2,6},{3,7},{4,8},{5,9},{6,10},{7,11},{8,12},{9,13},{1... | collective-permute-start | bytes 748808 | tf_op jit(solution)/shard_map/ppermute | solution.py:41
  (38 other events, 376.1 us)
Sparse Core Ops, SparseCore 0:
  9.8 113.2 all-gather.1

commit v10 on v9

--- a/solution.py
+++ b/solution.py
@@ -237,16 +237,21 @@
     return [pick(0)] + [pick(d).astype(jnp.bfloat16) for d in (1, 3, 2)]
 
 
-def sums_by_z(picked):
-    pieces = picked[:1] + [send(v, hop_z(d)) for v, d in zip(picked[1:], (1, 3, 2))]
-    return total(pieces).astype(jnp.bfloat16)
-
-
-def owned(blocks, here, hop):
-    def pick(d):
-        return lax.dynamic_index_in_dim(blocks, (here + d) % SIDE, 1, keepdims=False)
-
-    return [pick(0)] + [send(pick(d).astype(jnp.bfloat16), hop(d)) for d in (1, 3, 2)]
+def spread_by_z(picked):
+    return picked[:1] + [send(v, hop_z(d)) for v, d in zip(picked[1:], (1, 3, 2))]
+
+
+def cut(blocks, here):
+    return [
+        lax.dynamic_index_in_dim(blocks, (here + d) % SIDE, 1, keepdims=False)
+        for d in (0, 1, 3, 2)
+    ]
+
+
+def owned(pieces, hop):
+    return pieces[:1] + [
+        send(v.astype(jnp.bfloat16), hop(d)) for v, d in zip(pieces[1:], (1, 3, 2))
+    ]
 
 
 def total(pieces):
@@ -305,15 +310,20 @@
     send_d = together(a_l, a_r, b_u)
     send_r = together(b_d, b_u, a_l)
     send_l = together(b_d, b_u, b_r)
-    fits[1], send_u, send_d, send_r, send_l, a_u, b_l = after(
-        fits[1], send_u, send_d, send_r, send_l, a_u, b_l
+    fits[1], member, send_u, send_d, send_r, send_l, a_u, b_l = after(
+        fits[1], member, send_u, send_d, send_r, send_l, a_u, b_l
     )
     fits.append(ring_z(fits[-1]))
     one_d, one_u = up(send_u), down(send_d)
     one_l, one_r = right(send_r), left(send_l)
 
-    member, fits[2], one_d, one_u, one_l, one_r = after(
-        member, fits[2], one_d, one_u, one_l, one_r
+    rw = -nt(reconstructor, member)
+    rw_high = lax.reduce_precision(rw, 8, 7)
+    rw_low = jnp.where((lane % LANES < 12)[None, :], rw - rw_high, 0.0)
+    rw = jnp.concatenate([rw_high, rw_low], axis=1).astype(jnp.bfloat16)
+
+    rw, fits[2], one_d, one_u, one_l, one_r = after(
+        rw, fits[2], one_d, one_u, one_l, one_r
     )
     fits.append(ring_z(fits[-1]))
     far_x_a, far_y_b = one_l[2 * PART :], one_u[2 * PART :]
@@ -324,12 +334,8 @@
     two_d, two_u, two_l, two_r = after(two_d, two_u, two_l, two_r)
     get_d, get_u = up(two_d), down(two_u)
     get_l, get_r = right(two_l), left(two_r)
-    rw = -nt(reconstructor, member)
-    rw_high = lax.reduce_precision(rw, 8, 7)
-    rw_low = jnp.where((lane % LANES < 12)[None, :], rw - rw_high, 0.0)
-    rw = jnp.concatenate([rw_high, rw_low], axis=1).astype(jnp.bfloat16)
-
-    rw, get_u, get_r, *ends = after(rw, get_u, get_r, get_d[:PART], get_l[:PART])
+
+    get_u, get_r, *ends = after(get_u, get_r, get_d[:PART], get_l[:PART])
     end_d, end_l = up(ends[0]), right(ends[1])
     end_d, end_l, *fits = after(end_d, end_l, *fits)
 
@@ -365,25 +371,28 @@
     swapped = [swap_core(f) for f in fits]
     own, other, *swapped = after(own, other, *swapped)
     picked = picks_by_z(own, other, z)
-    *picked, late = after(*picked, late)
-    near = sums_by_z(picked)
+    terms = spread_by_z(picked)
+    terms[0], late = after(terms[0], late)
+    near = total(terms).astype(jnp.bfloat16)
 
     own, other = reconstruct(
         1, [late], [(0, 0, 16 * LATE, 0, 0, side) for side in (0, 1)],
         position, reconstructor, rw, tail,
     )
     own, other, near = after(own, other, near)
-    far = sums_by_z(picks_by_z(own, other, z))
+    far = total(spread_by_z(picks_by_z(own, other, z))).astype(jnp.bfloat16)
     points = jnp.concatenate([near, far], axis=1)
 
     rows = points.reshape(SIDE, SIDE, 8, width_p)
     rows = jnp.where(c == 0, rows, jnp.swapaxes(rows, 0, 1)).reshape(2 * ROWS, width_p)
     one = jnp.where(c == 0, y, x)
     two = jnp.where(c == 0, x, y)
-    half_a = owned(fit(rows, fits).reshape(4, SIDE, SIDE * 8, act), one, hop_one)
-    half_b = owned(fit(rows, swapped).reshape(4, SIDE, SIDE * 8, act), one, hop_one)
+    half_a = cut(fit(rows, fits).reshape(4, SIDE, SIDE * 8, act), one)
+    half_a = owned(half_a, hop_one)
+    half_b = cut(fit(rows, swapped).reshape(4, SIDE, SIDE * 8, act), one)
+    half_b = owned(half_b, hop_one)
     both = jnp.concatenate([total(half_a), total(half_b)], axis=0)
-    done = total(owned(both.reshape(8, SIDE, 8, act), two, hop_two))
+    done = total(owned(cut(both.reshape(8, SIDE, 8, act), two), hop_two))
 
     sens = lax.iota(jnp.int32, 8)
     step = jnp.where(sens % 2 == 0, z - sens // 2, sens // 2 - z) % SIDE

time: 215 us -> 213 us (level)
  waiting for transfers between devices: 72.6 us -> 78.1 us
  other arithmetic: 12.1 us -> 7.49 us
    ppermute x42, waiting for transfers between devices: 67.7 us -> 72.2 us  [send(): return lax.ppermute(x, AXES, moved(fn))]
  transfers between devices with their start and end apart: 44 -> 44, of which waited for: 23 -> 24; matrix products, arithmetic and copies ran while one was open for 9% -> 6% of each run, Pallas kernels for 20% -> 20%
where the time goes in v10:
time: 213 us; the launch traced here: 212 us
  waiting for transfers between devices  78.1 us (37%)
  starting transfers between devices  51.5 us (24%)
  Pallas kernels  46.5 us (22%)
  between operations  14 us (7%)
  matrix products  9.2 us (4%)
  other arithmetic  7.49 us (4%)
  local copies, waits for them, and re-layouts  5 us (2%)
    ppermute x42, waiting for transfers between devices, send(): return lax.ppermute(x, AXES, moved(fn))  72.2 us
    ppermute x42, starting transfers between devices, send(): return lax.ppermute(x, AXES, moved(fn))  46.1 us
    pallas_call x2, Pallas kernels, reconstruct(): pl.pallas_call(functools.partial(reconstruct_kernel, tuple(pieces), len(a...  37.1 us
    pallas_call x2, Pallas kernels, fit(): pl.pallas_call(fit_kernel, in_specs=[pl.BlockSpec(memory_space=pltpu.VMEM...  9.38 us
    dot_general x2, matrix products, nt(): lax.dot_general(a, b, (((1,), (1,)), ((), ())), preferred_element_type=jn...  9.2 us
    all_to_all x1, waiting for transfers between devices, per_device(): stats = jnp.sum(lax.all_to_all(stats, 'sens', 0, 0, tiled=True), axis=0)  5.91 us
    all_to_all x1, starting transfers between devices, per_device(): stats = jnp.sum(lax.all_to_all(stats, 'sens', 0, 0, tiled=True), axis=0)  5.4 us
  transfers between devices with their start and end apart: 44, of which 24 were waited for; matrix products, arithmetic and copies ran while one was open for 6% of the time, Pallas kernels for 20%

profile of v10, /device:TPU:24, one launch (start us, length us, event | category | flops | bytes accessed | tf_op | source)
XLA Modules:
  0.0 211.8 jit_solution(11191010333188932865)
XLA Ops:
  15.1 5.4 %all-to-all-start = ((f32[8,72,128]{2,1,0:T(8,128)}), f32[8,72,128]{2,1,0:T(8,128)S(1)}, u32[]{:S(2)}, u32[]{:S(2)}) async-start(f32[8,72,128]{2,1,0:T(8,128)} %broadcast_in_dim.79), calls=%async_computation | async-start | bytes 589824 | tf_op jit(solution)/shard_map/all_to_all | solution.py:296
  22.6 5.9 %all-to-all-done = f32[8,72,128]{2,1,0:T(8,128)S(1)} async-done(((f32[8,72,128]{2,1,0:T(8,128)}), f32[8,72,128]{2,1,0:T(8,128)S(1)}, u32[]{:S(2)}, u32[]{:S(2)}) %all-to-all-start) | async-done | bytes 294944 | tf_op jit(solution)/shard_map/all_to_all | solution.py:296
  34.8 4.2 %collective-permute-done.4.refs_9_ = bf16[16,4096]{1,0:T(8,128)(2,1)S(1)} collective-permute-done((bf16[16,4096]{1,0:T(8,128)(2,1)S(1)}, bf16[16,4096]{1,0:T(8,128)(2,1)S(1)}, u32[]{:S(2)}, u32[]{:S(2)}) %collective-permute-start.4) | collective-permute-done | bytes 131104 | tf_op jit(solution)/shard_map/ppermute | solution.py:41
  40.2 3.3 %collective-permute-done.7.refs_8_ = bf16[16,4096]{1,0:T(8,128)(2,1)S(1)} collective-permute-done((bf16[16,4096]{1,0:T(8,128)(2,1)S(1)}, bf16[16,4096]{1,0:T(8,128)(2,1)S(1)}, u32[]{:S(2)}, u32[]{:S(2)}) %collective-permute-start.7) | collective-permute-done | bytes 131104 | tf_op jit(solution)/shard_map/ppermute | solution.py:41
  45.2 4.4 %collective-permute-done.1.refs_1_ = bf16[975,1000]{1,0:T(8,128)(2,1)} collective-permute-done((bf16[975,1000]{1,0:T(8,128)(2,1)}, bf16[975,1000]{1,0:T(8,128)(2,1)}, u32[]{:S(2)}, u32[]{:S(2)}) %collective-permute-start.1) | collective-permute-done | bytes 1950032 | tf_op jit(solution)/shard_map/ppermute | solution.py:41
  51.9 3.0 %collective-permute-start.13 = (bf16[48,4096]{1,0:T(8,128)(2,1)S(1)}, bf16[48,4096]{1,0:T(8,128)(2,1)S(1)}, u32[]{:S(2)}, u32[]{:S(2)}) collective-permute-start(bf16[48,4096]{1,0:T(8,128)(2,1)S(1)} %get-tuple-element.56), channel_id=1, source_target_pairs={{0,3},{1,0},{2,1},{3,2},{4,7},{5,4},{6,5},{7,6},{8,11},{9,8},{10,9... | collective-permute-start | bytes 1179656 | tf_op jit(solution)/shard_map/ppermute | solution.py:41
  54.9 8.1 %reduce-precision_convert_fusion = (bf16[1000,128]{1,0:T(8,128)(2,1)S(1)}, bf16[1000,128]{1,0:T(8,128)(2,1)S(1)}) fusion(pred[128]{0:T(512)(128)(4,1)S(1)} %get-tuple-element.122, bf16[128,7950]{1,0:T(8,128)(2,1)S(1)} %fusion, bf16[1000,7950]{1,0:T(8,128)(2,1)} %refs_3_.1), kind=kOutput, calls=%fused_computation.13 | convolution fusion | flops 2035968000 | bytes 18447328 | tf_op jit(solution)/shard_map/dot_general | solution.py:85
  63.9 4.7 %collective-permute-done.10.refs_10_ = bf16[48,4096]{1,0:T(8,128)(2,1)S(1)} collective-permute-done((bf16[48,4096]{1,0:T(8,128)(2,1)S(1)}, bf16[48,4096]{1,0:T(8,128)(2,1)S(1)}, u32[]{:S(2)}, u32[]{:S(2)}) %collective-permute-start.10) | collective-permute-done | bytes 393248 | tf_op jit(solution)/shard_map/ppermute | solution.py:41
  68.6 3.9 %collective-permute-done.11.refs_11_ = bf16[48,4096]{1,0:T(8,128)(2,1)S(1)} collective-permute-done((bf16[48,4096]{1,0:T(8,128)(2,1)S(1)}, bf16[48,4096]{1,0:T(8,128)(2,1)S(1)}, u32[]{:S(2)}, u32[]{:S(2)}) %collective-permute-start.11) | collective-permute-done | bytes 393248 | tf_op jit(solution)/shard_map/ppermute | solution.py:41
  72.5 3.6 %collective-permute-done.9.refs_2_ = bf16[975,1000]{1,0:T(8,128)(2,1)} collective-permute-done((bf16[975,1000]{1,0:T(8,128)(2,1)}, bf16[975,1000]{1,0:T(8,128)(2,1)}, u32[]{:S(2)}, u32[]{:S(2)}) %collective-permute-start.9) | collective-permute-done | bytes 1950032 | tf_op jit(solution)/shard_map/ppermute | solution.py:41
  78.7 3.0 %collective-permute-start.16 = (bf16[32,4096]{1,0:T(8,128)(2,1)S(1)}, bf16[32,4096]{1,0:T(8,128)(2,1)S(1)}, u32[]{:S(2)}, u32[]{:S(2)}) collective-permute-start(bf16[32,4096]{1,0:T(8,128)(2,1)S(1)} %get-tuple-element.63), channel_id=1, source_target_pairs={{0,3},{1,0},{2,1},{3,2},{4,7},{5,4},{6,5},{7,6},{8,11},{9,8},{10,9... | collective-permute-start | bytes 786440 | tf_op jit(solution)/shard_map/ppermute | solution.py:41
  81.7 9.1 %collective-permute-done.14.refs_14_ = bf16[32,4096]{1,0:T(8,128)(2,1)S(1)} collective-permute-done((bf16[32,4096]{1,0:T(8,128)(2,1)S(1)}, bf16[32,4096]{1,0:T(8,128)(2,1)S(1)}, u32[]{:S(2)}, u32[]{:S(2)}) %collective-permute-start.14) | collective-permute-done | bytes 262176 | tf_op jit(solution)/shard_map/ppermute | solution.py:41
  90.8 2.7 %collective-permute-done.17.refs_16_ = bf16[32,4096]{1,0:T(8,128)(2,1)S(1)} collective-permute-done((bf16[32,4096]{1,0:T(8,128)(2,1)S(1)}, bf16[32,4096]{1,0:T(8,128)(2,1)S(1)}, u32[]{:S(2)}, u32[]{:S(2)}) %collective-permute-start.17) | collective-permute-done | bytes 262176 | tf_op jit(solution)/shard_map/ppermute | solution.py:41
  97.1 5.5 %collective-permute-done.18.refs_18_ = bf16[16,4096]{1,0:T(8,128)(2,1)S(1)} collective-permute-done((bf16[16,4096]{1,0:T(8,128)(2,1)S(1)}, bf16[16,4096]{1,0:T(8,128)(2,1)S(1)}, u32[]{:S(2)}, u32[]{:S(2)}) %collective-permute-start.18) | collective-permute-done | bytes 131104 | tf_op jit(solution)/shard_map/ppermute | solution.py:41
  102.5 3.4 %collective-permute-done.19.refs_19_ = bf16[16,4096]{1,0:T(8,128)(2,1)S(1)} collective-permute-done((bf16[16,4096]{1,0:T(8,128)(2,1)S(1)}, bf16[16,4096]{1,0:T(8,128)(2,1)S(1)}, u32[]{:S(2)}, u32[]{:S(2)}) %collective-permute-start.19) | collective-permute-done | bytes 131104 | tf_op jit(solution)/shard_map/ppermute | solution.py:41
  107.1 12.7 %shard_map.55 = (f32[128,1000]{1,0:T(8,128)}, bf16[128,1000]{1,0:T(8,128)(2,1)S(1)}, bf16[256,128]{1,0:T(8,128)(2,1)S(1)}) custom-call(bf16[16,4096]{1,0:T(8,128)(2,1)S(1)} %slice.70.refs_0_, bf16[16,4096]{1,0:T(8,128)(2,1)S(1)} %pad_add_fusion.refs_1_, bf16[16,4096]{1,0:T(8,128)(2,1)S(1)} %collective-permute-done.refs_2_, ...), custom_call_target="tpu_custom_call" | custom-call | tf_op jit(solution)/shard_map/pallas_call | solution.py:183
  122.8 3.2 %collective-permute-start.27 = (bf16[2,16,1000]{2,1,0:T(8,128)(2,1)S(1)}, bf16[2,16,1000]{2,1,0:T(8,128)(2,1)S(1)}, u32[]{:S(2)}, u32[]{:S(2)}) collective-permute-start(bf16[2,16,1000]{2,1,0:T(8,128)(2,1)S(1)} %get-tuple-element.107), channel_id=1, source_target_pairs={{0,96},{1,97},{2,98},{3,99},{4,100},{5,101},{6,102},{7,103},{8,104... | collective-permute-start | bytes 192008 | tf_op jit(solution)/shard_map/ppermute | solution.py:41
  126.0 24.4 %shard_map.56 = (f32[384,1000]{1,0:T(8,128)}, bf16[384,1000]{1,0:T(8,128)(2,1)S(1)}) custom-call(bf16[768,8064]{1,0:T(8,128)(2,1)} %all-gather.2.cloned.1.call-done.refs_0_, s32[3]{0:T(128)S(1)} %pad_add_fusion.1.refs_20_.refs_1_, bf16[1000,7950]{1,0:T(8,128)(2,1)} %refs_3_.1, bf16[1000,7950]{1,0:T(8,128)(2,1)} %refs_3_.1, bf16[1000,256]{1,0:T(8,128)(2,1)S(1)} %copy-done, ...), custom_call_target="tpu_custom_call" | custom-call | tf_op jit(solution)/shard_map/pallas_call | solution.py:183
  164.5 3.7 %collective-permute-done.32 = bf16[2,48,1000]{2,1,0:T(8,128)(2,1)S(1)} collective-permute-done((bf16[2,48,1000]{2,1,0:T(8,128)(2,1)S(1)}, bf16[2,48,1000]{2,1,0:T(8,128)(2,1)S(1)}, u32[]{:S(2)}, u32[]{:S(2)}) %collective-permute-start.32) | collective-permute-done | bytes 192032 | tf_op jit(solution)/shard_map/ppermute | solution.py:41
  168.4 4.7 %shard_map.57 = bf16[4,128,975]{2,1,0:T(8,128)(2,1)S(1)} custom-call(bf16[128,1000]{1,0:T(8,128)(2,1)S(1)} %bitcast.94, bf16[975,1000]{1,0:T(8,128)(2,1)} %refs_0_, bf16[975,1000]{1,0:T(8,128)(2,1)} %collective-permute-done.1.refs_1_, bf16[975,1000]{1,0:T(8,128)(2,1)} %collective-permute-done.9.refs_2_, bf16[975,1000]{1,0:T(8,128)(2,1)} %collective-permute-done.20.refs_3_), custom_call_target="tpu_custom_call" | custom-call | tf_op jit(solution)/shard_map/pallas_call | solution.py:215
  176.4 4.7 %shard_map.58 = bf16[4,128,975]{2,1,0:T(8,128)(2,1)S(1)} custom-call(bf16[128,1000]{1,0:T(8,128)(2,1)S(1)} %bitcast.95, bf16[975,1000]{1,0:T(8,128)(2,1)} %collective-permute-done.21.refs_0_, bf16[975,1000]{1,0:T(8,128)(2,1)} %collective-permute-done.22.refs_1_, bf16[975,1000]{1,0:T(8,128)(2,1)} %collective-permute-done.23.refs_2_, ...), custom_call_target="tpu_custom_call" | custom-call | tf_op jit(solution)/shard_map/pallas_call | solution.py:215
  187.6 5.6 %collective-permute-done.37 = bf16[4,32,975]{2,1,0:T(8,128)(2,1)S(1)} collective-permute-done((bf16[4,32,975]{2,1,0:T(8,128)(2,1)S(1)}, bf16[4,32,975]{2,1,0:T(8,128)(2,1)S(1)}, u32[]{:S(2)}, u32[]{:S(2)}) %collective-permute-start.37) | collective-permute-done | bytes 249632 | tf_op jit(solution)/shard_map/ppermute | solution.py:41
  193.6 3.2 %collective-permute-start.40 = (bf16[8,8,975]{2,1,0:T(8,128)(2,1)S(1)}, bf16[8,8,975]{2,1,0:T(8,128)(2,1)S(1)}, u32[]{:S(2)}, u32[]{:S(2)}) collective-permute-start(bf16[8,8,975]{2,1,0:T(8,128)(2,1)S(1)} %get-tuple-element.97), channel_id=1, source_target_pairs={{0,3},{1,0},{2,1},{3,2},{4,7},{5,4},{6,5},{7,6},{8,11},{9,8},{10,9... | collective-permute-start | bytes 374408 | tf_op jit(solution)/shard_map/ppermute | solution.py:41
  197.0 2.8 %collective-permute-done.39 = bf16[8,8,975]{2,1,0:T(8,128)(2,1)S(1)} collective-permute-done((bf16[8,8,975]{2,1,0:T(8,128)(2,1)S(1)}, bf16[8,8,975]{2,1,0:T(8,128)(2,1)S(1)}, u32[]{:S(2)}, u32[]{:S(2)}) %collective-permute-start.39) | collective-permute-done | bytes 124832 | tf_op jit(solution)/shard_map/ppermute | solution.py:41
  (146 shorter events, 62.8 us)
Async XLA Ops:
  6.5 119.5 %all-gather.2.cloned.1.call-start = ((), (), s32[]{:S(2)}) async-start(), calls=%async_computation.1 | async-start | bytes 13160448 | tf_op jit(solution)/shard_map/all_gather | solution.py:280
  9.7 20.7 %collective-permute-start = (bf16[16,4096]{1,0:T(8,128)(2,1)S(1)}, bf16[16,4096]{1,0:T(8,128)(2,1)S(1)}, u32[]{:S(2)}, u32[]{:S(2)}) collective-permute-start(bf16[16,4096]{1,0:T(8,128)(2,1)S(1)} %slice.70.refs_0_), channel_id=1, source_target_pairs={{0,1},{1,2},{2,3},{3,0},{4,5},{5,6},{6,7},{7,4},{8,9},{9,10},{10,1... | collective-permute-start | bytes 393224 | tf_op jit(solution)/shard_map/ppermute | solution.py:41
  11.3 20.6 %collective-permute-start.2 = (bf16[16,4096]{1,0:T(8,128)(2,1)S(1)}, bf16[16,4096]{1,0:T(8,128)(2,1)S(1)}, u32[]{:S(2)}, u32[]{:S(2)}) collective-permute-start(bf16[16,4096]{1,0:T(8,128)(2,1)S(1)} %slice.70.refs_0_), channel_id=1, source_target_pairs={{0,3},{1,0},{2,1},{3,2},{4,7},{5,4},{6,5},{7,6},{8,11},{9,8},{10,9... | collective-permute-start | bytes 393224 | tf_op jit(solution)/shard_map/ppermute | solution.py:41
  13.0 21.1 %collective-permute-start.3 = (bf16[16,4096]{1,0:T(8,128)(2,1)S(1)}, bf16[16,4096]{1,0:T(8,128)(2,1)S(1)}, u32[]{:S(2)}, u32[]{:S(2)}) collective-permute-start(bf16[16,4096]{1,0:T(8,128)(2,1)S(1)} %slice.70.refs_0_), channel_id=1, source_target_pairs={{0,4},{1,5},{2,6},{3,7},{4,8},{5,9},{6,10},{7,11},{8,12},{9,13},{1... | collective-permute-start | bytes 393224 | tf_op jit(solution)/shard_map/ppermute | solution.py:41
  15.1 13.4 %all-to-all-start = ((f32[8,72,128]{2,1,0:T(8,128)}), f32[8,72,128]{2,1,0:T(8,128)S(1)}, u32[]{:S(2)}, u32[]{:S(2)}) async-start(f32[8,72,128]{2,1,0:T(8,128)} %broadcast_in_dim.79), calls=%async_computation | async-start | bytes 589824 | tf_op jit(solution)/shard_map/all_to_all | solution.py:296
  20.5 29.1 %collective-permute-start.1 = (bf16[975,1000]{1,0:T(8,128)(2,1)}, bf16[975,1000]{1,0:T(8,128)(2,1)}, u32[]{:S(2)}, u32[]{:S(2)}) collective-permute-start(bf16[975,1000]{1,0:T(8,128)(2,1)} %refs_0_), channel_id=1, source_target_pairs={{0,32},{1,33},{2,34},{3,35},{4,36},{5,37},{6,38},{7,39},{8,40},{9,... | collective-permute-start | bytes 5850008 | tf_op jit(solution)/shard_map/ppermute | solution.py:41
  49.6 26.5 %collective-permute-start.9 = (bf16[975,1000]{1,0:T(8,128)(2,1)}, bf16[975,1000]{1,0:T(8,128)(2,1)}, u32[]{:S(2)}, u32[]{:S(2)}) collective-permute-start(bf16[975,1000]{1,0:T(8,128)(2,1)} %collective-permute-done.1.refs_1_), channel_id=1, source_target_pairs={{0,32},{1,33},{2,34},{3,35},{4,36},{5,37},{6,38},{7,39},{8,40},{9,... | collective-permute-start | bytes 5850008 | tf_op jit(solution)/shard_map/ppermute | solution.py:41
  49.6 19.0 %collective-permute-start.10 = (bf16[48,4096]{1,0:T(8,128)(2,1)S(1)}, bf16[48,4096]{1,0:T(8,128)(2,1)S(1)}, u32[]{:S(2)}, u32[]{:S(2)}) collective-permute-start(bf16[48,4096]{1,0:T(8,128)(2,1)S(1)} %get-tuple-element.53), channel_id=1, source_target_pairs={{0,4},{1,5},{2,6},{3,7},{4,8},{5,9},{6,10},{7,11},{8,12},{9,13},{1... | collective-permute-start | bytes 1179656 | tf_op jit(solution)/shard_map/ppermute | solution.py:41
  51.2 21.3 %collective-permute-start.11 = (bf16[48,4096]{1,0:T(8,128)(2,1)S(1)}, bf16[48,4096]{1,0:T(8,128)(2,1)S(1)}, u32[]{:S(2)}, u32[]{:S(2)}) collective-permute-start(bf16[48,4096]{1,0:T(8,128)(2,1)S(1)} %get-tuple-element.54), channel_id=1, source_target_pairs={{0,12},{1,13},{2,14},{3,15},{4,0},{5,1},{6,2},{7,3},{8,4},{9,5},{1... | collective-permute-start | bytes 1179656 | tf_op jit(solution)/shard_map/ppermute | solution.py:41
  51.6 20.9 %collective-permute-start.12 = (bf16[48,4096]{1,0:T(8,128)(2,1)S(1)}, bf16[48,4096]{1,0:T(8,128)(2,1)S(1)}, u32[]{:S(2)}, u32[]{:S(2)}) collective-permute-start(bf16[48,4096]{1,0:T(8,128)(2,1)S(1)} %get-tuple-element.55), channel_id=1, source_target_pairs={{0,1},{1,2},{2,3},{3,0},{4,5},{5,6},{6,7},{7,4},{8,9},{9,10},{10,1... | collective-permute-start | bytes 1179656 | tf_op jit(solution)/shard_map/ppermute | solution.py:41
  51.9 20.6 %collective-permute-start.13 = (bf16[48,4096]{1,0:T(8,128)(2,1)S(1)}, bf16[48,4096]{1,0:T(8,128)(2,1)S(1)}, u32[]{:S(2)}, u32[]{:S(2)}) collective-permute-start(bf16[48,4096]{1,0:T(8,128)(2,1)S(1)} %get-tuple-element.56), channel_id=1, source_target_pairs={{0,3},{1,0},{2,1},{3,2},{4,7},{5,4},{6,5},{7,6},{8,11},{9,8},{10,9... | collective-permute-start | bytes 1179656 | tf_op jit(solution)/shard_map/ppermute | solution.py:41
  76.1 29.8 %collective-permute-start.20 = (bf16[975,1000]{1,0:T(8,128)(2,1)}, bf16[975,1000]{1,0:T(8,128)(2,1)}, u32[]{:S(2)}, u32[]{:S(2)}) collective-permute-start(bf16[975,1000]{1,0:T(8,128)(2,1)} %collective-permute-done.9.refs_2_), channel_id=1, source_target_pairs={{0,32},{1,33},{2,34},{3,35},{4,36},{5,37},{6,38},{7,39},{8,40},{9,... | collective-permute-start | bytes 5850008 | tf_op jit(solution)/shard_map/ppermute | solution.py:41
  76.4 14.4 %collective-permute-start.14 = (bf16[32,4096]{1,0:T(8,128)(2,1)S(1)}, bf16[32,4096]{1,0:T(8,128)(2,1)S(1)}, u32[]{:S(2)}, u32[]{:S(2)}) collective-permute-start(bf16[32,4096]{1,0:T(8,128)(2,1)S(1)} %get-tuple-element.61), channel_id=1, source_target_pairs={{0,4},{1,5},{2,6},{3,7},{4,8},{5,9},{6,10},{7,11},{8,12},{9,13},{1... | collective-permute-start | bytes 786440 | tf_op jit(solution)/shard_map/ppermute | solution.py:41
  78.0 15.4 %collective-permute-start.17 = (bf16[32,4096]{1,0:T(8,128)(2,1)S(1)}, bf16[32,4096]{1,0:T(8,128)(2,1)S(1)}, u32[]{:S(2)}, u32[]{:S(2)}) collective-permute-start(bf16[32,4096]{1,0:T(8,128)(2,1)S(1)} %get-tuple-element.64), channel_id=1, source_target_pairs={{0,1},{1,2},{2,3},{3,0},{4,5},{5,6},{6,7},{7,4},{8,9},{9,10},{10,1... | collective-permute-start | bytes 786440 | tf_op jit(solution)/shard_map/ppermute | solution.py:41
  78.3 15.3 %collective-permute-start.15 = (bf16[32,4096]{1,0:T(8,128)(2,1)S(1)}, bf16[32,4096]{1,0:T(8,128)(2,1)S(1)}, u32[]{:S(2)}, u32[]{:S(2)}) collective-permute-start(bf16[32,4096]{1,0:T(8,128)(2,1)S(1)} %get-tuple-element.62), channel_id=1, source_target_pairs={{0,12},{1,13},{2,14},{3,15},{4,0},{5,1},{6,2},{7,3},{8,4},{9,5},{1... | collective-permute-start | bytes 786440 | tf_op jit(solution)/shard_map/ppermute | solution.py:41
  78.7 15.4 %collective-permute-start.16 = (bf16[32,4096]{1,0:T(8,128)(2,1)S(1)}, bf16[32,4096]{1,0:T(8,128)(2,1)S(1)}, u32[]{:S(2)}, u32[]{:S(2)}) collective-permute-start(bf16[32,4096]{1,0:T(8,128)(2,1)S(1)} %get-tuple-element.63), channel_id=1, source_target_pairs={{0,3},{1,0},{2,1},{3,2},{4,7},{5,4},{6,5},{7,6},{8,11},{9,8},{10,9... | collective-permute-start | bytes 786440 | tf_op jit(solution)/shard_map/ppermute | solution.py:41
  105.9 14.0 %collective-permute-start.21 = (bf16[975,1000]{1,0:T(8,128)(2,1)}, bf16[975,1000]{1,0:T(8,128)(2,1)}, u32[]{:S(2)}, u32[]{:S(2)}) collective-permute-start(bf16[975,1000]{1,0:T(8,128)(2,1)} %refs_0_), channel_id=1, source_target_pairs={{0,16},{1,17},{2,18},{3,19},{4,20},{5,21},{6,22},{7,23},{8,24},{9,... | collective-permute-start | bytes 5850008 | tf_op jit(solution)/shard_map/ppermute | solution.py:41
  106.0 13.9 %collective-permute-start.22 = (bf16[975,1000]{1,0:T(8,128)(2,1)}, bf16[975,1000]{1,0:T(8,128)(2,1)}, u32[]{:S(2)}, u32[]{:S(2)}) collective-permute-start(bf16[975,1000]{1,0:T(8,128)(2,1)} %collective-permute-done.1.refs_1_), channel_id=1, source_target_pairs={{0,16},{1,17},{2,18},{3,19},{4,20},{5,21},{6,22},{7,23},{8,24},{9,... | collective-permute-start | bytes 5850008 | tf_op jit(solution)/shard_map/ppermute | solution.py:41
  106.5 13.4 %collective-permute-start.23 = (bf16[975,1000]{1,0:T(8,128)(2,1)}, bf16[975,1000]{1,0:T(8,128)(2,1)}, u32[]{:S(2)}, u32[]{:S(2)}) collective-permute-start(bf16[975,1000]{1,0:T(8,128)(2,1)} %collective-permute-done.9.refs_2_), channel_id=1, source_target_pairs={{0,16},{1,17},{2,18},{3,19},{4,20},{5,21},{6,22},{7,23},{8,24},{9,... | collective-permute-start | bytes 5850008 | tf_op jit(solution)/shard_map/ppermute | solution.py:41
  106.6 13.3 %collective-permute-start.24 = (bf16[975,1000]{1,0:T(8,128)(2,1)}, bf16[975,1000]{1,0:T(8,128)(2,1)}, u32[]{:S(2)}, u32[]{:S(2)}) collective-permute-start(bf16[975,1000]{1,0:T(8,128)(2,1)} %collective-permute-done.20.refs_3_), channel_id=1, source_target_pairs={{0,16},{1,17},{2,18},{3,19},{4,20},{5,21},{6,22},{7,23},{8,24},{9,... | collective-permute-start | bytes 5850008 | tf_op jit(solution)/shard_map/ppermute | solution.py:41
  122.7 27.8 %collective-permute-start.26 = (bf16[2,16,1000]{2,1,0:T(8,128)(2,1)S(1)}, bf16[2,16,1000]{2,1,0:T(8,128)(2,1)S(1)}, u32[]{:S(2)}, u32[]{:S(2)}) collective-permute-start(bf16[2,16,1000]{2,1,0:T(8,128)(2,1)S(1)} %get-tuple-element.105), channel_id=1, source_target_pairs={{0,32},{1,33},{2,34},{3,35},{4,36},{5,37},{6,38},{7,39},{8,40},{9,... | collective-permute-start | bytes 192008 | tf_op jit(solution)/shard_map/ppermute | solution.py:41
  122.8 27.7 %collective-permute-start.27 = (bf16[2,16,1000]{2,1,0:T(8,128)(2,1)S(1)}, bf16[2,16,1000]{2,1,0:T(8,128)(2,1)S(1)}, u32[]{:S(2)}, u32[]{:S(2)}) collective-permute-start(bf16[2,16,1000]{2,1,0:T(8,128)(2,1)S(1)} %get-tuple-element.107), channel_id=1, source_target_pairs={{0,96},{1,97},{2,98},{3,99},{4,100},{5,101},{6,102},{7,103},{8,104... | collective-permute-start | bytes 192008 | tf_op jit(solution)/shard_map/ppermute | solution.py:41
  126.0 24.5 %collective-permute-start.28 = (bf16[2,16,1000]{2,1,0:T(8,128)(2,1)S(1)}, bf16[2,16,1000]{2,1,0:T(8,128)(2,1)S(1)}, u32[]{:S(2)}, u32[]{:S(2)}) collective-permute-start(bf16[2,16,1000]{2,1,0:T(8,128)(2,1)S(1)} %get-tuple-element.106), channel_id=1, source_target_pairs={{0,64},{1,65},{2,66},{3,67},{4,68},{5,69},{6,70},{7,71},{8,72},{9,... | collective-permute-start | bytes 192008 | tf_op jit(solution)/shard_map/ppermute | solution.py:41
  173.9 11.8 %collective-permute-start.34 = (bf16[4,32,975]{2,1,0:T(8,128)(2,1)S(1)}, bf16[4,32,975]{2,1,0:T(8,128)(2,1)S(1)}, u32[]{:S(2)}, u32[]{:S(2)}) collective-permute-start(bf16[4,32,975]{2,1,0:T(8,128)(2,1)S(1)} %get-tuple-element.101), channel_id=1, source_target_pairs={{0,12},{1,13},{2,14},{3,15},{4,0},{5,1},{6,2},{7,3},{8,4},{9,5},{1... | collective-permute-start | bytes 748808 | tf_op jit(solution)/shard_map/ppermute | solution.py:41
  (31 other events, 355.5 us)
Sparse Core Ops, SparseCore 0:
  9.8 112.7 all-gather.1

commit v11 on v10

--- a/solution.py
+++ b/solution.py
@@ -310,22 +310,20 @@
     send_d = together(a_l, a_r, b_u)
     send_r = together(b_d, b_u, a_l)
     send_l = together(b_d, b_u, b_r)
-    fits[1], member, send_u, send_d, send_r, send_l, a_u, b_l = after(
-        fits[1], member, send_u, send_d, send_r, send_l, a_u, b_l
+    member, send_u, send_d, send_r, send_l, a_u, b_l = after(
+        member, send_u, send_d, send_r, send_l, a_u, b_l
     )
-    fits.append(ring_z(fits[-1]))
     one_d, one_u = up(send_u), down(send_d)
     one_l, one_r = right(send_r), left(send_l)
 
+    fits[1], member = after(fits[1], member)
+    fits.append(ring_z(fits[-1]))
     rw = -nt(reconstructor, member)
     rw_high = lax.reduce_precision(rw, 8, 7)
     rw_low = jnp.where((lane % LANES < 12)[None, :], rw - rw_high, 0.0)
     rw = jnp.concatenate([rw_high, rw_low], axis=1).astype(jnp.bfloat16)
 
-    rw, fits[2], one_d, one_u, one_l, one_r = after(
-        rw, fits[2], one_d, one_u, one_l, one_r
-    )
-    fits.append(ring_z(fits[-1]))
+    rw, one_d, one_u, one_l, one_r = after(rw, one_d, one_u, one_l, one_r)
     far_x_a, far_y_b = one_l[2 * PART :], one_u[2 * PART :]
     two_d = together(far_x_a, one_d[:PART])
     two_u = together(far_x_a, one_u[PART : 2 * PART])
@@ -337,7 +335,7 @@
 
     get_u, get_r, *ends = after(get_u, get_r, get_d[:PART], get_l[:PART])
     end_d, end_l = up(ends[0]), right(ends[1])
-    end_d, end_l, *fits = after(end_d, end_l, *fits)
+    end_d, end_l, *fits[:2] = after(end_d, end_l, *fits[:2])
 
     arrays = [own_a, own_b, a_l, b_l, a_r, b_r, a_d, b_d, a_u, b_u, one_d, one_u, one_l, one_r]
     arrays += [get_d, get_u, get_l, get_r, end_d, end_l]
@@ -368,8 +366,9 @@
         pieces.append(piece(array_a, block_a, ry, rx, 0))
         pieces.append(piece(array_b, block_b, ry, rx, 1))
     own, other, tail = reconstruct(0, arrays, pieces, position, reconstructor, rw)
-    swapped = [swap_core(f) for f in fits]
-    own, other, *swapped = after(own, other, *swapped)
+    swapped = [swap_core(f) for f in fits[:2]]
+    own, other, fits[2], *swapped = after(own, other, fits[2], *swapped)
+    fits.append(ring_z(fits[-1]))
     picked = picks_by_z(own, other, z)
     terms = spread_by_z(picked)
     terms[0], late = after(terms[0], late)
@@ -379,7 +378,8 @@
         1, [late], [(0, 0, 16 * LATE, 0, 0, side) for side in (0, 1)],
         position, reconstructor, rw, tail,
     )
-    own, other, near = after(own, other, near)
+    own, other, near, *fits[2:] = after(own, other, near, *fits[2:])
+    swapped += [swap_core(f) for f in fits[2:]]
     far = total(spread_by_z(picks_by_z(own, other, z))).astype(jnp.bfloat16)
     points = jnp.concatenate([near, far], axis=1)
 

time: 213 us -> 207 us (0.972)
  waiting for transfers between devices: 78.1 us -> 64.8 us
  starting transfers between devices: 51.5 us -> 57.3 us
    ppermute x42, waiting for transfers between devices: 72.2 us -> 58.8 us  [send(): return lax.ppermute(x, AXES, moved(fn))]
    ppermute x42, starting transfers between devices: 46.1 us -> 51.9 us  [send(): return lax.ppermute(x, AXES, moved(fn))]
  transfers between devices with their start and end apart: 44 -> 44, of which waited for: 24 -> 18; matrix products, arithmetic and copies ran while one was open for 6% -> 8% of each run, Pallas kernels for 20% -> 23%
where the time goes in v11:
time: 207 us; the launch traced here: 206 us
  waiting for transfers between devices  64.8 us (31%)
  starting transfers between devices  57.3 us (28%)
  Pallas kernels  46.7 us (23%)
  between operations  14.1 us (7%)
  matrix products  10.1 us (5%)
  other arithmetic  7.54 us (4%)
  local copies, waits for them, and re-layouts  5.19 us (3%)
    ppermute x42, waiting for transfers between devices, send(): return lax.ppermute(x, AXES, moved(fn))  58.8 us
    ppermute x42, starting transfers between devices, send(): return lax.ppermute(x, AXES, moved(fn))  51.9 us
    pallas_call x2, Pallas kernels, reconstruct(): pl.pallas_call(functools.partial(reconstruct_kernel, tuple(pieces), len(a...  37.3 us
    dot_general x2, matrix products, nt(): lax.dot_general(a, b, (((1,), (1,)), ((), ())), preferred_element_type=jn...  10.1 us
    pallas_call x2, Pallas kernels, fit(): pl.pallas_call(fit_kernel, in_specs=[pl.BlockSpec(memory_space=pltpu.VMEM...  9.38 us
    all_to_all x1, waiting for transfers between devices, per_device(): stats = jnp.sum(lax.all_to_all(stats, 'sens', 0, 0, tiled=True), axis=0)  5.91 us
    all_to_all x1, starting transfers between devices, per_device(): stats = jnp.sum(lax.all_to_all(stats, 'sens', 0, 0, tiled=True), axis=0)  5.4 us
  transfers between devices with their start and end apart: 44, of which 18 were waited for; matrix products, arithmetic and copies ran while one was open for 8% of the time, Pallas kernels for 23%

profile of v11, /device:TPU:24, one launch (start us, length us, event | category | flops | bytes accessed | tf_op | source)
XLA Modules:
  0.0 205.7 jit_solution(3121713639947462157)
XLA Ops:
  15.1 5.4 %all-to-all-start = ((f32[8,72,128]{2,1,0:T(8,128)}), f32[8,72,128]{2,1,0:T(8,128)S(1)}, u32[]{:S(2)}, u32[]{:S(2)}) async-start(f32[8,72,128]{2,1,0:T(8,128)} %broadcast_in_dim.79), calls=%async_computation | async-start | bytes 589824 | tf_op jit(solution)/shard_map/all_to_all | solution.py:296
  22.6 5.9 %all-to-all-done = f32[8,72,128]{2,1,0:T(8,128)S(1)} async-done(((f32[8,72,128]{2,1,0:T(8,128)}), f32[8,72,128]{2,1,0:T(8,128)S(1)}, u32[]{:S(2)}, u32[]{:S(2)}) %all-to-all-start) | async-done | bytes 294944 | tf_op jit(solution)/shard_map/all_to_all | solution.py:296
  34.8 4.2 %collective-permute-done.3.refs_9_ = bf16[16,4096]{1,0:T(8,128)(2,1)S(1)} collective-permute-done((bf16[16,4096]{1,0:T(8,128)(2,1)S(1)}, bf16[16,4096]{1,0:T(8,128)(2,1)S(1)}, u32[]{:S(2)}, u32[]{:S(2)}) %collective-permute-start.3) | collective-permute-done | bytes 131104 | tf_op jit(solution)/shard_map/ppermute | solution.py:41
  40.2 3.3 %collective-permute-done.6.refs_8_ = bf16[16,4096]{1,0:T(8,128)(2,1)S(1)} collective-permute-done((bf16[16,4096]{1,0:T(8,128)(2,1)S(1)}, bf16[16,4096]{1,0:T(8,128)(2,1)S(1)}, u32[]{:S(2)}, u32[]{:S(2)}) %collective-permute-start.6) | collective-permute-done | bytes 131104 | tf_op jit(solution)/shard_map/ppermute | solution.py:41
  45.8 3.2 %collective-permute-start.12 = (bf16[48,4096]{1,0:T(8,128)(2,1)S(1)}, bf16[48,4096]{1,0:T(8,128)(2,1)S(1)}, u32[]{:S(2)}, u32[]{:S(2)}) collective-permute-start(bf16[48,4096]{1,0:T(8,128)(2,1)S(1)} %get-tuple-element.55), channel_id=1, source_target_pairs={{0,3},{1,0},{2,1},{3,2},{4,7},{5,4},{6,5},{7,6},{8,11},{9,8},{10,9... | collective-permute-start | bytes 1179656 | tf_op jit(solution)/shard_map/ppermute | solution.py:41
  49.0 2.6 %collective-permute-start.9 = (bf16[48,4096]{1,0:T(8,128)(2,1)S(1)}, bf16[48,4096]{1,0:T(8,128)(2,1)S(1)}, u32[]{:S(2)}, u32[]{:S(2)}) collective-permute-start(bf16[48,4096]{1,0:T(8,128)(2,1)S(1)} %get-tuple-element.52), channel_id=1, source_target_pairs={{0,4},{1,5},{2,6},{3,7},{4,8},{5,9},{6,10},{7,11},{8,12},{9,13},{1... | collective-permute-start | bytes 1179656 | tf_op jit(solution)/shard_map/ppermute | solution.py:41
  51.6 9.1 %reduce-precision_convert_fusion = (bf16[1000,128]{1,0:T(8,128)(2,1)S(1)}, bf16[1000,128]{1,0:T(8,128)(2,1)S(1)}) fusion(pred[128]{0:T(512)(128)(4,1)S(1)} %get-tuple-element.120, bf16[128,7950]{1,0:T(8,128)(2,1)S(1)} %fusion, bf16[1000,7950]{1,0:T(8,128)(2,1)} %refs_3_.1), kind=kOutput, calls=%fused_computation.13 | convolution fusion | flops 2035968000 | bytes 18447328 | tf_op jit(solution)/shard_map/dot_general | solution.py:85
  61.6 2.6 %collective-permute-done.9.refs_10_ = bf16[48,4096]{1,0:T(8,128)(2,1)S(1)} collective-permute-done((bf16[48,4096]{1,0:T(8,128)(2,1)S(1)}, bf16[48,4096]{1,0:T(8,128)(2,1)S(1)}, u32[]{:S(2)}, u32[]{:S(2)}) %collective-permute-start.9) | collective-permute-done | bytes 393248 | tf_op jit(solution)/shard_map/ppermute | solution.py:41
  64.5 3.8 %collective-permute-start.13 = (bf16[32,4096]{1,0:T(8,128)(2,1)S(1)}, bf16[32,4096]{1,0:T(8,128)(2,1)S(1)}, u32[]{:S(2)}, u32[]{:S(2)}) collective-permute-start(bf16[32,4096]{1,0:T(8,128)(2,1)S(1)} %get-tuple-element.60), channel_id=1, source_target_pairs={{0,4},{1,5},{2,6},{3,7},{4,8},{5,9},{6,10},{7,11},{8,12},{9,13},{1... | collective-permute-start | bytes 786440 | tf_op jit(solution)/shard_map/ppermute | solution.py:41
  68.2 3.2 %collective-permute-start.15 = (bf16[32,4096]{1,0:T(8,128)(2,1)S(1)}, bf16[32,4096]{1,0:T(8,128)(2,1)S(1)}, u32[]{:S(2)}, u32[]{:S(2)}) collective-permute-start(bf16[32,4096]{1,0:T(8,128)(2,1)S(1)} %get-tuple-element.62), channel_id=1, source_target_pairs={{0,3},{1,0},{2,1},{3,2},{4,7},{5,4},{6,5},{7,6},{8,11},{9,8},{10,9... | collective-permute-start | bytes 786440 | tf_op jit(solution)/shard_map/ppermute | solution.py:41
  71.5 7.4 %collective-permute-done.13.refs_14_ = bf16[32,4096]{1,0:T(8,128)(2,1)S(1)} collective-permute-done((bf16[32,4096]{1,0:T(8,128)(2,1)S(1)}, bf16[32,4096]{1,0:T(8,128)(2,1)S(1)}, u32[]{:S(2)}, u32[]{:S(2)}) %collective-permute-start.13) | collective-permute-done | bytes 262176 | tf_op jit(solution)/shard_map/ppermute | solution.py:41
  78.9 3.4 %collective-permute-done.16.refs_16_ = bf16[32,4096]{1,0:T(8,128)(2,1)S(1)} collective-permute-done((bf16[32,4096]{1,0:T(8,128)(2,1)S(1)}, bf16[32,4096]{1,0:T(8,128)(2,1)S(1)}, u32[]{:S(2)}, u32[]{:S(2)}) %collective-permute-start.16) | collective-permute-done | bytes 262176 | tf_op jit(solution)/shard_map/ppermute | solution.py:41
  84.3 6.4 %collective-permute-done.17.refs_18_ = bf16[16,4096]{1,0:T(8,128)(2,1)S(1)} collective-permute-done((bf16[16,4096]{1,0:T(8,128)(2,1)S(1)}, bf16[16,4096]{1,0:T(8,128)(2,1)S(1)}, u32[]{:S(2)}, u32[]{:S(2)}) %collective-permute-start.17) | collective-permute-done | bytes 131104 | tf_op jit(solution)/shard_map/ppermute | solution.py:41
  90.8 2.8 %collective-permute-done.18.refs_19_ = bf16[16,4096]{1,0:T(8,128)(2,1)S(1)} collective-permute-done((bf16[16,4096]{1,0:T(8,128)(2,1)S(1)}, bf16[16,4096]{1,0:T(8,128)(2,1)S(1)}, u32[]{:S(2)}, u32[]{:S(2)}) %collective-permute-start.18) | collective-permute-done | bytes 131104 | tf_op jit(solution)/shard_map/ppermute | solution.py:41
  94.2 12.9 %shard_map.55 = (f32[128,1000]{1,0:T(8,128)}, bf16[128,1000]{1,0:T(8,128)(2,1)S(1)}, bf16[256,128]{1,0:T(8,128)(2,1)S(1)}) custom-call(bf16[16,4096]{1,0:T(8,128)(2,1)S(1)} %slice.70.refs_0_, bf16[16,4096]{1,0:T(8,128)(2,1)S(1)} %pad_add_fusion.refs_1_, bf16[16,4096]{1,0:T(8,128)(2,1)S(1)} %collective-permute-done.refs_2_, ...), custom_call_target="tpu_custom_call" | custom-call | tf_op jit(solution)/shard_map/pallas_call | solution.py:183
  107.1 3.6 %collective-permute-done.19.refs_2_ = bf16[975,1000]{1,0:T(8,128)(2,1)} collective-permute-done((bf16[975,1000]{1,0:T(8,128)(2,1)}, bf16[975,1000]{1,0:T(8,128)(2,1)}, u32[]{:S(2)}, u32[]{:S(2)}) %collective-permute-start.19) | collective-permute-done | bytes 1950032 | tf_op jit(solution)/shard_map/ppermute | solution.py:41
  113.6 3.2 %collective-permute-start.24 = (bf16[2,16,1000]{2,1,0:T(8,128)(2,1)S(1)}, bf16[2,16,1000]{2,1,0:T(8,128)(2,1)S(1)}, u32[]{:S(2)}, u32[]{:S(2)}) collective-permute-start(bf16[2,16,1000]{2,1,0:T(8,128)(2,1)S(1)} %get-tuple-element.105), channel_id=1, source_target_pairs={{0,96},{1,97},{2,98},{3,99},{4,100},{5,101},{6,102},{7,103},{8,104... | collective-permute-start | bytes 192008 | tf_op jit(solution)/shard_map/ppermute | solution.py:41
  118.2 24.4 %shard_map.56 = (f32[384,1000]{1,0:T(8,128)}, bf16[384,1000]{1,0:T(8,128)(2,1)S(1)}) custom-call(bf16[768,8064]{1,0:T(8,128)(2,1)} %all-gather.2.cloned.1.call-done.refs_0_, s32[3]{0:T(128)S(1)} %pad_add_fusion.1.refs_20_.refs_1_, bf16[1000,7950]{1,0:T(8,128)(2,1)} %refs_3_.1, bf16[1000,7950]{1,0:T(8,128)(2,1)} %refs_3_.1, bf16[1000,256]{1,0:T(8,128)(2,1)S(1)} %copy-done, ...), custom_call_target="tpu_custom_call" | custom-call | tf_op jit(solution)/shard_map/pallas_call | solution.py:183
  151.9 8.2 %collective-permute-done.28 = bf16[2,48,1000]{2,1,0:T(8,128)(2,1)S(1)} collective-permute-done((bf16[2,48,1000]{2,1,0:T(8,128)(2,1)S(1)}, bf16[2,48,1000]{2,1,0:T(8,128)(2,1)S(1)}, u32[]{:S(2)}, u32[]{:S(2)}) %collective-permute-start.28) | collective-permute-done | bytes 192032 | tf_op jit(solution)/shard_map/ppermute | solution.py:41
  160.3 4.7 %shard_map.57 = bf16[4,128,975]{2,1,0:T(8,128)(2,1)S(1)} custom-call(bf16[128,1000]{1,0:T(8,128)(2,1)S(1)} %bitcast.94, bf16[975,1000]{1,0:T(8,128)(2,1)} %refs_0_, bf16[975,1000]{1,0:T(8,128)(2,1)} %collective-permute-done.8.refs_1_, bf16[975,1000]{1,0:T(8,128)(2,1)} %collective-permute-done.19.refs_2_, bf16[975,1000]{1,0:T(8,128)(2,1)} %collective-permute-done.26.refs_3_), custom_call_target="tpu_custom_call" | custom-call | tf_op jit(solution)/shard_map/pallas_call | solution.py:215
  168.0 4.7 %shard_map.58 = bf16[4,128,975]{2,1,0:T(8,128)(2,1)S(1)} custom-call(bf16[128,1000]{1,0:T(8,128)(2,1)S(1)} %bitcast.95, bf16[975,1000]{1,0:T(8,128)(2,1)} %collective-permute-done.20.refs_0_, bf16[975,1000]{1,0:T(8,128)(2,1)} %collective-permute-done.21.refs_1_, bf16[975,1000]{1,0:T(8,128)(2,1)} %collective-permute-done.34.refs_2_, ...), custom_call_target="tpu_custom_call" | custom-call | tf_op jit(solution)/shard_map/pallas_call | solution.py:215
  172.8 2.7 %collective-permute-start.36 = (bf16[4,32,975]{2,1,0:T(8,128)(2,1)S(1)}, bf16[4,32,975]{2,1,0:T(8,128)(2,1)S(1)}, u32[]{:S(2)}, u32[]{:S(2)}) collective-permute-start(bf16[4,32,975]{2,1,0:T(8,128)(2,1)S(1)} %get-tuple-element.100), channel_id=1, source_target_pairs={{0,4},{1,5},{2,6},{3,7},{4,8},{5,9},{6,10},{7,11},{8,12},{9,13},{1... | collective-permute-start | bytes 748808 | tf_op jit(solution)/shard_map/ppermute | solution.py:41
  179.4 6.5 %collective-permute-done.37 = bf16[4,32,975]{2,1,0:T(8,128)(2,1)S(1)} collective-permute-done((bf16[4,32,975]{2,1,0:T(8,128)(2,1)S(1)}, bf16[4,32,975]{2,1,0:T(8,128)(2,1)S(1)}, u32[]{:S(2)}, u32[]{:S(2)}) %collective-permute-start.37) | collective-permute-done | bytes 249632 | tf_op jit(solution)/shard_map/ppermute | solution.py:41
  189.6 4.6 %collective-permute-start.41 = (bf16[8,8,975]{2,1,0:T(8,128)(2,1)S(1)}, bf16[8,8,975]{2,1,0:T(8,128)(2,1)S(1)}, u32[]{:S(2)}, u32[]{:S(2)}) collective-permute-start(bf16[8,8,975]{2,1,0:T(8,128)(2,1)S(1)} %get-tuple-element.96), channel_id=1, source_target_pairs={{0,2},{1,3},{2,0},{3,1},{4,6},{5,7},{6,4},{7,5},{8,10},{9,11},{10,... | collective-permute-start | bytes 374408 | tf_op jit(solution)/shard_map/ppermute | solution.py:41
  (146 shorter events, 52.8 us)
Async XLA Ops:
  6.5 111.7 %all-gather.2.cloned.1.call-start = ((), (), s32[]{:S(2)}) async-start(), calls=%async_computation.1 | async-start | bytes 13160448 | tf_op jit(solution)/shard_map/all_gather | solution.py:280
  9.7 20.7 %collective-permute-start = (bf16[16,4096]{1,0:T(8,128)(2,1)S(1)}, bf16[16,4096]{1,0:T(8,128)(2,1)S(1)}, u32[]{:S(2)}, u32[]{:S(2)}) collective-permute-start(bf16[16,4096]{1,0:T(8,128)(2,1)S(1)} %slice.70.refs_0_), channel_id=1, source_target_pairs={{0,1},{1,2},{2,3},{3,0},{4,5},{5,6},{6,7},{7,4},{8,9},{9,10},{10,1... | collective-permute-start | bytes 393224 | tf_op jit(solution)/shard_map/ppermute | solution.py:41
  11.3 20.6 %collective-permute-start.1 = (bf16[16,4096]{1,0:T(8,128)(2,1)S(1)}, bf16[16,4096]{1,0:T(8,128)(2,1)S(1)}, u32[]{:S(2)}, u32[]{:S(2)}) collective-permute-start(bf16[16,4096]{1,0:T(8,128)(2,1)S(1)} %slice.70.refs_0_), channel_id=1, source_target_pairs={{0,3},{1,0},{2,1},{3,2},{4,7},{5,4},{6,5},{7,6},{8,11},{9,8},{10,9... | collective-permute-start | bytes 393224 | tf_op jit(solution)/shard_map/ppermute | solution.py:41
  13.0 21.1 %collective-permute-start.2 = (bf16[16,4096]{1,0:T(8,128)(2,1)S(1)}, bf16[16,4096]{1,0:T(8,128)(2,1)S(1)}, u32[]{:S(2)}, u32[]{:S(2)}) collective-permute-start(bf16[16,4096]{1,0:T(8,128)(2,1)S(1)} %slice.70.refs_0_), channel_id=1, source_target_pairs={{0,4},{1,5},{2,6},{3,7},{4,8},{5,9},{6,10},{7,11},{8,12},{9,13},{1... | collective-permute-start | bytes 393224 | tf_op jit(solution)/shard_map/ppermute | solution.py:41
  15.1 13.4 %all-to-all-start = ((f32[8,72,128]{2,1,0:T(8,128)}), f32[8,72,128]{2,1,0:T(8,128)S(1)}, u32[]{:S(2)}, u32[]{:S(2)}) async-start(f32[8,72,128]{2,1,0:T(8,128)} %broadcast_in_dim.79), calls=%async_computation | async-start | bytes 589824 | tf_op jit(solution)/shard_map/all_to_all | solution.py:296
  20.5 31.2 %collective-permute-start.8 = (bf16[975,1000]{1,0:T(8,128)(2,1)}, bf16[975,1000]{1,0:T(8,128)(2,1)}, u32[]{:S(2)}, u32[]{:S(2)}) collective-permute-start(bf16[975,1000]{1,0:T(8,128)(2,1)} %refs_0_), channel_id=1, source_target_pairs={{0,32},{1,33},{2,34},{3,35},{4,36},{5,37},{6,38},{7,39},{8,40},{9,... | collective-permute-start | bytes 5850008 | tf_op jit(solution)/shard_map/ppermute | solution.py:41
  45.2 16.5 %collective-permute-start.10 = (bf16[48,4096]{1,0:T(8,128)(2,1)S(1)}, bf16[48,4096]{1,0:T(8,128)(2,1)S(1)}, u32[]{:S(2)}, u32[]{:S(2)}) collective-permute-start(bf16[48,4096]{1,0:T(8,128)(2,1)S(1)} %get-tuple-element.53), channel_id=1, source_target_pairs={{0,12},{1,13},{2,14},{3,15},{4,0},{5,1},{6,2},{7,3},{8,4},{9,5},{1... | collective-permute-start | bytes 1179656 | tf_op jit(solution)/shard_map/ppermute | solution.py:41
  45.8 15.9 %collective-permute-start.11 = (bf16[48,4096]{1,0:T(8,128)(2,1)S(1)}, bf16[48,4096]{1,0:T(8,128)(2,1)S(1)}, u32[]{:S(2)}, u32[]{:S(2)}) collective-permute-start(bf16[48,4096]{1,0:T(8,128)(2,1)S(1)} %get-tuple-element.54), channel_id=1, source_target_pairs={{0,1},{1,2},{2,3},{3,0},{4,5},{5,6},{6,7},{7,4},{8,9},{9,10},{10,1... | collective-permute-start | bytes 1179656 | tf_op jit(solution)/shard_map/ppermute | solution.py:41
  45.8 15.9 %collective-permute-start.12 = (bf16[48,4096]{1,0:T(8,128)(2,1)S(1)}, bf16[48,4096]{1,0:T(8,128)(2,1)S(1)}, u32[]{:S(2)}, u32[]{:S(2)}) collective-permute-start(bf16[48,4096]{1,0:T(8,128)(2,1)S(1)} %get-tuple-element.55), channel_id=1, source_target_pairs={{0,3},{1,0},{2,1},{3,2},{4,7},{5,4},{6,5},{7,6},{8,11},{9,8},{10,9... | collective-permute-start | bytes 1179656 | tf_op jit(solution)/shard_map/ppermute | solution.py:41
  49.0 15.3 %collective-permute-start.9 = (bf16[48,4096]{1,0:T(8,128)(2,1)S(1)}, bf16[48,4096]{1,0:T(8,128)(2,1)S(1)}, u32[]{:S(2)}, u32[]{:S(2)}) collective-permute-start(bf16[48,4096]{1,0:T(8,128)(2,1)S(1)} %get-tuple-element.52), channel_id=1, source_target_pairs={{0,4},{1,5},{2,6},{3,7},{4,8},{5,9},{6,10},{7,11},{8,12},{9,13},{1... | collective-permute-start | bytes 1179656 | tf_op jit(solution)/shard_map/ppermute | solution.py:41
  64.5 14.4 %collective-permute-start.13 = (bf16[32,4096]{1,0:T(8,128)(2,1)S(1)}, bf16[32,4096]{1,0:T(8,128)(2,1)S(1)}, u32[]{:S(2)}, u32[]{:S(2)}) collective-permute-start(bf16[32,4096]{1,0:T(8,128)(2,1)S(1)} %get-tuple-element.60), channel_id=1, source_target_pairs={{0,4},{1,5},{2,6},{3,7},{4,8},{5,9},{6,10},{7,11},{8,12},{9,13},{1... | collective-permute-start | bytes 786440 | tf_op jit(solution)/shard_map/ppermute | solution.py:41
  68.2 14.0 %collective-permute-start.16 = (bf16[32,4096]{1,0:T(8,128)(2,1)S(1)}, bf16[32,4096]{1,0:T(8,128)(2,1)S(1)}, u32[]{:S(2)}, u32[]{:S(2)}) collective-permute-start(bf16[32,4096]{1,0:T(8,128)(2,1)S(1)} %get-tuple-element.63), channel_id=1, source_target_pairs={{0,1},{1,2},{2,3},{3,0},{4,5},{5,6},{6,7},{7,4},{8,9},{9,10},{10,1... | collective-permute-start | bytes 786440 | tf_op jit(solution)/shard_map/ppermute | solution.py:41
  68.2 14.0 %collective-permute-start.14 = (bf16[32,4096]{1,0:T(8,128)(2,1)S(1)}, bf16[32,4096]{1,0:T(8,128)(2,1)S(1)}, u32[]{:S(2)}, u32[]{:S(2)}) collective-permute-start(bf16[32,4096]{1,0:T(8,128)(2,1)S(1)} %get-tuple-element.61), channel_id=1, source_target_pairs={{0,12},{1,13},{2,14},{3,15},{4,0},{5,1},{6,2},{7,3},{8,4},{9,5},{1... | collective-permute-start | bytes 786440 | tf_op jit(solution)/shard_map/ppermute | solution.py:41
  68.2 14.7 %collective-permute-start.15 = (bf16[32,4096]{1,0:T(8,128)(2,1)S(1)}, bf16[32,4096]{1,0:T(8,128)(2,1)S(1)}, u32[]{:S(2)}, u32[]{:S(2)}) collective-permute-start(bf16[32,4096]{1,0:T(8,128)(2,1)S(1)} %get-tuple-element.62), channel_id=1, source_target_pairs={{0,3},{1,0},{2,1},{3,2},{4,7},{5,4},{6,5},{7,6},{8,11},{9,8},{10,9... | collective-permute-start | bytes 786440 | tf_op jit(solution)/shard_map/ppermute | solution.py:41
  84.2 26.5 %collective-permute-start.19 = (bf16[975,1000]{1,0:T(8,128)(2,1)}, bf16[975,1000]{1,0:T(8,128)(2,1)}, u32[]{:S(2)}, u32[]{:S(2)}) collective-permute-start(bf16[975,1000]{1,0:T(8,128)(2,1)} %collective-permute-done.8.refs_1_), channel_id=1, source_target_pairs={{0,32},{1,33},{2,34},{3,35},{4,36},{5,37},{6,38},{7,39},{8,40},{9,... | collective-permute-start | bytes 5850008 | tf_op jit(solution)/shard_map/ppermute | solution.py:41
  93.6 17.1 %collective-permute-start.20 = (bf16[975,1000]{1,0:T(8,128)(2,1)}, bf16[975,1000]{1,0:T(8,128)(2,1)}, u32[]{:S(2)}, u32[]{:S(2)}) collective-permute-start(bf16[975,1000]{1,0:T(8,128)(2,1)} %refs_0_), channel_id=1, source_target_pairs={{0,16},{1,17},{2,18},{3,19},{4,20},{5,21},{6,22},{7,23},{8,24},{9,... | collective-permute-start | bytes 5850008 | tf_op jit(solution)/shard_map/ppermute | solution.py:41
  93.6 17.1 %collective-permute-start.21 = (bf16[975,1000]{1,0:T(8,128)(2,1)}, bf16[975,1000]{1,0:T(8,128)(2,1)}, u32[]{:S(2)}, u32[]{:S(2)}) collective-permute-start(bf16[975,1000]{1,0:T(8,128)(2,1)} %collective-permute-done.8.refs_1_), channel_id=1, source_target_pairs={{0,16},{1,17},{2,18},{3,19},{4,20},{5,21},{6,22},{7,23},{8,24},{9,... | collective-permute-start | bytes 5850008 | tf_op jit(solution)/shard_map/ppermute | solution.py:41
  110.7 32.0 %collective-permute-start.26 = (bf16[975,1000]{1,0:T(8,128)(2,1)}, bf16[975,1000]{1,0:T(8,128)(2,1)}, u32[]{:S(2)}, u32[]{:S(2)}) collective-permute-start(bf16[975,1000]{1,0:T(8,128)(2,1)} %collective-permute-done.19.refs_2_), channel_id=1, source_target_pairs={{0,32},{1,33},{2,34},{3,35},{4,36},{5,37},{6,38},{7,39},{8,40},{9,... | collective-permute-start | bytes 5850008 | tf_op jit(solution)/shard_map/ppermute | solution.py:41
  113.5 29.2 %collective-permute-start.23 = (bf16[2,16,1000]{2,1,0:T(8,128)(2,1)S(1)}, bf16[2,16,1000]{2,1,0:T(8,128)(2,1)S(1)}, u32[]{:S(2)}, u32[]{:S(2)}) collective-permute-start(bf16[2,16,1000]{2,1,0:T(8,128)(2,1)S(1)} %get-tuple-element.103), channel_id=1, source_target_pairs={{0,32},{1,33},{2,34},{3,35},{4,36},{5,37},{6,38},{7,39},{8,40},{9,... | collective-permute-start | bytes 192008 | tf_op jit(solution)/shard_map/ppermute | solution.py:41
  113.6 29.1 %collective-permute-start.24 = (bf16[2,16,1000]{2,1,0:T(8,128)(2,1)S(1)}, bf16[2,16,1000]{2,1,0:T(8,128)(2,1)S(1)}, u32[]{:S(2)}, u32[]{:S(2)}) collective-permute-start(bf16[2,16,1000]{2,1,0:T(8,128)(2,1)S(1)} %get-tuple-element.105), channel_id=1, source_target_pairs={{0,96},{1,97},{2,98},{3,99},{4,100},{5,101},{6,102},{7,103},{8,104... | collective-permute-start | bytes 192008 | tf_op jit(solution)/shard_map/ppermute | solution.py:41
  116.8 25.9 %collective-permute-start.25 = (bf16[2,16,1000]{2,1,0:T(8,128)(2,1)S(1)}, bf16[2,16,1000]{2,1,0:T(8,128)(2,1)S(1)}, u32[]{:S(2)}, u32[]{:S(2)}) collective-permute-start(bf16[2,16,1000]{2,1,0:T(8,128)(2,1)S(1)} %get-tuple-element.104), channel_id=1, source_target_pairs={{0,64},{1,65},{2,66},{3,67},{4,68},{5,69},{6,70},{7,71},{8,72},{9,... | collective-permute-start | bytes 192008 | tf_op jit(solution)/shard_map/ppermute | solution.py:41
  143.2 24.8 %collective-permute-start.34 = (bf16[975,1000]{1,0:T(8,128)(2,1)}, bf16[975,1000]{1,0:T(8,128)(2,1)}, u32[]{:S(2)}, u32[]{:S(2)}) collective-permute-start(bf16[975,1000]{1,0:T(8,128)(2,1)} %collective-permute-done.19.refs_2_), channel_id=1, source_target_pairs={{0,16},{1,17},{2,18},{3,19},{4,20},{5,21},{6,22},{7,23},{8,24},{9,... | collective-permute-start | bytes 5850008 | tf_op jit(solution)/shard_map/ppermute | solution.py:41
  143.7 24.3 %collective-permute-start.35 = (bf16[975,1000]{1,0:T(8,128)(2,1)}, bf16[975,1000]{1,0:T(8,128)(2,1)}, u32[]{:S(2)}, u32[]{:S(2)}) collective-permute-start(bf16[975,1000]{1,0:T(8,128)(2,1)} %collective-permute-done.26.refs_3_), channel_id=1, source_target_pairs={{0,16},{1,17},{2,18},{3,19},{4,20},{5,21},{6,22},{7,23},{8,24},{9,... | collective-permute-start | bytes 5850008 | tf_op jit(solution)/shard_map/ppermute | solution.py:41
  147.7 12.4 %collective-permute-start.28 = (bf16[2,48,1000]{2,1,0:T(8,128)(2,1)S(1)}, bf16[2,48,1000]{2,1,0:T(8,128)(2,1)S(1)}, u32[]{:S(2)}, u32[]{:S(2)}) collective-permute-start(bf16[2,48,1000]{2,1,0:T(8,128)(2,1)S(1)} %get-tuple-element.91), channel_id=1, source_target_pairs={{0,32},{1,33},{2,34},{3,35},{4,36},{5,37},{6,38},{7,39},{8,40},{9,... | collective-permute-start | bytes 576008 | tf_op jit(solution)/shard_map/ppermute | solution.py:41
  (31 other events, 352.0 us)
Sparse Core Ops, SparseCore 0:
  9.8 105.6 all-gather.1
